TPU v7x, 32 devices: a whole 2x2x4 slice. The times are simulated.
32 devices in a mesh: tok: 8 (over y, x, core), tab: 4 (over z).
Axes of the slice: x: 2, y: 2, z: 4, core: 2. Of those that a mesh axis runs over, the one named last changes fastest.
Arguments:
- embedded: bfloat16 [32768, 1024], P(('tok', 'tab')), may hold values from -6 to 6
- cell_index: int32 [64, 512], P(('tok', 'tab')), may hold values from 0 to 127, never falling along the last dimension, each value on 1 to 60 neighbouring positions
- cell_boxes: int32 [64, 4, 512], P(('tok', 'tab')), may hold values from 0 to 1000
- box_tables: bfloat16 [4, 1001, 1024], P('tab'), may hold values from -2.390625 to 2.390625
- joined_weight: bfloat16 [1024, 3072], replicated, may hold values from -0.25 to 0.25
- output_weight: bfloat16 [1024, 1024], replicated, may hold values from -0.75 to 0.75
- expand_weight: bfloat16 [1024, 4096], replicated, may hold values from -0.1875 to 0.1875
- reduce_weight: bfloat16 [4096, 1024], replicated, may hold values from -0.09375 to 0.09375
- hidden_bias: float32 [4096], replicated, may hold values from -3 to 3
- bias_rows: float32 [4, 1024], replicated, may hold values from -3 to 3
- norm_gains: float32 [3, 1024], replicated, may hold values from 0.5 to 1.5
- norm_shifts: float32 [3, 1024], replicated, may hold values from -1.8 to 1.8
- cotangent: bfloat16 [32768, 1024], P(('tok', 'tab')), may hold values from -6 to 6
Outputs:
- layer_out: bfloat16 [32768, 1024], P(('tok', 'tab'))
- embedded_grad: float32 [32768, 1024], P(('tok', 'tab'))
- tables_grad: float32 [4, 1001, 1024], P('tab')
- joined_grad: float32 [1024, 3072], P('tok', 'tab')
- output_grad: float32 [1024, 1024], P('tok', 'tab')
- expand_grad: float32 [1024, 4096], P('tok', 'tab')
- reduce_grad: float32 [4096, 1024], P('tok', 'tab')
- hidden_bias_grad: float32 [4096], replicated
- biases_grad: float32 [4, 1024], replicated
- gains_grad: float32 [3, 1024], replicated
- shifts_grad: float32 [3, 1024], replicated
Inputs may be any that keep to these rules, and one draw needn't show every extreme that they name: `cell_index`: within a page the cell slot never falls from token to token, and each cell holds 1 to 60 tokens.
All inputs are finite; a program needn't handle non-finite values.
Results may differ from a plain program's by a relative error of at most 0.035.
Values may be sent and summed in bfloat16 or wider, within the bound.
A program may use at most 256 MiB of HBM per device.

v0:
```python
import jax
import jax.numpy as jnp
from jax import lax
from jax.sharding import PartitionSpec as P

HEADS = 16
HEAD_DIM = 64


EPSILON = 1e-05


def layer_norm(values, gain_row, shift_row):
    average = jnp.mean(values, axis=-1, keepdims=True)
    centred = values - average
    variance = jnp.mean(centred * centred, axis=-1, keepdims=True)
    return centred * lax.rsqrt(variance + EPSILON) * gain_row + shift_row


def gelu_exact(values):
    return jax.nn.gelu(values, approximate=False)


def box_indices(cell_index, cell_boxes):
    chosen = jnp.take_along_axis(
        cell_boxes, jnp.broadcast_to(cell_index[:, None, :], cell_boxes.shape), axis=2
    )
    left_edge = jnp.minimum(chosen[:, 0], chosen[:, 2]).reshape(-1)
    right_edge = jnp.maximum(chosen[:, 0], chosen[:, 2]).reshape(-1)
    top_edge = jnp.minimum(chosen[:, 1], chosen[:, 3]).reshape(-1)
    bottom_edge = jnp.maximum(chosen[:, 1], chosen[:, 3]).reshape(-1)
    return (
        left_edge,
        right_edge,
        top_edge,
        bottom_edge,
        right_edge - left_edge,
        bottom_edge - top_edge,
    )


def split_heads(values):
    length, width = values.shape
    return values.reshape(length, HEADS, width // HEADS)


def page_forward(operands):
    queries, keys_page, values_page = operands
    length, width = queries.shape
    scores = jnp.einsum(
        "qhd,khd->hqk",
        split_heads(queries),
        split_heads(keys_page),
        preferred_element_type=jnp.float32,
    )
    highest = jnp.max(scores, axis=-1, keepdims=True)
    raised = jnp.exp(scores - highest)
    totals = jnp.sum(raised, axis=-1, keepdims=True)
    weights_soft = (raised / totals).astype(jnp.bfloat16)
    mixed = jnp.einsum(
        "hqk,khd->qhd", weights_soft, split_heads(values_page), preferred_element_type=jnp.float32
    )
    return (mixed.reshape(length, width), (highest + jnp.log(totals))[..., 0])


def page_backward(operands):
    queries, keys_page, values_page, log_totals, grad_mixed = operands
    length, width = queries.shape
    split_query = split_heads(queries)
    split_key = split_heads(keys_page)
    split_grad = split_heads(grad_mixed)
    scores = jnp.einsum("qhd,khd->hqk", split_query, split_key, preferred_element_type=jnp.float32)
    probs = jnp.exp(scores - log_totals[..., None])
    grad_probs = jnp.einsum(
        "qhd,khd->hqk", split_grad, split_heads(values_page), preferred_element_type=jnp.float32
    )
    grad_values = jnp.einsum(
        "hqk,qhd->khd", probs.astype(jnp.bfloat16), split_grad, preferred_element_type=jnp.float32
    )
    grad_scores = (
        probs * (grad_probs - jnp.sum(probs * grad_probs, axis=-1, keepdims=True))
    ).astype(jnp.bfloat16)
    grad_queries = jnp.einsum(
        "hqk,khd->qhd", grad_scores, split_key, preferred_element_type=jnp.float32
    )
    grad_keys = jnp.einsum(
        "hqk,qhd->khd", grad_scores, split_query, preferred_element_type=jnp.float32
    )
    return (
        grad_queries.reshape(length, width).astype(jnp.bfloat16),
        grad_keys.reshape(length, width).astype(jnp.bfloat16),
        grad_values.reshape(length, width).astype(jnp.bfloat16),
    )


def body(
    embedded,
    cell_index,
    cell_boxes,
    box_tables,
    joined_weight,
    output_weight,
    expand_weight,
    reduce_weight,
    hidden_bias,
    bias_rows,
    norm_gains,
    norm_shifts,
    cotangent,
):
    token_rows, width = embedded.shape
    page_count, page_length = cell_index.shape
    wide = jnp.float32
    narrow = jnp.bfloat16
    score_scale = HEAD_DIM ** (-0.5)
    left_edge, right_edge, top_edge, bottom_edge, across, upward = box_indices(
        cell_index, cell_boxes
    )
    index_table = jnp.stack(
        [
            jnp.stack([left_edge, right_edge]),
            jnp.stack([top_edge, bottom_edge]),
            jnp.stack([across, across]),
            jnp.stack([upward, upward]),
        ]
    )
    group_index = lax.all_to_all(index_table, "tab", split_axis=0, concat_axis=2, tiled=True)[0]
    owner_index = lax.axis_index("tab")
    factor = jnp.where(owner_index < 2, 1.0, 0.5).astype(wide)
    own_table = box_tables[0]
    table_rows = own_table.shape[0]
    first_rows = group_index[0]
    second_rows = group_index[1]
    picked_first = jnp.take(own_table, first_rows, axis=0).astype(wide)
    picked_second = jnp.take(own_table, second_rows, axis=0).astype(wide)
    box_embed = lax.psum_scatter(
        (factor * (picked_first + picked_second)).astype(jnp.bfloat16),
        "tab",
        scatter_dimension=0,
        tiled=True,
    ).astype(jnp.float32)
    normed, first_pull = jax.vjp(
        layer_norm, embedded.astype(wide) + box_embed, norm_gains[0], norm_shifts[0]
    )
    normed_low = normed.astype(narrow)
    joined = jnp.dot(normed_low, joined_weight, preferred_element_type=wide)
    queries = ((joined[:, :width] + bias_rows[0]) * score_scale).astype(narrow)
    keys_all = joined[:, width : 2 * width].astype(narrow)
    values_all = (joined[:, 2 * width :] + bias_rows[1]).astype(narrow)
    paged = (page_count, page_length, width)
    paged_query = queries.reshape(paged)
    paged_key = keys_all.reshape(paged)
    paged_value = values_all.reshape(paged)
    mixed, log_totals = lax.map(page_forward, (paged_query, paged_key, paged_value))
    mixed_low = mixed.reshape(token_rows, width).astype(narrow)
    attn_sum = normed + (
        jnp.dot(mixed_low, output_weight, preferred_element_type=wide) + bias_rows[2]
    )
    after_attn, second_pull = jax.vjp(layer_norm, attn_sum, norm_gains[1], norm_shifts[1])
    after_low = after_attn.astype(narrow)
    hidden = jnp.dot(after_low, expand_weight, preferred_element_type=wide) + hidden_bias
    activated, gelu_pull = jax.vjp(gelu_exact, hidden)
    activated_low = activated.astype(narrow)
    ffn_sum = after_attn + (
        jnp.dot(activated_low, reduce_weight, preferred_element_type=wide) + bias_rows[3]
    )
    layer_out, third_pull = jax.vjp(layer_norm, ffn_sum, norm_gains[2], norm_shifts[2])
    grad_sum2, gain_grad2, shift_grad2 = third_pull(cotangent.astype(wide))
    grad_ffn = grad_sum2.astype(narrow)
    reduce_part = jnp.einsum("tf,td->fd", activated_low, grad_ffn, preferred_element_type=wide)
    grad_activated = jnp.einsum("td,fd->tf", grad_ffn, reduce_weight, preferred_element_type=wide)
    grad_hidden = gelu_pull(grad_activated)[0].astype(narrow)
    expand_part = jnp.einsum("td,tf->df", after_low, grad_hidden, preferred_element_type=wide)
    grad_after = grad_sum2 + jnp.einsum(
        "tf,df->td", grad_hidden, expand_weight, preferred_element_type=wide
    )
    grad_sum1, gain_grad1, shift_grad1 = second_pull(grad_after)
    grad_attn = grad_sum1.astype(narrow)
    output_part = jnp.einsum("te,td->ed", mixed_low, grad_attn, preferred_element_type=wide)
    grad_mixed = jnp.einsum(
        "td,ed->te", grad_attn, output_weight, preferred_element_type=wide
    ).astype(narrow)
    grad_query_pages, grad_key_pages, grad_value_pages = lax.map(
        page_backward, (paged_query, paged_key, paged_value, log_totals, grad_mixed.reshape(paged))
    )
    grad_queries = grad_query_pages.reshape(token_rows, width) * jnp.asarray(
        score_scale, dtype=narrow
    )
    grad_values = grad_value_pages.reshape(token_rows, width)
    grad_joined = jnp.concatenate(
        [grad_queries, grad_key_pages.reshape(token_rows, width), grad_values], axis=1
    )
    joined_part = jnp.einsum("td,te->de", normed_low, grad_joined, preferred_element_type=wide)
    grad_normed = grad_sum1 + jnp.einsum(
        "te,de->td", grad_joined, joined_weight, preferred_element_type=wide
    )
    embedded_grad, gain_grad0, shift_grad0 = first_pull(grad_normed)
    grad_box = embedded_grad.astype(narrow)
    shard_rows = lax.all_gather(grad_box, "tab", axis=0, tiled=True)
    span_rows = shard_rows.shape[0]
    first_rows = group_index[0]
    second_rows = group_index[1]
    row_number = lax.broadcasted_iota(jnp.int32, (table_rows, span_rows), 0)
    selection = (
        (row_number == first_rows[None, :]).astype(wide)
        + (row_number == second_rows[None, :]).astype(wide)
    ) * factor
    own_grad = jnp.dot(selection.astype(narrow), shard_rows, preferred_element_type=wide)
    tables_grad = lax.psum(own_grad, "tok")[None]
    bias_part = jnp.stack(
        [
            jnp.sum(grad_queries.astype(wide), 0),
            jnp.sum(grad_values.astype(wide), 0),
            jnp.sum(grad_attn.astype(wide), 0),
            jnp.sum(grad_ffn.astype(wide), 0),
        ]
    )
    gains_grad, shifts_grad, biases_grad, hidden_bias_grad = lax.psum(
        (
            jnp.stack([gain_grad0, gain_grad1, gain_grad2]),
            jnp.stack([shift_grad0, shift_grad1, shift_grad2]),
            bias_part,
            jnp.sum(grad_hidden.astype(wide), 0),
        ),
        ("tok", "tab"),
    )
    section_one = (
        lax.psum_scatter(joined_part, "tok", scatter_dimension=0, tiled=True),
        lax.psum_scatter(output_part, "tok", scatter_dimension=0, tiled=True),
        lax.psum_scatter(expand_part, "tok", scatter_dimension=0, tiled=True),
        lax.psum_scatter(reduce_part, "tok", scatter_dimension=0, tiled=True),
    )
    summed = (
        lax.psum_scatter(
            section_one[0].astype(jnp.bfloat16), "tab", scatter_dimension=1, tiled=True
        ).astype(jnp.float32),
        lax.psum_scatter(
            section_one[1].astype(jnp.bfloat16), "tab", scatter_dimension=1, tiled=True
        ).astype(jnp.float32),
        lax.psum_scatter(
            section_one[2].astype(jnp.bfloat16), "tab", scatter_dimension=1, tiled=True
        ).astype(jnp.float32),
        lax.psum_scatter(
            section_one[3].astype(jnp.bfloat16), "tab", scatter_dimension=1, tiled=True
        ).astype(jnp.float32),
    )
    return (
        layer_out.astype(narrow),
        embedded_grad,
        tables_grad,
        summed[0],
        summed[1],
        summed[2],
        summed[3],
        hidden_bias_grad,
        biases_grad,
        gains_grad,
        shifts_grad,
    )


def solution(mesh):
    return jax.shard_map(
        body,
        mesh=mesh,
        in_specs=(
            P(("tok", "tab"), None),
            P(("tok", "tab"), None),
            P(("tok", "tab"), None, None),
            P("tab", None, None),
            P(),
            P(),
            P(),
            P(),
            P(),
            P(),
            P(),
            P(),
            P(("tok", "tab"), None),
        ),
        out_specs=(
            P(("tok", "tab"), None),
            P(("tok", "tab"), None),
            P("tab", None, None),
            P("tok", "tab"),
            P("tok", "tab"),
            P("tok", "tab"),
            P("tok", "tab"),
            P(),
            P(),
            P(),
            P(),
        ),
        check_vma=False,
    )
```

profile of v0, /device:TPU:0, one launch (start us, length us, event | category | flops | bytes accessed | tf_op | source)
XLA Modules:
  0.0 1337.7 jit_solution(12232167450059098060)
XLA Ops:
  9.5 40.3 %gather_fusion = s32[4096]{0:T(1024)S(1)} fusion(s32[2,4,512]{2,1,0:T(4,128)S(1)} %copy-done.2, s32[4096]{0:T(1024)S(1)} %bitcast.162), kind=kCustom, calls=%fused_computation.2 | custom fusion | bytes 81920 | tf_op jit(solution)/shard_map/jit(take_along_axis)/gather | solution.py:25
  50.6 6.3 all-to-all-start
  56.9 5.7 all-to-all-done
  63.2 22.6 %gather_fusion.1 = bf16[4096,1024]{1,0:T(8,128)(2,1)} fusion(bf16[1001,1024]{1,0:T(8,128)(2,1)} %bitcast.158, s32[4096]{0:T(1024)S(1)} %fusion.35), kind=kCustom, calls=%fused_computation.clone | custom fusion | bytes 16793600 | tf_op jit(solution)/shard_map/jit(_take)/gather | solution.py:134
  85.9 11.3 copy.49
  97.2 22.6 %gather_fusion.2 = bf16[4096,1024]{1,0:T(8,128)(2,1)} fusion(bf16[1001,1024]{1,0:T(8,128)(2,1)} %bitcast.159, s32[4096]{0:T(1024)S(1)} %fusion.36), kind=kCustom, calls=%fused_computation.1.clone | custom fusion | bytes 16793600 | tf_op jit(solution)/shard_map/jit(_take)/gather | solution.py:135
  119.9 11.5 copy.50
  131.4 10.9 multiply_convert_fusion.2
  142.6 4.0 copy.48
  146.6 4.2 copy.55
  152.6 132.9 %reduce-scatter.10.cloned.1.call-done = bf16[1024,1024]{0,1:T(8,128)(2,1)} async-done(((bf16[4096,1024]{0,1:T(8,128)(2,1)}), bf16[1024,1024]{0,1:T(8,128)(2,1)}) %reduce-scatter.10.cloned.1.call-update) | async-done | bytes 2097168 | tf_op jit(solution)/shard_map/reduce_scatter | solution.py:136
  285.5 3.2 fusion.27
  290.0 10.2 fusion.48
  302.0 3.4 fusion.24
  305.4 3.9 copy.51
  309.3 4.0 copy.52
  313.3 4.0 copy.53
  317.3 59.0 %while.26 = (s32[]{:T(128)}, bf16[2,512,1024]{2,1,0:T(8,128)(2,1)}, f32[2,16,512]{2,1,0:T(8,128)S(1)}, bf16[2,512,1024]{1,2,0:T(8,128)(2,1)}, bf16[2,512,1024]{1...) while((s32[]{:T(128)}, bf16[2,512,1024]{2,1,0:T(8,128)(2,1)}, f32[2,16,512]{2,1,0:T(8,128)S(1)}, ...), condition=%wide.region_6.8_spmd, body=%wide.region_3.7_spmd.sunk | while | flops 1098899456 | bytes 73663088 | solution.py:154
  319.2 8.1 fusion.119
  327.3 8.4 fusion.120
  335.8 8.5 fusion.121
  348.5 8.1 fusion.119
  356.7 8.4 fusion.120
  365.2 8.5 fusion.121
  376.3 5.7 fusion.60
  387.0 46.9 %multiply_convert_fusion.1 = (bf16[1024,4096]{1,0:T(8,128)(2,1)}, f32[1024,4096]{1,0:T(8,128)}, f32[1024,4096]{1,0:T(8,128)}) fusion(f32[4096]{0:T(1024)S(1)} %copy-done.71, bf16[1024,4096]{1,0:T(8,128)(2,1)S(1)} %copy-done.69, bf16[1024,1024]{0,1:T(8,128)(2,1)S(1)} %fusion.46.clone.4), kind=kOutput, calls=%fused_computation.33 | convolution fusion | flops 8866758656 | bytes 52445184 | tf_op jit(solution)/shard_map/dot_general | solution.py:161
  433.9 16.4 %fusion.61 = (f32[1024]{0:T(1024)S(1)}, f32[1024,1024]{0,1:T(8,128)}) fusion(f32[1024]{0:T(1024)S(1)} %bitcast.232, bf16[1024,4096]{1,0:T(8,128)(2,1)} %get-tuple-element.207, bf16[4096,1024]{1,0:T(8,128)(2,1)} %param.26, f32[1024]{0:T(1024)S(1)} %bitcast.216, f32[1024]{0:T(1024)S(1)} %bitcast.201, f32[1024]{0:T(1024)S(1)} %fusion.38, ...), kind=kOutput, calls=%fused_computation.159 | convolution fusion | flops 8597273600 | bytes 25190400 | tf_op jit(solution)/shard_map/dot_general | solution.py:165
  450.3 4.4 fusion.21
  454.7 3.2 fusion.22
  457.9 4.3 convert_reduce_fusion.2
  462.2 24.5 %convert_reduce_fusion = (f32[4096]{0:T(1024)}, bf16[1024,4096]{1,0:T(8,128)(2,1)}) fusion(f32[1024,4096]{1,0:T(8,128)} %get-tuple-element.208, f32[1024,4096]{1,0:T(8,128)} %get-tuple-element.240, f32[4096]{0:T(1024)S(1)} %copy-done.71, bf16[1024,1024]{0,1:T(8,128)(2,1)} %get-tuple-element.200, bf16[4096,1024]{1,0:T(8,128)(2,1)} %param.26), kind=kOutput, calls=%fused_computation.31 | convolution fusion | flops 8661233664 | bytes 52461568 | tf_op jit(solution)/shard_map/td,fd->tf/dot_general | solution.py:171
  486.7 18.1 %multiply_reduce_fusion.1 = (f32[1024]{0:T(1024)}, f32[1024]{0:T(1024)S(1)}, f32[1024]{0:T(1024)}, f32[1024,1024]{0,1:T(8,128)S(1)}) fusion(f32[1024,1024]{0,1:T(8,128)S(1)} %copy-done.9, f32[1024]{0:T(1024)S(1)} %fusion.38, f32[1024]{0:T(1024)S(1)} %broadcast_multiply_fusion.2, f32[1024]{0:T(1024)S(1)} %bitcast.202, ...), kind=kOutput, calls=%fused_computation.72 | convolution fusion | flops 8607757312 | bytes 31502336 | tf_op jit(solution)/shard_map/tf,df->td/dot_general | solution.py:174
  507.4 3.7 convolution_convert_fusion.2
  511.1 4.4 fusion.63
  516.3 116.1 %while.27 = (s32[]{:T(128)}, bf16[2,512,1024]{2,1,0:T(8,128)(2,1)}, bf16[2,512,1024]{2,1,0:T(8,128)(2,1)}, bf16[2,512,1024]{1,2,0:T(8,128)(2,1)}, bf16[2,512,102...) while((s32[]{:T(128)}, bf16[2,512,1024]{2,1,0:T(8,128)(2,1)}, ...), condition=%wide.region_17.19_spmd, body=%wide.region_15.18_spmd.sunk | while | flops 2723667968 | bytes 224625920 | solution.py:183
  519.1 9.6 fusion.132
  531.3 8.6 fusion.133
  540.1 12.0 multiply_reduce_fusion.9
  552.0 12.1 multiply_convert_fusion.8
  569.0 4.8 convolution_convert_fusion.5
  578.1 8.1 fusion.132
  588.7 8.6 fusion.133
  597.6 11.9 multiply_reduce_fusion.9
  609.4 11.7 multiply_convert_fusion.8
  626.0 4.8 convolution_convert_fusion.5
  632.4 4.5 copy.63
  639.7 11.9 fusion.51
  654.2 3.8 fusion.52
  658.2 15.3 %fusion.30 = f32[1024,3072]{1,0:T(8,128)} fusion(bf16[1024,1024]{1,0:T(8,128)(2,1)} %bitcast.179, bf16[1024,1024]{1,0:T(8,128)(2,1)} %bitcast.235, bf16[1024,1024]{1,0:T(8,128)(2,1)} %bitcast.182, f32[1024]{0:T(1024)S(1)} %bitcast.231, f32[1024]{0:T(1024)S(1)} %bitcast.199, f32[1024]{0:T(1024)S(1)} %copy-done.37, f32[1024]{0:T(1024)S(1)} %copy-done.30, ...), kind=kOutput, calls=%fused_computation.97 | convolution fusion | flops 6469713920 | bytes 23085056 | tf_op jit(solution)/shard_map/td,te->de/dot_general | solution.py:193
  675.1 14.6 %fusion.64 = f32[4096,1024]{1,0:T(8,128)} fusion(bf16[1024,4096]{1,0:T(8,128)(2,1)} %get-tuple-element.207, bf16[1024,1024]{0,1:T(8,128)(2,1)S(1)} %copy-done.21), kind=kOutput, calls=%fused_computation.162 | convolution fusion | flops 8589934592 | bytes 27262976 | tf_op jit(solution)/shard_map/tf,td->fd/dot_general | solution.py:170
  690.4 16.7 %fusion.43 = f32[1024,4096]{1,0:T(8,128)} fusion(bf16[1024,4096]{1,0:T(8,128)(2,1)} %get-tuple-element.202, f32[1024,1024]{0,1:T(8,128)} %copy-done.8, f32[1024]{0:T(1024)S(1)} %bitcast.217, f32[1024]{0:T(1024)S(1)} %bitcast.204, f32[1024]{0:T(1024)S(1)} %copy-done.42, f32[1024]{0:T(1024)S(1)} %copy-done.33), kind=kOutput, calls=%fused_computation.146 | convolution fusion | flops 8595177472 | bytes 29376512 | tf_op jit(solution)/shard_map/td,tf->df/dot_general | solution.py:173
  709.0 99.4 %all-gather.2.cloned.1.call-done = bf16[4096,1024]{0,1:T(8,128)(2,1)} async-done(((bf16[1024,1024]{0,1:T(8,128)(2,1)}), bf16[4096,1024]{0,1:T(8,128)(2,1)}) %all-gather.2.cloned.1.call-update) | async-done | bytes 8388624 | tf_op jit(solution)/shard_map/all_gather | solution.py:199
  808.5 12.8 fusion.32
  821.3 81.0 %reduce-scatter.12.cloned.1.call-done = f32[128,3072]{1,0:T(8,128)} async-done(((f32[1024,3072]{1,0:T(8,128)}), f32[128,3072]{1,0:T(8,128)}) %reduce-scatter.12.cloned.1.call-update) | async-done | bytes 1572880 | tf_op jit(solution)/shard_map/reduce_scatter | solution.py:228
  904.8 117.1 %reduce-scatter.24.cloned.1.call-done = f32[512,1024]{1,0:T(8,128)} async-done(((f32[4096,1024]{1,0:T(8,128)}), f32[512,1024]{1,0:T(8,128)}) %reduce-scatter.24.cloned.1.call-update) | async-done | bytes 2097168 | tf_op jit(solution)/shard_map/reduce_scatter | solution.py:231
  1024.8 116.8 %reduce-scatter.20.cloned.1.call-done = f32[128,4096]{1,0:T(8,128)} async-done(((f32[1024,4096]{1,0:T(8,128)}), f32[128,4096]{1,0:T(8,128)}) %reduce-scatter.20.cloned.1.call-update) | async-done | bytes 2097168 | tf_op jit(solution)/shard_map/reduce_scatter | solution.py:230
  1144.3 5.3 copy.66
  1149.7 4.1 copy.65
  1156.4 40.8 %all-reduce = (f32[4096]{0:T(1024)}, f32[4,1024]{1,0:T(4,128)}, f32[3,1024]{1,0:T(4,128)}, f32[3,1024]{1,0:T(4,128)}) all-reduce(f32[4096]{0:T(1024)S(1)} %copy-done.58, f32[4,1024]{1,0:T(4,128)S(1)} %pad_maximum_fusion.5, f32[3,1024]{1,0:T(4,128)S(1)} %pad_maximum_fusion.6, ...), channel_id=1, replica_groups=mesh['tok'=8,'tab'=4] {'tok','tab'}, use_global_device_ids=true, to_apply=%region_30.32 | all-reduce | flops 14336 | bytes 114688 | tf_op jit(solution)/shard_map/psum | solution.py:218
  1198.8 47.7 %all-reduce.3.cloned.1.call-done = f32[1,1001,1024]{2,1,0:T(8,128)} async-done(((f32[1,1001,1024]{2,1,0:T(8,128)}), f32[1,1001,1024]{2,1,0:T(8,128)}) %all-reduce.3.cloned.1.call-update) | async-done | bytes 4100112 | tf_op jit(solution)/shard_map/psum | solution.py:209
  1246.5 8.4 copy.67
  1254.8 17.2 %reduce-scatter.14.cloned.1.call-done = bf16[128,768]{1,0:T(8,128)(2,1)} async-done(((bf16[128,3072]{1,0:T(8,128)(2,1)}), bf16[128,768]{1,0:T(8,128)(2,1)}) %reduce-scatter.14.cloned.1.call-update) | async-done | bytes 196624 | tf_op jit(solution)/shard_map/reduce_scatter | solution.py:234
  1273.7 27.3 %reduce-scatter.26.cloned.1.call-done = bf16[512,256]{1,0:T(8,128)(2,1)} async-done(((bf16[512,1024]{1,0:T(8,128)(2,1)}), bf16[512,256]{1,0:T(8,128)(2,1)}) %reduce-scatter.26.cloned.1.call-update) | async-done | bytes 262160 | tf_op jit(solution)/shard_map/reduce_scatter | solution.py:243
  1302.8 26.3 %reduce-scatter.22.cloned.1.call-done = bf16[128,1024]{1,0:T(8,128)(2,1)} async-done(((bf16[128,4096]{1,0:T(8,128)(2,1)}), bf16[128,1024]{1,0:T(8,128)(2,1)}) %reduce-scatter.22.cloned.1.call-update) | async-done | bytes 262160 | tf_op jit(solution)/shard_map/reduce_scatter | solution.py:240
  (269 shorter events, 76.2 us)
Async XLA Ops:
  7.2 369.1 %copy-start = (bf16[1024,1024]{1,0:T(8,128)(2,1)S(1)}, bf16[1024,1024]{1,0:T(8,128)(2,1)}, u32[]{:S(2)}) copy-start(bf16[1024,1024]{1,0:T(8,128)(2,1)} %param.24) | copy-start | bytes 6291460
  9.5 40.3 %copy-start.31 = (s32[2,512]{1,0:T(2,128)S(1)}, s32[2,512]{1,0:T(2,128)}, u32[]{:S(2)}) copy-start(s32[2,512]{1,0:T(2,128)} %param.20) | copy-start | bytes 12292
  50.6 12.0 all-to-all-start
  56.9 228.6 %reduce-scatter.10.cloned.1.call-start = ((), (), s32[]{:S(2)}) async-start(), calls=%async_computation.10 | async-start | bytes 10485760 | tf_op jit(solution)/shard_map/reduce_scatter | solution.py:136
  142.3 564.8 %reduce-scatter.16.cloned.1.call-start = ((), (), s32[]{:S(2)}) async-start(), calls=%async_computation.15 | async-start | bytes 4718592 | tf_op jit(solution)/shard_map/reduce_scatter | solution.py:229
  142.6 8.2 copy-start.60
  142.6 8.8 copy-start.61
  142.6 9.4 copy-start.57
  151.4 138.6 %copy-start.38 = (f32[1,1024]{1,0:T(1,128)}, f32[1,1024]{1,0:T(1,128)S(1)}, u32[]{:S(2)}) copy-start(f32[1,1024]{1,0:T(1,128)S(1)} %get-tuple-element.223) | copy-start | bytes 12292
  152.0 138.0 %copy-start.64 = (f32[1,1024]{1,0:T(1,128)}, f32[1,1024]{1,0:T(1,128)S(1)}, u32[]{:S(2)}) copy-start(f32[1,1024]{1,0:T(1,128)S(1)} %get-tuple-element.226) | copy-start | bytes 12292
  289.0 11.3 copy-start.28
  290.0 10.3 copy-start.45
  290.0 10.3 copy-start.35
  317.2 59.0 %copy-start.29 = (f32[1024]{0:T(1024)S(1)}, f32[1024]{0:T(1024)}, u32[]{:S(2)}) copy-start(f32[1024]{0:T(1024)} %copy-done.28) | copy-start | bytes 12292
  317.2 59.0 %copy-start.36 = (f32[1024]{0:T(1024)S(1)}, f32[1024]{0:T(1024)}, u32[]{:S(2)}) copy-start(f32[1024]{0:T(1024)} %copy-done.35) | copy-start | bytes 12292
  317.2 59.0 %copy-start.39 = (f32[1,1024]{1,0:T(1,128)S(1)}, f32[1,1024]{1,0:T(1,128)}, u32[]{:S(2)}) copy-start(f32[1,1024]{1,0:T(1,128)} %copy-done.38) | copy-start | bytes 12292
  317.2 59.0 %copy-start.65 = (f32[1,1024]{1,0:T(1,128)S(1)}, f32[1,1024]{1,0:T(1,128)}, u32[]{:S(2)}) copy-start(f32[1,1024]{1,0:T(1,128)} %copy-done.64) | copy-start | bytes 12292
  317.2 59.0 %copy-start.68 = (f32[1,1024]{1,0:T(1,128)S(1)}, f32[1,1024]{1,0:T(1,128)}, u32[]{:S(2)}) copy-start(f32[1,1024]{1,0:T(1,128)} %get-tuple-element.231) | copy-start | bytes 12292
  327.3 8.4 copy-start.4
  356.7 8.4 copy-start.4
  376.2 5.8 copy-start.22
  382.1 122.8 %copy-start.32 = (f32[1024]{0:T(1024)}, f32[1024]{0:T(1024)S(1)}, u32[]{:S(2)}) copy-start(f32[1024]{0:T(1024)S(1)} %broadcast_multiply_fusion.2) | copy-start | bytes 12292
  382.1 4.9 copy-start.69
  382.6 51.3 %copy-start.47 = (f32[1024]{0:T(1024)}, f32[1024]{0:T(1024)S(1)}, u32[]{:S(2)}) copy-start(f32[1024]{0:T(1024)S(1)} %multiply_reduce_fusion.6) | copy-start | bytes 12292
  382.6 4.4 copy-start.71
  382.6 122.3 %copy-start.41 = (f32[1024]{0:T(1024)}, f32[1024]{0:T(1024)S(1)}, u32[]{:S(2)}) copy-start(f32[1024]{0:T(1024)S(1)} %fusion.38) | copy-start | bytes 12292
  387.0 46.9 %copy-start.67 = (f32[1,1024]{1,0:T(1,128)S(1)}, f32[1,1024]{1,0:T(1,128)}, u32[]{:S(2)}) copy-start(f32[1,1024]{1,0:T(1,128)} %get-tuple-element.228) | copy-start | bytes 12292
  433.9 16.5 %copy-start.13 = (bf16[1024,1024]{0,1:T(8,128)(2,1)S(1)}, bf16[1024,1024]{0,1:T(8,128)(2,1)}, u32[]{:S(2)}) copy-start(bf16[1024,1024]{0,1:T(8,128)(2,1)} %copy.55) | copy-start | bytes 6291460
  433.9 16.4 %copy-start.34 = (f32[1,1024]{1,0:T(1,128)S(1)}, f32[1,1024]{1,0:T(1,128)}, u32[]{:S(2)}) copy-start(f32[1,1024]{1,0:T(1,128)} %get-tuple-element.222) | copy-start | bytes 12292
  450.3 4.4 copy-start.10
  462.2 24.5 %copy-start.9 = (f32[1024,1024]{0,1:T(8,128)S(1)}, f32[1024,1024]{0,1:T(8,128)}, u32[]{:S(2)}) copy-start(f32[1024,1024]{0,1:T(8,128)} %copy-done.8) | copy-start | bytes 12582916
  486.7 18.1 %copy-start.48 = (f32[1024]{0:T(1024)S(1)}, f32[1024]{0:T(1024)}, u32[]{:S(2)}) copy-start(f32[1024]{0:T(1024)} %copy-done.47) | copy-start | bytes 12292
  505.9 5.1 copy-start.14
  506.0 5.1 copy-start.50
  515.5 293.0 %all-gather.2.cloned.1.call-start = ((), (), s32[]{:S(2)}) async-start(), calls=%async_computation.11 | async-start | bytes 10485760 | tf_op jit(solution)/shard_map/all_gather | solution.py:199
  519.1 9.6 copy-start.15
  531.2 8.6 copy-start.5
  531.2 8.6 copy-start.16
  540.1 12.0 copy-start.17
  578.1 8.1 copy-start.15
  588.7 8.6 copy-start.5
  588.7 8.6 copy-start.16
  597.5 11.9 copy-start.17
  632.4 6.4 copy-start.7
  632.4 6.4 copy-start.30
  632.4 6.4 copy-start.40
  632.4 6.5 copy-start.51
  638.8 12.8 copy-start.20
  639.7 11.9 copy-start.46
  639.7 12.0 copy-start.37
  658.0 244.4 %reduce-scatter.12.cloned.1.call-start = ((), (), s32[]{:S(2)}) async-start(), calls=%async_computation.13 | async-start | bytes 14155776 | tf_op jit(solution)/shard_map/reduce_scatter | solution.py:228
  673.6 348.4 %reduce-scatter.24.cloned.1.call-start = ((), (), s32[]{:S(2)}) async-start(), calls=%async_computation.19 | async-start | bytes 18874368 | tf_op jit(solution)/shard_map/reduce_scatter | solution.py:231
  689.8 451.8 %reduce-scatter.20.cloned.1.call-start = ((), (), s32[]{:S(2)}) async-start(), calls=%async_computation.17 | async-start | bytes 18874368 | tf_op jit(solution)/shard_map/reduce_scatter | solution.py:230
  707.1 101.4 %copy-start.25 = (s32[1,1,4,1024]{3,1,2,0:T(1,128)S(1)}, s32[1,1,4,1024]{3,1,2,0:T(1,128)}, u32[]{:S(2)}) copy-start(s32[1,1,4,1024]{3,1,2,0:T(1,128)} %copy-done.24) | copy-start | bytes 49156
  707.1 101.4 %copy-start.27 = (s32[1,1,4,1024]{3,1,2,0:T(1,128)S(1)}, s32[1,1,4,1024]{3,1,2,0:T(1,128)}, u32[]{:S(2)}) copy-start(s32[1,1,4,1024]{3,1,2,0:T(1,128)} %copy-done.26) | copy-start | bytes 49156
  707.1 490.0 %reduce-scatter.18.cloned.1.call-start = ((), (), s32[]{:S(2)}) async-start(), calls=%async_computation.16 | async-start | bytes 327680 | tf_op jit(solution)/shard_map/reduce_scatter | solution.py:237
  709.0 537.5 %all-reduce.3.cloned.1.call-start = ((), (), s32[]{:S(2)}) async-start(), calls=%async_computation.12 | async-start | bytes 8257536 | tf_op jit(solution)/shard_map/psum | solution.py:209
  821.3 450.8 %reduce-scatter.14.cloned.1.call-start = ((), (), s32[]{:S(2)}) async-start(), calls=%async_computation.14 | async-start | bytes 983040 | tf_op jit(solution)/shard_map/reduce_scatter | solution.py:234
  904.8 396.2 %reduce-scatter.26.cloned.1.call-start = ((), (), s32[]{:S(2)}) async-start(), calls=%async_computation.20 | async-start | bytes 1310720 | tf_op jit(solution)/shard_map/reduce_scatter | solution.py:243
  1024.7 304.4 %reduce-scatter.22.cloned.1.call-start = ((), (), s32[]{:S(2)}) async-start(), calls=%async_computation.18 | async-start | bytes 1310720 | tf_op jit(solution)/shard_map/reduce_scatter | solution.py:240
  1149.7 6.6 copy-start.55
  1149.7 6.6 copy-start.56
  1149.7 6.6 copy-start.58
  1197.1 133.8 %copy-start.1 = (bf16[1024,1024]{1,0:T(8,128)(2,1)S(1)}, bf16[1024,1024]{1,0:T(8,128)(2,1)}, u32[]{:S(2)}) copy-start(bf16[1024,1024]{1,0:T(8,128)(2,1)} %param.24) | copy-start | bytes 6291460
  (26 other events, 62.3 us)
Sparse Core Ops, SparseCore 0:
  142.5 142.9 reduce-scatter.9
  515.6 51.7 reduce-scatter.15
  658.1 150.3 all-gather.1
  811.8 90.4 reduce-scatter.11
  905.7 116.1 reduce-scatter.23
  1025.4 116.1 reduce-scatter.19
  1144.4 19.9 reduce-scatter.17
  1167.8 78.6 all-reduce.2
  1248.8 23.2 reduce-scatter.13
  1274.2 26.7 reduce-scatter.25
  1303.3 25.7 reduce-scatter.21
where the time goes:
time: 1340 us
  waiting for transfers between devices  672 us (50%)
  matrix products  308 us (23%)
  local copies, waits for them, and re-layouts  189 us (14%)
  other arithmetic  105 us (8%)
  blocking collectives  40.8 us (3%)
  between operations  15 us (1%)
    reduce_scatter x1, waiting for transfers between devices, body(): lax.psum_scatter((factor * (picked_first + picked_second)).astype(jnp.bfl...  133 us
    reduce_scatter x1, waiting for transfers between devices, body(): lax.psum_scatter(reduce_part, 'tok', scatter_dimension=0, tiled=True)  117 us
    reduce_scatter x1, waiting for transfers between devices, body(): lax.psum_scatter(expand_part, 'tok', scatter_dimension=0, tiled=True)  117 us
    all_gather x1, waiting for transfers between devices, body(): shard_rows = lax.all_gather(grad_box, 'tab', axis=0, tiled=True)  99.4 us
    reduce_scatter x1, waiting for transfers between devices, body(): lax.psum_scatter(joined_part, 'tok', scatter_dimension=0, tiled=True)  81 us
    psum x1, waiting for transfers between devices, body(): tables_grad = lax.psum(own_grad, 'tok')[None]  47.7 us
    dot_general x1, matrix products, body(): jnp.dot(after_low, expand_weight, preferred_element_type=wide) + hidden_bias  46.9 us
    psum x1, blocking collectives, body(): lax.psum((jnp.stack([gain_grad0, gain_grad1, gain_grad2]), jnp.stack([shi...  40.8 us
  transfers between devices with their start and end apart: 12, of which 10 were waited for; matrix products, arithmetic and copies ran while one was open for 18% of the time, Pallas kernels for 0%

commit v1 on v0

v1 whole, which is shorter than its diff:
```python
import functools

import jax
import jax.numpy as jnp
from jax import lax
from jax.experimental import pallas as pl
from jax.experimental.pallas import tpu as pltpu
from jax.sharding import PartitionSpec as P

HEADS = 16
HEAD_DIM = 64
CELLS = 128
EPSILON = 1e-05
SCALE = HEAD_DIM ** (-0.5)
LOG2E = 1.4426950408889634
F32 = jnp.float32
BF = jnp.bfloat16
NN = ((1,), (0,))
NT = ((1,), (1,))
TN = ((0,), (0,))
ANY = pl.ANY

TAIL_P = 0.305
TAIL_C = (
    0.12164194255155772,
    0.12243138164026345,
    0.10365178645525906,
    0.12022714029486306,
    -0.03641303195181058,
    0.1839499605096701,
    -0.15192310059752684,
    0.03643391798251271,
)


def dot(a, b, dims):
    return lax.dot_general(a, b, (dims, ((), ())), preferred_element_type=F32)


def params(**kw):
    return pltpu.CompilerParams(vmem_limit_bytes=60 << 20, **kw)


def cost(flops, nbytes, trans=0):
    return pl.CostEstimate(
        flops=int(flops), bytes_accessed=int(nbytes), transcendentals=int(trans)
    )


def full(shape):
    zeros = (0,) * len(shape)
    return pl.BlockSpec(shape, lambda *_: zeros, pipeline_mode=pl.Buffered(1))


def gelu_parts(h):
    a = jnp.abs(h)
    t = 1.0 / (1.0 + TAIL_P * a)
    poly = jnp.full_like(t, TAIL_C[-1])
    for c in TAIL_C[-2::-1]:
        poly = poly * t + c
    e = jnp.exp2(h * h * (-0.5 * LOG2E))
    tail = poly * t * e
    phi_cdf = jnp.where(h > 0, 1.0 - tail, tail)
    act = h * phi_cdf
    slope = phi_cdf + h * e * 0.3989422804014327
    return act, slope


def norm_stats(v):
    mean = jnp.mean(v, axis=-1, keepdims=True)
    centred = v - mean
    var = jnp.mean(centred * centred, axis=-1, keepdims=True)
    rstd = lax.rsqrt(var + EPSILON)
    return centred * rstd, rstd


def norm_back(y, xh, rstd, gain):
    u = y * gain
    return (
        u - jnp.mean(u, axis=-1, keepdims=True) - xh * jnp.mean(u * xh, axis=-1, keepdims=True)
    ) * rstd


def colsum(v):
    return jnp.sum(v, axis=0, keepdims=True)


def lookup_kernel(idx, table, out):
    rows = table.shape[0]
    count = idx.shape[2]
    number = lax.broadcasted_iota(jnp.int32, (rows, count), 0)
    first = (number == idx[0, 0:1, :]).astype(F32)
    second = (number == idx[0, 1:2, :]).astype(F32)
    out[0] = dot((first + second).astype(BF), table[...], TN).astype(BF)


def lookup(idx, table):
    groups, _, count = idx.shape
    rows, width = table.shape
    return pl.pallas_call(
        lookup_kernel,
        grid=(groups,),
        in_specs=[
            pl.BlockSpec((1, 2, count), lambda i: (i, 0, 0)),
            full((rows, width)),
        ],
        out_specs=pl.BlockSpec((1, count, width), lambda i: (i, 0, 0)),
        out_shape=jax.ShapeDtypeStruct((groups, count, width), BF),
        compiler_params=params(),
        cost_estimate=cost(2 * groups * count * rows * width, 2 * groups * count * width),
        name="lookup",
    )(idx, table)


def embed_kernel(
    emb, ci, t0, t1, t2, t3, w, gains, shifts, bias, q, k, v, normed, low, rstd_out
):
    width = emb.shape[1]
    tokens = emb.shape[0]
    cells = jnp.concatenate([t0[...], t1[...], t2[...], t3[...]], axis=0)
    number = lax.broadcasted_iota(jnp.int32, (CELLS, tokens), 0)
    pick = (number == ci[0]).astype(F32).astype(BF)
    pick = jnp.concatenate([pick] * 4, axis=0)
    box = dot(pick, cells, TN)
    xh, rstd = norm_stats(emb[...].astype(F32) + box)
    y = xh * gains[0:1] + shifts[0:1]
    normed[...] = y
    rstd_out[...] = rstd
    y_low = y.astype(BF)
    low[...] = y_low
    q[...] = ((dot(y_low, w[:, :width], NN) + bias[0:1]) * SCALE).astype(BF)
    k[...] = dot(y_low, w[:, width : 2 * width], NN).astype(BF)
    v[...] = (dot(y_low, w[:, 2 * width :], NN) + bias[1:2]).astype(BF)


def embed(emb, ci, terms, w, gains, shifts, bias):
    tokens, width = emb.shape
    pages, length = ci.shape
    rows = pl.BlockSpec((length, width), lambda i: (i, 0))
    cell_rows = pl.BlockSpec((CELLS, width), lambda i: (i, 0))
    shape = lambda dt, n=width: jax.ShapeDtypeStruct((tokens, n), dt)
    return pl.pallas_call(
        embed_kernel,
        grid=(pages,),
        in_specs=[rows, pl.BlockSpec((1, 1, length), lambda i: (i, 0, 0))]
        + [cell_rows] * 4
        + [full(w.shape), full(gains.shape), full(shifts.shape), full(bias.shape)],
        out_specs=[rows] * 5 + [pl.BlockSpec((length, 1), lambda i: (i, 0))],
        out_shape=[shape(BF), shape(BF), shape(BF), shape(F32), shape(BF), shape(F32, 1)],
        compiler_params=params(),
        cost_estimate=cost(2 * tokens * width * 3 * width, 26 << 20),
        name="embed_joined",
    )(emb, ci.reshape(pages, 1, length), *terms, w, gains, shifts, bias)


HP = 4


def head_masks(length, pair):
    lane = lax.broadcasted_iota(jnp.int32, (length, pair), 1)
    return lane < HEAD_DIM


def attn_fwd_kernel(q, k, v, mixed, lse):
    length = q.shape[0]
    pair = 2 * HEAD_DIM
    low_half = head_masks(length, pair)
    zero = jnp.zeros((length, pair), BF)
    for p in range(HP // 2):
        cols = slice(p * pair, (p + 1) * pair)
        qp, kp, vp = q[:, cols], k[:, cols], v[:, cols]
        vt = vp.T
        outs = []
        for h in range(2):
            km = jnp.where(low_half, kp, zero) if h == 0 else jnp.where(low_half, zero, kp)
            st = dot(km, qp, NT)
            top = jnp.max(st, axis=0, keepdims=True)
            raised = jnp.exp2((st - top) * LOG2E)
            total = jnp.sum(raised, axis=0, keepdims=True)
            lse[0, 0, 2 * p + h : 2 * p + h + 1, :] = top + jnp.log(total)
            ot = dot(vt[h * HEAD_DIM : (h + 1) * HEAD_DIM], raised.astype(BF), NN)
            outs.append(ot * (1.0 / total))
        mixed[:, cols] = jnp.concatenate(outs, axis=0).T.astype(BF)


def attn_fwd(q, k, v, pages):
    tokens, width = q.shape
    length = tokens // pages
    steps = HEADS // HP
    blk = pl.BlockSpec((length, HP * HEAD_DIM), lambda i, j: (i, j))
    return pl.pallas_call(
        attn_fwd_kernel,
        grid=(pages, steps),
        in_specs=[blk] * 3,
        out_specs=[blk, pl.BlockSpec((1, 1, HP, length), lambda i, j: (i, j, 0, 0))],
        out_shape=[
            jax.ShapeDtypeStruct((tokens, width), BF),
            jax.ShapeDtypeStruct((pages, steps, HP, length), F32),
        ],
        compiler_params=params(),
        cost_estimate=cost(14e9, 8 << 20, pages * HEADS * length * length),
        name="attention",
    )(q, k, v)


def attn_bwd_kernel(q, k, v, mixed, go, lse, gj, sums):
    length = q.shape[0]
    pair = 2 * HEAD_DIM
    low_half = head_masks(length, pair)
    zero = jnp.zeros((length, pair), BF)
    page = pl.program_id(1)

    def pick(x, h):
        return jnp.where(low_half, x, zero) if h == 0 else jnp.where(low_half, zero, x)

    for p in range(HP // 2):
        cols = slice(p * pair, (p + 1) * pair)
        qp, kp, vp, op, gp = q[:, cols], k[:, cols], v[:, cols], mixed[:, cols], go[:, cols]
        kt = kp.T
        prod_t = (op.astype(F32) * gp.astype(F32)).T
        dq_t, dk, dv = [], None, None
        for h in range(2):
            st = dot(pick(kp, h), qp, NT)
            probs = jnp.exp2((st - lse[0, 0, 2 * p + h : 2 * p + h + 1, :]) * LOG2E)
            dv_h = dot(probs.astype(BF), pick(gp, h), NN)
            dpt = dot(pick(vp, h), gp, NT)
            delta = colsum(prod_t[h * HEAD_DIM : (h + 1) * HEAD_DIM])
            ds = (probs * (dpt - delta)).astype(BF)
            dk_h = dot(ds, pick(qp, h), NN)
            dq_t.append(dot(kt[h * HEAD_DIM : (h + 1) * HEAD_DIM], ds, NN))
            dv = dv_h if dv is None else dv + dv_h
            dk = dk_h if dk is None else dk + dk_h
        dq = (jnp.concatenate(dq_t, axis=0).T.astype(BF).astype(F32) * SCALE).astype(BF)
        dv = dv.astype(BF)
        gj[0, :, cols] = dq
        gj[1, :, cols] = dk.astype(BF)
        gj[2, :, cols] = dv
        part = jnp.concatenate([colsum(dq.astype(F32)), colsum(dv.astype(F32))], axis=0)

        @pl.when(page == 0)
        def _():
            sums[:, cols] = part

        @pl.when(page != 0)
        def _():
            sums[:, cols] = sums[:, cols] + part


def attn_bwd(q, k, v, mixed, go, lse, pages):
    tokens, width = q.shape
    length = tokens // pages
    steps = HEADS // HP
    wide = HP * HEAD_DIM
    blk = pl.BlockSpec((length, wide), lambda j, i: (i, j))
    return pl.pallas_call(
        attn_bwd_kernel,
        grid=(steps, pages),
        in_specs=[blk] * 5 + [pl.BlockSpec((1, 1, HP, length), lambda j, i: (i, j, 0, 0))],
        out_specs=[
            pl.BlockSpec((3, length, wide), lambda j, i: (0, i, j)),
            pl.BlockSpec((2, wide), lambda j, i: (0, j)),
        ],
        out_shape=[
            jax.ShapeDtypeStruct((3, tokens, width), BF),
            jax.ShapeDtypeStruct((2, width), F32),
        ],
        compiler_params=params(),
        cost_estimate=cost(35e9, 16 << 20, pages * HEADS * length * length),
        name="attention_back",
    )(q, k, v, mixed, go, lse)


FC = 1024


def ffn_fwd_kernel(
    mixed, normed, wo, we, wr, hb, bias, gains, shifts, cot,
    out, after_out, low_out, rstd_out, act_out, slope_out, gs2_out, gffn_out, sums,
):
    ff = we.shape[1]
    attn_sum = normed[...] + (dot(mixed[...], wo[...], NN) + bias[2:3])
    xh, rstd = norm_stats(attn_sum)
    after = xh * gains[1:2] + shifts[1:2]
    after_out[...] = after
    rstd_out[...] = rstd
    low = after.astype(BF)
    low_out[...] = low
    total = after + bias[3:4]
    for j in range(ff // FC):
        cols = slice(j * FC, (j + 1) * FC)
        act, slope = gelu_parts(dot(low, we[:, cols], NN) + hb[:, cols])
        act = act.astype(BF)
        act_out[:, cols] = act
        slope_out[:, cols] = slope.astype(BF)
        total = total + dot(act, wr[cols, :], NN)
    xh, rstd = norm_stats(total)
    out[...] = (xh * gains[2:3] + shifts[2:3]).astype(BF)
    y = cot[...].astype(F32)
    gs2 = norm_back(y, xh, rstd, gains[2:3])
    gs2_out[...] = gs2
    gffn = gs2.astype(BF)
    gffn_out[...] = gffn
    part = jnp.concatenate([colsum(y * xh), colsum(y), colsum(gffn.astype(F32))], axis=0)

    @pl.when(pl.program_id(0) == 0)
    def _():
        sums[...] = part

    @pl.when(pl.program_id(0) != 0)
    def _():
        sums[...] = sums[...] + part


def ffn_fwd(mixed, normed, wo, we, wr, hb, bias, gains, shifts, cot, tile):
    tokens, width = mixed.shape
    ff = we.shape[1]
    rows = pl.BlockSpec((tile, width), lambda i: (i, 0))
    long = pl.BlockSpec((tile, ff), lambda i: (i, 0))
    shape = lambda dt, n=width: jax.ShapeDtypeStruct((tokens, n), dt)
    hb = hb.reshape(1, ff)
    return pl.pallas_call(
        ffn_fwd_kernel,
        grid=(tokens // tile,),
        in_specs=[rows, rows]
        + [full(a.shape) for a in (wo, we, wr, hb, bias, gains, shifts)]
        + [rows],
        out_specs=[rows, rows, rows, pl.BlockSpec((tile, 1), lambda i: (i, 0)), long, long, rows, rows]
        + [pl.BlockSpec((3, width), lambda i: (0, 0))],
        out_shape=[
            shape(BF), shape(F32), shape(BF), shape(F32, 1), shape(BF, ff), shape(BF, ff),
            shape(F32), shape(BF), jax.ShapeDtypeStruct((3, width), F32),
        ],
        compiler_params=params(),
        cost_estimate=cost(2 * tokens * width * (width + 2 * ff), 60 << 20, tokens * ff * 2),
        name="ffn_forward",
    )(mixed, normed, wo, we, wr, hb, bias, gains, shifts, cot)


def ffn_bwd_kernel(
    gffn, slope, gs2, after, rstd, wr, we, wo, gains, shifts,
    gh_out, gs1_out, gattn_out, gmixed_out, hsum, sums,
):
    ff = we.shape[1]
    first = pl.program_id(0) == 0
    g = gffn[...]
    total = gs2[...]
    hparts = []
    for j in range(ff // FC):
        cols = slice(j * FC, (j + 1) * FC)
        gh = (dot(g, wr[cols, :], NT) * slope[:, cols].astype(F32)).astype(BF)
        gh_out[:, cols] = gh
        hparts.append(colsum(gh.astype(F32)))
        total = total + dot(gh, we[:, cols], NT)
    hpart = jnp.concatenate(hparts, axis=1)
    xh = (after[...] - shifts[1:2]) * (1.0 / gains[1:2])
    gs1 = norm_back(total, xh, rstd[...], gains[1:2])
    gs1_out[...] = gs1
    gattn = gs1.astype(BF)
    gattn_out[...] = gattn
    gmixed_out[...] = dot(gattn, wo[...], NT).astype(BF)
    part = jnp.concatenate(
        [colsum(total * xh), colsum(total), colsum(gattn.astype(F32))], axis=0
    )

    @pl.when(first)
    def _():
        sums[...] = part
        hsum[...] = hpart

    @pl.when(jnp.logical_not(first))
    def _():
        sums[...] = sums[...] + part
        hsum[...] = hsum[...] + hpart


def ffn_bwd(gffn, slope, gs2, after, rstd, wr, we, wo, gains, shifts, tile):
    tokens, width = gffn.shape
    ff = we.shape[1]
    rows = pl.BlockSpec((tile, width), lambda i: (i, 0))
    long = pl.BlockSpec((tile, ff), lambda i: (i, 0))
    shape = lambda dt, n=width: jax.ShapeDtypeStruct((tokens, n), dt)
    return pl.pallas_call(
        ffn_bwd_kernel,
        grid=(tokens // tile,),
        in_specs=[rows, long, rows, rows, pl.BlockSpec((tile, 1), lambda i: (i, 0))]
        + [full(a.shape) for a in (wr, we, wo, gains, shifts)],
        out_specs=[long, rows, rows, rows]
        + [pl.BlockSpec((1, ff), lambda i: (0, 0)), pl.BlockSpec((3, width), lambda i: (0, 0))],
        out_shape=[
            shape(BF, ff), shape(F32), shape(BF), shape(BF),
            jax.ShapeDtypeStruct((1, ff), F32), jax.ShapeDtypeStruct((3, width), F32),
        ],
        compiler_params=params(),
        cost_estimate=cost(2 * tokens * width * (width + 2 * ff), 60 << 20),
        name="ffn_backward",
    )(gffn, slope, gs2, after, rstd, wr, we, wo, gains, shifts)


def embed_bwd_kernel(gs1, gj, w, normed, rstd, ci, gains, shifts, out, cells, sums):
    width = gs1.shape[1]
    tokens = gs1.shape[0]
    total = gs1[...]
    for n in range(3):
        total = total + dot(gj[n], w[:, n * width : (n + 1) * width], NT)
    xh = (normed[...] - shifts[0:1]) * (1.0 / gains[0:1])
    grad = norm_back(total, xh, rstd[...], gains[0:1])
    out[...] = grad
    number = lax.broadcasted_iota(jnp.int32, (CELLS, tokens), 0)
    pick = (number == ci[0]).astype(F32).astype(BF)
    cells[...] = dot(pick, grad.astype(BF), NN).astype(BF)
    part = jnp.concatenate([colsum(total * xh), colsum(total)], axis=0)

    @pl.when(pl.program_id(0) == 0)
    def _():
        sums[...] = part

    @pl.when(pl.program_id(0) != 0)
    def _():
        sums[...] = sums[...] + part


def embed_bwd(gs1, gj, w, normed, rstd, ci, gains, shifts):
    tokens, width = gs1.shape
    pages, length = ci.shape
    rows = pl.BlockSpec((length, width), lambda i: (i, 0))
    return pl.pallas_call(
        embed_bwd_kernel,
        grid=(pages,),
        in_specs=[
            rows,
            pl.BlockSpec((3, length, width), lambda i: (0, i, 0)),
            full(w.shape),
            rows,
            pl.BlockSpec((length, 1), lambda i: (i, 0)),
            pl.BlockSpec((1, 1, length), lambda i: (i, 0, 0)),
            full(gains.shape),
            full(shifts.shape),
        ],
        out_specs=[
            rows,
            pl.BlockSpec((CELLS, width), lambda i: (i, 0)),
            pl.BlockSpec((2, width), lambda i: (0, 0)),
        ],
        out_shape=[
            jax.ShapeDtypeStruct((tokens, width), F32),
            jax.ShapeDtypeStruct((pages * CELLS, width), BF),
            jax.ShapeDtypeStruct((2, width), F32),
        ],
        compiler_params=params(),
        cost_estimate=cost(2 * tokens * width * 3 * width, 26 << 20),
        name="embed_backward",
    )(gs1, gj, w, normed, rstd, ci.reshape(pages, 1, length), gains, shifts)


def table_kernel(tok, idx, g0, g1, g2, g3, out_a, out_b):
    rows = out_a.shape[1]
    count = idx.shape[2]
    half = out_a.shape[2]
    base = (pl.program_id(0) ^ tok[0]) * rows
    number = lax.broadcasted_iota(jnp.int32, (rows, count), 0) + base
    picks = []
    for s in range(4):
        first = (number == idx[s, 0:1, :]).astype(F32)
        second = (number == idx[s, 1:2, :]).astype(F32)
        picks.append((first + second).astype(BF))
    pick = jnp.concatenate(picks, axis=1)
    grads = jnp.concatenate([g0[...], g1[...], g2[...], g3[...]], axis=0)
    total = dot(pick, grads, NN).astype(BF)
    out_a[0] = total[:, :half]
    out_b[0] = total[:, half:]


def table_part(tok, idx, grads, blocks):
    groups, _, count = idx.shape
    width = grads[0].shape[1]
    rows = 1024 // blocks
    half = width // 2
    out = pl.BlockSpec((1, rows, half), lambda i, t: (i, 0, 0))
    return pl.pallas_call(
        table_kernel,
        grid_spec=pltpu.PrefetchScalarGridSpec(
            num_scalar_prefetch=1,
            grid=(blocks,),
            in_specs=[full(idx.shape)] + [full((count, width))] * groups,
            out_specs=[out, out],
        ),
        out_shape=[jax.ShapeDtypeStruct((blocks, rows, half), BF)] * 2,
        compiler_params=params(),
        cost_estimate=cost(2 * 1024 * groups * count * width, 4 << 20),
        name="table_grad",
    )(tok, idx, *grads)


def table_out_kernel(tok, a, b, out):
    half = a.shape[2]
    out[0, :, :half] = a[0].astype(F32)
    out[0, :, half:] = b[0].astype(F32)


def table_out(tok, a, b, table_rows):
    blocks, rows, half = a.shape
    src = pl.BlockSpec((1, rows, half), lambda i, t: (i ^ t[0], 0, 0))
    return pl.pallas_call(
        table_out_kernel,
        grid_spec=pltpu.PrefetchScalarGridSpec(
            num_scalar_prefetch=1,
            grid=(blocks,),
            in_specs=[src, src],
            out_specs=pl.BlockSpec((1, rows, 2 * half), lambda i, t: (0, i, 0)),
        ),
        out_shape=jax.ShapeDtypeStruct((1, table_rows, 2 * half), F32),
        compiler_params=params(),
        cost_estimate=cost(0, 6 << 20),
        name="table_write",
    )(tok, a, b)


def block_of(tok, j, core):
    return (tok ^ (((j & 1) << 2) | (j & 2))) & 6 | core


def rows_partner_kernel(tok, lhs, *refs, count):
    rhs, (pa, pb, turned) = refs[:count], refs[count:]
    core = (tok[0] & 1) ^ 1
    turn_rows(tok, lhs, turned, core)
    g = dot(turned[...], jnp.concatenate([r[...].reshape(r.shape[-2:]) for r in rhs], axis=1), NN)
    rows = lhs.shape[1] // 8
    half = pa.shape[3]
    for j in range(4):
        pa[j, 0] = g[j * rows : (j + 1) * rows, :half].astype(BF)
        pb[j, 0] = g[j * rows : (j + 1) * rows, half:].astype(BF)


def turn_rows(tok, lhs, turned, core):
    rows = lhs.shape[1] // 8

    @pl.when(pl.program_id(0) == 0)
    def _():
        for j in range(4):
            start = pl.multiple_of(block_of(tok[0], j, core) * rows, rows)
            turned[j * rows : (j + 1) * rows, :] = lhs[:, pl.ds(start, rows)].T


def rows_own_kernel(tok, lhs, *refs, count):
    rhs = refs[:count]
    ra, rb, sa, ka, sb, kb, turned = refs[count:]
    turn_rows(tok, lhs, turned, tok[0] & 1)
    g = dot(turned[...], jnp.concatenate([r[...].reshape(r.shape[-2:]) for r in rhs], axis=1), NN)
    rows = lhs.shape[1] // 8
    half = ra.shape[3]
    for j in range(4):
        rx, ry = j >> 1, j & 1
        a = (g[j * rows : (j + 1) * rows, :half] + ra[j, 0].astype(F32)).astype(BF)
        b = (g[j * rows : (j + 1) * rows, half:] + rb[j, 0].astype(F32)).astype(BF)
        (sa if rx else ka)[ry, 0] = a
        (sb if ry else kb)[rx, 0] = b


def rows_call(tok, lhs, rhs_list, rhs_specs, width, received):
    tokens, d = lhs.shape
    rows = d // 8
    half = width // 2
    count = len(rhs_list)
    spec = lambda n: pl.BlockSpec((n, 1, rows, half), lambda z, t: (0, z, 0, 0))
    shape = lambda n: jax.ShapeDtypeStruct((n, 4, rows, half), BF)
    own = received is not None
    kernel = rows_own_kernel if own else rows_partner_kernel
    outs = [2, 2, 2, 2] if own else [4, 4]
    return pl.pallas_call(
        functools.partial(kernel, count=count),
        grid_spec=pltpu.PrefetchScalarGridSpec(
            num_scalar_prefetch=1,
            grid=(4,),
            in_specs=[full(lhs.shape)] + rhs_specs + ([spec(4)] * 2 if own else []),
            out_specs=[spec(n) for n in outs],
            scratch_shapes=[pltpu.VMEM((d // 2, tokens), BF)],
        ),
        out_shape=[shape(n) for n in outs],
        compiler_params=params(),
        cost_estimate=cost(4 * tokens * d * width, 6 * d * width + 2 * tokens * d),
        name="weight_grad_own" if own else "weight_grad_partner",
    )(tok, lhs, *rhs_list, *(received or ()))


def cols_partner_kernel(tok, lhs, rhs, pa, pb, turned):
    @pl.when(pl.program_id(0) == 0)
    def _():
        turned[...] = lhs[...].T

    g = dot(turned[...], rhs[...], NN)
    half = pa.shape[3]
    pa[0] = g[:, :half].astype(BF).reshape(pa.shape[1:])
    pb[0] = g[:, half:].astype(BF).reshape(pb.shape[1:])


def cols_own_kernel(tok, lhs, rhs, ra, rb, sa, ka, sb, kb, turned):
    step = pl.program_id(0)

    @pl.when(step == 0)
    def _():
        turned[...] = lhs[...].T

    g = dot(turned[...], rhs[...], NN)
    half = ra.shape[3]
    a = (g[:, :half].reshape(ra.shape[1:]) + ra[0].astype(F32)).astype(BF)
    b = (g[:, half:].reshape(rb.shape[1:]) + rb[0].astype(F32)).astype(BF)
    rx = step < 2
    ry = step % 2 == 0

    @pl.when(rx)
    def _():
        sa[0] = a

    @pl.when(jnp.logical_not(rx))
    def _():
        ka[0] = a

    @pl.when(ry)
    def _():
        sb[0] = b

    @pl.when(jnp.logical_not(ry))
    def _():
        kb[0] = b


def cols_call(tok, lhs, rhs, received):
    tokens, d = lhs.shape
    f = rhs.shape[1] // 8
    half = f // 2
    rows = d // 4
    own = received is not None
    flip = 0 if own else 1
    rhs_spec = pl.BlockSpec(
        (tokens, f), lambda s, t: (0, block_of(t[0], 3 - s, (t[0] & 1) ^ flip))
    )
    blk = lambda index: pl.BlockSpec((1, 4, rows, half), lambda s, t: (index(s), 0, 0, 0))
    whole = blk(lambda s: 3 - s)
    shape = lambda n: jax.ShapeDtypeStruct((n, 4, rows, half), BF)
    late = lambda s: 1 - s // 3
    if own:
        out_specs = [
            blk(lambda s: 1 - jnp.minimum(s, 1)),
            blk(late),
            blk(lambda s: 1 - s // 2),
            blk(late),
        ]
    else:
        out_specs = [whole, whole]
    return pl.pallas_call(
        cols_own_kernel if own else cols_partner_kernel,
        grid_spec=pltpu.PrefetchScalarGridSpec(
            num_scalar_prefetch=1,
            grid=(4,),
            in_specs=[full(lhs.shape), rhs_spec] + ([whole, whole] if own else []),
            out_specs=out_specs,
            scratch_shapes=[pltpu.VMEM((d, tokens), BF)],
        ),
        out_shape=[shape(2)] * 4 if own else [shape(4)] * 2,
        compiler_params=params(),
        cost_estimate=cost(8 * tokens * d * f, 24 * d * f + 2 * tokens * d),
        name="weight_grad_own" if own else "weight_grad_partner",
    )(tok, lhs, rhs, *(received or ()))


def flip_tok(value, bit, size):
    return lax.ppermute(value, "tok", [(i, i ^ bit) for i in range(size)])


def shift_tab(value, shift, size):
    return lax.ppermute(value, "tab", [(i, (i + shift) % size) for i in range(size)])


def plus(a, b):
    return (a.astype(F32) + b.astype(F32)).astype(BF)


def scatter_sum(send, keep, bits, n_tok, n_tab):
    got = flip_tok(send, bits[0], n_tok)
    send = plus(keep[1], got[1])
    keep = plus(keep[0], got[0])
    got = flip_tok(send, bits[1], n_tok)
    part = plus(keep, got)
    z = lax.axis_index("tab")
    take = lambda i: lax.dynamic_index_in_dim(part, i, 0, keepdims=False)
    total = take(z).astype(F32)
    for shift in range(1, n_tab):
        total = total + shift_tab(take((z + shift) % n_tab), shift, n_tab).astype(F32)
    return total


def weight_grad(call, n_tok, n_tab):
    pa, pb = call(None)
    received = (flip_tok(pa, 1, n_tok), flip_tok(pb, 1, n_tok))
    sa, ka, sb, kb = call(received)
    return (
        scatter_sum(sa, ka, (2, 4), n_tok, n_tab),
        scatter_sum(sb, kb, (4, 2), n_tok, n_tab),
    )


def table_sum(part, bits, n_tok):
    rows, cols = part.shape[1:]
    block = {i: part[i] for i in range(8)}
    order = list(bits)
    for bit in order:
        sent = [i for i in sorted(block) if i & bit]
        got = flip_tok(jnp.stack([block[i] for i in sent]), bit, n_tok)
        for n, i in enumerate(sent):
            block[i ^ bit] = plus(block[i ^ bit], got[n])
            del block[i]
    for bit in reversed(order):
        held = sorted(block)
        got = flip_tok(jnp.stack([block[i] for i in held]), bit, n_tok)
        for n, i in enumerate(held):
            block[i ^ bit] = got[n]
    return jnp.stack([block[i] for i in range(8)])


def small_sum(value, n_tok, n_tab):
    bit = 1
    while bit < n_tok:
        value = value + flip_tok(value, bit, n_tok)
        bit *= 2
    total = value
    for shift in range(1, n_tab):
        total = total + shift_tab(value, shift, n_tab)
    return total


def body(
    n_tok, n_tab,
    embedded, cell_index, cell_boxes, box_tables, joined_weight, output_weight,
    expand_weight, reduce_weight, hidden_bias, bias_rows, norm_gains, norm_shifts, cotangent,
):
    tokens, width = embedded.shape
    pages, length = cell_index.shape
    table_rows = box_tables.shape[1]
    ff = expand_weight.shape[1]
    tok = lax.axis_index("tok").astype(jnp.int32).reshape(1)
    z = lax.axis_index("tab")
    cubic = n_tok == 8

    corners = cell_boxes[:, :, :CELLS]
    lo = lambda n: jnp.minimum(corners[:, n], corners[:, n + 2]).reshape(-1)
    hi = lambda n: jnp.maximum(corners[:, n], corners[:, n + 2]).reshape(-1)
    left, right, top, bottom = lo(0), hi(0), lo(1), hi(1)
    none = jnp.full_like(left, -1)
    index_table = jnp.stack(
        [
            jnp.stack([left, right]),
            jnp.stack([top, bottom]),
            jnp.stack([right - left, none]),
            jnp.stack([bottom - top, none]),
        ]
    )
    pick_table = lambda i: lax.dynamic_index_in_dim(index_table, i, 0, keepdims=False)
    group_index = jnp.stack(
        [pick_table(z)]
        + [shift_tab(pick_table((z + s) % n_tab), s, n_tab) for s in range(1, n_tab)]
    )
    padded = jnp.pad(box_tables[0], ((0, 1024 - table_rows), (0, 0)))
    found = lookup(group_index, padded)
    terms = [found[0]] + [shift_tab(found[s], n_tab - s, n_tab) for s in range(1, n_tab)]

    q, k, v, normed, normed_low, rstd0 = embed(
        embedded, cell_index, terms, joined_weight, norm_gains, norm_shifts, bias_rows
    )
    mixed, lse = attn_fwd(q, k, v, pages)
    layer_out, after, after_low, rstd1, act, slope, gs2, gffn, sums2 = ffn_fwd(
        mixed, normed, output_weight, expand_weight, reduce_weight, hidden_bias,
        bias_rows, norm_gains, norm_shifts, cotangent, 256,
    )
    gh, gs1, gattn, gmixed, hidden_sum, sums1 = ffn_bwd(
        gffn, slope, gs2, after, rstd1, reduce_weight, expand_weight, output_weight,
        norm_gains, norm_shifts, 256,
    )
    gj, sums_qv = attn_bwd(q, k, v, mixed, gmixed, lse, pages)
    embedded_grad, cell_grad, sums0 = embed_bwd(
        gs1, gj, joined_weight, normed, rstd0, cell_index, norm_gains, norm_shifts
    )

    cell_grads = [cell_grad] + [shift_tab(cell_grad, s, n_tab) for s in range(1, n_tab)]
    part_a, part_b = table_part(tok if cubic else jnp.zeros_like(tok), group_index, cell_grads, 8)
    if cubic:
        whole_a = table_sum(part_a, (1, 2, 4), n_tok)
        whole_b = table_sum(part_b, (1, 4, 2), n_tok)
        tables_grad = table_out(tok, whole_a, whole_b, table_rows)
    else:
        both = jnp.concatenate([part_a, part_b], axis=2).astype(F32)
        tables_grad = lax.psum(both.reshape(1, -1, width)[:, :table_rows], "tok")

    small = jnp.concatenate(
        [
            sums0.reshape(-1), sums1.reshape(-1), sums2.reshape(-1),
            sums_qv.reshape(-1), hidden_sum.reshape(-1),
        ]
    ).reshape(-1, 128)
    small = small_sum(small, n_tok, n_tab).reshape(-1)
    row = small.reshape(-1, width)
    gains_grad = jnp.stack([row[0], row[2], row[5]])
    shifts_grad = jnp.stack([row[1], row[3], row[6]])
    biases_grad = jnp.stack([row[8], row[9], row[4], row[7]])
    hidden_bias_grad = small[10 * width :]

    if cubic:
        wide_spec = pl.BlockSpec((tokens, ff // 4), lambda s, t: (0, s))
        out_spec = pl.BlockSpec((tokens, width // 4), lambda s, t: (0, s))
        quarter = width // 4
        third = lambda n: pl.BlockSpec(
            (1, tokens, quarter), lambda s, t: ((3 * s + n) // 4, 0, (3 * s + n) % 4)
        )
        ra, rb = weight_grad(lambda r: cols_call(tok, gffn, act, r), n_tok, n_tab)
        ea, eb = weight_grad(
            lambda r: rows_call(tok, after_low, [gh], [wide_spec], ff // 4, r), n_tok, n_tab
        )
        oa, ob = weight_grad(
            lambda r: rows_call(tok, mixed, [gattn], [out_spec], width // 4, r), n_tok, n_tab
        )
        ja, jb = weight_grad(
            lambda r: rows_call(
                tok, normed_low, [gj, gj, gj], [third(0), third(1), third(2)], 3 * quarter, r
            ),
            n_tok, n_tab,
        )
        reduce_grad = jnp.concatenate([ra, rb], axis=1).T
        expand_grad = jnp.concatenate([ea, eb], axis=1)
        output_grad = jnp.concatenate([oa, ob], axis=1)
        joined_grad = jnp.concatenate([ja, jb], axis=1)
    else:
        both = lambda a, b: jnp.einsum("ta,tb->ab", a, b, preferred_element_type=F32).astype(BF)

        def scattered(part):
            part = lax.psum_scatter(part, "tok", scatter_dimension=0, tiled=True)
            return lax.psum_scatter(part, "tab", scatter_dimension=1, tiled=True).astype(F32)

        reduce_grad = scattered(both(act, gffn))
        expand_grad = scattered(both(after_low, gh))
        output_grad = scattered(both(mixed, gattn))
        joined_grad = scattered(both(normed_low, jnp.concatenate([gj[0], gj[1], gj[2]], axis=1)))

    return (
        layer_out, embedded_grad, tables_grad, joined_grad, output_grad, expand_grad,
        reduce_grad, hidden_bias_grad, biases_grad, gains_grad, shifts_grad,
    )


def solution(mesh):
    rows = P(("tok", "tab"), None)
    return jax.shard_map(
        functools.partial(body, mesh.shape["tok"], mesh.shape["tab"]),
        mesh=mesh,
        in_specs=(
            rows, rows, P(("tok", "tab"), None, None), P("tab", None, None),
            P(), P(), P(), P(), P(), P(), P(), P(), rows,
        ),
        out_specs=(
            rows, rows, P("tab", None, None), P("tok", "tab"), P("tok", "tab"),
            P("tok", "tab"), P("tok", "tab"), P(), P(), P(), P(),
        ),
        check_vma=False,
    )
```

time: 1340 us -> 550 us (0.41)
  waiting for transfers between devices: 672 us -> 147 us
  matrix products: 308 us -> 0 us
  Pallas kernels: 0 us -> 255 us
  local copies, waits for them, and re-layouts: 189 us -> 30.8 us
  other arithmetic: 105 us -> 22.8 us
  starting transfers between devices: 7.32 us -> 86.6 us
  blocking collectives: 40.8 us -> 0 us
    reduce_scatter x9 -> x0, waiting for transfers between devices: 519 us -> none  [the longest x1 133 us: body(): lax.psum_scatter((factor * (picked_first + picked_second)).astype(jnp.bfl...]
    dot_general x27 -> x0, matrix products: 308 us -> none  [the longest x1 46.9 us: body(): jnp.dot(after_low, expand_weight, preferred_element_type=wide) + hidden_bias]
    pallas_call x0 -> x17, Pallas kernels: none -> 255 us  [the longest x1 49.5 us: ffn_fwd(): pl.pallas_call(ffn_fwd_kernel, grid=(tokens // tile,), in_specs=[rows, ro...]
    ppermute x0 -> x75, waiting for transfers between devices: none -> 147 us  [the longest x39 76.7 us: flip_tok(): return lax.ppermute(value, 'tok', [(i, i ^ bit) for i in range(size)])]
    gather x6 -> x0, local copies, waits for them, and re-layouts: 108 us -> none  [the longest x2 40.3 us: box_indices(): jnp.take_along_axis(cell_boxes, jnp.broadcast_to(cell_index[:, None, :],...]
    all_gather x1 -> x0, waiting for transfers between devices: 99.4 us -> none  [body(): shard_rows = lax.all_gather(grad_box, 'tab', axis=0, tiled=True)]
    ppermute x0 -> x75, starting transfers between devices: none -> 86.6 us  [the longest x36 60.6 us: shift_tab(): lax.ppermute(value, 'tab', [(i, (i + shift) % size) for i in range(size)])]
    psum x1 -> x0, waiting for transfers between devices: 47.7 us -> none  [body(): tables_grad = lax.psum(own_grad, 'tok')[None]]
  transfers between devices with their start and end apart: 12 -> 75, of which waited for: 10 -> 28; matrix products, arithmetic and copies ran while one was open for 18% -> 8% of each run, Pallas kernels for 0% -> 15%
where the time goes in v1:
time: 550 us; the launch traced here: 543 us
  Pallas kernels  255 us (46%)
  waiting for transfers between devices  147 us (27%)
  starting transfers between devices  86.6 us (16%)
  local copies, waits for them, and re-layouts  30.8 us (6%)
  other arithmetic  22.8 us (4%)
    ppermute x39, waiting for transfers between devices, flip_tok(): return lax.ppermute(value, 'tok', [(i, i ^ bit) for i in range(size)])  76.7 us
    ppermute x36, waiting for transfers between devices, shift_tab(): lax.ppermute(value, 'tab', [(i, (i + shift) % size) for i in range(size)])  70 us
    ppermute x36, starting transfers between devices, shift_tab(): lax.ppermute(value, 'tab', [(i, (i + shift) % size) for i in range(size)])  60.6 us
    pallas_call x1, Pallas kernels, ffn_fwd(): pl.pallas_call(ffn_fwd_kernel, grid=(tokens // tile,), in_specs=[rows, ro...  49.5 us
    pallas_call x6, Pallas kernels, rows_call(): pl.pallas_call(functools.partial(kernel, count=count), grid_spec=pltpu.Pr...  47.9 us
    pallas_call x1, Pallas kernels, attn_bwd(): pl.pallas_call(attn_bwd_kernel, grid=(steps, pages), in_specs=[blk] * 5 +...  35 us
    pallas_call x1, Pallas kernels, ffn_bwd(): pl.pallas_call(ffn_bwd_kernel, grid=(tokens // tile,), in_specs=[rows, lo...  34.3 us
    ppermute x39, starting transfers between devices, flip_tok(): return lax.ppermute(value, 'tok', [(i, i ^ bit) for i in range(size)])  26 us
  transfers between devices with their start and end apart: 75, of which 28 were waited for; matrix products, arithmetic and copies ran while one was open for 8% of the time, Pallas kernels for 15%

profile of v1, /device:TPU:0, one launch (start us, length us, event | category | flops | bytes accessed | tf_op | source)
XLA Modules:
  0.0 543.3 jit_solution(3230629860838250013)
XLA Ops:
  1.6 4.1 collective-permute-start.1
  7.8 3.1 pad.6.table
  10.9 1.6 collective-permute-done
  13.1 5.6 %lookup.1 = bf16[4,256,1024]{2,1,0:T(8,128)(2,1)} custom-call(s32[4,2,256]{2,1,0:T(2,128)} %pad_add_fusion.1.idx, bf16[1024,1024]{1,0:T(8,128)(2,1)} %pad.6.table), custom_call_target="tpu_custom_call" | custom-call | flops 2147483648 | bytes 2097152 | tf_op jit(solution)/shard_map/lookup/pallas_call | solution.py:100
  18.7 2.5 slice_bitcast_fusion
  23.9 11.2 %collective-permute-done.3.t1 = bf16[256,1024]{1,0:T(8,128)(2,1)S(1)} collective-permute-done((bf16[256,1024]{1,0:T(8,128)(2,1)S(1)}, bf16[256,1024]{1,0:T(8,128)(2,1)S(1)}, u32[]{:S(2)}, u32[]{:S(2)}) %collective-permute-start.3) | collective-permute-done | bytes 524320 | tf_op jit(solution)/shard_map/ppermute | solution.py:671
  35.1 32.0 %collective-permute-done.4.t2 = bf16[256,1024]{1,0:T(8,128)(2,1)S(1)} collective-permute-done((bf16[256,1024]{1,0:T(8,128)(2,1)S(1)}, bf16[256,1024]{1,0:T(8,128)(2,1)S(1)}, u32[]{:S(2)}, u32[]{:S(2)}) %collective-permute-start.4) | collective-permute-done | bytes 524320 | tf_op jit(solution)/shard_map/ppermute | solution.py:671
  68.1 14.4 %embed_joined.1 = (bf16[1024,1024]{1,0:T(8,128)(2,1)}, bf16[1024,1024]{1,0:T(8,128)(2,1)}, bf16[1024,1024]{1,0:T(8,128)(2,1)}, f32[1024,1024]{1,0:T(8,128)}, bf1...) custom-call(bf16[1024,1024]{1,0:T(8,128)(2,1)} %emb.1, s32[2,1,512]{2,1,0:T(1,128)} %reshape.280.ci, ...), custom_call_target="tpu_custom_call" | custom-call | flops 6442450944 | bytes 27262976 | tf_op jit(solution)/shard_map/embed_joined/pallas_call | solution.py:142
  82.5 20.0 %attention.1 = (bf16[1024,1024]{1,0:T(8,128)(2,1)}, f32[2,4,4,512]{3,2,1,0:T(4,128)}) custom-call(bf16[1024,1024]{1,0:T(8,128)(2,1)} %get-tuple-element.65.q, bf16[1024,1024]{1,0:T(8,128)(2,1)} %get-tuple-element.66.k, bf16[1024,1024]{1,0:T(8,128)(2,1)} %get-tuple-element.67.v), custom_call_target="tpu_custom_call" | custom-call | flops 14000000000 | bytes 8388608 | tf_op jit(solution)/shard_map/attention/pallas_call | solution.py:191
  102.5 49.5 %ffn_forward.1 = (bf16[1024,1024]{1,0:T(8,128)(2,1)}, f32[1024,1024]{1,0:T(8,128)}, bf16[1024,1024]{1,0:T(8,128)(2,1)}, f32[1024,1]{1,0:T(8,128)}, bf16[1024,409...) custom-call(bf16[1024,1024]{1,0:T(8,128)(2,1)} %get-tuple-element.68, ...), custom_call_target="tpu_custom_call" | custom-call | flops 19327352832 | bytes 62914560 | tf_op jit(solution)/shard_map/ffn_forward/pallas_call | solution.py:321
  152.0 34.3 %ffn_backward.1 = (bf16[1024,4096]{1,0:T(8,128)(2,1)}, f32[1024,1024]{1,0:T(8,128)}, bf16[1024,1024]{1,0:T(8,128)(2,1)}, bf16[1024,1024]{1,0:T(8,128)(2,1)}, f32[1,4096]{1,0:T(1,128)}, /*index=5*/f32[3,1024]{1,0:T(4,128)}) custom-call(bf16[1024,1024]{1,0:T(8,128)(2,1)} %get-tuple-element.71.gffn.lhs, bf16[1024,4096]{1,0:T(8,128)(2,1)} %get-tuple-element.72.slope, ...), custom_call_target="tpu_custom_call" | custom-call | flops 19327352832 | bytes 62914560 | tf_op jit(solution)/shard_map/ffn_backward/pallas_call | solution.py:382
  186.4 35.0 %attention_back.1 = (bf16[3,1024,1024]{2,1,0:T(8,128)(2,1)}, f32[2,1024]{1,0:T(2,128)}) custom-call(bf16[1024,1024]{1,0:T(8,128)(2,1)} %get-tuple-element.65.q, bf16[1024,1024]{1,0:T(8,128)(2,1)} %get-tuple-element.66.k, bf16[1024,1024]{1,0:T(8,128)(2,1)} %get-tuple-element.67.v, bf16[1024,1024]{1,0:T(8,128)(2,1)} %get-tuple-element.68.mixed.lhs, ...), custom_call_target="tpu_custom_call" | custom-call | flops 35000000512 | bytes 16777216 | tf_op jit(solution)/shard_map/attention_back/pallas_call | solution.py:255
  221.4 15.8 %embed_backward.1 = (f32[1024,1024]{1,0:T(8,128)}, bf16[256,1024]{1,0:T(8,128)(2,1)}, f32[2,1024]{1,0:T(2,128)}) custom-call(f32[1024,1024]{1,0:T(8,128)} %get-tuple-element.76.gs1, bf16[3,1024,1024]{2,1,0:T(8,128)(2,1)} %get-tuple-element.79.gj.refs_0_.refs_1_.refs_2_, bf16[1024,3072]{1,0:T(8,128)(2,1)} %w.3, f32[1024,1024]{1,0:T(8,128)} %get-tuple-element.69.normed, ...), custom_call_target="tpu_custom_call" | custom-call | flops 6442450944 | bytes 27262976 | tf_op jit(solution)/shard_map/embed_backward/pallas_call | solution.py:426
  237.3 2.0 collective-permute-start.7
  240.2 9.1 %weight_grad_partner.7 = (bf16[4,4,256,256]{3,2,1,0:T(8,128)(2,1)}, bf16[4,4,256,256]{3,2,1,0:T(8,128)(2,1)}) custom-call(s32[1]{0:T(128)} %bitcast.20.tok, bf16[1024,1024]{1,0:T(8,128)(2,1)} %get-tuple-element.71.gffn.lhs, bf16[1024,4096]{1,0:T(8,128)(2,1)} %get-tuple-element.107.rhs), custom_call_target="tpu_custom_call" | custom-call | flops 4294967296 | bytes 14680064 | tf_op jit(solution)/shard_map/weight_grad_partner/pallas_call | solution.py:650
  249.2 1.6 collective-permute-start.70
  250.8 9.5 %weight_grad_partner.6 = (bf16[4,4,128,512]{3,2,1,0:T(8,128)(2,1)}, bf16[4,4,128,512]{3,2,1,0:T(8,128)(2,1)}) custom-call(s32[1]{0:T(128)} %bitcast.20.tok, bf16[1024,1024]{1,0:T(8,128)(2,1)} %get-tuple-element.99.lhs, bf16[1024,4096]{1,0:T(8,128)(2,1)} %get-tuple-element.100.refs_0_), custom_call_target="tpu_custom_call" | custom-call | flops 4294967296 | bytes 8388608 | tf_op jit(solution)/shard_map/weight_grad_partner/pallas_call | solution.py:569
  260.3 1.6 collective-permute-start.71
  261.9 8.4 %weight_grad_partner.4 = (bf16[4,4,128,384]{3,2,1,0:T(8,128)(2,1)}, bf16[4,4,128,384]{3,2,1,0:T(8,128)(2,1)}) custom-call(s32[1]{0:T(128)} %bitcast.20.tok, bf16[1024,1024]{1,0:T(8,128)(2,1)} %get-tuple-element.85.lhs, bf16[3,1024,1024]{2,1,0:T(8,128)(2,1)} %get-tuple-element.79.gj.refs_0_.refs_1_.refs_2_, ...), custom_call_target="tpu_custom_call" | custom-call | flops 3221225472 | bytes 6815744 | tf_op jit(solution)/shard_map/weight_grad_partner/pallas_call | solution.py:569
  270.3 2.3 collective-permute-start.72
  275.0 5.4 %weight_grad_partner.5 = (bf16[4,4,128,128]{3,2,1,0:T(8,128)(2,1)}, bf16[4,4,128,128]{3,2,1,0:T(8,128)(2,1)}) custom-call(s32[1]{0:T(128)} %bitcast.20.tok, bf16[1024,1024]{1,0:T(8,128)(2,1)} %get-tuple-element.68.mixed.lhs, bf16[1024,1024]{1,0:T(8,128)(2,1)} %get-tuple-element.92.refs_0_), custom_call_target="tpu_custom_call" | custom-call | flops 1073741824 | bytes 3670016 | tf_op jit(solution)/shard_map/weight_grad_partner/pallas_call | solution.py:569
  280.5 1.9 collective-permute-start.8
  286.2 5.6 %weight_grad_own.5 = (bf16[2,4,128,128]{3,2,1,0:T(8,128)(2,1)}, bf16[2,4,128,128]{3,2,1,0:T(8,128)(2,1)}, bf16[2,4,128,128]{3,2,1,0:T(8,128)(2,1)}, bf16[2,4,128,128]{3,2,1,0:T(8,128)(2,1)}) custom-call(s32[1]{0:T(128)} %bitcast.20.tok, bf16[1024,1024]{1,0:T(8,128)(2,1)} %get-tuple-element.68.mixed.lhs, bf16[1024,1024]{1,0:T(8,128)(2,1)} %get-tuple-element.92.refs_0_, ...), custom_call_target="tpu_custom_call" | custom-call | flops 1073741824 | bytes 3670016 | tf_op jit(solution)/shard_map/weight_grad_own/pallas_call | solution.py:569
  294.0 6.4 %table_grad.1 = (bf16[8,128,512]{2,1,0:T(8,128)(2,1)}, bf16[8,128,512]{2,1,0:T(8,128)(2,1)}) custom-call(s32[1]{0:T(128)} %bitcast.20.tok, s32[4,2,256]{2,1,0:T(2,128)} %pad_add_fusion.1.idx, bf16[256,1024]{1,0:T(8,128)(2,1)} %get-tuple-element.82.g0, bf16[256,1024]{1,0:T(8,128)(2,1)} %collective-permute-done.6.g1, ...), custom_call_target="tpu_custom_call" | custom-call | flops 2147483648 | bytes 4194304 | tf_op jit(solution)/shard_map/table_grad/pallas_call | solution.py:479
  304.1 4.9 collective-permute-done.36
  310.6 3.4 collective-permute-done.41
  314.6 3.7 collective-permute-start.38
  319.9 1.9 collective-permute-start.39
  322.4 1.8 collective-permute-done.39
  325.4 2.3 collective-permute-done.42
  329.0 3.6 collective-permute-done.43
  333.6 5.0 collective-permute-done.17
  339.7 3.8 collective-permute-done.11
  345.2 4.3 collective-permute-done.18
  350.0 4.4 collective-permute-done.12
  356.4 4.6 collective-permute-done.19
  361.4 8.8 %weight_grad_own.4 = (bf16[2,4,128,384]{3,2,1,0:T(8,128)(2,1)}, bf16[2,4,128,384]{3,2,1,0:T(8,128)(2,1)}, bf16[2,4,128,384]{3,2,1,0:T(8,128)(2,1)}, bf16[2,4,128,384]{3,2,1,0:T(8,128)(2,1)}) custom-call(s32[1]{0:T(128)} %bitcast.20.tok, bf16[1024,1024]{1,0:T(8,128)(2,1)} %get-tuple-element.85.lhs, ...), custom_call_target="tpu_custom_call" | custom-call | flops 3221225472 | bytes 6815744 | tf_op jit(solution)/shard_map/weight_grad_own/pallas_call | solution.py:569
  370.2 1.8 pad_maximum_fusion.3
  372.0 1.6 collective-permute-start.23
  375.0 10.6 %weight_grad_own.7 = (bf16[2,4,256,256]{3,2,1,0:T(8,128)(2,1)}, bf16[2,4,256,256]{3,2,1,0:T(8,128)(2,1)}, bf16[2,4,256,256]{3,2,1,0:T(8,128)(2,1)}, bf16[2,4,256,256]{3,2,1,0:T(8,128)(2,1)}) custom-call(s32[1]{0:T(128)} %bitcast.20.tok, bf16[1024,1024]{1,0:T(8,128)(2,1)} %get-tuple-element.71.gffn.lhs, bf16[1024,4096]{1,0:T(8,128)(2,1)} %get-tuple-element.107.rhs, ...), custom_call_target="tpu_custom_call" | custom-call | flops 4294967296 | bytes 14680064 | tf_op jit(solution)/shard_map/weight_grad_own/pallas_call | solution.py:650
  386.6 10.2 %weight_grad_own.6 = (bf16[2,4,128,512]{3,2,1,0:T(8,128)(2,1)}, bf16[2,4,128,512]{3,2,1,0:T(8,128)(2,1)}, bf16[2,4,128,512]{3,2,1,0:T(8,128)(2,1)}, bf16[2,4,128,512]{3,2,1,0:T(8,128)(2,1)}) custom-call(s32[1]{0:T(128)} %bitcast.20.tok, bf16[1024,1024]{1,0:T(8,128)(2,1)} %get-tuple-element.99.lhs, bf16[1024,4096]{1,0:T(8,128)(2,1)} %get-tuple-element.100.refs_0_, ...), custom_call_target="tpu_custom_call" | custom-call | flops 4294967296 | bytes 8388608 | tf_op jit(solution)/shard_map/weight_grad_own/pallas_call | solution.py:569
  396.8 1.6 collective-permute-start.64
  401.8 1.6 collective-permute-start.29
  412.0 18.3 %collective-permute-done.24 = bf16[4,128,384]{2,1,0:T(8,128)(2,1)S(1)} collective-permute-done((bf16[4,128,384]{2,1,0:T(8,128)(2,1)S(1)}, bf16[4,128,384]{2,1,0:T(8,128)(2,1)S(1)}, u32[]{:S(2)}, u32[]{:S(2)}) %collective-permute-start.24) | collective-permute-done | bytes 393248 | tf_op jit(solution)/shard_map/ppermute | solution.py:667
  430.6 1.7 collective-permute-start.25
  432.3 1.9 collective-permute-start.26
  441.6 6.2 %table_write.1 = f32[1,1001,1024]{2,1,0:T(8,128)} custom-call(s32[1]{0:T(128)} %bitcast.20.tok, bf16[8,128,512]{2,1,0:T(8,128)(2,1)} %copy-done.5, bf16[8,128,512]{2,1,0:T(8,128)(2,1)} %copy-done.3), custom_call_target="tpu_custom_call" | custom-call | bytes 6291456 | tf_op jit(solution)/shard_map/table_write/pallas_call | solution.py:503
  447.8 8.4 %copy.24 = f32[1,1001,1024]{2,0,1:T(1,128)} copy(f32[1,1001,1024]{2,1,0:T(8,128)} %table_write.1) | data formatting | bytes 8200192
  456.3 1.6 collective-permute-start.47
  457.9 2.5 collective-permute-start.31
  460.4 2.9 collective-permute-start.32
  470.8 11.7 %collective-permute-done.47 = bf16[2,4,128,512]{3,2,1,0:T(8,128)(2,1)S(1)} collective-permute-done((bf16[2,4,128,512]{3,2,1,0:T(8,128)(2,1)}, bf16[2,4,128,512]{3,2,1,0:T(8,128)(2,1)S(1)}, u32[]{:S(2)}, u32[]{:S(2)}) %collective-permute-start.47) | collective-permute-done | bytes 1048608 | tf_op jit(solution)/shard_map/ppermute | solution.py:667
  482.6 1.6 collective-permute-start.48
  484.2 5.4 collective-permute-done.52
  490.3 10.4 %collective-permute-done.60 = bf16[4,256,256]{2,1,0:T(8,128)(2,1)S(1)} collective-permute-done((bf16[4,256,256]{2,1,0:T(8,128)(2,1)S(1)}, bf16[4,256,256]{2,1,0:T(8,128)(2,1)S(1)}, u32[]{:S(2)}, u32[]{:S(2)}) %collective-permute-start.60) | collective-permute-done | bytes 524320 | tf_op jit(solution)/shard_map/ppermute | solution.py:667
  502.4 2.6 collective-permute-start.62
  510.2 2.5 collective-permute-start.68
  512.8 4.0 collective-permute-done.62
  516.7 6.1 %collective-permute-start.50 = (bf16[128,512]{1,0:T(8,128)(2,1)S(1)}, bf16[128,512]{1,0:T(8,128)(2,1)S(1)}, u32[]{:S(2)}, u32[]{:S(2)}) collective-permute-start(bf16[128,512]{1,0:T(8,128)(2,1)S(1)} %get-tuple-element.164), channel_id=1, source_target_pairs={{0,2},{1,3},{2,0},{3,1},{4,6},{5,7},{6,4},{7,5},{8,10},{9,11},{10,... | collective-permute-start | bytes 393224 | tf_op jit(solution)/shard_map/ppermute | solution.py:671
  522.9 3.4 collective-permute-start.51
  526.4 4.0 collective-permute-done.67
  530.9 3.5 collective-permute-start.55
  535.5 1.6 collective-permute-start.56
  537.4 4.8 collective-permute-done.55
  (255 shorter events, 73.8 us)
Async XLA Ops:
  1.6 9.3 %collective-permute-start.1 = (s32[2,256]{1,0:T(2,128)S(1)}, s32[2,256]{1,0:T(2,128)S(1)}, u32[]{:S(2)}, u32[]{:S(2)}) collective-permute-start(s32[2,256]{1,0:T(2,128)S(1)} %get-tuple-element.197), channel_id=1, source_target_pairs={{0,2},{1,3},{2,0},{3,1},{4,6},{5,7},{6,4},{7,5},{8,10},{9,11},{10,... | collective-permute-start | bytes 6152 | tf_op jit(solution)/shard_map/ppermute | solution.py:671
  21.2 13.9 %collective-permute-start.3 = (bf16[256,1024]{1,0:T(8,128)(2,1)S(1)}, bf16[256,1024]{1,0:T(8,128)(2,1)S(1)}, u32[]{:S(2)}, u32[]{:S(2)}) collective-permute-start(bf16[256,1024]{1,0:T(8,128)(2,1)S(1)} %get-tuple-element.142), channel_id=1, source_target_pairs={{0,3},{1,0},{2,1},{3,2},{4,7},{5,4},{6,5},{7,6},{8,11},{9,8},{10,9... | collective-permute-start | bytes 1572872 | tf_op jit(solution)/shard_map/ppermute | solution.py:671
  22.7 44.4 %collective-permute-start.4 = (bf16[256,1024]{1,0:T(8,128)(2,1)S(1)}, bf16[256,1024]{1,0:T(8,128)(2,1)S(1)}, u32[]{:S(2)}, u32[]{:S(2)}) collective-permute-start(bf16[256,1024]{1,0:T(8,128)(2,1)S(1)} %get-tuple-element.141), channel_id=1, source_target_pairs={{0,2},{1,3},{2,0},{3,1},{4,6},{5,7},{6,4},{7,5},{8,10},{9,11},{10,... | collective-permute-start | bytes 1572872 | tf_op jit(solution)/shard_map/ppermute | solution.py:671
  22.7 44.4 %collective-permute-start.5 = (bf16[256,1024]{1,0:T(8,128)(2,1)S(1)}, bf16[256,1024]{1,0:T(8,128)(2,1)S(1)}, u32[]{:S(2)}, u32[]{:S(2)}) collective-permute-start(bf16[256,1024]{1,0:T(8,128)(2,1)S(1)} %get-tuple-element.140), channel_id=1, source_target_pairs={{0,1},{1,2},{2,3},{3,0},{4,5},{5,6},{6,7},{7,4},{8,9},{9,10},{10,1... | collective-permute-start | bytes 1572872 | tf_op jit(solution)/shard_map/ppermute | solution.py:671
  237.2 54.7 %collective-permute-start.6 = (bf16[256,1024]{1,0:T(8,128)(2,1)}, bf16[256,1024]{1,0:T(8,128)(2,1)}, u32[]{:S(2)}, u32[]{:S(2)}) collective-permute-start(bf16[256,1024]{1,0:T(8,128)(2,1)} %get-tuple-element.82.g0), channel_id=1, source_target_pairs={{0,1},{1,2},{2,3},{3,0},{4,5},{5,6},{6,7},{7,4},{8,9},{9,10},{10,1... | collective-permute-start | bytes 1572872 | tf_op jit(solution)/shard_map/ppermute | solution.py:671
  237.3 55.2 %collective-permute-start.7 = (bf16[256,1024]{1,0:T(8,128)(2,1)}, bf16[256,1024]{1,0:T(8,128)(2,1)}, u32[]{:S(2)}, u32[]{:S(2)}) collective-permute-start(bf16[256,1024]{1,0:T(8,128)(2,1)} %get-tuple-element.82.g0), channel_id=1, source_target_pairs={{0,2},{1,3},{2,0},{3,1},{4,6},{5,7},{6,4},{7,5},{8,10},{9,11},{10,... | collective-permute-start | bytes 1572872 | tf_op jit(solution)/shard_map/ppermute | solution.py:671
  240.1 9.1 %collective-permute-start.69 = (f32[112,128]{1,0:T(8,128)S(1)}, f32[112,128]{1,0:T(8,128)S(1)}, u32[]{:S(2)}, u32[]{:S(2)}) collective-permute-start(f32[112,128]{1,0:T(8,128)S(1)} %bitcast.194), channel_id=1, source_target_pairs={{0,4},{4,0},{8,12},{12,8},{16,20},{20,16},{24,28},{28,24},{1,5},{5... | collective-permute-start | bytes 172040 | tf_op jit(solution)/shard_map/ppermute | solution.py:667
  249.2 11.0 %collective-permute-start.70 = (f32[112,128]{1,0:T(8,128)S(1)}, f32[112,128]{1,0:T(8,128)S(1)}, u32[]{:S(2)}, u32[]{:S(2)}) collective-permute-start(f32[112,128]{1,0:T(8,128)S(1)} %bitcast_add_fusion), channel_id=1, source_target_pairs={{0,8},{4,12},{8,0},{12,4},{16,24},{20,28},{24,16},{28,20},{1,9},{5... | collective-permute-start | bytes 172040 | tf_op jit(solution)/shard_map/ppermute | solution.py:667
  260.3 10.0 %collective-permute-start.71 = (f32[112,128]{1,0:T(8,128)S(1)}, f32[112,128]{1,0:T(8,128)S(1)}, u32[]{:S(2)}, u32[]{:S(2)}) collective-permute-start(f32[112,128]{1,0:T(8,128)S(1)} %fusion.49), channel_id=1, source_target_pairs={{0,16},{4,20},{8,24},{12,28},{16,0},{20,4},{24,8},{28,12},{1,17},{... | collective-permute-start | bytes 172040 | tf_op jit(solution)/shard_map/ppermute | solution.py:667
  270.3 10.2 %collective-permute-start.72 = (f32[112,128]{1,0:T(8,128)S(1)}, f32[112,128]{1,0:T(8,128)S(1)}, u32[]{:S(2)}, u32[]{:S(2)}) collective-permute-start(f32[112,128]{1,0:T(8,128)S(1)} %add.430), channel_id=1, source_target_pairs={{0,1},{1,2},{2,3},{3,0},{4,5},{5,6},{6,7},{7,4},{8,9},{9,10},{10,1... | collective-permute-start | bytes 172040 | tf_op jit(solution)/shard_map/ppermute | solution.py:671
  272.6 9.8 %collective-permute-start.73 = (f32[112,128]{1,0:T(8,128)S(1)}, f32[112,128]{1,0:T(8,128)S(1)}, u32[]{:S(2)}, u32[]{:S(2)}) collective-permute-start(f32[112,128]{1,0:T(8,128)S(1)} %add.430), channel_id=1, source_target_pairs={{0,2},{1,3},{2,0},{3,1},{4,6},{5,7},{6,4},{7,5},{8,10},{9,11},{10,... | collective-permute-start | bytes 172040 | tf_op jit(solution)/shard_map/ppermute | solution.py:671
  273.7 8.7 %collective-permute-start.74 = (f32[112,128]{1,0:T(8,128)S(1)}, f32[112,128]{1,0:T(8,128)S(1)}, u32[]{:S(2)}, u32[]{:S(2)}) collective-permute-start(f32[112,128]{1,0:T(8,128)S(1)} %add.430), channel_id=1, source_target_pairs={{0,3},{1,0},{2,1},{3,2},{4,7},{5,4},{6,5},{7,6},{8,11},{9,8},{10,9... | collective-permute-start | bytes 172040 | tf_op jit(solution)/shard_map/ppermute | solution.py:671
  280.5 13.5 %collective-permute-start.8 = (bf16[256,1024]{1,0:T(8,128)(2,1)}, bf16[256,1024]{1,0:T(8,128)(2,1)}, u32[]{:S(2)}, u32[]{:S(2)}) collective-permute-start(bf16[256,1024]{1,0:T(8,128)(2,1)} %get-tuple-element.82.g0), channel_id=1, source_target_pairs={{0,3},{1,0},{2,1},{3,2},{4,7},{5,4},{6,5},{7,6},{8,11},{9,8},{10,9... | collective-permute-start | bytes 1572872 | tf_op jit(solution)/shard_map/ppermute | solution.py:671
  284.8 58.7 %collective-permute-start.21 = (bf16[4,4,128,384]{3,2,1,0:T(8,128)(2,1)}, bf16[4,4,128,384]{3,2,1,0:T(8,128)(2,1)S(1)}, u32[]{:S(2)}, u32[]{:S(2)}) collective-permute-start(bf16[4,4,128,384]{3,2,1,0:T(8,128)(2,1)} %get-tuple-element.86), channel_id=1, source_target_pairs={{0,4},{4,0},{8,12},{12,8},{16,20},{20,16},{24,28},{28,24},{1,5},{5... | collective-permute-start | bytes 4718600 | tf_op jit(solution)/shard_map/ppermute | solution.py:667
  286.1 57.9 %collective-permute-start.22 = (bf16[4,4,128,384]{3,2,1,0:T(8,128)(2,1)}, bf16[4,4,128,384]{3,2,1,0:T(8,128)(2,1)S(1)}, u32[]{:S(2)}, u32[]{:S(2)}) collective-permute-start(bf16[4,4,128,384]{3,2,1,0:T(8,128)(2,1)} %get-tuple-element.87), channel_id=1, source_target_pairs={{0,4},{4,0},{8,12},{12,8},{16,20},{20,16},{24,28},{28,24},{1,5},{5... | collective-permute-start | bytes 4718600 | tf_op jit(solution)/shard_map/ppermute | solution.py:667
  291.9 10.2 %collective-permute-start.35 = (bf16[2,4,128,128]{3,2,1,0:T(8,128)(2,1)}, bf16[2,4,128,128]{3,2,1,0:T(8,128)(2,1)}, u32[]{:S(2)}, u32[]{:S(2)}) collective-permute-start(bf16[2,4,128,128]{3,2,1,0:T(8,128)(2,1)} %get-tuple-element.96), channel_id=1, source_target_pairs={{0,8},{4,12},{8,0},{12,4},{16,24},{20,28},{24,16},{28,20},{1,9},{5... | collective-permute-start | bytes 786440 | tf_op jit(solution)/shard_map/ppermute | solution.py:667
  292.5 11.0 %collective-permute-start.40 = (bf16[2,4,128,128]{3,2,1,0:T(8,128)(2,1)}, bf16[2,4,128,128]{3,2,1,0:T(8,128)(2,1)S(1)}, u32[]{:S(2)}, u32[]{:S(2)}) collective-permute-start(bf16[2,4,128,128]{3,2,1,0:T(8,128)(2,1)} %get-tuple-element.98), channel_id=1, source_target_pairs={{0,16},{4,20},{8,24},{12,28},{16,0},{20,4},{24,8},{28,12},{1,17},{... | collective-permute-start | bytes 786440 | tf_op jit(solution)/shard_map/ppermute | solution.py:667
  301.8 12.8 %collective-permute-start.15 = (bf16[4,128,512]{2,1,0:T(8,128)(2,1)S(1)}, bf16[4,128,512]{2,1,0:T(8,128)(2,1)S(1)}, u32[]{:S(2)}, u32[]{:S(2)}) collective-permute-start(bf16[4,128,512]{2,1,0:T(8,128)(2,1)S(1)} %pad_maximum_fusion.2), channel_id=1, source_target_pairs={{0,4},{4,0},{8,12},{12,8},{16,20},{20,16},{24,28},{28,24},{1,5},{5... | collective-permute-start | bytes 1572872 | tf_op jit(solution)/shard_map/ppermute | solution.py:667
  302.0 16.3 %collective-permute-start.9 = (bf16[4,128,512]{2,1,0:T(8,128)(2,1)S(1)}, bf16[4,128,512]{2,1,0:T(8,128)(2,1)S(1)}, u32[]{:S(2)}, u32[]{:S(2)}) collective-permute-start(bf16[4,128,512]{2,1,0:T(8,128)(2,1)S(1)} %pad_maximum_fusion), channel_id=1, source_target_pairs={{0,4},{4,0},{8,12},{12,8},{16,20},{20,16},{24,28},{28,24},{1,5},{5... | collective-permute-start | bytes 1572872 | tf_op jit(solution)/shard_map/ppermute | solution.py:667
  303.5 5.6 %collective-permute-start.36 = (bf16[4,128,128]{2,1,0:T(8,128)(2,1)S(1)}, bf16[4,128,128]{2,1,0:T(8,128)(2,1)S(1)}, u32[]{:S(2)}, u32[]{:S(2)}) collective-permute-start(bf16[4,128,128]{2,1,0:T(8,128)(2,1)S(1)} %fusion.33), channel_id=1, source_target_pairs={{0,16},{4,20},{8,24},{12,28},{16,0},{20,4},{24,8},{28,12},{1,17},{... | collective-permute-start | bytes 393224 | tf_op jit(solution)/shard_map/ppermute | solution.py:667
  314.0 5.9 %collective-permute-start.37 = (bf16[128,128]{1,0:T(8,128)(2,1)S(1)}, bf16[128,128]{1,0:T(8,128)(2,1)S(1)}, u32[]{:S(2)}, u32[]{:S(2)}) collective-permute-start(bf16[128,128]{1,0:T(8,128)(2,1)S(1)} %get-tuple-element.176), channel_id=1, source_target_pairs={{0,1},{1,2},{2,3},{3,0},{4,5},{5,6},{6,7},{7,4},{8,9},{9,10},{10,1... | collective-permute-start | bytes 98312 | tf_op jit(solution)/shard_map/ppermute | solution.py:671
  314.6 7.3 %collective-permute-start.38 = (bf16[128,128]{1,0:T(8,128)(2,1)S(1)}, bf16[128,128]{1,0:T(8,128)(2,1)S(1)}, u32[]{:S(2)}, u32[]{:S(2)}) collective-permute-start(bf16[128,128]{1,0:T(8,128)(2,1)S(1)} %get-tuple-element.178), channel_id=1, source_target_pairs={{0,2},{1,3},{2,0},{3,1},{4,6},{5,7},{6,4},{7,5},{8,10},{9,11},{10,... | collective-permute-start | bytes 98312 | tf_op jit(solution)/shard_map/ppermute | solution.py:671
  318.3 9.9 %collective-permute-start.16 = (bf16[2,128,512]{2,1,0:T(8,128)(2,1)S(1)}, bf16[2,128,512]{2,1,0:T(8,128)(2,1)S(1)}, u32[]{:S(2)}, u32[]{:S(2)}) collective-permute-start(bf16[2,128,512]{2,1,0:T(8,128)(2,1)S(1)} %pad_maximum_fusion.8), channel_id=1, source_target_pairs={{0,16},{4,20},{8,24},{12,28},{16,0},{20,4},{24,8},{28,12},{1,17},{... | collective-permute-start | bytes 786440 | tf_op jit(solution)/shard_map/ppermute | solution.py:667
  321.8 5.9 %collective-permute-start.42 = (bf16[128,128]{1,0:T(8,128)(2,1)S(1)}, bf16[128,128]{1,0:T(8,128)(2,1)S(1)}, u32[]{:S(2)}, u32[]{:S(2)}) collective-permute-start(bf16[128,128]{1,0:T(8,128)(2,1)S(1)} %get-tuple-element.179), channel_id=1, source_target_pairs={{0,1},{1,2},{2,3},{3,0},{4,5},{5,6},{6,7},{7,4},{8,9},{9,10},{10,1... | collective-permute-start | bytes 98312 | tf_op jit(solution)/shard_map/ppermute | solution.py:671
  324.2 8.8 %collective-permute-start.10 = (bf16[2,128,512]{2,1,0:T(8,128)(2,1)S(1)}, bf16[2,128,512]{2,1,0:T(8,128)(2,1)S(1)}, u32[]{:S(2)}, u32[]{:S(2)}) collective-permute-start(bf16[2,128,512]{2,1,0:T(8,128)(2,1)S(1)} %pad_maximum_fusion.6), channel_id=1, source_target_pairs={{0,8},{4,12},{8,0},{12,4},{16,24},{20,28},{24,16},{28,20},{1,9},{5... | collective-permute-start | bytes 786440 | tf_op jit(solution)/shard_map/ppermute | solution.py:667
  332.5 42.0 %collective-permute-start.57 = (bf16[4,4,256,256]{3,2,1,0:T(8,128)(2,1)}, bf16[4,4,256,256]{3,2,1,0:T(8,128)(2,1)}, u32[]{:S(2)}, u32[]{:S(2)}) collective-permute-start(bf16[4,4,256,256]{3,2,1,0:T(8,128)(2,1)} %get-tuple-element.108), channel_id=1, source_target_pairs={{0,4},{4,0},{8,12},{12,8},{16,20},{20,16},{24,28},{28,24},{1,5},{5... | collective-permute-start | bytes 6291464 | tf_op jit(solution)/shard_map/ppermute | solution.py:667
  332.5 42.5 %collective-permute-start.58 = (bf16[4,4,256,256]{3,2,1,0:T(8,128)(2,1)}, bf16[4,4,256,256]{3,2,1,0:T(8,128)(2,1)}, u32[]{:S(2)}, u32[]{:S(2)}) collective-permute-start(bf16[4,4,256,256]{3,2,1,0:T(8,128)(2,1)} %get-tuple-element.109), channel_id=1, source_target_pairs={{0,4},{4,0},{8,12},{12,8},{16,20},{20,16},{24,28},{28,24},{1,5},{5... | collective-permute-start | bytes 6291464 | tf_op jit(solution)/shard_map/ppermute | solution.py:667
  333.0 5.5 %collective-permute-start.17 = (bf16[1,128,512]{2,1,0:T(8,128)(2,1)S(1)}, bf16[1,128,512]{2,1,0:T(8,128)(2,1)S(1)}, u32[]{:S(2)}, u32[]{:S(2)}) collective-permute-start(bf16[1,128,512]{2,1,0:T(8,128)(2,1)S(1)} %add_convert_fusion.17), channel_id=1, source_target_pairs={{0,8},{4,12},{8,0},{12,4},{16,24},{20,28},{24,16},{28,20},{1,9},{5... | collective-permute-start | bytes 393224 | tf_op jit(solution)/shard_map/ppermute | solution.py:667
  343.5 42.1 %collective-permute-start.45 = (bf16[4,4,128,512]{3,2,1,0:T(8,128)(2,1)}, bf16[4,4,128,512]{3,2,1,0:T(8,128)(2,1)}, u32[]{:S(2)}, u32[]{:S(2)}) collective-permute-start(bf16[4,4,128,512]{3,2,1,0:T(8,128)(2,1)} %get-tuple-element.101), channel_id=1, source_target_pairs={{0,4},{4,0},{8,12},{12,8},{16,20},{20,16},{24,28},{28,24},{1,5},{5... | collective-permute-start | bytes 6291464 | tf_op jit(solution)/shard_map/ppermute | solution.py:667
  343.5 42.6 %collective-permute-start.46 = (bf16[4,4,128,512]{3,2,1,0:T(8,128)(2,1)}, bf16[4,4,128,512]{3,2,1,0:T(8,128)(2,1)}, u32[]{:S(2)}, u32[]{:S(2)}) collective-permute-start(bf16[4,4,128,512]{3,2,1,0:T(8,128)(2,1)} %get-tuple-element.102), channel_id=1, source_target_pairs={{0,4},{4,0},{8,12},{12,8},{16,20},{20,16},{24,28},{28,24},{1,5},{5... | collective-permute-start | bytes 6291464 | tf_op jit(solution)/shard_map/ppermute | solution.py:667
  344.0 5.5 %collective-permute-start.18 = (bf16[1,128,512]{2,1,0:T(8,128)(2,1)S(1)}, bf16[1,128,512]{2,1,0:T(8,128)(2,1)S(1)}, u32[]{:S(2)}, u32[]{:S(2)}) collective-permute-start(bf16[1,128,512]{2,1,0:T(8,128)(2,1)S(1)} %get-tuple-element.131), channel_id=1, source_target_pairs={{0,8},{4,12},{8,0},{12,4},{16,24},{20,28},{24,16},{28,20},{1,9},{5... | collective-permute-start | bytes 393224 | tf_op jit(solution)/shard_map/ppermute | solution.py:667
  354.5 6.5 %collective-permute-start.19 = (bf16[2,128,512]{2,1,0:T(8,128)(2,1)S(1)}, bf16[2,128,512]{2,1,0:T(8,128)(2,1)}, u32[]{:S(2)}, u32[]{:S(2)}) collective-permute-start(bf16[2,128,512]{2,1,0:T(8,128)(2,1)S(1)} %pad_maximum_fusion.9), channel_id=1, source_target_pairs={{0,16},{4,20},{8,24},{12,28},{16,0},{20,4},{24,8},{28,12},{1,17},{... | collective-permute-start | bytes 786440 | tf_op jit(solution)/shard_map/ppermute | solution.py:667
  360.9 11.1 %collective-permute-start.13 = (bf16[2,128,512]{2,1,0:T(8,128)(2,1)}, bf16[2,128,512]{2,1,0:T(8,128)(2,1)S(1)}, u32[]{:S(2)}, u32[]{:S(2)}) collective-permute-start(bf16[2,128,512]{2,1,0:T(8,128)(2,1)} %pad_maximum_fusion.7), channel_id=1, source_target_pairs={{0,8},{4,12},{8,0},{12,4},{16,24},{20,28},{24,16},{28,20},{1,9},{5... | collective-permute-start | bytes 786440 | tf_op jit(solution)/shard_map/ppermute | solution.py:667
  372.0 24.7 %collective-permute-start.23 = (bf16[2,4,128,384]{3,2,1,0:T(8,128)(2,1)}, bf16[2,4,128,384]{3,2,1,0:T(8,128)(2,1)S(1)}, u32[]{:S(2)}, u32[]{:S(2)}) collective-permute-start(bf16[2,4,128,384]{3,2,1,0:T(8,128)(2,1)} %get-tuple-element.89), channel_id=1, source_target_pairs={{0,8},{4,12},{8,0},{12,4},{16,24},{20,28},{24,16},{28,20},{1,9},{5... | collective-permute-start | bytes 2359304 | tf_op jit(solution)/shard_map/ppermute | solution.py:667
  374.5 25.2 %collective-permute-start.28 = (bf16[2,4,128,384]{3,2,1,0:T(8,128)(2,1)}, bf16[2,4,128,384]{3,2,1,0:T(8,128)(2,1)}, u32[]{:S(2)}, u32[]{:S(2)}) collective-permute-start(bf16[2,4,128,384]{3,2,1,0:T(8,128)(2,1)} %get-tuple-element.91), channel_id=1, source_target_pairs={{0,16},{4,20},{8,24},{12,28},{16,0},{20,4},{24,8},{28,12},{1,17},{... | collective-permute-start | bytes 2359304 | tf_op jit(solution)/shard_map/ppermute | solution.py:667
  375.0 26.8 %collective-permute-start.20 = (bf16[4,128,512]{2,1,0:T(8,128)(2,1)}, bf16[4,128,512]{2,1,0:T(8,128)(2,1)}, u32[]{:S(2)}, u32[]{:S(2)}) collective-permute-start(bf16[4,128,512]{2,1,0:T(8,128)(2,1)} %pad_maximum_fusion.3), channel_id=1, source_target_pairs={{0,4},{4,0},{8,12},{12,8},{16,20},{20,16},{24,28},{28,24},{1,5},{5... | collective-permute-start | bytes 1572872 | tf_op jit(solution)/shard_map/ppermute | solution.py:667
  385.5 23.5 %collective-permute-start.14 = (bf16[4,128,512]{2,1,0:T(8,128)(2,1)}, bf16[4,128,512]{2,1,0:T(8,128)(2,1)}, u32[]{:S(2)}, u32[]{:S(2)}) collective-permute-start(bf16[4,128,512]{2,1,0:T(8,128)(2,1)} %pad_maximum_fusion.1), channel_id=1, source_target_pairs={{0,4},{4,0},{8,12},{12,8},{16,20},{20,16},{24,28},{28,24},{1,5},{5... | collective-permute-start | bytes 1572872 | tf_op jit(solution)/shard_map/ppermute | solution.py:667
  386.1 80.2 %collective-permute-start.59 = (bf16[2,4,256,256]{3,2,1,0:T(8,128)(2,1)}, bf16[2,4,256,256]{3,2,1,0:T(8,128)(2,1)}, u32[]{:S(2)}, u32[]{:S(2)}) collective-permute-start(bf16[2,4,256,256]{3,2,1,0:T(8,128)(2,1)} %get-tuple-element.111), channel_id=1, source_target_pairs={{0,8},{4,12},{8,0},{12,4},{16,24},{20,28},{24,16},{28,20},{1,9},{5... | collective-permute-start | bytes 3145736 | tf_op jit(solution)/shard_map/ppermute | solution.py:667
  396.8 72.2 %collective-permute-start.64 = (bf16[2,4,256,256]{3,2,1,0:T(8,128)(2,1)}, bf16[2,4,256,256]{3,2,1,0:T(8,128)(2,1)}, u32[]{:S(2)}, u32[]{:S(2)}) collective-permute-start(bf16[2,4,256,256]{3,2,1,0:T(8,128)(2,1)} %get-tuple-element.113), channel_id=1, source_target_pairs={{0,16},{4,20},{8,24},{12,28},{16,0},{20,4},{24,8},{28,12},{1,17},{... | collective-permute-start | bytes 3145736 | tf_op jit(solution)/shard_map/ppermute | solution.py:667
  399.7 30.7 %collective-permute-start.24 = (bf16[4,128,384]{2,1,0:T(8,128)(2,1)S(1)}, bf16[4,128,384]{2,1,0:T(8,128)(2,1)S(1)}, u32[]{:S(2)}, u32[]{:S(2)}) collective-permute-start(bf16[4,128,384]{2,1,0:T(8,128)(2,1)S(1)} %fusion.15), channel_id=1, source_target_pairs={{0,16},{4,20},{8,24},{12,28},{16,0},{20,4},{24,8},{28,12},{1,17},{... | collective-permute-start | bytes 1179656 | tf_op jit(solution)/shard_map/ppermute | solution.py:667
  401.8 32.4 %collective-permute-start.29 = (bf16[4,128,384]{2,1,0:T(8,128)(2,1)S(1)}, bf16[4,128,384]{2,1,0:T(8,128)(2,1)S(1)}, u32[]{:S(2)}, u32[]{:S(2)}) collective-permute-start(bf16[4,128,384]{2,1,0:T(8,128)(2,1)S(1)} %fusion.17), channel_id=1, source_target_pairs={{0,8},{4,12},{8,0},{12,4},{16,24},{20,28},{24,16},{28,20},{1,9},{5... | collective-permute-start | bytes 1179656 | tf_op jit(solution)/shard_map/ppermute | solution.py:667
  430.6 7.6 %collective-permute-start.25 = (bf16[128,384]{1,0:T(8,128)(2,1)S(1)}, bf16[128,384]{1,0:T(8,128)(2,1)S(1)}, u32[]{:S(2)}, u32[]{:S(2)}) collective-permute-start(bf16[128,384]{1,0:T(8,128)(2,1)S(1)} %get-tuple-element.168), channel_id=1, source_target_pairs={{0,1},{1,2},{2,3},{3,0},{4,5},{5,6},{6,7},{7,4},{8,9},{9,10},{10,1... | collective-permute-start | bytes 294920 | tf_op jit(solution)/shard_map/ppermute | solution.py:671
  432.3 24.0 %collective-permute-start.26 = (bf16[128,384]{1,0:T(8,128)(2,1)S(1)}, bf16[128,384]{1,0:T(8,128)(2,1)S(1)}, u32[]{:S(2)}, u32[]{:S(2)}) collective-permute-start(bf16[128,384]{1,0:T(8,128)(2,1)S(1)} %get-tuple-element.170), channel_id=1, source_target_pairs={{0,2},{1,3},{2,0},{3,1},{4,6},{5,7},{6,4},{7,5},{8,10},{9,11},{10,... | collective-permute-start | bytes 294920 | tf_op jit(solution)/shard_map/ppermute | solution.py:671
  434.1 23.7 %collective-permute-start.27 = (bf16[128,384]{1,0:T(8,128)(2,1)S(1)}, bf16[128,384]{1,0:T(8,128)(2,1)S(1)}, u32[]{:S(2)}, u32[]{:S(2)}) collective-permute-start(bf16[128,384]{1,0:T(8,128)(2,1)S(1)} %get-tuple-element.169), channel_id=1, source_target_pairs={{0,3},{1,0},{2,1},{3,2},{4,7},{5,4},{6,5},{7,6},{8,11},{9,8},{10,9... | collective-permute-start | bytes 294920 | tf_op jit(solution)/shard_map/ppermute | solution.py:671
  438.2 22.2 %collective-permute-start.30 = (bf16[128,384]{1,0:T(8,128)(2,1)S(1)}, bf16[128,384]{1,0:T(8,128)(2,1)S(1)}, u32[]{:S(2)}, u32[]{:S(2)}) collective-permute-start(bf16[128,384]{1,0:T(8,128)(2,1)S(1)} %get-tuple-element.171), channel_id=1, source_target_pairs={{0,1},{1,2},{2,3},{3,0},{4,5},{5,6},{6,7},{7,4},{8,9},{9,10},{10,1... | collective-permute-start | bytes 294920 | tf_op jit(solution)/shard_map/ppermute | solution.py:671
  456.3 26.2 %collective-permute-start.47 = (bf16[2,4,128,512]{3,2,1,0:T(8,128)(2,1)}, bf16[2,4,128,512]{3,2,1,0:T(8,128)(2,1)S(1)}, u32[]{:S(2)}, u32[]{:S(2)}) collective-permute-start(bf16[2,4,128,512]{3,2,1,0:T(8,128)(2,1)} %get-tuple-element.104), channel_id=1, source_target_pairs={{0,8},{4,12},{8,0},{12,4},{16,24},{20,28},{24,16},{28,20},{1,9},{5... | collective-permute-start | bytes 3145736 | tf_op jit(solution)/shard_map/ppermute | solution.py:667
  457.9 5.5 %collective-permute-start.31 = (bf16[128,384]{1,0:T(8,128)(2,1)S(1)}, bf16[128,384]{1,0:T(8,128)(2,1)S(1)}, u32[]{:S(2)}, u32[]{:S(2)}) collective-permute-start(bf16[128,384]{1,0:T(8,128)(2,1)S(1)} %get-tuple-element.173), channel_id=1, source_target_pairs={{0,2},{1,3},{2,0},{3,1},{4,6},{5,7},{6,4},{7,5},{8,10},{9,11},{10,... | collective-permute-start | bytes 294920 | tf_op jit(solution)/shard_map/ppermute | solution.py:671
  463.4 26.3 %collective-permute-start.52 = (bf16[2,4,128,512]{3,2,1,0:T(8,128)(2,1)}, bf16[2,4,128,512]{3,2,1,0:T(8,128)(2,1)S(1)}, u32[]{:S(2)}, u32[]{:S(2)}) collective-permute-start(bf16[2,4,128,512]{3,2,1,0:T(8,128)(2,1)} %get-tuple-element.106), channel_id=1, source_target_pairs={{0,16},{4,20},{8,24},{12,28},{16,0},{20,4},{24,8},{28,12},{1,17},{... | collective-permute-start | bytes 3145736 | tf_op jit(solution)/shard_map/ppermute | solution.py:667
  467.6 33.0 %collective-permute-start.60 = (bf16[4,256,256]{2,1,0:T(8,128)(2,1)S(1)}, bf16[4,256,256]{2,1,0:T(8,128)(2,1)S(1)}, u32[]{:S(2)}, u32[]{:S(2)}) collective-permute-start(bf16[4,256,256]{2,1,0:T(8,128)(2,1)S(1)} %fusion.11), channel_id=1, source_target_pairs={{0,16},{4,20},{8,24},{12,28},{16,0},{20,4},{24,8},{28,12},{1,17},{... | collective-permute-start | bytes 1572872 | tf_op jit(solution)/shard_map/ppermute | solution.py:667
  470.2 34.8 %collective-permute-start.65 = (bf16[4,256,256]{2,1,0:T(8,128)(2,1)S(1)}, bf16[4,256,256]{2,1,0:T(8,128)(2,1)S(1)}, u32[]{:S(2)}, u32[]{:S(2)}) collective-permute-start(bf16[4,256,256]{2,1,0:T(8,128)(2,1)S(1)} %fusion.13), channel_id=1, source_target_pairs={{0,8},{4,12},{8,0},{12,4},{16,24},{20,28},{24,16},{28,20},{1,9},{5... | collective-permute-start | bytes 1572872 | tf_op jit(solution)/shard_map/ppermute | solution.py:667
  482.6 24.5 %collective-permute-start.48 = (bf16[4,128,512]{2,1,0:T(8,128)(2,1)S(1)}, bf16[4,128,512]{2,1,0:T(8,128)(2,1)S(1)}, u32[]{:S(2)}, u32[]{:S(2)}) collective-permute-start(bf16[4,128,512]{2,1,0:T(8,128)(2,1)S(1)} %fusion.7), channel_id=1, source_target_pairs={{0,16},{4,20},{8,24},{12,28},{16,0},{20,4},{24,8},{28,12},{1,17},{... | collective-permute-start | bytes 1572872 | tf_op jit(solution)/shard_map/ppermute | solution.py:667
  489.8 18.7 %collective-permute-start.53 = (bf16[4,128,512]{2,1,0:T(8,128)(2,1)S(1)}, bf16[4,128,512]{2,1,0:T(8,128)(2,1)S(1)}, u32[]{:S(2)}, u32[]{:S(2)}) collective-permute-start(bf16[4,128,512]{2,1,0:T(8,128)(2,1)S(1)} %fusion.9), channel_id=1, source_target_pairs={{0,8},{4,12},{8,0},{12,4},{16,24},{20,28},{24,16},{28,20},{1,9},{5... | collective-permute-start | bytes 1572872 | tf_op jit(solution)/shard_map/ppermute | solution.py:667
  501.9 8.3 %collective-permute-start.61 = (bf16[256,256]{1,0:T(8,128)(2,1)S(1)}, bf16[256,256]{1,0:T(8,128)(2,1)S(1)}, u32[]{:S(2)}, u32[]{:S(2)}) collective-permute-start(bf16[256,256]{1,0:T(8,128)(2,1)S(1)} %get-tuple-element.156), channel_id=1, source_target_pairs={{0,1},{1,2},{2,3},{3,0},{4,5},{5,6},{6,7},{7,4},{8,9},{9,10},{10,1... | collective-permute-start | bytes 393224 | tf_op jit(solution)/shard_map/ppermute | solution.py:671
  502.4 14.3 %collective-permute-start.62 = (bf16[256,256]{1,0:T(8,128)(2,1)S(1)}, bf16[256,256]{1,0:T(8,128)(2,1)S(1)}, u32[]{:S(2)}, u32[]{:S(2)}) collective-permute-start(bf16[256,256]{1,0:T(8,128)(2,1)S(1)} %get-tuple-element.158), channel_id=1, source_target_pairs={{0,2},{1,3},{2,0},{3,1},{4,6},{5,7},{6,4},{7,5},{8,10},{9,11},{10,... | collective-permute-start | bytes 393224 | tf_op jit(solution)/shard_map/ppermute | solution.py:671
  505.0 11.8 %collective-permute-start.63 = (bf16[256,256]{1,0:T(8,128)(2,1)S(1)}, bf16[256,256]{1,0:T(8,128)(2,1)S(1)}, u32[]{:S(2)}, u32[]{:S(2)}) collective-permute-start(bf16[256,256]{1,0:T(8,128)(2,1)S(1)} %get-tuple-element.157), channel_id=1, source_target_pairs={{0,3},{1,0},{2,1},{3,2},{4,7},{5,4},{6,5},{7,6},{8,11},{9,8},{10,9... | collective-permute-start | bytes 393224 | tf_op jit(solution)/shard_map/ppermute | solution.py:671
  507.1 15.8 %collective-permute-start.66 = (bf16[256,256]{1,0:T(8,128)(2,1)S(1)}, bf16[256,256]{1,0:T(8,128)(2,1)S(1)}, u32[]{:S(2)}, u32[]{:S(2)}) collective-permute-start(bf16[256,256]{1,0:T(8,128)(2,1)S(1)} %get-tuple-element.159), channel_id=1, source_target_pairs={{0,1},{1,2},{2,3},{3,0},{4,5},{5,6},{6,7},{7,4},{8,9},{9,10},{10,1... | collective-permute-start | bytes 393224 | tf_op jit(solution)/shard_map/ppermute | solution.py:671
  508.5 21.8 %collective-permute-start.67 = (bf16[256,256]{1,0:T(8,128)(2,1)S(1)}, bf16[256,256]{1,0:T(8,128)(2,1)S(1)}, u32[]{:S(2)}, u32[]{:S(2)}) collective-permute-start(bf16[256,256]{1,0:T(8,128)(2,1)S(1)} %get-tuple-element.161), channel_id=1, source_target_pairs={{0,2},{1,3},{2,0},{3,1},{4,6},{5,7},{6,4},{7,5},{8,10},{9,11},{10,... | collective-permute-start | bytes 393224 | tf_op jit(solution)/shard_map/ppermute | solution.py:671
  510.2 20.6 %collective-permute-start.68 = (bf16[256,256]{1,0:T(8,128)(2,1)S(1)}, bf16[256,256]{1,0:T(8,128)(2,1)S(1)}, u32[]{:S(2)}, u32[]{:S(2)}) collective-permute-start(bf16[256,256]{1,0:T(8,128)(2,1)S(1)} %get-tuple-element.160), channel_id=1, source_target_pairs={{0,3},{1,0},{2,1},{3,2},{4,7},{5,4},{6,5},{7,6},{8,11},{9,8},{10,9... | collective-permute-start | bytes 393224 | tf_op jit(solution)/shard_map/ppermute | solution.py:671
  516.7 18.8 %collective-permute-start.49 = (bf16[128,512]{1,0:T(8,128)(2,1)S(1)}, bf16[128,512]{1,0:T(8,128)(2,1)S(1)}, u32[]{:S(2)}, u32[]{:S(2)}) collective-permute-start(bf16[128,512]{1,0:T(8,128)(2,1)S(1)} %get-tuple-element.162), channel_id=1, source_target_pairs={{0,1},{1,2},{2,3},{3,0},{4,5},{5,6},{6,7},{7,4},{8,9},{9,10},{10,1... | collective-permute-start | bytes 393224 | tf_op jit(solution)/shard_map/ppermute | solution.py:671
  516.7 20.6 %collective-permute-start.50 = (bf16[128,512]{1,0:T(8,128)(2,1)S(1)}, bf16[128,512]{1,0:T(8,128)(2,1)S(1)}, u32[]{:S(2)}, u32[]{:S(2)}) collective-permute-start(bf16[128,512]{1,0:T(8,128)(2,1)S(1)} %get-tuple-element.164), channel_id=1, source_target_pairs={{0,2},{1,3},{2,0},{3,1},{4,6},{5,7},{6,4},{7,5},{8,10},{9,11},{10,... | collective-permute-start | bytes 393224 | tf_op jit(solution)/shard_map/ppermute | solution.py:671
  522.9 14.4 %collective-permute-start.51 = (bf16[128,512]{1,0:T(8,128)(2,1)S(1)}, bf16[128,512]{1,0:T(8,128)(2,1)S(1)}, u32[]{:S(2)}, u32[]{:S(2)}) collective-permute-start(bf16[128,512]{1,0:T(8,128)(2,1)S(1)} %get-tuple-element.163), channel_id=1, source_target_pairs={{0,3},{1,0},{2,1},{3,2},{4,7},{5,4},{6,5},{7,6},{8,11},{9,8},{10,9... | collective-permute-start | bytes 393224 | tf_op jit(solution)/shard_map/ppermute | solution.py:671
  530.3 7.1 %collective-permute-start.54 = (bf16[128,512]{1,0:T(8,128)(2,1)S(1)}, bf16[128,512]{1,0:T(8,128)(2,1)S(1)}, u32[]{:S(2)}, u32[]{:S(2)}) collective-permute-start(bf16[128,512]{1,0:T(8,128)(2,1)S(1)} %get-tuple-element.165), channel_id=1, source_target_pairs={{0,1},{1,2},{2,3},{3,0},{4,5},{5,6},{6,7},{7,4},{8,9},{9,10},{10,1... | collective-permute-start | bytes 393224 | tf_op jit(solution)/shard_map/ppermute | solution.py:671
  530.9 11.3 %collective-permute-start.55 = (bf16[128,512]{1,0:T(8,128)(2,1)S(1)}, bf16[128,512]{1,0:T(8,128)(2,1)S(1)}, u32[]{:S(2)}, u32[]{:S(2)}) collective-permute-start(bf16[128,512]{1,0:T(8,128)(2,1)S(1)} %get-tuple-element.167), channel_id=1, source_target_pairs={{0,2},{1,3},{2,0},{3,1},{4,6},{5,7},{6,4},{7,5},{8,10},{9,11},{10,... | collective-permute-start | bytes 393224 | tf_op jit(solution)/shard_map/ppermute | solution.py:671
  535.5 6.7 %collective-permute-start.56 = (bf16[128,512]{1,0:T(8,128)(2,1)S(1)}, bf16[128,512]{1,0:T(8,128)(2,1)S(1)}, u32[]{:S(2)}, u32[]{:S(2)}) collective-permute-start(bf16[128,512]{1,0:T(8,128)(2,1)S(1)} %get-tuple-element.166), channel_id=1, source_target_pairs={{0,3},{1,0},{2,1},{3,2},{4,7},{5,4},{6,5},{7,6},{8,11},{9,8},{10,9... | collective-permute-start | bytes 393224 | tf_op jit(solution)/shard_map/ppermute | solution.py:671
  (40 other events, 445.2 us)

commit v2 on v1

--- a/solution.py
+++ b/solution.py
@@ -151,6 +151,134 @@
         cost_estimate=cost(2 * tokens * width * 3 * width, 26 << 20),
         name="embed_joined",
     )(emb, ci.reshape(pages, 1, length), *terms, w, gains, shifts, bias)
+
+
+STAGES = 4
+
+
+def neighbours():
+    tok, z = lax.axis_index("tok"), lax.axis_index("tab")
+    core = {"tok": tok + 1 - 2 * (tok % 2)}
+    x = {"tok": tok + 2 - 4 * ((tok // 2) % 2)}
+    y = {"tok": tok + 4 - 8 * (tok // 4)}
+    peers = [{"tab": (z + s) % 4} for s in range(1, 4)]
+    return core, x, y, peers
+
+
+def meet(devices):
+    barrier = pltpu.get_barrier_semaphore()
+    for d in devices:
+        pl.semaphore_signal(barrier, inc=1, device_id=d, device_id_type=pl.DeviceIdType.MESH)
+    pl.semaphore_wait(barrier, len(devices))
+
+
+def sum_scratch(rows, cols):
+    part = lambda *n: pltpu.VMEM((*n, rows, cols), BF)
+    return [
+        part(2, 4, 4), part(2, 4, 4), part(2, 4, 2), part(2, 4), part(2, 3),
+        pltpu.SemaphoreType.DMA((2, 4)),
+        pltpu.SemaphoreType.DMA((STAGES, 2, 4)),
+        pltpu.SemaphoreType.DMA((STAGES, 2, 4)),
+    ]
+
+
+class Summing:
+    def __init__(self, grads, out, scratch):
+        self.grads, self.out = grads, out
+        self.own, self.r0, self.r1, self.r2, self.r3, self.local, self.sent, self.got = scratch
+        core, x, y, peers = neighbours()
+        self.core, self.first, self.second, self.peers = core, (x, y), (y, x), peers
+        self.z = lax.axis_index("tab")
+
+    def devices(self):
+        return [self.core, self.first[0], self.first[1], *self.peers]
+
+    def copy(self, stage, ch, i):
+        zc = (self.z + (i + 1)) % 4
+        src, dst, to = (
+            (lambda: self.grads[ch].at[1, zc], self.r0.at[ch, i], self.core),
+            (lambda: self.own.at[ch, i, pl.ds(2, 2)], self.r1.at[ch, i], self.first[ch]),
+            (lambda: self.own.at[ch, i, 1], self.r2.at[ch, i], self.second[ch]),
+            (lambda: self.own.at[ch, i, 0], self.r3.at[ch, min(i, 2)], self.peers[min(i, 2)]),
+        )[stage]
+        return pltpu.make_async_remote_copy(
+            src_ref=src(), dst_ref=dst,
+            send_sem=self.sent.at[stage, ch, i], recv_sem=self.got.at[stage, ch, i],
+            device_id=to, device_id_type=pl.DeviceIdType.MESH,
+        )
+
+    def load(self, ch, i):
+        zc = (self.z + (i + 1)) % 4
+        return pltpu.make_async_copy(
+            self.grads[ch].at[0, zc], self.own.at[ch, i], self.local.at[ch, i]
+        )
+
+    def start(self):
+        for i in range(4):
+            for ch in range(2):
+                self.copy(0, ch, i).start()
+                self.load(ch, i).start()
+
+    def step(self, stage, i):
+        for ch in range(2):
+            self.copy(stage - 1, ch, i).wait_recv()
+            if stage == 1:
+                self.load(ch, i).wait()
+
+                def add(j, _, ch=ch):
+                    self.own[ch, i, j] = self.own[ch, i, j] + self.r0[ch, i, j]
+                    return 0
+
+                lax.fori_loop(0, 4, add, 0)
+            elif stage == 2:
+
+                def add(j, _, ch=ch):
+                    self.own[ch, i, j] = self.own[ch, i, j] + self.r1[ch, i, j]
+                    return 0
+
+                lax.fori_loop(0, 2, add, 0)
+            elif i < 3:
+                self.own[ch, i, 0] = self.own[ch, i, 0] + self.r2[ch, i]
+            if stage < 3 or i < 3:
+                self.copy(stage, ch, i).start()
+
+    def finish(self):
+        for ch in range(2):
+            total = self.own[ch, 3, 0].astype(F32) + self.r2[ch, 3].astype(F32)
+            for i in range(3):
+                self.copy(3, ch, i).wait_recv()
+                total = total + self.r3[ch, i].astype(F32)
+            self.out[ch] = total
+        for stage in range(STAGES):
+            for ch in range(2):
+                for i in range(4 if stage < 3 else 3):
+                    self.copy(stage, ch, i).wait_send()
+
+    def run(self, step, plan):
+        for at, events in plan.items():
+
+            @pl.when(step == at)
+            def _(events=events):
+                for stage, i in events:
+                    if stage == 0:
+                        self.start()
+                    elif stage == 4:
+                        self.finish()
+                    else:
+                        self.step(stage, i)
+
+
+def sum_specs(grads, number):
+    if grads is None:
+        return [], [], [], [], {}
+    rows, cols = grads[0].shape[3:]
+    return (
+        [pl.BlockSpec(memory_space=pl.ANY)] * 2,
+        [full((2, rows, cols))],
+        [jax.ShapeDtypeStruct((2, rows, cols), F32)],
+        sum_scratch(rows, cols),
+        {"has_side_effects": True, "collective_id": number},
+    )
 
 
 HP = 4
@@ -203,7 +331,33 @@
     )(q, k, v)
 
 
-def attn_bwd_kernel(q, k, v, mixed, go, lse, gj, sums):
+ATTN_PLAN = {
+    0: [(0, 0)],
+    1: [(1, 0)],
+    2: [(1, 1)],
+    3: [(2, 0), (1, 2)],
+    5: [(2, 1), (1, 3)],
+    6: [(3, 0)],
+}
+ATTN_TAIL = [(2, 2), (3, 1), (2, 3), (3, 2), (3, 3), (4, 0)]
+
+
+def attn_bwd_kernel(*refs, summed):
+    q, k, v, mixed, go, lse = refs[:6]
+    refs = refs[6:]
+    grads, refs = refs[: 2 * summed], refs[2 * summed :]
+    gj, sums = refs[:2]
+    refs = refs[2:]
+    step = pl.program_id(0) * pl.num_programs(1) + pl.program_id(1)
+    last = pl.num_programs(0) * pl.num_programs(1) - 1
+    if summed:
+        summing = Summing(grads, refs[0], refs[1:])
+
+        @pl.when(step == 0)
+        def _():
+            meet(summing.devices())
+
+        summing.run(step, ATTN_PLAN)
     length = q.shape[0]
     pair = 2 * HEAD_DIM
     low_half = head_masks(length, pair)
@@ -245,32 +399,44 @@
         def _():
             sums[:, cols] = sums[:, cols] + part
 
-
-def attn_bwd(q, k, v, mixed, go, lse, pages):
+    if summed:
+        summing.run(step, {last: ATTN_TAIL})
+
+
+def attn_bwd(q, k, v, mixed, go, lse, pages, grads):
     tokens, width = q.shape
+    more_in, more_out, more_shape, more_scratch, more = sum_specs(grads, 2)
     length = tokens // pages
     steps = HEADS // HP
     wide = HP * HEAD_DIM
     blk = pl.BlockSpec((length, wide), lambda j, i: (i, j))
     return pl.pallas_call(
-        attn_bwd_kernel,
+        functools.partial(attn_bwd_kernel, summed=grads is not None),
         grid=(steps, pages),
-        in_specs=[blk] * 5 + [pl.BlockSpec((1, 1, HP, length), lambda j, i: (i, j, 0, 0))],
+        in_specs=[blk] * 5
+        + [pl.BlockSpec((1, 1, HP, length), lambda j, i: (i, j, 0, 0))]
+        + more_in,
         out_specs=[
             pl.BlockSpec((3, length, wide), lambda j, i: (0, i, j)),
             pl.BlockSpec((2, wide), lambda j, i: (0, j)),
-        ],
+        ]
+        + more_out,
         out_shape=[
             jax.ShapeDtypeStruct((3, tokens, width), BF),
             jax.ShapeDtypeStruct((2, width), F32),
-        ],
-        compiler_params=params(),
+        ]
+        + more_shape,
+        scratch_shapes=more_scratch,
+        compiler_params=params(**more),
         cost_estimate=cost(35e9, 16 << 20, pages * HEADS * length * length),
         name="attention_back",
-    )(q, k, v, mixed, go, lse)
-
-
-FC = 1024
+    )(q, k, v, mixed, go, lse, *(grads or ()))
+
+
+FC = 512
+FWD = 1024
+RC = 128
+MC = 512
 
 
 def ffn_fwd_kernel(
@@ -286,8 +452,8 @@
     low = after.astype(BF)
     low_out[...] = low
     total = after + bias[3:4]
-    for j in range(ff // FC):
-        cols = slice(j * FC, (j + 1) * FC)
+    for j in range(ff // FWD):
+        cols = slice(j * FWD, (j + 1) * FWD)
         act, slope = gelu_parts(dot(low, we[:, cols], NN) + hb[:, cols])
         act = act.astype(BF)
         act_out[:, cols] = act
@@ -336,67 +502,127 @@
     )(mixed, normed, wo, we, wr, hb, bias, gains, shifts, cot)
 
 
-def ffn_bwd_kernel(
-    gffn, slope, gs2, after, rstd, wr, we, wo, gains, shifts,
-    gh_out, gs1_out, gattn_out, gmixed_out, hsum, sums,
-):
-    ff = we.shape[1]
-    first = pl.program_id(0) == 0
-    g = gffn[...]
-    total = gs2[...]
-    hparts = []
-    for j in range(ff // FC):
-        cols = slice(j * FC, (j + 1) * FC)
-        gh = (dot(g, wr[cols, :], NT) * slope[:, cols].astype(F32)).astype(BF)
-        gh_out[:, cols] = gh
-        hparts.append(colsum(gh.astype(F32)))
-        total = total + dot(gh, we[:, cols], NT)
-    hpart = jnp.concatenate(hparts, axis=1)
-    xh = (after[...] - shifts[1:2]) * (1.0 / gains[1:2])
-    gs1 = norm_back(total, xh, rstd[...], gains[1:2])
-    gs1_out[...] = gs1
-    gattn = gs1.astype(BF)
-    gattn_out[...] = gattn
-    gmixed_out[...] = dot(gattn, wo[...], NT).astype(BF)
-    part = jnp.concatenate(
-        [colsum(total * xh), colsum(total), colsum(gattn.astype(F32))], axis=0
-    )
-
-    @pl.when(first)
+FFN_PLAN = {
+    0: [(0, 0)],
+    1: [(1, 0)],
+    2: [(1, 1)],
+    3: [(2, 0), (1, 2)],
+    4: [(2, 1), (1, 3)],
+    5: [(3, 0)],
+    7: [(2, 2), (3, 1)],
+}
+FFN_TAIL = [(2, 3), (3, 2), (3, 3), (4, 0)]
+
+
+def ffn_bwd_kernel(*refs, summed):
+    gffn, gs2, after, rstd, wo, gains, shifts, slope, wr, we = refs[:10]
+    refs = refs[10:]
+    grads, refs = refs[: 2 * summed], refs[2 * summed :]
+    gh_out, gs1_out, gattn_out, gmixed_out, hsum, sums = refs[:6]
+    refs = refs[6:]
+    step, last = pl.program_id(0), pl.num_programs(0) - 1
+    tokens, width = gffn.shape
+    if summed:
+        summing = Summing(grads, refs[0], refs[1:])
+
+        @pl.when(step == 0)
+        def _():
+            meet(summing.devices())
+
+        summing.run(step, FFN_PLAN)
+
+    @pl.when(step == 0)
     def _():
-        sums[...] = part
-        hsum[...] = hpart
-
-    @pl.when(jnp.logical_not(first))
+        gs1_out[...] = gs2[...]
+
+    part = jnp.zeros((1, slope.shape[1]), F32)
+    for m in range(0, tokens, MC):
+        rows = slice(m, m + MC)
+        gh = (dot(gffn[rows, :], wr[...], NT) * slope[rows, :].astype(F32)).astype(BF)
+        gh_out[rows, :] = gh
+        part = part + colsum(gh.astype(F32))
+        gs1_out[rows, :] = gs1_out[rows, :] + dot(gh, we[...], NT)
+    hsum[...] = part
+
+    @pl.when(step == last)
     def _():
-        sums[...] = sums[...] + part
-        hsum[...] = hsum[...] + hpart
-
-
-def ffn_bwd(gffn, slope, gs2, after, rstd, wr, we, wo, gains, shifts, tile):
+        def norm(i, carry):
+            rows = pl.ds(pl.multiple_of(i * RC, RC), RC)
+            total = gs1_out[rows, :]
+            xh = (after[rows, :] - shifts[1:2]) * (1.0 / gains[1:2])
+            gs1 = norm_back(total, xh, rstd[rows, :], gains[1:2])
+            gs1_out[rows, :] = gs1
+            gattn = gs1.astype(BF)
+            gattn_out[rows, :] = gattn
+            g, s, b = carry
+            return g + colsum(total * xh), s + colsum(total), b + colsum(gattn.astype(F32))
+
+        zero = jnp.zeros((1, width), F32)
+        sums[...] = jnp.concatenate(
+            lax.fori_loop(0, tokens // RC, norm, (zero, zero, zero)), axis=0
+        )
+        for m in range(0, tokens, MC):
+            rows = slice(m, m + MC)
+            gmixed_out[rows, :] = dot(gattn_out[rows, :], wo[...], NT).astype(BF)
+
+    if summed:
+        summing.run(step, {last: FFN_TAIL})
+
+
+def ffn_bwd(gffn, slope, gs2, after, rstd, wr, we, wo, gains, shifts, grads):
     tokens, width = gffn.shape
     ff = we.shape[1]
-    rows = pl.BlockSpec((tile, width), lambda i: (i, 0))
-    long = pl.BlockSpec((tile, ff), lambda i: (i, 0))
+    whole = full((tokens, width))
+    long = pl.BlockSpec((tokens, FC), lambda s: (0, s))
     shape = lambda dt, n=width: jax.ShapeDtypeStruct((tokens, n), dt)
+    more_in, more_out, more_shape, more_scratch, more = sum_specs(grads, 1)
     return pl.pallas_call(
-        ffn_bwd_kernel,
-        grid=(tokens // tile,),
-        in_specs=[rows, long, rows, rows, pl.BlockSpec((tile, 1), lambda i: (i, 0))]
-        + [full(a.shape) for a in (wr, we, wo, gains, shifts)],
-        out_specs=[long, rows, rows, rows]
-        + [pl.BlockSpec((1, ff), lambda i: (0, 0)), pl.BlockSpec((3, width), lambda i: (0, 0))],
+        functools.partial(ffn_bwd_kernel, summed=grads is not None),
+        grid=(ff // FC,),
+        in_specs=[whole, whole, whole, full((tokens, 1))]
+        + [full(a.shape) for a in (wo, gains, shifts)]
+        + [
+            long,
+            pl.BlockSpec((FC, width), lambda s: (s, 0)),
+            pl.BlockSpec((width, FC), lambda s: (0, s)),
+        ]
+        + more_in,
+        out_specs=[long, whole, whole, whole]
+        + [pl.BlockSpec((1, FC), lambda s: (0, s)), full((3, width))]
+        + more_out,
         out_shape=[
             shape(BF, ff), shape(F32), shape(BF), shape(BF),
             jax.ShapeDtypeStruct((1, ff), F32), jax.ShapeDtypeStruct((3, width), F32),
-        ],
-        compiler_params=params(),
+        ]
+        + more_shape,
+        scratch_shapes=more_scratch,
+        compiler_params=params(**more),
         cost_estimate=cost(2 * tokens * width * (width + 2 * ff), 60 << 20),
         name="ffn_backward",
-    )(gffn, slope, gs2, after, rstd, wr, we, wo, gains, shifts)
-
-
-def embed_bwd_kernel(gs1, gj, w, normed, rstd, ci, gains, shifts, out, cells, sums):
+    )(gffn, gs2, after, rstd, wo, gains, shifts, slope, wr, we, *(grads or ()))
+
+
+EMBED_PLAN = {0: [(0, 0)], 1: [(1, 0), (1, 1)]}
+EMBED_TAIL = [
+    (2, 0), (1, 2), (2, 1), (3, 0), (1, 3), (2, 2), (3, 1), (2, 3), (3, 2), (3, 3), (4, 0),
+]
+
+
+def embed_bwd_kernel(*refs, summed):
+    gs1, gj, w, normed, rstd, ci, gains, shifts = refs[:8]
+    refs = refs[8:]
+    grads, refs = refs[: 2 * summed], refs[2 * summed :]
+    out, cells, sums = refs[:3]
+    refs = refs[3:]
+    step, last = pl.program_id(0), pl.num_programs(0) - 1
+    if summed:
+        summing = Summing(grads, refs[0], refs[1:])
+
+        @pl.when(step == 0)
+        def _():
+            meet(summing.devices())
+
+        summing.run(step, EMBED_PLAN)
     width = gs1.shape[1]
     tokens = gs1.shape[0]
     total = gs1[...]
@@ -418,13 +644,17 @@
     def _():
         sums[...] = sums[...] + part
 
-
-def embed_bwd(gs1, gj, w, normed, rstd, ci, gains, shifts):
+    if summed:
+        summing.run(step, {last: EMBED_TAIL})
+
+
+def embed_bwd(gs1, gj, w, normed, rstd, ci, gains, shifts, grads):
     tokens, width = gs1.shape
+    more_in, more_out, more_shape, more_scratch, more = sum_specs(grads, 3)
     pages, length = ci.shape
     rows = pl.BlockSpec((length, width), lambda i: (i, 0))
     return pl.pallas_call(
-        embed_bwd_kernel,
+        functools.partial(embed_bwd_kernel, summed=grads is not None),
         grid=(pages,),
         in_specs=[
             rows,
@@ -435,21 +665,27 @@
             pl.BlockSpec((1, 1, length), lambda i: (i, 0, 0)),
             full(gains.shape),
             full(shifts.shape),
-        ],
+        ]
+        + more_in,
         out_specs=[
             rows,
             pl.BlockSpec((CELLS, width), lambda i: (i, 0)),
             pl.BlockSpec((2, width), lambda i: (0, 0)),
-        ],
+        ]
+        + more_out,
         out_shape=[
             jax.ShapeDtypeStruct((tokens, width), F32),
             jax.ShapeDtypeStruct((pages * CELLS, width), BF),
             jax.ShapeDtypeStruct((2, width), F32),
-        ],
-        compiler_params=params(),
+        ]
+        + more_shape,
+        scratch_shapes=more_scratch,
+        compiler_params=params(**more),
         cost_estimate=cost(2 * tokens * width * 3 * width, 26 << 20),
         name="embed_backward",
-    )(gs1, gj, w, normed, rstd, ci.reshape(pages, 1, length), gains, shifts)
+    )(
+        gs1, gj, w, normed, rstd, ci.reshape(pages, 1, length), gains, shifts, *(grads or ())
+    )
 
 
 def table_kernel(tok, idx, g0, g1, g2, g3, out_a, out_b):
@@ -515,152 +751,102 @@
     )(tok, a, b)
 
 
-def block_of(tok, j, core):
-    return (tok ^ (((j & 1) << 2) | (j & 2))) & 6 | core
-
-
-def rows_partner_kernel(tok, lhs, *refs, count):
-    rhs, (pa, pb, turned) = refs[:count], refs[count:]
-    core = (tok[0] & 1) ^ 1
-    turn_rows(tok, lhs, turned, core)
-    g = dot(turned[...], jnp.concatenate([r[...].reshape(r.shape[-2:]) for r in rhs], axis=1), NN)
-    rows = lhs.shape[1] // 8
-    half = pa.shape[3]
-    for j in range(4):
-        pa[j, 0] = g[j * rows : (j + 1) * rows, :half].astype(BF)
-        pb[j, 0] = g[j * rows : (j + 1) * rows, half:].astype(BF)
-
-
-def turn_rows(tok, lhs, turned, core):
-    rows = lhs.shape[1] // 8
+def split_rel(r):
+    return r & 1, (r >> 1) & 1, r >> 2
+
+
+def reduce_kernel(tok, gffn, act, ga, gb):
+    g = dot(gffn[...], act[...], TN)
+    half = ga.shape[4]
+    ga[0, :, 0] = g[:, :half].astype(BF).reshape(ga.shape[1], *ga.shape[3:])
+    gb[0, :, 0] = g[:, half:].astype(BF).reshape(gb.shape[1], *gb.shape[3:])
+
+
+def reduce_part(tok, gffn, act):
+    tokens, d = gffn.shape
+    f = act.shape[1] // 8
+    rows, half = d // 4, f // 2
+
+    def index(ch):
+        def at(s, t):
+            core, x, y = split_rel(7 - s)
+            return (core, 0, 2 * y + x if ch else 2 * x + y, 0, 0)
+
+        return at
+
+    shape = jax.ShapeDtypeStruct((2, 4, 4, rows, half), BF)
+    return pl.pallas_call(
+        reduce_kernel,
+        grid_spec=pltpu.PrefetchScalarGridSpec(
+            num_scalar_prefetch=1,
+            grid=(8,),
+            in_specs=[
+                full(gffn.shape),
+                pl.BlockSpec((tokens, f), lambda s, t: (0, t[0] ^ (7 - s))),
+            ],
+            out_specs=[pl.BlockSpec((1, 4, 1, rows, half), index(ch)) for ch in range(2)],
+        ),
+        out_shape=[shape, shape],
+        compiler_params=params(),
+        cost_estimate=cost(16 * tokens * d * f, 20 << 20),
+        name="reduce_grad",
+    )(tok, gffn, act)
+
+
+def rows_kernel(tok, *refs, groups):
+    count = len(groups)
+    lhs, refs = refs[:count], refs[count:]
+    rhs = []
+    for n in groups:
+        rhs.append(refs[:n])
+        refs = refs[n:]
+    ga, gb = refs[:2]
+    turned = refs[2:]
+    rows = lhs[0].shape[1] // 8
+    half = rows // 2
 
     @pl.when(pl.program_id(0) == 0)
     def _():
-        for j in range(4):
-            start = pl.multiple_of(block_of(tok[0], j, core) * rows, rows)
-            turned[j * rows : (j + 1) * rows, :] = lhs[:, pl.ds(start, rows)].T
-
-
-def rows_own_kernel(tok, lhs, *refs, count):
-    rhs = refs[:count]
-    ra, rb, sa, ka, sb, kb, turned = refs[count:]
-    turn_rows(tok, lhs, turned, tok[0] & 1)
-    g = dot(turned[...], jnp.concatenate([r[...].reshape(r.shape[-2:]) for r in rhs], axis=1), NN)
-    rows = lhs.shape[1] // 8
-    half = ra.shape[3]
-    for j in range(4):
-        rx, ry = j >> 1, j & 1
-        a = (g[j * rows : (j + 1) * rows, :half] + ra[j, 0].astype(F32)).astype(BF)
-        b = (g[j * rows : (j + 1) * rows, half:] + rb[j, 0].astype(F32)).astype(BF)
-        (sa if rx else ka)[ry, 0] = a
-        (sb if ry else kb)[rx, 0] = b
-
-
-def rows_call(tok, lhs, rhs_list, rhs_specs, width, received):
-    tokens, d = lhs.shape
-    rows = d // 8
-    half = width // 2
-    count = len(rhs_list)
-    spec = lambda n: pl.BlockSpec((n, 1, rows, half), lambda z, t: (0, z, 0, 0))
-    shape = lambda n: jax.ShapeDtypeStruct((n, 4, rows, half), BF)
-    own = received is not None
-    kernel = rows_own_kernel if own else rows_partner_kernel
-    outs = [2, 2, 2, 2] if own else [4, 4]
+        for a, b in zip(lhs, turned):
+            for r in range(8):
+                start = pl.multiple_of((tok[0] ^ r) * rows, rows)
+                b[:, r * rows : (r + 1) * rows] = a[:, pl.ds(start, rows)]
+
+    at = 0
+    for a, blocks in zip(turned, rhs):
+        for block in blocks:
+            block = block[...].reshape(block.shape[-2:])
+            for n in range(0, block.shape[1], 512):
+                piece = block[:, n : n + 512]
+                g = dot(a[...], piece, TN).astype(BF)
+                cols = slice(at, at + piece.shape[1])
+                at += piece.shape[1]
+                for r in range(8):
+                    core, x, y = split_rel(r)
+                    ga[core, 0, 2 * x + y, :, cols] = g[r * rows : r * rows + half]
+                    gb[core, 0, 2 * y + x, :, cols] = g[r * rows + half : (r + 1) * rows]
+
+
+def rows_part(tok, pairs, name):
+    tokens, d = pairs[0][0].shape
+    half = d // 16
+    width = sum(spec.block_shape[-1] for _, _, specs in pairs for spec in specs)
+    shape = jax.ShapeDtypeStruct((2, 4, 4, half, width), BF)
+    out = pl.BlockSpec((2, 1, 4, half, width), lambda s, t: (0, s, 0, 0, 0))
     return pl.pallas_call(
-        functools.partial(kernel, count=count),
+        functools.partial(rows_kernel, groups=[len(p[1]) for p in pairs]),
         grid_spec=pltpu.PrefetchScalarGridSpec(
             num_scalar_prefetch=1,
             grid=(4,),
-            in_specs=[full(lhs.shape)] + rhs_specs + ([spec(4)] * 2 if own else []),
-            out_specs=[spec(n) for n in outs],
-            scratch_shapes=[pltpu.VMEM((d // 2, tokens), BF)],
+            in_specs=[full(p[0].shape) for p in pairs] + [s for p in pairs for s in p[2]],
+            out_specs=[out, out],
+            scratch_shapes=[pltpu.VMEM((tokens, d), BF) for _ in pairs],
         ),
-        out_shape=[shape(n) for n in outs],
+        out_shape=[shape, shape],
         compiler_params=params(),
-        cost_estimate=cost(4 * tokens * d * width, 6 * d * width + 2 * tokens * d),
-        name="weight_grad_own" if own else "weight_grad_partner",
-    )(tok, lhs, *rhs_list, *(received or ()))
-
-
-def cols_partner_kernel(tok, lhs, rhs, pa, pb, turned):
-    @pl.when(pl.program_id(0) == 0)
-    def _():
-        turned[...] = lhs[...].T
-
-    g = dot(turned[...], rhs[...], NN)
-    half = pa.shape[3]
-    pa[0] = g[:, :half].astype(BF).reshape(pa.shape[1:])
-    pb[0] = g[:, half:].astype(BF).reshape(pb.shape[1:])
-
-
-def cols_own_kernel(tok, lhs, rhs, ra, rb, sa, ka, sb, kb, turned):
-    step = pl.program_id(0)
-
-    @pl.when(step == 0)
-    def _():
-        turned[...] = lhs[...].T
-
-    g = dot(turned[...], rhs[...], NN)
-    half = ra.shape[3]
-    a = (g[:, :half].reshape(ra.shape[1:]) + ra[0].astype(F32)).astype(BF)
-    b = (g[:, half:].reshape(rb.shape[1:]) + rb[0].astype(F32)).astype(BF)
-    rx = step < 2
-    ry = step % 2 == 0
-
-    @pl.when(rx)
-    def _():
-        sa[0] = a
-
-    @pl.when(jnp.logical_not(rx))
-    def _():
-        ka[0] = a
-
-    @pl.when(ry)
-    def _():
-        sb[0] = b
-
-    @pl.when(jnp.logical_not(ry))
-    def _():
-        kb[0] = b
-
-
-def cols_call(tok, lhs, rhs, received):
-    tokens, d = lhs.shape
-    f = rhs.shape[1] // 8
-    half = f // 2
-    rows = d // 4
-    own = received is not None
-    flip = 0 if own else 1
-    rhs_spec = pl.BlockSpec(
-        (tokens, f), lambda s, t: (0, block_of(t[0], 3 - s, (t[0] & 1) ^ flip))
-    )
-    blk = lambda index: pl.BlockSpec((1, 4, rows, half), lambda s, t: (index(s), 0, 0, 0))
-    whole = blk(lambda s: 3 - s)
-    shape = lambda n: jax.ShapeDtypeStruct((n, 4, rows, half), BF)
-    late = lambda s: 1 - s // 3
-    if own:
-        out_specs = [
-            blk(lambda s: 1 - jnp.minimum(s, 1)),
-            blk(late),
-            blk(lambda s: 1 - s // 2),
-            blk(late),
-        ]
-    else:
-        out_specs = [whole, whole]
-    return pl.pallas_call(
-        cols_own_kernel if own else cols_partner_kernel,
-        grid_spec=pltpu.PrefetchScalarGridSpec(
-            num_scalar_prefetch=1,
-            grid=(4,),
-            in_specs=[full(lhs.shape), rhs_spec] + ([whole, whole] if own else []),
-            out_specs=out_specs,
-            scratch_shapes=[pltpu.VMEM((d, tokens), BF)],
-        ),
-        out_shape=[shape(2)] * 4 if own else [shape(4)] * 2,
-        compiler_params=params(),
-        cost_estimate=cost(8 * tokens * d * f, 24 * d * f + 2 * tokens * d),
-        name="weight_grad_own" if own else "weight_grad_partner",
-    )(tok, lhs, rhs, *(received or ()))
+        cost_estimate=cost(8 * tokens * d * width, 24 << 20),
+        name=name,
+    )(tok, *[p[0] for p in pairs], *[r for p in pairs for r in p[1]])
 
 
 def flip_tok(value, bit, size):
@@ -673,30 +859,6 @@
 
 def plus(a, b):
     return (a.astype(F32) + b.astype(F32)).astype(BF)
-
-
-def scatter_sum(send, keep, bits, n_tok, n_tab):
-    got = flip_tok(send, bits[0], n_tok)
-    send = plus(keep[1], got[1])
-    keep = plus(keep[0], got[0])
-    got = flip_tok(send, bits[1], n_tok)
-    part = plus(keep, got)
-    z = lax.axis_index("tab")
-    take = lambda i: lax.dynamic_index_in_dim(part, i, 0, keepdims=False)
-    total = take(z).astype(F32)
-    for shift in range(1, n_tab):
-        total = total + shift_tab(take((z + shift) % n_tab), shift, n_tab).astype(F32)
-    return total
-
-
-def weight_grad(call, n_tok, n_tab):
-    pa, pb = call(None)
-    received = (flip_tok(pa, 1, n_tok), flip_tok(pb, 1, n_tok))
-    sa, ka, sb, kb = call(received)
-    return (
-        scatter_sum(sa, ka, (2, 4), n_tok, n_tab),
-        scatter_sum(sb, kb, (4, 2), n_tok, n_tab),
-    )
 
 
 def table_sum(part, bits, n_tok):
@@ -769,15 +931,31 @@
     mixed, lse = attn_fwd(q, k, v, pages)
     layer_out, after, after_low, rstd1, act, slope, gs2, gffn, sums2 = ffn_fwd(
         mixed, normed, output_weight, expand_weight, reduce_weight, hidden_bias,
-        bias_rows, norm_gains, norm_shifts, cotangent, 256,
+        bias_rows, norm_gains, norm_shifts, cotangent, min(256, tokens),
     )
-    gh, gs1, gattn, gmixed, hidden_sum, sums1 = ffn_bwd(
+    quarter = width // 4
+    parts = reduce_part(tok, gffn, act) if cubic else None
+    gh, gs1, gattn, gmixed, hidden_sum, sums1, *reduce_sum = ffn_bwd(
         gffn, slope, gs2, after, rstd1, reduce_weight, expand_weight, output_weight,
-        norm_gains, norm_shifts, 256,
+        norm_gains, norm_shifts, parts,
     )
-    gj, sums_qv = attn_bwd(q, k, v, mixed, gmixed, lse, pages)
-    embedded_grad, cell_grad, sums0 = embed_bwd(
-        gs1, gj, joined_weight, normed, rstd0, cell_index, norm_gains, norm_shifts
+    if cubic:
+        columns = lambda n: pl.BlockSpec((tokens, n), lambda s, t: (0, s))
+        parts = rows_part(
+            tok,
+            [(after_low, [gh], [columns(ff // 4)]), (mixed, [gattn], [columns(quarter)])],
+            "expand_output_grad",
+        )
+    gj, sums_qv, *expand_sum = attn_bwd(q, k, v, mixed, gmixed, lse, pages, parts)
+    if cubic:
+        third = lambda n: pl.BlockSpec(
+            (1, tokens, quarter), lambda s, t: ((3 * s + n) // 4, 0, (3 * s + n) % 4)
+        )
+        parts = rows_part(
+            tok, [(normed_low, [gj, gj, gj], [third(0), third(1), third(2)])], "joined_grad"
+        )
+    embedded_grad, cell_grad, sums0, *joined_sum = embed_bwd(
+        gs1, gj, joined_weight, normed, rstd0, cell_index, norm_gains, norm_shifts, parts
     )
 
     cell_grads = [cell_grad] + [shift_tab(cell_grad, s, n_tab) for s in range(1, n_tab)]
@@ -804,29 +982,11 @@
     hidden_bias_grad = small[10 * width :]
 
     if cubic:
-        wide_spec = pl.BlockSpec((tokens, ff // 4), lambda s, t: (0, s))
-        out_spec = pl.BlockSpec((tokens, width // 4), lambda s, t: (0, s))
-        quarter = width // 4
-        third = lambda n: pl.BlockSpec(
-            (1, tokens, quarter), lambda s, t: ((3 * s + n) // 4, 0, (3 * s + n) % 4)
-        )
-        ra, rb = weight_grad(lambda r: cols_call(tok, gffn, act, r), n_tok, n_tab)
-        ea, eb = weight_grad(
-            lambda r: rows_call(tok, after_low, [gh], [wide_spec], ff // 4, r), n_tok, n_tab
-        )
-        oa, ob = weight_grad(
-            lambda r: rows_call(tok, mixed, [gattn], [out_spec], width // 4, r), n_tok, n_tab
-        )
-        ja, jb = weight_grad(
-            lambda r: rows_call(
-                tok, normed_low, [gj, gj, gj], [third(0), third(1), third(2)], 3 * quarter, r
-            ),
-            n_tok, n_tab,
-        )
-        reduce_grad = jnp.concatenate([ra, rb], axis=1).T
-        expand_grad = jnp.concatenate([ea, eb], axis=1)
-        output_grad = jnp.concatenate([oa, ob], axis=1)
-        joined_grad = jnp.concatenate([ja, jb], axis=1)
+        reduce_grad = jnp.concatenate([reduce_sum[0][0], reduce_sum[0][1]], axis=1).T
+        expand_sum = expand_sum[0].reshape(-1, expand_sum[0].shape[2])
+        expand_grad = expand_sum[:, : ff // 4]
+        output_grad = expand_sum[:, ff // 4 :]
+        joined_grad = joined_sum[0].reshape(-1, joined_sum[0].shape[2])
     else:
         both = lambda a, b: jnp.einsum("ta,tb->ab", a, b, preferred_element_type=F32).astype(BF)
 

time: 550 us -> 483 us (0.88)
  waiting for transfers between devices: 147 us -> 61.1 us
  Pallas kernels: 255 us -> 322 us
  starting transfers between devices: 86.6 us -> 59.7 us
  other arithmetic: 22.8 us -> 4.17 us
    pallas_call x11 -> x6, Pallas kernels: 153 us -> 220 us  [the longest x1 68.9 us: ffn_bwd(): pl.pallas_call(functools.partial(ffn_bwd_kernel, summed=grads is not None...]
    ppermute x39 -> x15, waiting for transfers between devices: 76.7 us -> 17.1 us  [flip_tok(): return lax.ppermute(value, 'tok', [(i, i ^ bit) for i in range(size)])]
    ppermute x36 -> x12, waiting for transfers between devices: 70 us -> 43.9 us  [shift_tab(): lax.ppermute(value, 'tab', [(i, (i + shift) % size) for i in range(size)])]
    ppermute x36 -> x12, starting transfers between devices: 60.6 us -> 43.2 us  [shift_tab(): lax.ppermute(value, 'tab', [(i, (i + shift) % size) for i in range(size)])]
    convert_element_type x20 -> x4, other arithmetic: 11.6 us -> 0.24 us  [plus(): return (a.astype(F32) + b.astype(F32)).astype(BF)]
    ppermute x39 -> x15, starting transfers between devices: 26 us -> 16.5 us  [flip_tok(): return lax.ppermute(value, 'tok', [(i, i ^ bit) for i in range(size)])]
    unnamed x76 -> x54, local copies, waits for them, and re-layouts: 20.6 us -> 16.6 us
  transfers between devices with their start and end apart: 75 -> 27, of which waited for: 28 -> 15; matrix products, arithmetic and copies ran while one was open for 8% -> 3% of each run, Pallas kernels for 15% -> 1%
where the time goes in v2:
time: 483 us; the launch traced here: 477 us
  Pallas kernels  322 us (67%)
  waiting for transfers between devices  61.1 us (13%)
  starting transfers between devices  59.7 us (12%)
  local copies, waits for them, and re-layouts  28.9 us (6%)
    pallas_call x1, Pallas kernels, ffn_bwd(): pl.pallas_call(functools.partial(ffn_bwd_kernel, summed=grads is not None...  68.9 us
    pallas_call x1, Pallas kernels, attn_bwd(): pl.pallas_call(functools.partial(attn_bwd_kernel, summed=grads is not Non...  62.1 us
    pallas_call x1, Pallas kernels, ffn_fwd(): pl.pallas_call(ffn_fwd_kernel, grid=(tokens // tile,), in_specs=[rows, ro...  49.3 us
    pallas_call x1, Pallas kernels, embed_bwd(): pl.pallas_call(functools.partial(embed_bwd_kernel, summed=grads is not No...  44.7 us
    ppermute x12, waiting for transfers between devices, shift_tab(): lax.ppermute(value, 'tab', [(i, (i + shift) % size) for i in range(size)])  43.9 us
    ppermute x12, starting transfers between devices, shift_tab(): lax.ppermute(value, 'tab', [(i, (i + shift) % size) for i in range(size)])  43.2 us
    pallas_call x2, Pallas kernels, rows_part(): pl.pallas_call(functools.partial(rows_kernel, groups=[len(p[1]) for p in...  29.4 us
    pallas_call x1, Pallas kernels, attn_fwd(): pl.pallas_call(attn_fwd_kernel, grid=(pages, steps), in_specs=[blk] * 3,...  20 us
  transfers between devices with their start and end apart: 27, of which 15 were waited for; matrix products, arithmetic and copies ran while one was open for 3% of the time, Pallas kernels for 1%

profile of v2, /device:TPU:0, one launch (start us, length us, event | category | flops | bytes accessed | tf_op | source)
XLA Modules:
  0.0 476.8 jit_solution(9819392747698859078)
XLA Ops:
  0.7 0.8 fusion
  1.6 5.1 %collective-permute-start.2 = (s32[2,256]{1,0:T(2,128)S(1)}, s32[2,256]{1,0:T(2,128)S(1)}, u32[]{:S(2)}, u32[]{:S(2)}) collective-permute-start(s32[2,256]{1,0:T(2,128)S(1)} %get-tuple-element.144), channel_id=1, source_target_pairs={{0,3},{1,0},{2,1},{3,2},{4,7},{5,4},{6,5},{7,6},{8,11},{9,8},{10,9... | collective-permute-start | bytes 6152 | tf_op jit(solution)/shard_map/ppermute | solution.py:857
  6.7 1.0 collective-permute-start
  7.8 3.1 pad.6.table
  11.2 0.9 collective-permute-done
  12.7 5.6 %lookup.1 = bf16[4,256,1024]{2,1,0:T(8,128)(2,1)} custom-call(s32[4,2,256]{2,1,0:T(2,128)} %pad_add_fusion.1.idx, bf16[1024,1024]{1,0:T(8,128)(2,1)} %pad.6.table), custom_call_target="tpu_custom_call" | custom-call | flops 2147483648 | bytes 2097152 | tf_op jit(solution)/shard_map/lookup/pallas_call | solution.py:100
  18.3 2.5 slice_bitcast_fusion
  20.8 1.2 collective-permute-start.5
  22.0 0.9 collective-permute-start.4
  22.9 1.9 collective-permute-start.3
  25.5 12.0 %collective-permute-done.5.t3 = bf16[256,1024]{1,0:T(8,128)(2,1)S(1)} collective-permute-done((bf16[256,1024]{1,0:T(8,128)(2,1)S(1)}, bf16[256,1024]{1,0:T(8,128)(2,1)S(1)}, u32[]{:S(2)}, u32[]{:S(2)}) %collective-permute-start.5) | collective-permute-done | bytes 524320 | tf_op jit(solution)/shard_map/ppermute | solution.py:857
  37.5 19.9 %collective-permute-done.4.t2 = bf16[256,1024]{1,0:T(8,128)(2,1)S(1)} collective-permute-done((bf16[256,1024]{1,0:T(8,128)(2,1)S(1)}, bf16[256,1024]{1,0:T(8,128)(2,1)S(1)}, u32[]{:S(2)}, u32[]{:S(2)}) %collective-permute-start.4) | collective-permute-done | bytes 524320 | tf_op jit(solution)/shard_map/ppermute | solution.py:857
  57.5 0.8 copy-done.15
  58.4 14.3 %embed_joined.1 = (bf16[1024,1024]{1,0:T(8,128)(2,1)}, bf16[1024,1024]{1,0:T(8,128)(2,1)}, bf16[1024,1024]{1,0:T(8,128)(2,1)}, f32[1024,1024]{1,0:T(8,128)}, bf1...) custom-call(bf16[1024,1024]{1,0:T(8,128)(2,1)} %emb.1, s32[2,1,512]{2,1,0:T(1,128)} %reshape.190.ci.refs_5_, ...), custom_call_target="tpu_custom_call" | custom-call | flops 6442450944 | bytes 27262976 | tf_op jit(solution)/shard_map/embed_joined/pallas_call | solution.py:142
  72.8 20.0 %attention.1 = (bf16[1024,1024]{1,0:T(8,128)(2,1)}, f32[2,4,4,512]{3,2,1,0:T(4,128)}) custom-call(bf16[1024,1024]{1,0:T(8,128)(2,1)} %get-tuple-element.50.q.refs_0_, bf16[1024,1024]{1,0:T(8,128)(2,1)} %get-tuple-element.51.k.refs_1_, bf16[1024,1024]{1,0:T(8,128)(2,1)} %get-tuple-element.52.v.refs_2_), custom_call_target="tpu_custom_call" | custom-call | flops 14000000000 | bytes 8388608 | tf_op jit(solution)/shard_map/attention/pallas_call | solution.py:319
  92.8 49.3 %ffn_forward.1 = (bf16[1024,1024]{1,0:T(8,128)(2,1)}, f32[1024,1024]{1,0:T(8,128)}, bf16[1024,1024]{1,0:T(8,128)(2,1)}, f32[1024,1]{1,0:T(8,128)}, bf16[1024,409...) custom-call(bf16[1024,1024]{1,0:T(8,128)(2,1)} %get-tuple-element.53, ...), custom_call_target="tpu_custom_call" | custom-call | flops 19327352832 | bytes 62914560 | tf_op jit(solution)/shard_map/ffn_forward/pallas_call | solution.py:487
  142.1 0.7 reshape.197
  142.8 14.4 %reduce_grad.1 = (bf16[2,4,4,256,256]{4,3,2,1,0:T(8,128)(2,1)}, bf16[2,4,4,256,256]{4,3,2,1,0:T(8,128)(2,1)}) custom-call(s32[1]{0:T(128)} %bitcast.20.tok, bf16[1024,1024]{1,0:T(8,128)(2,1)} %get-tuple-element.56.gffn.refs_0_, bf16[1024,4096]{1,0:T(8,128)(2,1)} %get-tuple-element.61.act), custom_call_target="tpu_custom_call" | custom-call | flops 8589934592 | bytes 20971520 | tf_op jit(solution)/shard_map/reduce_grad/pallas_call | solution.py:778
  157.3 68.9 %ffn_backward.1 = (bf16[1024,4096]{1,0:T(8,128)(2,1)}, f32[1024,1024]{1,0:T(8,128)}, bf16[1024,1024]{1,0:T(8,128)(2,1)}, bf16[1024,1024]{1,0:T(8,128)(2,1)}, f32...) custom-call(bf16[1024,1024]{1,0:T(8,128)(2,1)} %get-tuple-element.56.gffn.refs_0_, ...), custom_call_target="tpu_custom_call" | custom-call | flops 19327352832 | bytes 62914560 | tf_op jit(solution)/shard_map/ffn_backward/pallas_call | solution.py:579
  226.2 0.7 reshape.196
  226.9 17.7 %expand_output_grad.1 = (bf16[2,4,4,64,1280]{4,3,2,1,0:T(8,128)(2,1)}, bf16[2,4,4,64,1280]{4,3,2,1,0:T(8,128)(2,1)}) custom-call(s32[1]{0:T(128)} %bitcast.20.tok, bf16[1024,1024]{1,0:T(8,128)(2,1)} %get-tuple-element.67.refs_0_, bf16[1024,1024]{1,0:T(8,128)(2,1)} %get-tuple-element.53.mixed.refs_1_.refs_3_, bf16[1024,4096]{1,0:T(8,128)(2,1)} %get-tuple-element.68.refs_2_, ...), custom_call_target="tpu_custom_call" | custom-call | flops 10737418240 | bytes 25165824 | tf_op jit(solution)/shard_map/expand_output_grad/pallas_call | solution.py:836
  244.6 62.1 %attention_back.1 = (bf16[3,1024,1024]{2,1,0:T(8,128)(2,1)}, f32[2,1024]{1,0:T(2,128)}, f32[2,64,1280]{2,1,0:T(8,128)}) custom-call(bf16[1024,1024]{1,0:T(8,128)(2,1)} %get-tuple-element.50.q.refs_0_, bf16[1024,1024]{1,0:T(8,128)(2,1)} %get-tuple-element.51.k.refs_1_, bf16[1024,1024]{1,0:T(8,128)(2,1)} %get-tuple-element.52.v.refs_2_, ...), custom_call_target="tpu_custom_call" | custom-call | flops 35000000512 | bytes 16777216 | tf_op jit(solution)/shard_map/attention_back/pallas_call | solution.py:413
  306.7 11.8 %joined_grad.1 = (bf16[2,4,4,64,768]{4,3,2,1,0:T(8,128)(2,1)}, bf16[2,4,4,64,768]{4,3,2,1,0:T(8,128)(2,1)}) custom-call(s32[1]{0:T(128)} %bitcast.20.tok, bf16[1024,1024]{1,0:T(8,128)(2,1)} %get-tuple-element.74.refs_0_, bf16[3,1024,1024]{2,1,0:T(8,128)(2,1)} %get-tuple-element.72.refs_1_.refs_2_.refs_3_, ...), custom_call_target="tpu_custom_call" | custom-call | flops 6442450944 | bytes 25165824 | tf_op jit(solution)/shard_map/joined_grad/pallas_call | solution.py:836
  318.5 44.7 %embed_backward.1 = (f32[1024,1024]{1,0:T(8,128)}, bf16[256,1024]{1,0:T(8,128)(2,1)}, f32[2,1024]{1,0:T(2,128)}, f32[2,64,768]{2,1,0:T(8,128)}) custom-call(f32[1024,1024]{1,0:T(8,128)} %get-tuple-element.64.refs_0_, bf16[3,1024,1024]{2,1,0:T(8,128)(2,1)} %get-tuple-element.72.refs_1_.refs_2_.refs_3_, bf16[1024,3072]{1,0:T(8,128)(2,1)} %refs_2_.1, ...), custom_call_target="tpu_custom_call" | custom-call | flops 6442450944 | bytes 27262976 | tf_op jit(solution)/shard_map/embed_backward/pallas_call | solution.py:656
  363.3 0.7 constant_dynamic-update-slice_fusion.6
  364.1 1.8 collective-permute-start.8
  365.9 1.3 collective-permute-start.7
  367.5 1.6 collective-permute-start.22
  369.1 2.6 collective-permute-done.22
  371.7 1.6 collective-permute-start.23
  373.4 0.7 slice.334
  374.0 0.8 slice.335
  374.9 1.0 copy.25
  376.0 3.9 collective-permute-start.26
  379.8 25.8 %collective-permute-start.24 = (f32[112,128]{1,0:T(8,128)S(1)}, f32[112,128]{1,0:T(8,128)S(1)}, u32[]{:S(2)}, u32[]{:S(2)}) collective-permute-start(f32[112,128]{1,0:T(8,128)S(1)} %add.138), channel_id=1, source_target_pairs={{0,1},{1,2},{2,3},{3,0},{4,5},{5,6},{6,7},{7,4},{8,9},{9,10},{10,1... | collective-permute-start | bytes 172040 | tf_op jit(solution)/shard_map/ppermute | solution.py:857
  405.7 10.7 %collective-permute-done.7.g2 = bf16[256,1024]{1,0:T(8,128)(2,1)S(1)} collective-permute-done((bf16[256,1024]{1,0:T(8,128)(2,1)}, bf16[256,1024]{1,0:T(8,128)(2,1)S(1)}, u32[]{:S(2)}, u32[]{:S(2)}) %collective-permute-start.7) | collective-permute-done | bytes 524320 | tf_op jit(solution)/shard_map/ppermute | solution.py:857
  416.3 0.8 copy-done.12
  417.1 0.8 copy-done.13
  417.9 6.5 %table_grad.1 = (bf16[8,128,512]{2,1,0:T(8,128)(2,1)}, bf16[8,128,512]{2,1,0:T(8,128)(2,1)}) custom-call(s32[1]{0:T(128)} %bitcast.20.tok, s32[4,2,256]{2,1,0:T(2,128)} %pad_add_fusion.1.idx, bf16[256,1024]{1,0:T(8,128)(2,1)} %get-tuple-element.78.g0, bf16[256,1024]{1,0:T(8,128)(2,1)} %copy-done.13, bf16[256,1024]{1,0:T(8,128)(2,1)} %copy-done.12, ...), custom_call_target="tpu_custom_call" | custom-call | flops 2147483648 | bytes 4194304 | tf_op jit(solution)/shard_map/table_grad/pallas_call | solution.py:715
  424.4 1.3 fusion.2
  425.8 1.1 fusion.3
  427.8 1.6 collective-permute-start.16
  429.5 1.6 collective-permute-start.10
  431.1 5.2 %collective-permute-done.16 = bf16[2,128,512]{2,1,0:T(8,128)(2,1)S(1)} collective-permute-done((bf16[2,128,512]{2,1,0:T(8,128)(2,1)S(1)}, bf16[2,128,512]{2,1,0:T(8,128)(2,1)S(1)}, u32[]{:S(2)}, u32[]{:S(2)}) %collective-permute-start.16) | collective-permute-done | bytes 262176 | tf_op jit(solution)/shard_map/ppermute | solution.py:853
  436.3 1.6 collective-permute-start.17
  437.9 1.6 collective-permute-start.11
  439.5 1.8 collective-permute-done.17
  441.4 1.6 collective-permute-start.18
  443.0 1.6 collective-permute-start.12
  444.6 1.8 collective-permute-done.18
  446.5 1.6 collective-permute-start.19
  448.0 0.6 slice_bitcast_fusion.6
  448.6 0.6 pad_maximum_fusion.10
  449.5 1.6 collective-permute-start.13
  451.1 2.1 collective-permute-done.19
  453.3 0.6 pad_maximum_fusion.9
  453.9 0.6 pad_maximum_fusion.8
  454.5 1.4 collective-permute-done.13
  456.3 1.7 collective-permute-done.14
  458.2 1.0 copy-done.1
  459.1 6.2 %table_write.1 = f32[1,1001,1024]{2,1,0:T(8,128)} custom-call(s32[1]{0:T(128)} %bitcast.20.tok, bf16[8,128,512]{2,1,0:T(8,128)(2,1)} %copy-done.1, bf16[8,128,512]{2,1,0:T(8,128)(2,1)} %copy-done.2), custom_call_target="tpu_custom_call" | custom-call | bytes 6291456 | tf_op jit(solution)/shard_map/table_write/pallas_call | solution.py:739
  465.3 8.5 %copy.24 = f32[1,1001,1024]{2,0,1:T(1,128)} copy(f32[1,1001,1024]{2,1,0:T(8,128)} %table_write.1) | data formatting | bytes 8200192
  473.9 2.0 copy.50
  475.9 0.7 copy.51
  (100 shorter events, 4.5 us)
Async XLA Ops:
  1.6 9.2 %collective-permute-start.2 = (s32[2,256]{1,0:T(2,128)S(1)}, s32[2,256]{1,0:T(2,128)S(1)}, u32[]{:S(2)}, u32[]{:S(2)}) collective-permute-start(s32[2,256]{1,0:T(2,128)S(1)} %get-tuple-element.144), channel_id=1, source_target_pairs={{0,3},{1,0},{2,1},{3,2},{4,7},{5,4},{6,5},{7,6},{8,11},{9,8},{10,9... | collective-permute-start | bytes 6152 | tf_op jit(solution)/shard_map/ppermute | solution.py:857
  6.7 4.5 collective-permute-start.1
  6.7 5.4 %collective-permute-start = (s32[2,256]{1,0:T(2,128)S(1)}, s32[2,256]{1,0:T(2,128)S(1)}, u32[]{:S(2)}, u32[]{:S(2)}) collective-permute-start(s32[2,256]{1,0:T(2,128)S(1)} %get-tuple-element.146), channel_id=1, source_target_pairs={{0,1},{1,2},{2,3},{3,0},{4,5},{5,6},{6,7},{7,4},{8,9},{9,10},{10,1... | collective-permute-start | bytes 6152 | tf_op jit(solution)/shard_map/ppermute | solution.py:857
  12.7 12.1 %copy-start.10 = (s32[2,512]{1,0:T(2,128)S(1)}, s32[2,512]{1,0:T(2,128)}, u32[]{:S(2)}) copy-start(s32[2,512]{1,0:T(2,128)} %param.14) | copy-start | bytes 12292
  20.8 16.7 %collective-permute-start.5 = (bf16[256,1024]{1,0:T(8,128)(2,1)S(1)}, bf16[256,1024]{1,0:T(8,128)(2,1)S(1)}, u32[]{:S(2)}, u32[]{:S(2)}) collective-permute-start(bf16[256,1024]{1,0:T(8,128)(2,1)S(1)} %get-tuple-element.110), channel_id=1, source_target_pairs={{0,1},{1,2},{2,3},{3,0},{4,5},{5,6},{6,7},{7,4},{8,9},{9,10},{10,1... | collective-permute-start | bytes 1572872 | tf_op jit(solution)/shard_map/ppermute | solution.py:857
  22.0 35.4 %collective-permute-start.4 = (bf16[256,1024]{1,0:T(8,128)(2,1)S(1)}, bf16[256,1024]{1,0:T(8,128)(2,1)S(1)}, u32[]{:S(2)}, u32[]{:S(2)}) collective-permute-start(bf16[256,1024]{1,0:T(8,128)(2,1)S(1)} %get-tuple-element.111), channel_id=1, source_target_pairs={{0,2},{1,3},{2,0},{3,1},{4,6},{5,7},{6,4},{7,5},{8,10},{9,11},{10,... | collective-permute-start | bytes 1572872 | tf_op jit(solution)/shard_map/ppermute | solution.py:857
  22.9 34.5 %collective-permute-start.3 = (bf16[256,1024]{1,0:T(8,128)(2,1)S(1)}, bf16[256,1024]{1,0:T(8,128)(2,1)S(1)}, u32[]{:S(2)}, u32[]{:S(2)}) collective-permute-start(bf16[256,1024]{1,0:T(8,128)(2,1)S(1)} %get-tuple-element.112), channel_id=1, source_target_pairs={{0,3},{1,0},{2,1},{3,2},{4,7},{5,4},{6,5},{7,6},{8,11},{9,8},{10,9... | collective-permute-start | bytes 1572872 | tf_op jit(solution)/shard_map/ppermute | solution.py:857
  37.5 20.0 %copy-start.14 = (bf16[256,1024]{1,0:T(8,128)(2,1)}, bf16[256,1024]{1,0:T(8,128)(2,1)S(1)}, u32[]{:S(2)}) copy-start(bf16[256,1024]{1,0:T(8,128)(2,1)S(1)} %collective-permute-done.5.t3) | copy-start | bytes 1572868
  57.5 0.8 copy-start.15
  57.5 1.0 copy-start.16
  318.5 45.5 %copy-start.9 = (f32[2,1024]{1,0:T(2,128)S(1)}, f32[2,1024]{1,0:T(2,128)}, u32[]{:S(2)}) copy-start(f32[2,1024]{1,0:T(2,128)} %get-tuple-element.87) | copy-start | bytes 24580
  318.5 45.5 %copy-start.8 = (f32[1,4096]{1,0:T(1,128)S(1)}, f32[1,4096]{1,0:T(1,128)}, u32[]{:S(2)}) copy-start(f32[1,4096]{1,0:T(1,128)} %get-tuple-element.88) | copy-start | bytes 49156
  318.5 50.5 %copy-start.6 = (f32[2,256,256]{2,1,0:T(8,128)S(1)}, f32[2,256,256]{2,1,0:T(8,128)}, u32[]{:S(2)}) copy-start(f32[2,256,256]{2,1,0:T(8,128)} %get-tuple-element.83) | copy-start | bytes 1572868
  318.5 54.8 %copy-start.5 = (f32[2,64,1280]{2,1,0:T(8,128)S(1)}, f32[2,64,1280]{2,1,0:T(8,128)}, u32[]{:S(2)}) copy-start(f32[2,64,1280]{2,1,0:T(8,128)} %get-tuple-element.82) | copy-start | bytes 1966084
  364.0 3.4 collective-permute-start.21
  364.1 15.7 %collective-permute-start.8 = (bf16[256,1024]{1,0:T(8,128)(2,1)}, bf16[256,1024]{1,0:T(8,128)(2,1)S(1)}, u32[]{:S(2)}, u32[]{:S(2)}) collective-permute-start(bf16[256,1024]{1,0:T(8,128)(2,1)} %get-tuple-element.78.g0), channel_id=1, source_target_pairs={{0,3},{1,0},{2,1},{3,2},{4,7},{5,4},{6,5},{7,6},{8,11},{9,8},{10,9... | collective-permute-start | bytes 1572872 | tf_op jit(solution)/shard_map/ppermute | solution.py:857
  365.9 50.5 %collective-permute-start.7 = (bf16[256,1024]{1,0:T(8,128)(2,1)}, bf16[256,1024]{1,0:T(8,128)(2,1)S(1)}, u32[]{:S(2)}, u32[]{:S(2)}) collective-permute-start(bf16[256,1024]{1,0:T(8,128)(2,1)} %get-tuple-element.78.g0), channel_id=1, source_target_pairs={{0,2},{1,3},{2,0},{3,1},{4,6},{5,7},{6,4},{7,5},{8,10},{9,11},{10,... | collective-permute-start | bytes 1572872 | tf_op jit(solution)/shard_map/ppermute | solution.py:857
  367.2 49.1 %collective-permute-start.6 = (bf16[256,1024]{1,0:T(8,128)(2,1)}, bf16[256,1024]{1,0:T(8,128)(2,1)S(1)}, u32[]{:S(2)}, u32[]{:S(2)}) collective-permute-start(bf16[256,1024]{1,0:T(8,128)(2,1)} %get-tuple-element.78.g0), channel_id=1, source_target_pairs={{0,1},{1,2},{2,3},{3,0},{4,5},{5,6},{6,7},{7,4},{8,9},{9,10},{10,1... | collective-permute-start | bytes 1572872 | tf_op jit(solution)/shard_map/ppermute | solution.py:857
  367.5 4.2 collective-permute-start.22
  371.7 4.2 collective-permute-start.23
  376.0 51.6 %collective-permute-start.26 = (f32[112,128]{1,0:T(8,128)S(1)}, f32[112,128]{1,0:T(8,128)S(1)}, u32[]{:S(2)}, u32[]{:S(2)}) collective-permute-start(f32[112,128]{1,0:T(8,128)S(1)} %add.138), channel_id=1, source_target_pairs={{0,3},{1,0},{2,1},{3,2},{4,7},{5,4},{6,5},{7,6},{8,11},{9,8},{10,9... | collective-permute-start | bytes 172040 | tf_op jit(solution)/shard_map/ppermute | solution.py:857
  379.8 47.8 %collective-permute-start.25 = (f32[112,128]{1,0:T(8,128)S(1)}, f32[112,128]{1,0:T(8,128)S(1)}, u32[]{:S(2)}, u32[]{:S(2)}) collective-permute-start(f32[112,128]{1,0:T(8,128)S(1)} %add.138), channel_id=1, source_target_pairs={{0,2},{1,3},{2,0},{3,1},{4,6},{5,7},{6,4},{7,5},{8,10},{9,11},{10,... | collective-permute-start | bytes 172040 | tf_op jit(solution)/shard_map/ppermute | solution.py:857
  379.8 36.5 %copy-start.11 = (bf16[256,1024]{1,0:T(8,128)(2,1)}, bf16[256,1024]{1,0:T(8,128)(2,1)S(1)}, u32[]{:S(2)}) copy-start(bf16[256,1024]{1,0:T(8,128)(2,1)S(1)} %collective-permute-done.8.g3) | copy-start | bytes 1572868
  379.8 47.8 %collective-permute-start.24 = (f32[112,128]{1,0:T(8,128)S(1)}, f32[112,128]{1,0:T(8,128)S(1)}, u32[]{:S(2)}, u32[]{:S(2)}) collective-permute-start(f32[112,128]{1,0:T(8,128)S(1)} %add.138), channel_id=1, source_target_pairs={{0,1},{1,2},{2,3},{3,0},{4,5},{5,6},{6,7},{7,4},{8,9},{9,10},{10,1... | collective-permute-start | bytes 172040 | tf_op jit(solution)/shard_map/ppermute | solution.py:857
  416.3 0.8 copy-start.12
  417.1 0.8 copy-start.13
  424.4 3.3 copy-start.4
  424.4 5.0 %copy-start.3 = (bf16[8,128,512]{2,1,0:T(8,128)(2,1)S(1)}, bf16[8,128,512]{2,1,0:T(8,128)(2,1)}, u32[]{:S(2)}) copy-start(bf16[8,128,512]{2,1,0:T(8,128)(2,1)} %get-tuple-element.79) | copy-start | bytes 3145732
  425.7 2.0 collective-permute-start.15
  427.0 2.4 collective-permute-start.9
  427.8 8.4 %collective-permute-start.16 = (bf16[2,128,512]{2,1,0:T(8,128)(2,1)S(1)}, bf16[2,128,512]{2,1,0:T(8,128)(2,1)S(1)}, u32[]{:S(2)}, u32[]{:S(2)}) collective-permute-start(bf16[2,128,512]{2,1,0:T(8,128)(2,1)S(1)} %pad_maximum_fusion.6), channel_id=1, source_target_pairs={{0,16},{4,20},{8,24},{12,28},{16,0},{20,4},{24,8},{28,12},{1,17},{... | collective-permute-start | bytes 786440 | tf_op jit(solution)/shard_map/ppermute | solution.py:853
  429.5 8.4 %collective-permute-start.10 = (bf16[2,128,512]{2,1,0:T(8,128)(2,1)S(1)}, bf16[2,128,512]{2,1,0:T(8,128)(2,1)S(1)}, u32[]{:S(2)}, u32[]{:S(2)}) collective-permute-start(bf16[2,128,512]{2,1,0:T(8,128)(2,1)S(1)} %pad_maximum_fusion.4), channel_id=1, source_target_pairs={{0,8},{4,12},{8,0},{12,4},{16,24},{20,28},{24,16},{28,20},{1,9},{5... | collective-permute-start | bytes 786440 | tf_op jit(solution)/shard_map/ppermute | solution.py:853
  436.3 5.0 %collective-permute-start.17 = (bf16[1,128,512]{2,1,0:T(8,128)(2,1)S(1)}, bf16[1,128,512]{2,1,0:T(8,128)(2,1)S(1)}, u32[]{:S(2)}, u32[]{:S(2)}) collective-permute-start(bf16[1,128,512]{2,1,0:T(8,128)(2,1)S(1)} %add_convert_fusion.1), channel_id=1, source_target_pairs={{0,8},{4,12},{8,0},{12,4},{16,24},{20,28},{24,16},{28,20},{1,9},{5... | collective-permute-start | bytes 393224 | tf_op jit(solution)/shard_map/ppermute | solution.py:853
  437.9 5.0 %collective-permute-start.11 = (bf16[1,128,512]{2,1,0:T(8,128)(2,1)S(1)}, bf16[1,128,512]{2,1,0:T(8,128)(2,1)S(1)}, u32[]{:S(2)}, u32[]{:S(2)}) collective-permute-start(bf16[1,128,512]{2,1,0:T(8,128)(2,1)S(1)} %add_convert_fusion.8), channel_id=1, source_target_pairs={{0,16},{4,20},{8,24},{12,28},{16,0},{20,4},{24,8},{28,12},{1,17},{... | collective-permute-start | bytes 393224 | tf_op jit(solution)/shard_map/ppermute | solution.py:853
  441.4 5.0 %collective-permute-start.18 = (bf16[1,128,512]{2,1,0:T(8,128)(2,1)S(1)}, bf16[1,128,512]{2,1,0:T(8,128)(2,1)S(1)}, u32[]{:S(2)}, u32[]{:S(2)}) collective-permute-start(bf16[1,128,512]{2,1,0:T(8,128)(2,1)S(1)} %get-tuple-element.101), channel_id=1, source_target_pairs={{0,8},{4,12},{8,0},{12,4},{16,24},{20,28},{24,16},{28,20},{1,9},{5... | collective-permute-start | bytes 393224 | tf_op jit(solution)/shard_map/ppermute | solution.py:853
  443.0 6.4 %collective-permute-start.12 = (bf16[1,128,512]{2,1,0:T(8,128)(2,1)S(1)}, bf16[1,128,512]{2,1,0:T(8,128)(2,1)S(1)}, u32[]{:S(2)}, u32[]{:S(2)}) collective-permute-start(bf16[1,128,512]{2,1,0:T(8,128)(2,1)S(1)} %get-tuple-element.103), channel_id=1, source_target_pairs={{0,16},{4,20},{8,24},{12,28},{16,0},{20,4},{24,8},{28,12},{1,17},{... | collective-permute-start | bytes 393224 | tf_op jit(solution)/shard_map/ppermute | solution.py:853
  446.5 6.7 %collective-permute-start.19 = (bf16[2,128,512]{2,1,0:T(8,128)(2,1)S(1)}, bf16[2,128,512]{2,1,0:T(8,128)(2,1)S(1)}, u32[]{:S(2)}, u32[]{:S(2)}) collective-permute-start(bf16[2,128,512]{2,1,0:T(8,128)(2,1)S(1)} %pad_maximum_fusion.7), channel_id=1, source_target_pairs={{0,16},{4,20},{8,24},{12,28},{16,0},{20,4},{24,8},{28,12},{1,17},{... | collective-permute-start | bytes 786440 | tf_op jit(solution)/shard_map/ppermute | solution.py:853
  449.5 6.4 %collective-permute-start.13 = (bf16[2,128,512]{2,1,0:T(8,128)(2,1)S(1)}, bf16[2,128,512]{2,1,0:T(8,128)(2,1)S(1)}, u32[]{:S(2)}, u32[]{:S(2)}) collective-permute-start(bf16[2,128,512]{2,1,0:T(8,128)(2,1)S(1)} %pad_maximum_fusion.5), channel_id=1, source_target_pairs={{0,8},{4,12},{8,0},{12,4},{16,24},{20,28},{24,16},{28,20},{1,9},{5... | collective-permute-start | bytes 786440 | tf_op jit(solution)/shard_map/ppermute | solution.py:853
  453.2 2.9 collective-permute-start.20
  456.0 2.0 collective-permute-start.14
  456.3 1.9 copy-start.2
  458.2 1.0 copy-start.1
  465.3 8.5 %copy-start = (f32[1024,1024]{1,0:T(8,128)S(1)}, f32[1024,1024]{1,0:T(8,128)}, u32[]{:S(2)}) copy-start(f32[1024,1024]{1,0:T(8,128)} %get-tuple-element.163) | copy-start | bytes 12582916
  473.9 2.0 copy-start.7

commit v3 on v2

--- a/solution.py
+++ b/solution.py
@@ -602,27 +602,7 @@
     )(gffn, gs2, after, rstd, wo, gains, shifts, slope, wr, we, *(grads or ()))
 
 
-EMBED_PLAN = {0: [(0, 0)], 1: [(1, 0), (1, 1)]}
-EMBED_TAIL = [
-    (2, 0), (1, 2), (2, 1), (3, 0), (1, 3), (2, 2), (3, 1), (2, 3), (3, 2), (3, 3), (4, 0),
-]
-
-
-def embed_bwd_kernel(*refs, summed):
-    gs1, gj, w, normed, rstd, ci, gains, shifts = refs[:8]
-    refs = refs[8:]
-    grads, refs = refs[: 2 * summed], refs[2 * summed :]
-    out, cells, sums = refs[:3]
-    refs = refs[3:]
-    step, last = pl.program_id(0), pl.num_programs(0) - 1
-    if summed:
-        summing = Summing(grads, refs[0], refs[1:])
-
-        @pl.when(step == 0)
-        def _():
-            meet(summing.devices())
-
-        summing.run(step, EMBED_PLAN)
+def embed_bwd_kernel(gs1, gj, w, normed, rstd, ci, gains, shifts, out, cells, sums):
     width = gs1.shape[1]
     tokens = gs1.shape[0]
     total = gs1[...]
@@ -644,17 +624,13 @@
     def _():
         sums[...] = sums[...] + part
 
-    if summed:
-        summing.run(step, {last: EMBED_TAIL})
-
-
-def embed_bwd(gs1, gj, w, normed, rstd, ci, gains, shifts, grads):
+
+def embed_bwd(gs1, gj, w, normed, rstd, ci, gains, shifts):
     tokens, width = gs1.shape
-    more_in, more_out, more_shape, more_scratch, more = sum_specs(grads, 3)
     pages, length = ci.shape
     rows = pl.BlockSpec((length, width), lambda i: (i, 0))
     return pl.pallas_call(
-        functools.partial(embed_bwd_kernel, summed=grads is not None),
+        embed_bwd_kernel,
         grid=(pages,),
         in_specs=[
             rows,
@@ -665,27 +641,21 @@
             pl.BlockSpec((1, 1, length), lambda i: (i, 0, 0)),
             full(gains.shape),
             full(shifts.shape),
-        ]
-        + more_in,
+        ],
         out_specs=[
             rows,
             pl.BlockSpec((CELLS, width), lambda i: (i, 0)),
             pl.BlockSpec((2, width), lambda i: (0, 0)),
-        ]
-        + more_out,
+        ],
         out_shape=[
             jax.ShapeDtypeStruct((tokens, width), F32),
             jax.ShapeDtypeStruct((pages * CELLS, width), BF),
             jax.ShapeDtypeStruct((2, width), F32),
-        ]
-        + more_shape,
-        scratch_shapes=more_scratch,
-        compiler_params=params(**more),
+        ],
+        compiler_params=params(),
         cost_estimate=cost(2 * tokens * width * 3 * width, 26 << 20),
         name="embed_backward",
-    )(
-        gs1, gj, w, normed, rstd, ci.reshape(pages, 1, length), gains, shifts, *(grads or ())
-    )
+    )(gs1, gj, w, normed, rstd, ci.reshape(pages, 1, length), gains, shifts)
 
 
 def table_kernel(tok, idx, g0, g1, g2, g3, out_a, out_b):
@@ -727,28 +697,226 @@
     )(tok, idx, *grads)
 
 
-def table_out_kernel(tok, a, b, out):
-    half = a.shape[2]
-    out[0, :, :half] = a[0].astype(F32)
-    out[0, :, half:] = b[0].astype(F32)
-
-
-def table_out(tok, a, b, table_rows):
-    blocks, rows, half = a.shape
-    src = pl.BlockSpec((1, rows, half), lambda i, t: (i ^ t[0], 0, 0))
+BLOCK = 128
+
+
+class TableSum:
+    def __init__(self, scratch, done):
+        self.part, self.r0, self.r1, self.r2, self.sent, self.got = scratch
+        self.done = done
+        tok = lax.axis_index("tok")
+        core, x, y, _ = neighbours()
+        self.c, cx, cy = tok % 2, (tok // 2) % 2, tok // 4
+        self.core, self.first, self.second = core, (x, y), (y, x)
+        self.f, self.g = (cx, cy), (cy, cx)
+
+    def copy(self, stage, ch, u):
+        c, f, g = self.c, self.f[ch], self.g[ch]
+        part, done = self.part.at[ch, u], self.done.at[ch, u]
+        src, dst, to = (
+            (lambda: part.at[1 - c], self.r0.at[ch, u], self.core),
+            (lambda: part.at[c, 1 - f], self.r1.at[ch, u], self.first[ch]),
+            (lambda: part.at[c, f, 1 - g], self.r2.at[ch, u], self.second[ch]),
+            (lambda: done.at[c, f, g], None, self.second[ch]),
+            (lambda: done.at[c, f], None, self.first[ch]),
+            (lambda: done.at[c], None, self.core),
+        )[stage]
+        src = src()
+        return pltpu.make_async_remote_copy(
+            src_ref=src, dst_ref=src if dst is None else dst,
+            send_sem=self.sent.at[stage, ch, u], recv_sem=self.got.at[stage, ch, u],
+            device_id=to, device_id_type=pl.DeviceIdType.MESH,
+        )
+
+    def store(self, u, ch, value):
+        for b in range(8):
+            c, x, y = split_rel(b)
+            f, g = (x, y) if ch == 0 else (y, x)
+            self.part[ch, u, c, f, g] = value[b * BLOCK : (b + 1) * BLOCK]
+        self.copy(0, ch, u).start()
+
+    def step(self, stage, u):
+        for ch in range(2):
+            c, f, g = self.c, self.f[ch], self.g[ch]
+            self.copy(stage - 1, ch, u).wait_recv()
+            if stage == 1:
+                self.part[ch, u, c] = self.part[ch, u, c] + self.r0[ch, u]
+            elif stage == 2:
+                self.part[ch, u, c, f] = self.part[ch, u, c, f] + self.r1[ch, u]
+            elif stage == 3:
+                self.done[ch, u, c, f, g] = self.part[ch, u, c, f, g] + self.r2[ch, u]
+            if stage < 6:
+                self.copy(stage, ch, u).start()
+
+    def finish(self):
+        for stage in range(6):
+            for ch in range(2):
+                for u in range(2):
+                    self.copy(stage, ch, u).wait_send()
+
+
+def closing_kernel(
+    cells, idx, small, ga, gb, done, joined, small_out,
+    ring, total, ring_sent, ring_got, held, arrived, small_sent, small_got, *scratch,
+):
+    summing = Summing((ga, gb), joined, scratch[:8])
+    table = TableSum(scratch[8:], done)
+    core, x, y, peers = neighbours()
+    z = lax.axis_index("tab")
+    hops = [core, x, y, {"tab": z + 1 - 2 * (z % 2)}, {"tab": z + 2 - 4 * (z // 2)}]
+    meet([core, x, y, *peers])
+    count = cells.shape[0]
+    half = count // 2
+
+    def pass_on(k, h):
+        rows = pl.ds(h * half, half)
+        src = cells.at[rows] if k == 0 else ring.at[k - 1, rows]
+        return pltpu.make_async_remote_copy(
+            src_ref=src, dst_ref=ring.at[k, rows],
+            send_sem=ring_sent.at[k, h], recv_sem=ring_got.at[k, h],
+            device_id=peers[0], device_id_type=pl.DeviceIdType.MESH,
+        )
+
+    def small_copy(n):
+        return pltpu.make_async_remote_copy(
+            src_ref=held.at[n], dst_ref=arrived.at[n],
+            send_sem=small_sent.at[n], recv_sem=small_got.at[n],
+            device_id=hops[n], device_id_type=pl.DeviceIdType.MESH,
+        )
+
+    def small_step(n):
+        small_copy(n - 1).wait_recv()
+        value = held[n - 1] + arrived[n - 1]
+        if n < 5:
+            held[n] = value
+            small_copy(n).start()
+        else:
+            small_out[...] = value
+
+    def relay(k, h):
+        pass_on(k - 1, h).wait_recv()
+        pass_on(k, h).start()
+
+    def pick(s):
+        number = lax.broadcasted_iota(jnp.int32, (total.shape[0], count), 0)
+        first = (number == idx[s, 0:1, :]).astype(F32)
+        second = (number == idx[s, 1:2, :]).astype(F32)
+        return (first + second).astype(BF)
+
+    pass_on(0, 0).start()
+    pass_on(0, 1).start()
+    held[0] = small[...]
+    small_copy(0).start()
+    summing.start()
+    total[...] = dot(pick(0), cells[...], NN)
+    small_step(1)
+    summing.step(1, 0)
+    small_step(2)
+    summing.step(1, 1)
+    small_step(3)
+    relay(1, 0)
+    summing.step(2, 0)
+    summing.step(1, 2)
+    relay(1, 1)
+    total[...] = total[...] + dot(pick(1), ring[0], NN)
+    summing.step(2, 1)
+    summing.step(1, 3)
+    relay(2, 0)
+    small_step(4)
+    summing.step(2, 2)
+    relay(2, 1)
+    summing.step(3, 0)
+    summing.step(3, 1)
+    total[...] = total[...] + dot(pick(2), ring[1], NN)
+    summing.step(2, 3)
+    summing.step(3, 2)
+    small_step(5)
+    last = pick(3)
+    pass_on(2, 0).wait_recv()
+    pass_on(2, 1).wait_recv()
+    wide = total.shape[1] // 4
+    for u in range(2):
+        for ch in range(2):
+            cols = slice((2 * ch + u) * wide, (2 * ch + u + 1) * wide)
+            value = total[:, cols] + dot(last, ring[2, :, cols], NN)
+            table.store(u, ch, value.astype(BF))
+    summing.step(3, 3)
+    table.step(1, 0)
+    table.step(1, 1)
+    table.step(2, 0)
+    table.step(2, 1)
+    table.step(3, 0)
+    table.step(3, 1)
+    table.step(4, 0)
+    table.step(4, 1)
+    summing.finish()
+    table.step(5, 0)
+    table.step(5, 1)
+    table.step(6, 0)
+    table.step(6, 1)
+    table.finish()
+    for k in range(3):
+        for h in range(2):
+            pass_on(k, h).wait_send()
+    for n in range(5):
+        small_copy(n).wait_send()
+
+
+def closing(cells, idx, small, grads):
+    count, width = cells.shape
+    rows, cols = grads[0].shape[3:]
+    wide = width // 4
+    part = lambda *n: pltpu.VMEM((2, 2, *n, BLOCK, wide), BF)
+    done = (2, 2, 2, 2, 2, BLOCK, wide)
+    dma = pltpu.SemaphoreType.DMA
     return pl.pallas_call(
+        closing_kernel,
+        grid=(1,),
+        in_specs=[full(cells.shape), full(idx.shape), full(small.shape)]
+        + [pl.BlockSpec(memory_space=pl.ANY)] * 2,
+        out_specs=[full(done), full((2, rows, cols)), full(small.shape)],
+        out_shape=[
+            jax.ShapeDtypeStruct(done, BF),
+            jax.ShapeDtypeStruct((2, rows, cols), F32),
+            jax.ShapeDtypeStruct(small.shape, F32),
+        ],
+        scratch_shapes=[
+            pltpu.VMEM((3, count, width), BF), pltpu.VMEM((8 * BLOCK, width), F32),
+            dma((3, 2)), dma((3, 2)),
+            pltpu.VMEM((5, *small.shape), F32), pltpu.VMEM((5, *small.shape), F32), dma((5,)), dma((5,)),
+        ]
+        + sum_scratch(rows, cols)
+        + [part(2, 2, 2), part(2, 2), part(2), part(), dma((6, 2, 2)), dma((6, 2, 2))],
+        compiler_params=params(has_side_effects=True, collective_id=3),
+        cost_estimate=cost(8 * count * width * 1024, 24 << 20),
+        name="closing",
+    )(cells, idx, small, *grads)
+
+
+def table_out_kernel(a, b, out):
+    wide = a.shape[6]
+    for n, piece in enumerate((a, b)):
+        for u in range(2):
+            at = (2 * n + u) * wide
+            out[:, 0, at : at + wide] = piece[0, u, 0, 0, 0].astype(F32)
+
+
+def table_out(done, table_rows):
+    wide = done.shape[6]
+    block = (1, 2, 1, 1, 1, BLOCK, wide)
+    first = lambda i: (0, 0, i % 2, (i // 2) % 2, i // 4, 0, 0)
+    second = lambda i: (1, 0, i % 2, i // 4, (i // 2) % 2, 0, 0)
+    out = pl.pallas_call(
         table_out_kernel,
-        grid_spec=pltpu.PrefetchScalarGridSpec(
-            num_scalar_prefetch=1,
-            grid=(blocks,),
-            in_specs=[src, src],
-            out_specs=pl.BlockSpec((1, rows, 2 * half), lambda i, t: (0, i, 0)),
-        ),
-        out_shape=jax.ShapeDtypeStruct((1, table_rows, 2 * half), F32),
+        grid=(8,),
+        in_specs=[pl.BlockSpec(block, first), pl.BlockSpec(block, second)],
+        out_specs=pl.BlockSpec((BLOCK, 1, 4 * wide), lambda i: (i, 0, 0)),
+        out_shape=jax.ShapeDtypeStruct((table_rows, 1, 4 * wide), F32),
         compiler_params=params(),
         cost_estimate=cost(0, 6 << 20),
         name="table_write",
-    )(tok, a, b)
+    )(done, done)
+    return out.transpose(1, 0, 2)
 
 
 def split_rel(r):
@@ -857,28 +1025,6 @@
     return lax.ppermute(value, "tab", [(i, (i + shift) % size) for i in range(size)])
 
 
-def plus(a, b):
-    return (a.astype(F32) + b.astype(F32)).astype(BF)
-
-
-def table_sum(part, bits, n_tok):
-    rows, cols = part.shape[1:]
-    block = {i: part[i] for i in range(8)}
-    order = list(bits)
-    for bit in order:
-        sent = [i for i in sorted(block) if i & bit]
-        got = flip_tok(jnp.stack([block[i] for i in sent]), bit, n_tok)
-        for n, i in enumerate(sent):
-            block[i ^ bit] = plus(block[i ^ bit], got[n])
-            del block[i]
-    for bit in reversed(order):
-        held = sorted(block)
-        got = flip_tok(jnp.stack([block[i] for i in held]), bit, n_tok)
-        for n, i in enumerate(held):
-            block[i ^ bit] = got[n]
-    return jnp.stack([block[i] for i in range(8)])
-
-
 def small_sum(value, n_tok, n_tab):
     bit = 1
     while bit < n_tok:
@@ -901,7 +1047,7 @@
     ff = expand_weight.shape[1]
     tok = lax.axis_index("tok").astype(jnp.int32).reshape(1)
     z = lax.axis_index("tab")
-    cubic = n_tok == 8
+    cubic = n_tok == 8 and n_tab == 4
 
     corners = cell_boxes[:, :, :CELLS]
     lo = lambda n: jnp.minimum(corners[:, n], corners[:, n + 2]).reshape(-1)
@@ -954,19 +1100,9 @@
         parts = rows_part(
             tok, [(normed_low, [gj, gj, gj], [third(0), third(1), third(2)])], "joined_grad"
         )
-    embedded_grad, cell_grad, sums0, *joined_sum = embed_bwd(
-        gs1, gj, joined_weight, normed, rstd0, cell_index, norm_gains, norm_shifts, parts
+    embedded_grad, cell_grad, sums0 = embed_bwd(
+        gs1, gj, joined_weight, normed, rstd0, cell_index, norm_gains, norm_shifts
     )
-
-    cell_grads = [cell_grad] + [shift_tab(cell_grad, s, n_tab) for s in range(1, n_tab)]
-    part_a, part_b = table_part(tok if cubic else jnp.zeros_like(tok), group_index, cell_grads, 8)
-    if cubic:
-        whole_a = table_sum(part_a, (1, 2, 4), n_tok)
-        whole_b = table_sum(part_b, (1, 4, 2), n_tok)
-        tables_grad = table_out(tok, whole_a, whole_b, table_rows)
-    else:
-        both = jnp.concatenate([part_a, part_b], axis=2).astype(F32)
-        tables_grad = lax.psum(both.reshape(1, -1, width)[:, :table_rows], "tok")
 
     small = jnp.concatenate(
         [
@@ -974,7 +1110,16 @@
             sums_qv.reshape(-1), hidden_sum.reshape(-1),
         ]
     ).reshape(-1, 128)
-    small = small_sum(small, n_tok, n_tab).reshape(-1)
+    if cubic:
+        done, joined_sum, small = closing(cell_grad, group_index, small, parts)
+        tables_grad = table_out(done, table_rows)
+    else:
+        cell_grads = [cell_grad] + [shift_tab(cell_grad, s, n_tab) for s in range(1, n_tab)]
+        part_a, part_b = table_part(jnp.zeros_like(tok), group_index, cell_grads, 8)
+        both = jnp.concatenate([part_a, part_b], axis=2).astype(F32)
+        tables_grad = lax.psum(both.reshape(1, -1, width)[:, :table_rows], "tok")
+        small = small_sum(small, n_tok, n_tab)
+    small = small.reshape(-1)
     row = small.reshape(-1, width)
     gains_grad = jnp.stack([row[0], row[2], row[5]])
     shifts_grad = jnp.stack([row[1], row[3], row[6]])
@@ -986,7 +1131,7 @@
         expand_sum = expand_sum[0].reshape(-1, expand_sum[0].shape[2])
         expand_grad = expand_sum[:, : ff // 4]
         output_grad = expand_sum[:, ff // 4 :]
-        joined_grad = joined_sum[0].reshape(-1, joined_sum[0].shape[2])
+        joined_grad = joined_sum.reshape(-1, joined_sum.shape[2])
     else:
         both = lambda a, b: jnp.einsum("ta,tb->ab", a, b, preferred_element_type=F32).astype(BF)
 

time: 483 us -> 435 us (0.901)
  starting transfers between devices: 59.7 us -> 10.2 us
  Pallas kernels: 322 us -> 365 us
  waiting for transfers between devices: 61.1 us -> 33.3 us
  local copies, waits for them, and re-layouts: 28.9 us -> 15.8 us
    pallas_call x3, Pallas kernels: 57.4 us -> 101 us  [the longest x1 78.9 us: closing(): pl.pallas_call(closing_kernel, grid=(1,), in_specs=[full(cells.shape), fu...]
    ppermute x12 -> x6, starting transfers between devices: 43.2 us -> 10.2 us  [shift_tab(): lax.ppermute(value, 'tab', [(i, (i + shift) % size) for i in range(size)])]
    ppermute x15 -> x0, waiting for transfers between devices: 17.1 us -> none  [flip_tok(): return lax.ppermute(value, 'tok', [(i, i ^ bit) for i in range(size)])]
    ppermute x15 -> x0, starting transfers between devices: 16.5 us -> none  [flip_tok(): return lax.ppermute(value, 'tok', [(i, i ^ bit) for i in range(size)])]
    unnamed x54 -> x28, local copies, waits for them, and re-layouts: 16.6 us -> 4.05 us
    ppermute x12 -> x6, waiting for transfers between devices: 43.9 us -> 33.3 us  [shift_tab(): lax.ppermute(value, 'tab', [(i, (i + shift) % size) for i in range(size)])]
  transfers between devices with their start and end apart: 27 -> 6, of which waited for: 15 -> 4; matrix products, arithmetic and copies ran while one was open for 3% -> 1% of each run, Pallas kernels for 1% -> 0%
where the time goes in v3:
time: 435 us; the launch traced here: 429 us
  Pallas kernels  365 us (84%)
  waiting for transfers between devices  33.3 us (8%)
  local copies, waits for them, and re-layouts  15.8 us (4%)
  starting transfers between devices  10.2 us (2%)
    pallas_call x1, Pallas kernels, closing(): pl.pallas_call(closing_kernel, grid=(1,), in_specs=[full(cells.shape), fu...  78.9 us
    pallas_call x1, Pallas kernels, ffn_bwd(): pl.pallas_call(functools.partial(ffn_bwd_kernel, summed=grads is not None...  68.7 us
    pallas_call x1, Pallas kernels, attn_bwd(): pl.pallas_call(functools.partial(attn_bwd_kernel, summed=grads is not Non...  62.3 us
    pallas_call x1, Pallas kernels, ffn_fwd(): pl.pallas_call(ffn_fwd_kernel, grid=(tokens // tile,), in_specs=[rows, ro...  49.1 us
    ppermute x6, waiting for transfers between devices, shift_tab(): lax.ppermute(value, 'tab', [(i, (i + shift) % size) for i in range(size)])  33.3 us
    pallas_call x2, Pallas kernels, rows_part(): pl.pallas_call(functools.partial(rows_kernel, groups=[len(p[1]) for p in...  29.5 us
    pallas_call x1, Pallas kernels, attn_fwd(): pl.pallas_call(attn_fwd_kernel, grid=(pages, steps), in_specs=[blk] * 3,...  20.1 us
    pallas_call x1, Pallas kernels, embed_bwd(): pl.pallas_call(embed_bwd_kernel, grid=(pages,), in_specs=[rows, pl.BlockS...  15.6 us
  transfers between devices with their start and end apart: 6, of which 4 were waited for; matrix products, arithmetic and copies ran while one was open for 1% of the time, Pallas kernels for 0%

profile of v3, /device:TPU:0, one launch (start us, length us, event | category | flops | bytes accessed | tf_op | source)
XLA Modules:
  0.0 429.4 jit_solution(17427085260917533483)
XLA Ops:
  0.7 0.8 fusion
  1.6 5.1 %collective-permute-start.2 = (s32[2,256]{1,0:T(2,128)S(1)}, s32[2,256]{1,0:T(2,128)S(1)}, u32[]{:S(2)}, u32[]{:S(2)}) collective-permute-start(s32[2,256]{1,0:T(2,128)S(1)} %get-tuple-element.126), channel_id=1, source_target_pairs={{0,3},{1,0},{2,1},{3,2},{4,7},{5,4},{6,5},{7,6},{8,11},{9,8},{10,9... | collective-permute-start | bytes 6152 | tf_op jit(solution)/shard_map/ppermute | solution.py:1025
  6.7 0.0 collective-permute-start.1
  6.7 1.0 collective-permute-start
  7.8 3.1 pad.6.table
  10.9 0.0 collective-permute-done.2
  10.9 0.4 collective-permute-done.1
  11.2 0.9 collective-permute-done
  12.1 0.6 pad_add_fusion.1.idx
  12.7 5.6 %lookup.1 = bf16[4,256,1024]{2,1,0:T(8,128)(2,1)} custom-call(s32[4,2,256]{2,1,0:T(2,128)} %pad_add_fusion.1.idx, bf16[1024,1024]{1,0:T(8,128)(2,1)} %pad.6.table), custom_call_target="tpu_custom_call" | custom-call | flops 2147483648 | bytes 2097152 | tf_op jit(solution)/shard_map/lookup/pallas_call | solution.py:100
  18.3 0.0 copy-start.6
  18.3 2.5 slice_bitcast_fusion
  20.8 1.2 collective-permute-start.5
  22.0 0.9 collective-permute-start.4
  22.9 1.9 collective-permute-start.3
  24.9 0.0 copy-done.6
  24.9 0.6 reshape.190.ci
  25.5 12.0 %collective-permute-done.5.t3 = bf16[256,1024]{1,0:T(8,128)(2,1)S(1)} collective-permute-done((bf16[256,1024]{1,0:T(8,128)(2,1)S(1)}, bf16[256,1024]{1,0:T(8,128)(2,1)S(1)}, u32[]{:S(2)}, u32[]{:S(2)}) %collective-permute-start.5) | collective-permute-done | bytes 524320 | tf_op jit(solution)/shard_map/ppermute | solution.py:1025
  37.5 0.0 copy-start.8
  37.5 19.9 %collective-permute-done.4.t2 = bf16[256,1024]{1,0:T(8,128)(2,1)S(1)} collective-permute-done((bf16[256,1024]{1,0:T(8,128)(2,1)S(1)}, bf16[256,1024]{1,0:T(8,128)(2,1)S(1)}, u32[]{:S(2)}, u32[]{:S(2)}) %collective-permute-start.4) | collective-permute-done | bytes 524320 | tf_op jit(solution)/shard_map/ppermute | solution.py:1025
  57.5 0.0 copy-start.9
  57.5 0.0 collective-permute-done.3.t1
  57.5 0.0 copy-start.10
  57.5 0.0 copy-done.8
  57.5 0.8 copy-done.9
  58.3 0.2 copy-done.10
  58.4 14.4 %embed_joined.1 = (bf16[1024,1024]{1,0:T(8,128)(2,1)}, bf16[1024,1024]{1,0:T(8,128)(2,1)}, bf16[1024,1024]{1,0:T(8,128)(2,1)}, f32[1024,1024]{1,0:T(8,128)}, bf1...) custom-call(bf16[1024,1024]{1,0:T(8,128)(2,1)} %emb.1, s32[2,1,512]{2,1,0:T(1,128)} %reshape.190.ci, ...), custom_call_target="tpu_custom_call" | custom-call | flops 6442450944 | bytes 27262976 | tf_op jit(solution)/shard_map/embed_joined/pallas_call | solution.py:142
  72.8 20.1 %attention.1 = (bf16[1024,1024]{1,0:T(8,128)(2,1)}, f32[2,4,4,512]{3,2,1,0:T(4,128)}) custom-call(bf16[1024,1024]{1,0:T(8,128)(2,1)} %get-tuple-element.50.q.refs_0_, bf16[1024,1024]{1,0:T(8,128)(2,1)} %get-tuple-element.51.k.refs_1_, bf16[1024,1024]{1,0:T(8,128)(2,1)} %get-tuple-element.52.v.refs_2_), custom_call_target="tpu_custom_call" | custom-call | flops 14000000000 | bytes 8388608 | tf_op jit(solution)/shard_map/attention/pallas_call | solution.py:319
  92.8 49.1 %ffn_forward.1 = (bf16[1024,1024]{1,0:T(8,128)(2,1)}, f32[1024,1024]{1,0:T(8,128)}, bf16[1024,1024]{1,0:T(8,128)(2,1)}, f32[1024,1]{1,0:T(8,128)}, bf16[1024,409...) custom-call(bf16[1024,1024]{1,0:T(8,128)(2,1)} %get-tuple-element.53, ...), custom_call_target="tpu_custom_call" | custom-call | flops 19327352832 | bytes 62914560 | tf_op jit(solution)/shard_map/ffn_forward/pallas_call | solution.py:487
  142.0 14.4 %reduce_grad.1 = (bf16[2,4,4,256,256]{4,3,2,1,0:T(8,128)(2,1)}, bf16[2,4,4,256,256]{4,3,2,1,0:T(8,128)(2,1)}) custom-call(s32[1]{0:T(128)} %bitcast.20.tok, bf16[1024,1024]{1,0:T(8,128)(2,1)} %get-tuple-element.56.gffn.refs_0_, bf16[1024,4096]{1,0:T(8,128)(2,1)} %get-tuple-element.61.act), custom_call_target="tpu_custom_call" | custom-call | flops 8589934592 | bytes 20971520 | tf_op jit(solution)/shard_map/reduce_grad/pallas_call | solution.py:946
  156.4 68.7 %ffn_backward.1 = (bf16[1024,4096]{1,0:T(8,128)(2,1)}, f32[1024,1024]{1,0:T(8,128)}, bf16[1024,1024]{1,0:T(8,128)(2,1)}, bf16[1024,1024]{1,0:T(8,128)(2,1)}, f32...) custom-call(bf16[1024,1024]{1,0:T(8,128)(2,1)} %get-tuple-element.56.gffn.refs_0_, ...), custom_call_target="tpu_custom_call" | custom-call | flops 19327352832 | bytes 62914560 | tf_op jit(solution)/shard_map/ffn_backward/pallas_call | solution.py:579
  225.2 17.7 %expand_output_grad.1 = (bf16[2,4,4,64,1280]{4,3,2,1,0:T(8,128)(2,1)}, bf16[2,4,4,64,1280]{4,3,2,1,0:T(8,128)(2,1)}) custom-call(s32[1]{0:T(128)} %bitcast.20.tok, bf16[1024,1024]{1,0:T(8,128)(2,1)} %get-tuple-element.67.refs_0_, bf16[1024,1024]{1,0:T(8,128)(2,1)} %get-tuple-element.53.mixed.refs_1_.refs_3_, bf16[1024,4096]{1,0:T(8,128)(2,1)} %get-tuple-element.68.refs_2_, ...), custom_call_target="tpu_custom_call" | custom-call | flops 10737418240 | bytes 25165824 | tf_op jit(solution)/shard_map/expand_output_grad/pallas_call | solution.py:1004
  242.9 0.0 copy-start.2
  242.9 0.0 copy-start.3
  242.9 62.3 %attention_back.1 = (bf16[3,1024,1024]{2,1,0:T(8,128)(2,1)}, f32[2,1024]{1,0:T(2,128)}, f32[2,64,1280]{2,1,0:T(8,128)}) custom-call(bf16[1024,1024]{1,0:T(8,128)(2,1)} %get-tuple-element.50.q.refs_0_, bf16[1024,1024]{1,0:T(8,128)(2,1)} %get-tuple-element.51.k.refs_1_, bf16[1024,1024]{1,0:T(8,128)(2,1)} %get-tuple-element.52.v.refs_2_, ...), custom_call_target="tpu_custom_call" | custom-call | flops 35000000512 | bytes 16777216 | tf_op jit(solution)/shard_map/attention_back/pallas_call | solution.py:413
  305.2 1.6 slice.149
  306.8 1.9 slice.150
  308.7 0.0 copy-done.2
  308.7 0.0 copy-done.3
  308.7 15.6 %embed_backward.1 = (f32[1024,1024]{1,0:T(8,128)}, bf16[256,1024]{1,0:T(8,128)(2,1)}, f32[2,1024]{1,0:T(2,128)}) custom-call(f32[1024,1024]{1,0:T(8,128)} %get-tuple-element.64.gs1, bf16[3,1024,1024]{2,1,0:T(8,128)(2,1)} %get-tuple-element.72.gj.refs_1_.refs_2_.refs_3_, bf16[1024,3072]{1,0:T(8,128)(2,1)} %w.3, f32[1024,1024]{1,0:T(8,128)} %get-tuple-element.54.normed, ...), custom_call_target="tpu_custom_call" | custom-call | flops 6442450944 | bytes 27262976 | tf_op jit(solution)/shard_map/embed_backward/pallas_call | solution.py:632
  324.3 0.7 bitcast_dynamic-update-slice_fusion.1
  325.0 0.0 copy-start.5
  325.0 0.0 copy-start.4
  325.0 11.8 %joined_grad.1 = (bf16[2,4,4,64,768]{4,3,2,1,0:T(8,128)(2,1)}, bf16[2,4,4,64,768]{4,3,2,1,0:T(8,128)(2,1)}) custom-call(s32[1]{0:T(128)} %bitcast.20.tok, bf16[1024,1024]{1,0:T(8,128)(2,1)} %get-tuple-element.81.refs_0_, bf16[3,1024,1024]{2,1,0:T(8,128)(2,1)} %get-tuple-element.72.gj.refs_1_.refs_2_.refs_3_, ...), custom_call_target="tpu_custom_call" | custom-call | flops 6442450944 | bytes 25165824 | tf_op jit(solution)/shard_map/joined_grad/pallas_call | solution.py:1004
  336.8 0.0 copy-done.5
  336.8 0.0 copy-done.4
  336.8 0.0 copy-start.7
  336.9 0.6 copy-done.7
  337.5 0.0 copy-start
  337.5 78.9 %closing.1 = (bf16[2,2,2,2,2,128,256]{6,5,4,3,2,1,0:T(8,128)(2,1)}, f32[2,64,768]{2,1,0:T(8,128)}, f32[112,128]{1,0:T(8,128)}) custom-call(bf16[256,1024]{1,0:T(8,128)(2,1)} %get-tuple-element.75.cells, s32[4,2,256]{2,1,0:T(2,128)} %pad_add_fusion.1.idx, f32[112,128]{1,0:T(8,128)} %bitcast.90, bf16[2,4,4,64,768]{4,3,2,1,0:T(8,128)(2,1)} %get-tuple-element.82.ga, ...), custom_call_target="tpu_custom_call" | custom-call | flops 2147483648 | bytes 25165824 | tf_op jit(solution)/shard_map/closing/pallas_call | solution.py:872
  416.3 1.3 slice_bitcast_fusion.6
  417.7 0.7 fusion.2
  418.4 0.0 copy-done
  418.4 0.1 maximum_bitcast_fusion
  418.5 1.0 copy.24
  419.5 0.0 copy-start.1
  419.5 6.7 %table_write.1 = f32[1001,1,1024]{2,1,0:T(1,128)} custom-call(bf16[2,2,2,2,2,128,256]{6,5,4,3,2,1,0:T(8,128)(2,1)} %get-tuple-element.84.a.b, bf16[2,2,2,2,2,128,256]{6,5,4,3,2,1,0:T(8,128)(2,1)} %get-tuple-element.84.a.b), custom_call_target="tpu_custom_call" | custom-call | bytes 6291456 | tf_op jit(solution)/shard_map/table_write/pallas_call | solution.py:909
  426.2 0.6 pad_maximum_fusion.2
  426.9 0.6 pad_maximum_fusion.1
  427.5 0.6 pad_maximum_fusion
  428.1 0.0 copy-done.1
  428.1 0.7 copy.34
  (11 shorter events, 0.1 us)
Async XLA Ops:
  1.6 9.2 %collective-permute-start.2 = (s32[2,256]{1,0:T(2,128)S(1)}, s32[2,256]{1,0:T(2,128)S(1)}, u32[]{:S(2)}, u32[]{:S(2)}) collective-permute-start(s32[2,256]{1,0:T(2,128)S(1)} %get-tuple-element.126), channel_id=1, source_target_pairs={{0,3},{1,0},{2,1},{3,2},{4,7},{5,4},{6,5},{7,6},{8,11},{9,8},{10,9... | collective-permute-start | bytes 6152 | tf_op jit(solution)/shard_map/ppermute | solution.py:1025
  6.7 4.5 %collective-permute-start.1 = (s32[2,256]{1,0:T(2,128)S(1)}, s32[2,256]{1,0:T(2,128)S(1)}, u32[]{:S(2)}, u32[]{:S(2)}) collective-permute-start(s32[2,256]{1,0:T(2,128)S(1)} %get-tuple-element.127), channel_id=1, source_target_pairs={{0,2},{1,3},{2,0},{3,1},{4,6},{5,7},{6,4},{7,5},{8,10},{9,11},{10,... | collective-permute-start | bytes 6152 | tf_op jit(solution)/shard_map/ppermute | solution.py:1025
  6.7 5.4 %collective-permute-start = (s32[2,256]{1,0:T(2,128)S(1)}, s32[2,256]{1,0:T(2,128)S(1)}, u32[]{:S(2)}, u32[]{:S(2)}) collective-permute-start(s32[2,256]{1,0:T(2,128)S(1)} %get-tuple-element.128), channel_id=1, source_target_pairs={{0,1},{1,2},{2,3},{3,0},{4,5},{5,6},{6,7},{7,4},{8,9},{9,10},{10,1... | collective-permute-start | bytes 6152 | tf_op jit(solution)/shard_map/ppermute | solution.py:1025
  18.3 6.5 %copy-start.6 = (s32[2,512]{1,0:T(2,128)S(1)}, s32[2,512]{1,0:T(2,128)}, u32[]{:S(2)}) copy-start(s32[2,512]{1,0:T(2,128)} %param.14) | copy-start | bytes 12292
  20.8 16.7 %collective-permute-start.5 = (bf16[256,1024]{1,0:T(8,128)(2,1)S(1)}, bf16[256,1024]{1,0:T(8,128)(2,1)S(1)}, u32[]{:S(2)}, u32[]{:S(2)}) collective-permute-start(bf16[256,1024]{1,0:T(8,128)(2,1)S(1)} %get-tuple-element.106), channel_id=1, source_target_pairs={{0,1},{1,2},{2,3},{3,0},{4,5},{5,6},{6,7},{7,4},{8,9},{9,10},{10,1... | collective-permute-start | bytes 1572872 | tf_op jit(solution)/shard_map/ppermute | solution.py:1025
  22.0 35.4 %collective-permute-start.4 = (bf16[256,1024]{1,0:T(8,128)(2,1)S(1)}, bf16[256,1024]{1,0:T(8,128)(2,1)S(1)}, u32[]{:S(2)}, u32[]{:S(2)}) collective-permute-start(bf16[256,1024]{1,0:T(8,128)(2,1)S(1)} %get-tuple-element.107), channel_id=1, source_target_pairs={{0,2},{1,3},{2,0},{3,1},{4,6},{5,7},{6,4},{7,5},{8,10},{9,11},{10,... | collective-permute-start | bytes 1572872 | tf_op jit(solution)/shard_map/ppermute | solution.py:1025
  22.9 34.5 %collective-permute-start.3 = (bf16[256,1024]{1,0:T(8,128)(2,1)S(1)}, bf16[256,1024]{1,0:T(8,128)(2,1)S(1)}, u32[]{:S(2)}, u32[]{:S(2)}) collective-permute-start(bf16[256,1024]{1,0:T(8,128)(2,1)S(1)} %get-tuple-element.108), channel_id=1, source_target_pairs={{0,3},{1,0},{2,1},{3,2},{4,7},{5,4},{6,5},{7,6},{8,11},{9,8},{10,9... | collective-permute-start | bytes 1572872 | tf_op jit(solution)/shard_map/ppermute | solution.py:1025
  37.5 20.0 %copy-start.8 = (bf16[256,1024]{1,0:T(8,128)(2,1)}, bf16[256,1024]{1,0:T(8,128)(2,1)S(1)}, u32[]{:S(2)}) copy-start(bf16[256,1024]{1,0:T(8,128)(2,1)S(1)} %collective-permute-done.5.t3) | copy-start | bytes 1572868
  57.5 0.8 copy-start.9
  57.5 1.0 copy-start.10
  242.9 65.8 %copy-start.2 = (f32[3,1024]{1,0:T(4,128)S(1)}, f32[3,1024]{1,0:T(4,128)}, u32[]{:S(2)}) copy-start(f32[3,1024]{1,0:T(4,128)} %get-tuple-element.78) | copy-start | bytes 36868
  242.9 65.8 %copy-start.3 = (f32[3,1024]{1,0:T(4,128)S(1)}, f32[3,1024]{1,0:T(4,128)}, u32[]{:S(2)}) copy-start(f32[3,1024]{1,0:T(4,128)} %get-tuple-element.77) | copy-start | bytes 36868
  325.0 11.8 %copy-start.5 = (f32[2,1024]{1,0:T(2,128)S(1)}, f32[2,1024]{1,0:T(2,128)}, u32[]{:S(2)}) copy-start(f32[2,1024]{1,0:T(2,128)} %get-tuple-element.79) | copy-start | bytes 24580
  325.0 11.8 %copy-start.4 = (f32[1,4096]{1,0:T(1,128)S(1)}, f32[1,4096]{1,0:T(1,128)}, u32[]{:S(2)}) copy-start(f32[1,4096]{1,0:T(1,128)} %get-tuple-element.80) | copy-start | bytes 49156
  336.8 0.6 copy-start.7
  337.5 80.9 %copy-start = (f32[2,256,256]{2,1,0:T(8,128)S(1)}, f32[2,256,256]{2,1,0:T(8,128)}, u32[]{:S(2)}) copy-start(f32[2,256,256]{2,1,0:T(8,128)} %get-tuple-element.87) | copy-start | bytes 1572868
  419.5 8.6 %copy-start.1 = (f32[2,64,768]{2,1,0:T(8,128)S(1)}, f32[2,64,768]{2,1,0:T(8,128)}, u32[]{:S(2)}) copy-start(f32[2,64,768]{2,1,0:T(8,128)} %get-tuple-element.85) | copy-start | bytes 1179652

commit v4 on v3

--- a/solution.py
+++ b/solution.py
@@ -331,38 +331,11 @@
     )(q, k, v)
 
 
-ATTN_PLAN = {
-    0: [(0, 0)],
-    1: [(1, 0)],
-    2: [(1, 1)],
-    3: [(2, 0), (1, 2)],
-    5: [(2, 1), (1, 3)],
-    6: [(3, 0)],
-}
-ATTN_TAIL = [(2, 2), (3, 1), (2, 3), (3, 2), (3, 3), (4, 0)]
-
-
-def attn_bwd_kernel(*refs, summed):
-    q, k, v, mixed, go, lse = refs[:6]
-    refs = refs[6:]
-    grads, refs = refs[: 2 * summed], refs[2 * summed :]
-    gj, sums = refs[:2]
-    refs = refs[2:]
-    step = pl.program_id(0) * pl.num_programs(1) + pl.program_id(1)
-    last = pl.num_programs(0) * pl.num_programs(1) - 1
-    if summed:
-        summing = Summing(grads, refs[0], refs[1:])
-
-        @pl.when(step == 0)
-        def _():
-            meet(summing.devices())
-
-        summing.run(step, ATTN_PLAN)
+def attn_back(q, k, v, mixed, go, lse, put):
     length = q.shape[0]
     pair = 2 * HEAD_DIM
     low_half = head_masks(length, pair)
     zero = jnp.zeros((length, pair), BF)
-    page = pl.program_id(1)
 
     def pick(x, h):
         return jnp.where(low_half, x, zero) if h == 0 else jnp.where(low_half, zero, x)
@@ -385,52 +358,7 @@
             dv = dv_h if dv is None else dv + dv_h
             dk = dk_h if dk is None else dk + dk_h
         dq = (jnp.concatenate(dq_t, axis=0).T.astype(BF).astype(F32) * SCALE).astype(BF)
-        dv = dv.astype(BF)
-        gj[0, :, cols] = dq
-        gj[1, :, cols] = dk.astype(BF)
-        gj[2, :, cols] = dv
-        part = jnp.concatenate([colsum(dq.astype(F32)), colsum(dv.astype(F32))], axis=0)
-
-        @pl.when(page == 0)
-        def _():
-            sums[:, cols] = part
-
-        @pl.when(page != 0)
-        def _():
-            sums[:, cols] = sums[:, cols] + part
-
-    if summed:
-        summing.run(step, {last: ATTN_TAIL})
-
-
-def attn_bwd(q, k, v, mixed, go, lse, pages, grads):
-    tokens, width = q.shape
-    more_in, more_out, more_shape, more_scratch, more = sum_specs(grads, 2)
-    length = tokens // pages
-    steps = HEADS // HP
-    wide = HP * HEAD_DIM
-    blk = pl.BlockSpec((length, wide), lambda j, i: (i, j))
-    return pl.pallas_call(
-        functools.partial(attn_bwd_kernel, summed=grads is not None),
-        grid=(steps, pages),
-        in_specs=[blk] * 5
-        + [pl.BlockSpec((1, 1, HP, length), lambda j, i: (i, j, 0, 0))]
-        + more_in,
-        out_specs=[
-            pl.BlockSpec((3, length, wide), lambda j, i: (0, i, j)),
-            pl.BlockSpec((2, wide), lambda j, i: (0, j)),
-        ]
-        + more_out,
-        out_shape=[
-            jax.ShapeDtypeStruct((3, tokens, width), BF),
-            jax.ShapeDtypeStruct((2, width), F32),
-        ]
-        + more_shape,
-        scratch_shapes=more_scratch,
-        compiler_params=params(**more),
-        cost_estimate=cost(35e9, 16 << 20, pages * HEADS * length * length),
-        name="attention_back",
-    )(q, k, v, mixed, go, lse, *(grads or ()))
+        put(p * pair, pair, dq, dk.astype(BF), dv.astype(BF))
 
 
 FC = 512
@@ -602,60 +530,190 @@
     )(gffn, gs2, after, rstd, wo, gains, shifts, slope, wr, we, *(grads or ()))
 
 
-def embed_bwd_kernel(gs1, gj, w, normed, rstd, ci, gains, shifts, out, cells, sums):
+BACK_PLAN = {
+    0: [(0, 0)],
+    1: [(1, 0)],
+    2: [(1, 1)],
+    3: [(2, 0), (1, 2)],
+    5: [(2, 1), (1, 3)],
+    6: [(3, 0)],
+    8: [(2, 2)],
+    9: [(3, 1)],
+    11: [(2, 3)],
+    12: [(3, 2)],
+    13: [(3, 3)],
+}
+
+
+def rel_of(b):
+    tok = lax.axis_index("tok")
+    core, x, y = split_rel(b)
+    flip = lambda static, mine: 1 - mine if static else mine
+    return flip(core, tok % 2), flip(x, (tok // 2) % 2), flip(y, tok // 4)
+
+
+def put_rows(g, ga, gb, cols, rows):
+    half = rows // 2
+    for b in range(8):
+        core, x, y = rel_of(b)
+        ga[core, 0, 2 * x + y, :, cols] = g[b * rows : b * rows + half]
+        gb[core, 0, 2 * y + x, :, cols] = g[b * rows + half : (b + 1) * rows]
+
+
+def back_kernel(*refs, pages, summed):
+    q, k, v, mixed, go, lse, low, gs1, w, normed, rstd, ci, gains, shifts = refs[:14]
+    refs = refs[14:]
+    grads, refs = refs[: 2 * summed], refs[2 * summed :]
+    out, cells, sums0, sums_qv = refs[:4]
+    refs = refs[4:]
+    if summed:
+        ga, gb, summed_out, gj = refs[:4]
+        summing = Summing(grads, summed_out, refs[4:])
+    else:
+        gj_out, gj = refs
+    step = pl.program_id(0)
     width = gs1.shape[1]
-    tokens = gs1.shape[0]
-    total = gs1[...]
-    for n in range(3):
-        total = total + dot(gj[n], w[:, n * width : (n + 1) * width], NT)
-    xh = (normed[...] - shifts[0:1]) * (1.0 / gains[0:1])
-    grad = norm_back(total, xh, rstd[...], gains[0:1])
-    out[...] = grad
-    number = lax.broadcasted_iota(jnp.int32, (CELLS, tokens), 0)
-    pick = (number == ci[0]).astype(F32).astype(BF)
-    cells[...] = dot(pick, grad.astype(BF), NN).astype(BF)
-    part = jnp.concatenate([colsum(total * xh), colsum(total)], axis=0)
-
-    @pl.when(pl.program_id(0) == 0)
+    length = q.shape[0]
+    groups = HEADS // HP
+    wide = HP * HEAD_DIM
+    n_attn = groups * pages
+    n_joined = 4 if summed else 0
+
+    if summed:
+
+        @pl.when(step == 0)
+        def _():
+            meet(summing.devices())
+
+        summing.run(step, BACK_PLAN)
+
+    @pl.when(step < n_attn)
     def _():
-        sums[...] = part
-
-    @pl.when(pl.program_id(0) != 0)
+        group, page = step // pages, step % pages
+        rows = pl.ds(pl.multiple_of(page * length, length), length)
+
+        def put(at, size, dq, dk, dv):
+            cols = pl.ds(pl.multiple_of(group * wide + at, size), size)
+            gj[0, rows, cols] = dq
+            gj[1, rows, cols] = dk
+            gj[2, rows, cols] = dv
+            part = jnp.concatenate([colsum(dq.astype(F32)), colsum(dv.astype(F32))], axis=0)
+
+            @pl.when(page == 0)
+            def _():
+                sums_qv[:, cols] = part
+
+            @pl.when(page != 0)
+            def _():
+                sums_qv[:, cols] = sums_qv[:, cols] + part
+
+        attn_back(q, k, v, mixed, go, lse, put)
+
+    if summed:
+        quarter = width // 4
+        for n in range(n_joined):
+
+            @pl.when(step == n_attn + n)
+            def _(n=n):
+                for m in range(3):
+                    third, at = (3 * n + m) // 4, (3 * n + m) % 4
+                    piece = gj[third, :, at * quarter : (at + 1) * quarter]
+                    g = dot(low[...], piece, TN).astype(BF)
+                    put_rows(g, ga, gb, slice(m * quarter, (m + 1) * quarter), width // 8)
+
+    @pl.when(step >= n_attn + n_joined)
     def _():
-        sums[...] = sums[...] + part
-
-
-def embed_bwd(gs1, gj, w, normed, rstd, ci, gains, shifts):
-    tokens, width = gs1.shape
+        page = step - (n_attn + n_joined)
+        rows = pl.ds(pl.multiple_of(page * length, length), length)
+        total = gs1[...]
+        for n in range(3):
+            total = total + dot(gj[n, rows, :], w[:, n * width : (n + 1) * width], NT)
+        xh = (normed[...] - shifts[0:1]) * (1.0 / gains[0:1])
+        grad = norm_back(total, xh, rstd[...], gains[0:1])
+        out[...] = grad
+        number = lax.broadcasted_iota(jnp.int32, (CELLS, length), 0)
+        pick = (number == ci[0]).astype(F32).astype(BF)
+        cells[...] = dot(pick, grad.astype(BF), NN).astype(BF)
+        part = jnp.concatenate([colsum(total * xh), colsum(total)], axis=0)
+
+        @pl.when(page == 0)
+        def _():
+            sums0[...] = part
+
+        @pl.when(page != 0)
+        def _():
+            sums0[...] = sums0[...] + part
+
+    if summed:
+
+        @pl.when(step == pl.num_programs(0) - 1)
+        def _():
+            summing.finish()
+    else:
+        gj_out[...] = gj[...]
+
+
+def back(q, k, v, mixed, go, lse, low, gs1, w, normed, rstd, ci, gains, shifts, grads):
+    tokens, width = q.shape
     pages, length = ci.shape
-    rows = pl.BlockSpec((length, width), lambda i: (i, 0))
+    groups = HEADS // HP
+    wide = HP * HEAD_DIM
+    summed = grads is not None
+    n_attn = groups * pages
+    before = n_attn + (4 if summed else 0)
+    at = lambda s: jnp.minimum(s, n_attn - 1)
+    page = lambda s: jnp.maximum(s - before, 0)
+    block = lambda s: jnp.clip(s - n_attn, 0, 3)
+    blk = pl.BlockSpec((length, wide), lambda s: (at(s) % pages, at(s) // pages))
+    rows = pl.BlockSpec((length, width), lambda s: (page(s), 0))
+    out_specs = [
+        rows,
+        pl.BlockSpec((CELLS, width), lambda s: (page(s), 0)),
+        full((2, width)),
+        full((2, width)),
+    ]
+    out_shape = [
+        jax.ShapeDtypeStruct((tokens, width), F32),
+        jax.ShapeDtypeStruct((pages * CELLS, width), BF),
+        jax.ShapeDtypeStruct((2, width), F32),
+        jax.ShapeDtypeStruct((2, width), F32),
+    ]
+    whole_gj = (3, tokens, width)
+    more_in, more_out, more_shape, more_scratch, more = sum_specs(grads, 2)
+    if summed:
+        half = width // 16
+        piece = pl.BlockSpec((2, 1, 4, half, 3 * width // 4), lambda s: (0, block(s), 0, 0, 0))
+        out_specs += [piece, piece]
+        out_shape += [jax.ShapeDtypeStruct((2, 4, 4, half, 3 * width // 4), BF)] * 2
+    else:
+        out_specs += [full(whole_gj)]
+        out_shape += [jax.ShapeDtypeStruct(whole_gj, BF)]
     return pl.pallas_call(
-        embed_bwd_kernel,
-        grid=(pages,),
-        in_specs=[
+        functools.partial(back_kernel, pages=pages, summed=summed),
+        grid=(before + pages,),
+        in_specs=[blk] * 5
+        + [
+            pl.BlockSpec((1, 1, HP, length), lambda s: (at(s) % pages, at(s) // pages, 0, 0)),
+            full(low.shape),
             rows,
-            pl.BlockSpec((3, length, width), lambda i: (0, i, 0)),
             full(w.shape),
             rows,
-            pl.BlockSpec((length, 1), lambda i: (i, 0)),
-            pl.BlockSpec((1, 1, length), lambda i: (i, 0, 0)),
+            pl.BlockSpec((length, 1), lambda s: (page(s), 0)),
+            pl.BlockSpec((1, 1, length), lambda s: (page(s), 0, 0)),
             full(gains.shape),
             full(shifts.shape),
-        ],
-        out_specs=[
-            rows,
-            pl.BlockSpec((CELLS, width), lambda i: (i, 0)),
-            pl.BlockSpec((2, width), lambda i: (0, 0)),
-        ],
-        out_shape=[
-            jax.ShapeDtypeStruct((tokens, width), F32),
-            jax.ShapeDtypeStruct((pages * CELLS, width), BF),
-            jax.ShapeDtypeStruct((2, width), F32),
-        ],
-        compiler_params=params(),
-        cost_estimate=cost(2 * tokens * width * 3 * width, 26 << 20),
-        name="embed_backward",
-    )(gs1, gj, w, normed, rstd, ci.reshape(pages, 1, length), gains, shifts)
+        ]
+        + more_in,
+        out_specs=out_specs + more_out,
+        out_shape=out_shape + more_shape,
+        scratch_shapes=[pltpu.VMEM(whole_gj, BF)] + more_scratch,
+        compiler_params=params(**more),
+        cost_estimate=cost(70e9, 40 << 20, pages * HEADS * length * length),
+        name="attention_joined_embed_back",
+    )(
+        q, k, v, mixed, go, lse, low, gs1, w, normed, rstd, ci.reshape(pages, 1, length),
+        gains, shifts, *(grads or ()),
+    )
 
 
 def table_kernel(tok, idx, g0, g1, g2, g3, out_a, out_b):
@@ -1092,17 +1150,14 @@
             [(after_low, [gh], [columns(ff // 4)]), (mixed, [gattn], [columns(quarter)])],
             "expand_output_grad",
         )
-    gj, sums_qv, *expand_sum = attn_bwd(q, k, v, mixed, gmixed, lse, pages, parts)
+    embedded_grad, cell_grad, sums0, sums_qv, *more = back(
+        q, k, v, mixed, gmixed, lse, normed_low, gs1, joined_weight, normed, rstd0, cell_index,
+        norm_gains, norm_shifts, parts,
+    )
     if cubic:
-        third = lambda n: pl.BlockSpec(
-            (1, tokens, quarter), lambda s, t: ((3 * s + n) // 4, 0, (3 * s + n) % 4)
-        )
-        parts = rows_part(
-            tok, [(normed_low, [gj, gj, gj], [third(0), third(1), third(2)])], "joined_grad"
-        )
-    embedded_grad, cell_grad, sums0 = embed_bwd(
-        gs1, gj, joined_weight, normed, rstd0, cell_index, norm_gains, norm_shifts
-    )
+        parts, expand_sum = more[:2], more[2:]
+    else:
+        gj = more[0]
 
     small = jnp.concatenate(
         [

time: 435 us -> 420 us (0.966)
  Pallas kernels: 365 us -> 345 us
  local copies, waits for them, and re-layouts: 15.8 us -> 20.8 us
    pallas_call x2 -> x1, Pallas kernels: 29.5 us -> 17.7 us  [rows_part(): pl.pallas_call(functools.partial(rows_kernel, groups=[len(p[1]) for p in...]
    pallas_call x2 -> x1, Pallas kernels: 77.9 us -> 69 us  [back(): pl.pallas_call(functools.partial(back_kernel, pages=pages, summed=summed)...]
    unnamed x28 -> x25, local copies, waits for them, and re-layouts: 4.05 us -> 9.58 us
where the time goes in v4:
time: 420 us; the launch traced here: 414 us
  Pallas kernels  345 us (82%)
  waiting for transfers between devices  33.3 us (8%)
  local copies, waits for them, and re-layouts  20.8 us (5%)
  starting transfers between devices  10.2 us (2%)
    pallas_call x1, Pallas kernels, closing(): pl.pallas_call(closing_kernel, grid=(1,), in_specs=[full(cells.shape), fu...  79.1 us
    pallas_call x1, Pallas kernels, back(): pl.pallas_call(functools.partial(back_kernel, pages=pages, summed=summed)...  69 us
    pallas_call x1, Pallas kernels, ffn_bwd(): pl.pallas_call(functools.partial(ffn_bwd_kernel, summed=grads is not None...  69 us
    pallas_call x1, Pallas kernels, ffn_fwd(): pl.pallas_call(ffn_fwd_kernel, grid=(tokens // tile,), in_specs=[rows, ro...  49.2 us
    ppermute x6, waiting for transfers between devices, shift_tab(): lax.ppermute(value, 'tab', [(i, (i + shift) % size) for i in range(size)])  33.3 us
    pallas_call x1, Pallas kernels, attn_fwd(): pl.pallas_call(attn_fwd_kernel, grid=(pages, steps), in_specs=[blk] * 3,...  20.1 us
    pallas_call x1, Pallas kernels, rows_part(): pl.pallas_call(functools.partial(rows_kernel, groups=[len(p[1]) for p in...  17.7 us
    pallas_call x1, Pallas kernels, reduce_part(): pl.pallas_call(reduce_kernel, grid_spec=pltpu.PrefetchScalarGridSpec(num_...  14.4 us
  transfers between devices with their start and end apart: 6, of which 4 were waited for; matrix products, arithmetic and copies ran while one was open for 1% of the time, Pallas kernels for 0%

profile of v4, /device:TPU:0, one launch (start us, length us, event | category | flops | bytes accessed | tf_op | source)
XLA Modules:
  0.0 413.9 jit_solution(10851292320410294316)
XLA Ops:
  0.7 0.8 fusion
  1.6 5.1 %collective-permute-start.2 = (s32[2,256]{1,0:T(2,128)S(1)}, s32[2,256]{1,0:T(2,128)S(1)}, u32[]{:S(2)}, u32[]{:S(2)}) collective-permute-start(s32[2,256]{1,0:T(2,128)S(1)} %get-tuple-element.124), channel_id=1, source_target_pairs={{0,3},{1,0},{2,1},{3,2},{4,7},{5,4},{6,5},{7,6},{8,11},{9,8},{10,9... | collective-permute-start | bytes 6152 | tf_op jit(solution)/shard_map/ppermute | solution.py:1083
  6.7 0.0 collective-permute-start.1
  6.7 1.0 collective-permute-start
  7.8 3.1 pad.6.table
  10.9 0.0 collective-permute-done.2
  10.9 0.4 collective-permute-done.1
  11.2 0.9 collective-permute-done
  12.1 0.6 pad_add_fusion.1.idx
  12.7 5.6 %lookup.1 = bf16[4,256,1024]{2,1,0:T(8,128)(2,1)} custom-call(s32[4,2,256]{2,1,0:T(2,128)} %pad_add_fusion.1.idx, bf16[1024,1024]{1,0:T(8,128)(2,1)} %pad.6.table), custom_call_target="tpu_custom_call" | custom-call | flops 2147483648 | bytes 2097152 | tf_op jit(solution)/shard_map/lookup/pallas_call | solution.py:100
  18.3 0.0 copy-start.4
  18.3 2.5 slice_bitcast_fusion
  20.8 1.2 collective-permute-start.5
  22.0 0.9 collective-permute-start.4
  22.9 1.9 collective-permute-start.3
  24.9 0.0 copy-done.4
  24.9 0.6 reshape.190.ci.refs_11_
  25.5 12.0 %collective-permute-done.5.t3 = bf16[256,1024]{1,0:T(8,128)(2,1)S(1)} collective-permute-done((bf16[256,1024]{1,0:T(8,128)(2,1)S(1)}, bf16[256,1024]{1,0:T(8,128)(2,1)S(1)}, u32[]{:S(2)}, u32[]{:S(2)}) %collective-permute-start.5) | collective-permute-done | bytes 524320 | tf_op jit(solution)/shard_map/ppermute | solution.py:1083
  37.5 0.0 copy-start.6
  37.5 19.9 %collective-permute-done.4.t2 = bf16[256,1024]{1,0:T(8,128)(2,1)S(1)} collective-permute-done((bf16[256,1024]{1,0:T(8,128)(2,1)S(1)}, bf16[256,1024]{1,0:T(8,128)(2,1)S(1)}, u32[]{:S(2)}, u32[]{:S(2)}) %collective-permute-start.4) | collective-permute-done | bytes 524320 | tf_op jit(solution)/shard_map/ppermute | solution.py:1083
  57.5 0.0 copy-start.7
  57.5 0.0 collective-permute-done.3.t1
  57.5 0.0 copy-start.8
  57.5 0.0 copy-done.6
  57.5 0.8 copy-done.7
  58.3 0.2 copy-done.8
  58.4 14.4 %embed_joined.1 = (bf16[1024,1024]{1,0:T(8,128)(2,1)}, bf16[1024,1024]{1,0:T(8,128)(2,1)}, bf16[1024,1024]{1,0:T(8,128)(2,1)}, f32[1024,1024]{1,0:T(8,128)}, bf1...) custom-call(bf16[1024,1024]{1,0:T(8,128)(2,1)} %emb.1, s32[2,1,512]{2,1,0:T(1,128)} %reshape.190.ci.refs_11_, ...), custom_call_target="tpu_custom_call" | custom-call | flops 6442450944 | bytes 27262976 | tf_op jit(solution)/shard_map/embed_joined/pallas_call | solution.py:142
  72.8 20.1 %attention.1 = (bf16[1024,1024]{1,0:T(8,128)(2,1)}, f32[2,4,4,512]{3,2,1,0:T(4,128)}) custom-call(bf16[1024,1024]{1,0:T(8,128)(2,1)} %get-tuple-element.49.q.refs_0_, bf16[1024,1024]{1,0:T(8,128)(2,1)} %get-tuple-element.50.k.refs_1_, bf16[1024,1024]{1,0:T(8,128)(2,1)} %get-tuple-element.51.v.refs_2_), custom_call_target="tpu_custom_call" | custom-call | flops 14000000000 | bytes 8388608 | tf_op jit(solution)/shard_map/attention/pallas_call | solution.py:319
  92.9 49.2 %ffn_forward.1 = (bf16[1024,1024]{1,0:T(8,128)(2,1)}, f32[1024,1024]{1,0:T(8,128)}, bf16[1024,1024]{1,0:T(8,128)(2,1)}, f32[1024,1]{1,0:T(8,128)}, bf16[1024,409...) custom-call(bf16[1024,1024]{1,0:T(8,128)(2,1)} %get-tuple-element.52, ...), custom_call_target="tpu_custom_call" | custom-call | flops 19327352832 | bytes 62914560 | tf_op jit(solution)/shard_map/ffn_forward/pallas_call | solution.py:415
  142.1 0.7 reshape.195
  142.9 14.4 %reduce_grad.1 = (bf16[2,4,4,256,256]{4,3,2,1,0:T(8,128)(2,1)}, bf16[2,4,4,256,256]{4,3,2,1,0:T(8,128)(2,1)}) custom-call(s32[1]{0:T(128)} %bitcast.20.tok, bf16[1024,1024]{1,0:T(8,128)(2,1)} %get-tuple-element.55.gffn.refs_0_, bf16[1024,4096]{1,0:T(8,128)(2,1)} %get-tuple-element.60.act), custom_call_target="tpu_custom_call" | custom-call | flops 8589934592 | bytes 20971520 | tf_op jit(solution)/shard_map/reduce_grad/pallas_call | solution.py:1004
  157.3 69.0 %ffn_backward.1 = (bf16[1024,4096]{1,0:T(8,128)(2,1)}, f32[1024,1024]{1,0:T(8,128)}, bf16[1024,1024]{1,0:T(8,128)(2,1)}, bf16[1024,1024]{1,0:T(8,128)(2,1)}, f32...) custom-call(bf16[1024,1024]{1,0:T(8,128)(2,1)} %get-tuple-element.55.gffn.refs_0_, ...), custom_call_target="tpu_custom_call" | custom-call | flops 19327352832 | bytes 62914560 | tf_op jit(solution)/shard_map/ffn_backward/pallas_call | solution.py:507
  226.3 0.7 reshape.194
  227.0 17.7 %expand_output_grad.1 = (bf16[2,4,4,64,1280]{4,3,2,1,0:T(8,128)(2,1)}, bf16[2,4,4,64,1280]{4,3,2,1,0:T(8,128)(2,1)}) custom-call(s32[1]{0:T(128)} %bitcast.20.tok, bf16[1024,1024]{1,0:T(8,128)(2,1)} %get-tuple-element.68.refs_0_, bf16[1024,1024]{1,0:T(8,128)(2,1)} %get-tuple-element.52.mixed.refs_1_.refs_3_, bf16[1024,4096]{1,0:T(8,128)(2,1)} %get-tuple-element.69.refs_2_, ...), custom_call_target="tpu_custom_call" | custom-call | flops 10737418240 | bytes 25165824 | tf_op jit(solution)/shard_map/expand_output_grad/pallas_call | solution.py:1062
  244.7 0.0 copy-start.3
  244.7 69.0 %attention_joined_embed_back.1 = (f32[1024,1024]{1,0:T(8,128)}, bf16[256,1024]{1,0:T(8,128)(2,1)}, f32[2,1024]{1,0:T(2,128)}, f32[2,1024]{1,0:T(2,128)}, bf16[2,...) custom-call(bf16[1024,1024]{1,0:T(8,128)(2,1)} %get-tuple-element.49.q.refs_0_, ...), custom_call_target="tpu_custom_call" | custom-call | flops 70000001024 | bytes 41943040 | tf_op jit(solution)/shard_map/attention_joined_embed_back/pallas_call | solution.py:691
  313.7 0.7 bitcast_dynamic-update-slice_fusion.1
  314.4 0.7 bitcast_dynamic-update-slice_fusion
  315.1 0.0 copy-done.3
  315.1 0.0 copy-start.5
  315.1 0.6 copy-done.5
  315.7 0.0 copy-start
  315.7 0.0 copy-start.1
  315.7 79.1 %closing.1 = (bf16[2,2,2,2,2,128,256]{6,5,4,3,2,1,0:T(8,128)(2,1)}, f32[2,64,768]{2,1,0:T(8,128)}, f32[112,128]{1,0:T(8,128)}) custom-call(bf16[256,1024]{1,0:T(8,128)(2,1)} %get-tuple-element.74.cells, s32[4,2,256]{2,1,0:T(2,128)} %pad_add_fusion.1.idx, f32[112,128]{1,0:T(8,128)} %bitcast.90, bf16[2,4,4,64,768]{4,3,2,1,0:T(8,128)(2,1)} %get-tuple-element.80.ga, ...), custom_call_target="tpu_custom_call" | custom-call | flops 2147483648 | bytes 25165824 | tf_op jit(solution)/shard_map/closing/pallas_call | solution.py:930
  394.8 1.3 slice_bitcast_fusion.6
  396.2 0.7 fusion.2
  396.9 0.0 copy-done
  396.9 0.7 slice.149
  397.6 0.8 slice.150
  398.4 0.0 copy-done.1
  398.5 0.1 maximum_bitcast_fusion
  398.5 1.0 copy.24
  399.5 6.7 %table_write.1 = f32[1001,1,1024]{2,1,0:T(1,128)} custom-call(bf16[2,2,2,2,2,128,256]{6,5,4,3,2,1,0:T(8,128)(2,1)} %get-tuple-element.82.a.b, bf16[2,2,2,2,2,128,256]{6,5,4,3,2,1,0:T(8,128)(2,1)} %get-tuple-element.82.a.b), custom_call_target="tpu_custom_call" | custom-call | bytes 6291456 | tf_op jit(solution)/shard_map/table_write/pallas_call | solution.py:967
  406.2 0.6 pad_maximum_fusion.2
  406.8 0.6 pad_maximum_fusion.1
  407.4 0.6 pad_maximum_fusion
  408.1 0.0 copy-start.2
  408.1 4.8 %copy.35 = f32[1024,1024]{1,0:T(8,128)} copy(f32[1024,1024]{1,0:T(8,128)} %get-tuple-element.143) | data formatting | bytes 8388608
  412.9 0.0 copy-done.2
  412.9 0.7 copy.36
  (8 shorter events, 0.1 us)
Async XLA Ops:
  1.6 9.2 %collective-permute-start.2 = (s32[2,256]{1,0:T(2,128)S(1)}, s32[2,256]{1,0:T(2,128)S(1)}, u32[]{:S(2)}, u32[]{:S(2)}) collective-permute-start(s32[2,256]{1,0:T(2,128)S(1)} %get-tuple-element.124), channel_id=1, source_target_pairs={{0,3},{1,0},{2,1},{3,2},{4,7},{5,4},{6,5},{7,6},{8,11},{9,8},{10,9... | collective-permute-start | bytes 6152 | tf_op jit(solution)/shard_map/ppermute | solution.py:1083
  6.7 4.5 %collective-permute-start.1 = (s32[2,256]{1,0:T(2,128)S(1)}, s32[2,256]{1,0:T(2,128)S(1)}, u32[]{:S(2)}, u32[]{:S(2)}) collective-permute-start(s32[2,256]{1,0:T(2,128)S(1)} %get-tuple-element.125), channel_id=1, source_target_pairs={{0,2},{1,3},{2,0},{3,1},{4,6},{5,7},{6,4},{7,5},{8,10},{9,11},{10,... | collective-permute-start | bytes 6152 | tf_op jit(solution)/shard_map/ppermute | solution.py:1083
  6.7 5.4 %collective-permute-start = (s32[2,256]{1,0:T(2,128)S(1)}, s32[2,256]{1,0:T(2,128)S(1)}, u32[]{:S(2)}, u32[]{:S(2)}) collective-permute-start(s32[2,256]{1,0:T(2,128)S(1)} %get-tuple-element.126), channel_id=1, source_target_pairs={{0,1},{1,2},{2,3},{3,0},{4,5},{5,6},{6,7},{7,4},{8,9},{9,10},{10,1... | collective-permute-start | bytes 6152 | tf_op jit(solution)/shard_map/ppermute | solution.py:1083
  18.3 6.5 %copy-start.4 = (s32[2,512]{1,0:T(2,128)S(1)}, s32[2,512]{1,0:T(2,128)}, u32[]{:S(2)}) copy-start(s32[2,512]{1,0:T(2,128)} %param.14) | copy-start | bytes 12292
  20.8 16.7 %collective-permute-start.5 = (bf16[256,1024]{1,0:T(8,128)(2,1)S(1)}, bf16[256,1024]{1,0:T(8,128)(2,1)S(1)}, u32[]{:S(2)}, u32[]{:S(2)}) collective-permute-start(bf16[256,1024]{1,0:T(8,128)(2,1)S(1)} %get-tuple-element.104), channel_id=1, source_target_pairs={{0,1},{1,2},{2,3},{3,0},{4,5},{5,6},{6,7},{7,4},{8,9},{9,10},{10,1... | collective-permute-start | bytes 1572872 | tf_op jit(solution)/shard_map/ppermute | solution.py:1083
  22.0 35.4 %collective-permute-start.4 = (bf16[256,1024]{1,0:T(8,128)(2,1)S(1)}, bf16[256,1024]{1,0:T(8,128)(2,1)S(1)}, u32[]{:S(2)}, u32[]{:S(2)}) collective-permute-start(bf16[256,1024]{1,0:T(8,128)(2,1)S(1)} %get-tuple-element.105), channel_id=1, source_target_pairs={{0,2},{1,3},{2,0},{3,1},{4,6},{5,7},{6,4},{7,5},{8,10},{9,11},{10,... | collective-permute-start | bytes 1572872 | tf_op jit(solution)/shard_map/ppermute | solution.py:1083
  22.9 34.5 %collective-permute-start.3 = (bf16[256,1024]{1,0:T(8,128)(2,1)S(1)}, bf16[256,1024]{1,0:T(8,128)(2,1)S(1)}, u32[]{:S(2)}, u32[]{:S(2)}) collective-permute-start(bf16[256,1024]{1,0:T(8,128)(2,1)S(1)} %get-tuple-element.106), channel_id=1, source_target_pairs={{0,3},{1,0},{2,1},{3,2},{4,7},{5,4},{6,5},{7,6},{8,11},{9,8},{10,9... | collective-permute-start | bytes 1572872 | tf_op jit(solution)/shard_map/ppermute | solution.py:1083
  37.5 20.0 %copy-start.6 = (bf16[256,1024]{1,0:T(8,128)(2,1)}, bf16[256,1024]{1,0:T(8,128)(2,1)S(1)}, u32[]{:S(2)}) copy-start(bf16[256,1024]{1,0:T(8,128)(2,1)S(1)} %collective-permute-done.5.t3) | copy-start | bytes 1572868
  57.5 0.8 copy-start.7
  57.5 1.0 copy-start.8
  244.7 70.4 %copy-start.3 = (f32[1,4096]{1,0:T(1,128)S(1)}, f32[1,4096]{1,0:T(1,128)}, u32[]{:S(2)}) copy-start(f32[1,4096]{1,0:T(1,128)} %get-tuple-element.79) | copy-start | bytes 49156
  315.1 0.6 copy-start.5
  315.7 81.2 %copy-start = (f32[2,64,1280]{2,1,0:T(8,128)S(1)}, f32[2,64,1280]{2,1,0:T(8,128)}, u32[]{:S(2)}) copy-start(f32[2,64,1280]{2,1,0:T(8,128)} %get-tuple-element.84) | copy-start | bytes 1966084
  315.7 82.7 %copy-start.1 = (f32[2,256,256]{2,1,0:T(8,128)S(1)}, f32[2,256,256]{2,1,0:T(8,128)}, u32[]{:S(2)}) copy-start(f32[2,256,256]{2,1,0:T(8,128)} %get-tuple-element.85) | copy-start | bytes 1572868
  408.1 4.8 %copy-start.2 = (f32[2,64,768]{2,1,0:T(8,128)S(1)}, f32[2,64,768]{2,1,0:T(8,128)}, u32[]{:S(2)}) copy-start(f32[2,64,768]{2,1,0:T(8,128)} %get-tuple-element.83) | copy-start | bytes 1179652

commit v5 on v4

--- a/solution.py
+++ b/solution.py
@@ -185,6 +185,9 @@
 class Summing:
     def __init__(self, grads, out, scratch):
         self.grads, self.out = grads, out
+        if grads is None:
+            both, scratch = scratch[0], (scratch[0].at[0], *scratch[1:5], None, *scratch[5:])
+            self.part = both.at[1]
         self.own, self.r0, self.r1, self.r2, self.r3, self.local, self.sent, self.got = scratch
         core, x, y, peers = neighbours()
         self.core, self.first, self.second, self.peers = core, (x, y), (y, x), peers
@@ -196,7 +199,11 @@
     def copy(self, stage, ch, i):
         zc = (self.z + (i + 1)) % 4
         src, dst, to = (
-            (lambda: self.grads[ch].at[1, zc], self.r0.at[ch, i], self.core),
+            (
+                lambda: self.part.at[ch, i] if self.grads is None else self.grads[ch].at[1, zc],
+                self.r0.at[ch, i],
+                self.core,
+            ),
             (lambda: self.own.at[ch, i, pl.ds(2, 2)], self.r1.at[ch, i], self.first[ch]),
             (lambda: self.own.at[ch, i, 1], self.r2.at[ch, i], self.second[ch]),
             (lambda: self.own.at[ch, i, 0], self.r3.at[ch, min(i, 2)], self.peers[min(i, 2)]),
@@ -217,13 +224,15 @@
         for i in range(4):
             for ch in range(2):
                 self.copy(0, ch, i).start()
-                self.load(ch, i).start()
+                if self.grads is not None:
+                    self.load(ch, i).start()
 
     def step(self, stage, i):
         for ch in range(2):
             self.copy(stage - 1, ch, i).wait_recv()
             if stage == 1:
-                self.load(ch, i).wait()
+                if self.grads is not None:
+                    self.load(ch, i).wait()
 
                 def add(j, _, ch=ch):
                     self.own[ch, i, j] = self.own[ch, i, j] + self.r0[ch, i, j]
@@ -266,6 +275,25 @@
                         self.finish()
                     else:
                         self.step(stage, i)
+
+
+def split_rel(r):
+    return r & 1, (r >> 1) & 1, r >> 2
+
+
+def rel_of(b):
+    tok = lax.axis_index("tok")
+    core, x, y = split_rel(b)
+    flip = lambda static, mine: 1 - mine if static else mine
+    return flip(core, tok % 2), flip(x, (tok // 2) % 2), flip(y, tok // 4)
+
+
+def put_rows(g, ga, gb, cols, rows):
+    half = rows // 2
+    for b in range(8):
+        core, x, y = rel_of(b)
+        ga[core, 0, 2 * x + y, :, cols] = g[b * rows : b * rows + half]
+        gb[core, 0, 2 * y + x, :, cols] = g[b * rows + half : (b + 1) * rows]
 
 
 def sum_specs(grads, number):
@@ -430,34 +458,30 @@
     )(mixed, normed, wo, we, wr, hb, bias, gains, shifts, cot)
 
 
-FFN_PLAN = {
-    0: [(0, 0)],
-    1: [(1, 0)],
-    2: [(1, 1)],
-    3: [(2, 0), (1, 2)],
-    4: [(2, 1), (1, 3)],
-    5: [(3, 0)],
-    7: [(2, 2), (3, 1)],
-}
-FFN_TAIL = [(2, 3), (3, 2), (3, 3), (4, 0)]
-
-
-def ffn_bwd_kernel(*refs, summed):
-    gffn, gs2, after, rstd, wo, gains, shifts, slope, wr, we = refs[:10]
-    refs = refs[10:]
-    grads, refs = refs[: 2 * summed], refs[2 * summed :]
-    gh_out, gs1_out, gattn_out, gmixed_out, hsum, sums = refs[:6]
-    refs = refs[6:]
+def second_norm_back(gs1_out, after, rstd, gains, shifts, gattn_out, sums):
+    tokens, width = after.shape
+
+    def norm(i, carry):
+        rows = pl.ds(pl.multiple_of(i * RC, RC), RC)
+        total = gs1_out[rows, :]
+        xh = (after[rows, :] - shifts[1:2]) * (1.0 / gains[1:2])
+        gs1 = norm_back(total, xh, rstd[rows, :], gains[1:2])
+        gs1_out[rows, :] = gs1
+        gattn = gs1.astype(BF)
+        gattn_out[rows, :] = gattn
+        g, s, b = carry
+        return g + colsum(total * xh), s + colsum(total), b + colsum(gattn.astype(F32))
+
+    zero = jnp.zeros((1, width), F32)
+    sums[...] = jnp.concatenate(lax.fori_loop(0, tokens // RC, norm, (zero, zero, zero)), axis=0)
+
+
+def ffn_bwd_kernel(
+    gffn, gs2, after, rstd, wo, gains, shifts, slope, wr, we,
+    gh_out, gs1_out, gattn_out, gmixed_out, hsum, sums,
+):
     step, last = pl.program_id(0), pl.num_programs(0) - 1
     tokens, width = gffn.shape
-    if summed:
-        summing = Summing(grads, refs[0], refs[1:])
-
-        @pl.when(step == 0)
-        def _():
-            meet(summing.devices())
-
-        summing.run(step, FFN_PLAN)
 
     @pl.when(step == 0)
     def _():
@@ -474,38 +498,20 @@
 
     @pl.when(step == last)
     def _():
-        def norm(i, carry):
-            rows = pl.ds(pl.multiple_of(i * RC, RC), RC)
-            total = gs1_out[rows, :]
-            xh = (after[rows, :] - shifts[1:2]) * (1.0 / gains[1:2])
-            gs1 = norm_back(total, xh, rstd[rows, :], gains[1:2])
-            gs1_out[rows, :] = gs1
-            gattn = gs1.astype(BF)
-            gattn_out[rows, :] = gattn
-            g, s, b = carry
-            return g + colsum(total * xh), s + colsum(total), b + colsum(gattn.astype(F32))
-
-        zero = jnp.zeros((1, width), F32)
-        sums[...] = jnp.concatenate(
-            lax.fori_loop(0, tokens // RC, norm, (zero, zero, zero)), axis=0
-        )
+        second_norm_back(gs1_out, after, rstd, gains, shifts, gattn_out, sums)
         for m in range(0, tokens, MC):
             rows = slice(m, m + MC)
             gmixed_out[rows, :] = dot(gattn_out[rows, :], wo[...], NT).astype(BF)
 
-    if summed:
-        summing.run(step, {last: FFN_TAIL})
-
-
-def ffn_bwd(gffn, slope, gs2, after, rstd, wr, we, wo, gains, shifts, grads):
+
+def ffn_bwd(gffn, slope, gs2, after, rstd, wr, we, wo, gains, shifts):
     tokens, width = gffn.shape
     ff = we.shape[1]
     whole = full((tokens, width))
     long = pl.BlockSpec((tokens, FC), lambda s: (0, s))
     shape = lambda dt, n=width: jax.ShapeDtypeStruct((tokens, n), dt)
-    more_in, more_out, more_shape, more_scratch, more = sum_specs(grads, 1)
     return pl.pallas_call(
-        functools.partial(ffn_bwd_kernel, summed=grads is not None),
+        ffn_bwd_kernel,
         grid=(ff // FC,),
         in_specs=[whole, whole, whole, full((tokens, 1))]
         + [full(a.shape) for a in (wo, gains, shifts)]
@@ -513,21 +519,167 @@
             long,
             pl.BlockSpec((FC, width), lambda s: (s, 0)),
             pl.BlockSpec((width, FC), lambda s: (0, s)),
-        ]
-        + more_in,
+        ],
         out_specs=[long, whole, whole, whole]
-        + [pl.BlockSpec((1, FC), lambda s: (0, s)), full((3, width))]
-        + more_out,
+        + [pl.BlockSpec((1, FC), lambda s: (0, s)), full((3, width))],
         out_shape=[
             shape(BF, ff), shape(F32), shape(BF), shape(BF),
             jax.ShapeDtypeStruct((1, ff), F32), jax.ShapeDtypeStruct((3, width), F32),
-        ]
-        + more_shape,
-        scratch_shapes=more_scratch,
-        compiler_params=params(**more),
+        ],
+        compiler_params=params(),
         cost_estimate=cost(2 * tokens * width * (width + 2 * ff), 60 << 20),
         name="ffn_backward",
-    )(gffn, gs2, after, rstd, wo, gains, shifts, slope, wr, we, *(grads or ()))
+    )(gffn, gs2, after, rstd, wo, gains, shifts, slope, wr, we)
+
+
+FFN_PLAN = {
+    4: [(0, 0)],
+    8: [(1, 0), (1, 1)],
+    10: [(2, 0), (1, 2)],
+    11: [(2, 1), (1, 3)],
+    12: [(3, 0)],
+    13: [(2, 2)],
+    14: [(3, 1)],
+    15: [(2, 3)],
+    16: [(3, 2)],
+    17: [(3, 3)],
+}
+N_TOK, N_TAB = 8, 4
+
+
+def block_of_step(s):
+    s = jnp.minimum(s, N_TOK - 1)
+    return 1 - s // 4, 1 - (s // 2) % 2, 1 - s % 2
+
+
+def ffn_grads_kernel(
+    gffn_in, gs2_in, after, rstd, low, mixed, wo, gains, shifts, act, slope, wr, we,
+    gs1_out, gmixed_out, hsum, sums, ga, gb, reduce_out,
+    gffn, gh, local, *scratch,
+):
+    step, last = pl.program_id(0), pl.num_programs(0) - 1
+    tokens, width = after.shape
+    summing = Summing(None, reduce_out, scratch)
+    both = scratch[0]
+    z = lax.axis_index("tab")
+    first = pltpu.make_async_copy(gffn_in, gffn, local.at[0])
+    later = pltpu.make_async_copy(gs2_in, gs1_out, local.at[1])
+
+    @pl.when(step == 0)
+    def _():
+        first.start()
+        later.start()
+        meet(summing.devices())
+        first.wait()
+
+    @pl.when(step == N_TOK)
+    def _():
+        later.wait()
+
+    summing.run(step, FFN_PLAN)
+
+    @pl.when(step < N_TOK)
+    def _():
+        core, x, y = block_of_step(step)
+        g = dot(gffn[...], act[...], TN).astype(BF)
+        rows, half = both.shape[4:]
+        for zc in range(N_TAB):
+            i = (zc + N_TAB - 1 - z) % N_TAB
+            for ch in range(2):
+                piece = g[zc * rows : (zc + 1) * rows, ch * half : (ch + 1) * half]
+                both[core, ch, i, (2 * x + y, 2 * y + x)[ch]] = piece
+
+    @pl.when((step >= N_TOK) & (step < 2 * N_TOK))
+    def _():
+        part = jnp.zeros((1, slope.shape[1]), F32)
+        for m in range(0, tokens, MC):
+            rows = slice(m, m + MC)
+            g = (dot(gffn[rows, :], wr[...], NT) * slope[rows, :].astype(F32)).astype(BF)
+            gh[step - N_TOK, rows, :] = g
+            part = part + colsum(g.astype(F32))
+            gs1_out[rows, :] = gs1_out[rows, :] + dot(g, we[...], NT)
+        hsum[...] = part
+
+    @pl.when(step == 2 * N_TOK - 1)
+    def _():
+        second_norm_back(gs1_out, after, rstd, gains, shifts, gffn, sums)
+        for m in range(0, tokens, MC):
+            rows = slice(m, m + MC)
+            gmixed_out[rows, :] = dot(gffn[rows, :], wo[...], NT).astype(BF)
+
+    @pl.when(step >= 2 * N_TOK)
+    def _():
+        n = step - 2 * N_TOK
+        quarter = width // N_TAB
+        rows = width // N_TOK
+        wide = gh.shape[2]
+        for m in range(2):
+            g = dot(low[...], gh[2 * n + m], TN).astype(BF)
+            put_rows(g, ga, gb, slice(m * wide, (m + 1) * wide), rows)
+        piece = gffn[:, pl.ds(pl.multiple_of(n * quarter, quarter), quarter)]
+        g = dot(mixed[...], piece, TN).astype(BF)
+        put_rows(g, ga, gb, slice(2 * wide, 2 * wide + quarter), rows)
+
+    @pl.when(step == last)
+    def _():
+        summing.finish()
+
+
+def ffn_grads(gffn, act, slope, gs2, after, low, rstd, mixed, wr, we, wo, gains, shifts):
+    tokens, width = gffn.shape
+    ff = we.shape[1]
+    whole = full((tokens, width))
+    anywhere = pl.BlockSpec(memory_space=pl.ANY)
+    wide = ff // N_TOK
+    half = width // (2 * N_TOK)
+    out_wide = (ff + width) // N_TAB
+    back = lambda s: jnp.clip(s - N_TOK, 0, N_TOK - 1)
+    grad = lambda s: jnp.clip(s - 2 * N_TOK, 0, N_TAB - 1)
+
+    def act_block(s):
+        core, x, y = block_of_step(s)
+        tok = lax.axis_index("tok")
+        flip = lambda rel, mine: rel + mine - 2 * rel * mine
+        return 0, 4 * flip(y, tok // 4) + 2 * flip(x, (tok // 2) % 2) + flip(core, tok % 2)
+
+    rows, cols = width // N_TAB, wide // 2
+    part = lambda *n: pltpu.VMEM((*n, rows, cols), BF)
+    dma = pltpu.SemaphoreType.DMA
+    shape = lambda dt: jax.ShapeDtypeStruct((tokens, width), dt)
+    piece = pl.BlockSpec((2, 1, 4, half, out_wide), lambda s: (0, grad(s), 0, 0, 0))
+    return pl.pallas_call(
+        ffn_grads_kernel,
+        grid=(2 * N_TOK + N_TAB,),
+        in_specs=[anywhere, anywhere, whole, full((tokens, 1)), whole, whole]
+        + [full(a.shape) for a in (wo, gains, shifts)]
+        + [
+            pl.BlockSpec((tokens, wide), act_block),
+            pl.BlockSpec((tokens, wide), lambda s: (0, back(s))),
+            pl.BlockSpec((wide, width), lambda s: (back(s), 0)),
+            pl.BlockSpec((width, wide), lambda s: (0, back(s))),
+        ],
+        out_specs=[
+            whole, whole, pl.BlockSpec((1, wide), lambda s: (0, back(s))), full((3, width)),
+            piece, piece, full((2, rows, cols)),
+        ],
+        out_shape=[
+            shape(F32), shape(BF),
+            jax.ShapeDtypeStruct((1, ff), F32), jax.ShapeDtypeStruct((3, width), F32),
+            jax.ShapeDtypeStruct((2, 4, 4, half, out_wide), BF),
+            jax.ShapeDtypeStruct((2, 4, 4, half, out_wide), BF),
+            jax.ShapeDtypeStruct((2, rows, cols), F32),
+        ],
+        scratch_shapes=[
+            pltpu.VMEM((tokens, width), BF), pltpu.VMEM((N_TOK, tokens, wide), BF), dma((2,)),
+            part(2, 2, 4, 4), part(2, 4, 4), part(2, 4, 2), part(2, 4), part(2, 3),
+            dma((STAGES, 2, 4)), dma((STAGES, 2, 4)),
+        ],
+        compiler_params=pltpu.CompilerParams(
+            vmem_limit_bytes=67043328, has_side_effects=True, collective_id=1
+        ),
+        cost_estimate=cost(2 * tokens * width * (2 * width + 4 * ff), 60 << 20),
+        name="ffn_backward_grads",
+    )(gffn, gs2, after, rstd, low, mixed, wo, gains, shifts, act, slope, wr, we)
 
 
 BACK_PLAN = {
@@ -543,21 +695,6 @@
     12: [(3, 2)],
     13: [(3, 3)],
 }
-
-
-def rel_of(b):
-    tok = lax.axis_index("tok")
-    core, x, y = split_rel(b)
-    flip = lambda static, mine: 1 - mine if static else mine
-    return flip(core, tok % 2), flip(x, (tok // 2) % 2), flip(y, tok // 4)
-
-
-def put_rows(g, ga, gb, cols, rows):
-    half = rows // 2
-    for b in range(8):
-        core, x, y = rel_of(b)
-        ga[core, 0, 2 * x + y, :, cols] = g[b * rows : b * rows + half]
-        gb[core, 0, 2 * y + x, :, cols] = g[b * rows + half : (b + 1) * rows]
 
 
 def back_kernel(*refs, pages, summed):
@@ -824,13 +961,13 @@
     hops = [core, x, y, {"tab": z + 1 - 2 * (z % 2)}, {"tab": z + 2 - 4 * (z // 2)}]
     meet([core, x, y, *peers])
     count = cells.shape[0]
-    half = count // 2
+    half = cells.shape[1] // 2
 
     def pass_on(k, h):
-        rows = pl.ds(h * half, half)
-        src = cells.at[rows] if k == 0 else ring.at[k - 1, rows]
+        cols = pl.ds(h * half, half)
+        src = cells.at[:, cols] if k == 0 else ring.at[k - 1, :, cols]
         return pltpu.make_async_remote_copy(
-            src_ref=src, dst_ref=ring.at[k, rows],
+            src_ref=src, dst_ref=ring.at[k, :, cols],
             send_sem=ring_sent.at[k, h], recv_sem=ring_got.at[k, h],
             device_id=peers[0], device_id_type=pl.DeviceIdType.MESH,
         )
@@ -860,6 +997,13 @@
         first = (number == idx[s, 0:1, :]).astype(F32)
         second = (number == idx[s, 1:2, :]).astype(F32)
         return (first + second).astype(BF)
+
+    def last_arrival(u):
+        pass_on(2, u).wait_recv()
+        for ch in range(2):
+            cols = slice((2 * u + ch) * half // 2, (2 * u + ch + 1) * half // 2)
+            value = total[:, cols] + dot(last, ring[2, :, cols], NN)
+            table.store(u, ch, value.astype(BF))
 
     pass_on(0, 0).start()
     pass_on(0, 1).start()
@@ -871,10 +1015,10 @@
     summing.step(1, 0)
     small_step(2)
     summing.step(1, 1)
-    small_step(3)
     relay(1, 0)
     summing.step(2, 0)
     summing.step(1, 2)
+    small_step(3)
     relay(1, 1)
     total[...] = total[...] + dot(pick(1), ring[0], NN)
     summing.step(2, 1)
@@ -885,32 +1029,26 @@
     relay(2, 1)
     summing.step(3, 0)
     summing.step(3, 1)
+    summing.step(2, 3)
     total[...] = total[...] + dot(pick(2), ring[1], NN)
-    summing.step(2, 3)
+    last = pick(3)
+    last_arrival(0)
+    table.step(1, 0)
+    last_arrival(1)
     summing.step(3, 2)
     small_step(5)
-    last = pick(3)
-    pass_on(2, 0).wait_recv()
-    pass_on(2, 1).wait_recv()
-    wide = total.shape[1] // 4
-    for u in range(2):
-        for ch in range(2):
-            cols = slice((2 * ch + u) * wide, (2 * ch + u + 1) * wide)
-            value = total[:, cols] + dot(last, ring[2, :, cols], NN)
-            table.store(u, ch, value.astype(BF))
+    table.step(2, 0)
+    table.step(1, 1)
+    table.step(3, 0)
+    table.step(2, 1)
+    table.step(4, 0)
+    table.step(3, 1)
+    table.step(5, 0)
+    table.step(4, 1)
+    table.step(6, 0)
+    table.step(5, 1)
     summing.step(3, 3)
-    table.step(1, 0)
-    table.step(1, 1)
-    table.step(2, 0)
-    table.step(2, 1)
-    table.step(3, 0)
-    table.step(3, 1)
-    table.step(4, 0)
-    table.step(4, 1)
     summing.finish()
-    table.step(5, 0)
-    table.step(5, 1)
-    table.step(6, 0)
     table.step(6, 1)
     table.finish()
     for k in range(3):
@@ -955,7 +1093,7 @@
     wide = a.shape[6]
     for n, piece in enumerate((a, b)):
         for u in range(2):
-            at = (2 * n + u) * wide
+            at = (2 * u + n) * wide
             out[:, 0, at : at + wide] = piece[0, u, 0, 0, 0].astype(F32)
 
 
@@ -975,104 +1113,6 @@
         name="table_write",
     )(done, done)
     return out.transpose(1, 0, 2)
-
-
-def split_rel(r):
-    return r & 1, (r >> 1) & 1, r >> 2
-
-
-def reduce_kernel(tok, gffn, act, ga, gb):
-    g = dot(gffn[...], act[...], TN)
-    half = ga.shape[4]
-    ga[0, :, 0] = g[:, :half].astype(BF).reshape(ga.shape[1], *ga.shape[3:])
-    gb[0, :, 0] = g[:, half:].astype(BF).reshape(gb.shape[1], *gb.shape[3:])
-
-
-def reduce_part(tok, gffn, act):
-    tokens, d = gffn.shape
-    f = act.shape[1] // 8
-    rows, half = d // 4, f // 2
-
-    def index(ch):
-        def at(s, t):
-            core, x, y = split_rel(7 - s)
-            return (core, 0, 2 * y + x if ch else 2 * x + y, 0, 0)
-
-        return at
-
-    shape = jax.ShapeDtypeStruct((2, 4, 4, rows, half), BF)
-    return pl.pallas_call(
-        reduce_kernel,
-        grid_spec=pltpu.PrefetchScalarGridSpec(
-            num_scalar_prefetch=1,
-            grid=(8,),
-            in_specs=[
-                full(gffn.shape),
-                pl.BlockSpec((tokens, f), lambda s, t: (0, t[0] ^ (7 - s))),
-            ],
-            out_specs=[pl.BlockSpec((1, 4, 1, rows, half), index(ch)) for ch in range(2)],
-        ),
-        out_shape=[shape, shape],
-        compiler_params=params(),
-        cost_estimate=cost(16 * tokens * d * f, 20 << 20),
-        name="reduce_grad",
-    )(tok, gffn, act)
-
-
-def rows_kernel(tok, *refs, groups):
-    count = len(groups)
-    lhs, refs = refs[:count], refs[count:]
-    rhs = []
-    for n in groups:
-        rhs.append(refs[:n])
-        refs = refs[n:]
-    ga, gb = refs[:2]
-    turned = refs[2:]
-    rows = lhs[0].shape[1] // 8
-    half = rows // 2
-
-    @pl.when(pl.program_id(0) == 0)
-    def _():
-        for a, b in zip(lhs, turned):
-            for r in range(8):
-                start = pl.multiple_of((tok[0] ^ r) * rows, rows)
-                b[:, r * rows : (r + 1) * rows] = a[:, pl.ds(start, rows)]
-
-    at = 0
-    for a, blocks in zip(turned, rhs):
-        for block in blocks:
-            block = block[...].reshape(block.shape[-2:])
-            for n in range(0, block.shape[1], 512):
-                piece = block[:, n : n + 512]
-                g = dot(a[...], piece, TN).astype(BF)
-                cols = slice(at, at + piece.shape[1])
-                at += piece.shape[1]
-                for r in range(8):
-                    core, x, y = split_rel(r)
-                    ga[core, 0, 2 * x + y, :, cols] = g[r * rows : r * rows + half]
-                    gb[core, 0, 2 * y + x, :, cols] = g[r * rows + half : (r + 1) * rows]
-
-
-def rows_part(tok, pairs, name):
-    tokens, d = pairs[0][0].shape
-    half = d // 16
-    width = sum(spec.block_shape[-1] for _, _, specs in pairs for spec in specs)
-    shape = jax.ShapeDtypeStruct((2, 4, 4, half, width), BF)
-    out = pl.BlockSpec((2, 1, 4, half, width), lambda s, t: (0, s, 0, 0, 0))
-    return pl.pallas_call(
-        functools.partial(rows_kernel, groups=[len(p[1]) for p in pairs]),
-        grid_spec=pltpu.PrefetchScalarGridSpec(
-            num_scalar_prefetch=1,
-            grid=(4,),
-            in_specs=[full(p[0].shape) for p in pairs] + [s for p in pairs for s in p[2]],
-            out_specs=[out, out],
-            scratch_shapes=[pltpu.VMEM((tokens, d), BF) for _ in pairs],
-        ),
-        out_shape=[shape, shape],
-        compiler_params=params(),
-        cost_estimate=cost(8 * tokens * d * width, 24 << 20),
-        name=name,
-    )(tok, *[p[0] for p in pairs], *[r for p in pairs for r in p[1]])
 
 
 def flip_tok(value, bit, size):
@@ -1137,18 +1177,16 @@
         mixed, normed, output_weight, expand_weight, reduce_weight, hidden_bias,
         bias_rows, norm_gains, norm_shifts, cotangent, min(256, tokens),
     )
-    quarter = width // 4
-    parts = reduce_part(tok, gffn, act) if cubic else None
-    gh, gs1, gattn, gmixed, hidden_sum, sums1, *reduce_sum = ffn_bwd(
-        gffn, slope, gs2, after, rstd1, reduce_weight, expand_weight, output_weight,
-        norm_gains, norm_shifts, parts,
-    )
     if cubic:
-        columns = lambda n: pl.BlockSpec((tokens, n), lambda s, t: (0, s))
-        parts = rows_part(
-            tok,
-            [(after_low, [gh], [columns(ff // 4)]), (mixed, [gattn], [columns(quarter)])],
-            "expand_output_grad",
+        gs1, gmixed, hidden_sum, sums1, *parts, reduce_sum = ffn_grads(
+            gffn, act, slope, gs2, after, after_low, rstd1, mixed, reduce_weight, expand_weight,
+            output_weight, norm_gains, norm_shifts,
+        )
+    else:
+        parts = None
+        gh, gs1, gattn, gmixed, hidden_sum, sums1 = ffn_bwd(
+            gffn, slope, gs2, after, rstd1, reduce_weight, expand_weight, output_weight,
+            norm_gains, norm_shifts,
         )
     embedded_grad, cell_grad, sums0, sums_qv, *more = back(
         q, k, v, mixed, gmixed, lse, normed_low, gs1, joined_weight, normed, rstd0, cell_index,
@@ -1182,7 +1220,7 @@
     hidden_bias_grad = small[10 * width :]
 
     if cubic:
-        reduce_grad = jnp.concatenate([reduce_sum[0][0], reduce_sum[0][1]], axis=1).T
+        reduce_grad = jnp.concatenate([reduce_sum[0], reduce_sum[1]], axis=1).T
         expand_sum = expand_sum[0].reshape(-1, expand_sum[0].shape[2])
         expand_grad = expand_sum[:, : ff // 4]
         output_grad = expand_sum[:, ff // 4 :]

time: 420 us -> 402 us (0.957)
  Pallas kernels: 345 us -> 327 us
    pallas_call x3 -> x1, Pallas kernels: 101 us -> 87.5 us  [ffn_grads(): pl.pallas_call(ffn_grads_kernel, grid=(2 * N_TOK + N_TAB,), in_specs=[any...]
    pallas_call x1, Pallas kernels: 79.1 us -> 74.6 us  [closing(): pl.pallas_call(closing_kernel, grid=(1,), in_specs=[full(cells.shape), fu...]
    unnamed x25 -> x27, local copies, waits for them, and re-layouts: 9.58 us -> 9.59 us
where the time goes in v5:
time: 402 us; the launch traced here: 396 us
  Pallas kernels  327 us (81%)
  waiting for transfers between devices  33.3 us (8%)
  local copies, waits for them, and re-layouts  21.5 us (5%)
  starting transfers between devices  10.2 us (3%)
    pallas_call x1, Pallas kernels, ffn_grads(): pl.pallas_call(ffn_grads_kernel, grid=(2 * N_TOK + N_TAB,), in_specs=[any...  87.5 us
    pallas_call x1, Pallas kernels, closing(): pl.pallas_call(closing_kernel, grid=(1,), in_specs=[full(cells.shape), fu...  74.6 us
    pallas_call x1, Pallas kernels, back(): pl.pallas_call(functools.partial(back_kernel, pages=pages, summed=summed)...  68.5 us
    pallas_call x1, Pallas kernels, ffn_fwd(): pl.pallas_call(ffn_fwd_kernel, grid=(tokens // tile,), in_specs=[rows, ro...  49.3 us
    ppermute x6, waiting for transfers between devices, shift_tab(): lax.ppermute(value, 'tab', [(i, (i + shift) % size) for i in range(size)])  33.3 us
    pallas_call x1, Pallas kernels, attn_fwd(): pl.pallas_call(attn_fwd_kernel, grid=(pages, steps), in_specs=[blk] * 3,...  20 us
    pallas_call x1, Pallas kernels, embed(): pl.pallas_call(embed_kernel, grid=(pages,), in_specs=[rows, pl.BlockSpec(...  14.4 us
    ppermute x6, starting transfers between devices, shift_tab(): lax.ppermute(value, 'tab', [(i, (i + shift) % size) for i in range(size)])  10.2 us
  transfers between devices with their start and end apart: 6, of which 4 were waited for; matrix products, arithmetic and copies ran while one was open for 1% of the time, Pallas kernels for 0%

profile of v5, /device:TPU:0, one launch (start us, length us, event | category | flops | bytes accessed | tf_op | source)
XLA Modules:
  0.0 396.0 jit_solution(10617650505527080452)
XLA Ops:
  0.7 0.8 fusion
  1.6 5.1 %collective-permute-start.2 = (s32[2,256]{1,0:T(2,128)S(1)}, s32[2,256]{1,0:T(2,128)S(1)}, u32[]{:S(2)}, u32[]{:S(2)}) collective-permute-start(s32[2,256]{1,0:T(2,128)S(1)} %get-tuple-element.116), channel_id=1, source_target_pairs={{0,3},{1,0},{2,1},{3,2},{4,7},{5,4},{6,5},{7,6},{8,11},{9,8},{10,9... | collective-permute-start | bytes 6152 | tf_op jit(solution)/shard_map/ppermute | solution.py:1123
  6.7 0.0 collective-permute-start.1
  6.8 1.0 collective-permute-start
  7.8 3.1 pad.6.table
  10.9 0.0 collective-permute-done.2
  10.9 0.4 collective-permute-done.1
  11.2 0.9 collective-permute-done
  12.1 0.6 pad_add_fusion.1.idx
  12.7 5.6 %lookup.1 = bf16[4,256,1024]{2,1,0:T(8,128)(2,1)} custom-call(s32[4,2,256]{2,1,0:T(2,128)} %pad_add_fusion.1.idx, bf16[1024,1024]{1,0:T(8,128)(2,1)} %pad.6.table), custom_call_target="tpu_custom_call" | custom-call | flops 2147483648 | bytes 2097152 | tf_op jit(solution)/shard_map/lookup/pallas_call | solution.py:100
  18.3 0.0 copy-start.5
  18.3 2.5 slice_bitcast_fusion
  20.9 1.2 collective-permute-start.5
  22.1 0.9 collective-permute-start.4
  23.0 1.9 collective-permute-start.3
  24.9 0.0 copy-done.5
  24.9 0.6 reshape.187.ci.refs_11_
  25.5 12.0 %collective-permute-done.5.t3 = bf16[256,1024]{1,0:T(8,128)(2,1)S(1)} collective-permute-done((bf16[256,1024]{1,0:T(8,128)(2,1)S(1)}, bf16[256,1024]{1,0:T(8,128)(2,1)S(1)}, u32[]{:S(2)}, u32[]{:S(2)}) %collective-permute-start.5) | collective-permute-done | bytes 524320 | tf_op jit(solution)/shard_map/ppermute | solution.py:1123
  37.6 0.0 copy-start.7
  37.6 19.9 %collective-permute-done.4.t2 = bf16[256,1024]{1,0:T(8,128)(2,1)S(1)} collective-permute-done((bf16[256,1024]{1,0:T(8,128)(2,1)S(1)}, bf16[256,1024]{1,0:T(8,128)(2,1)S(1)}, u32[]{:S(2)}, u32[]{:S(2)}) %collective-permute-start.4) | collective-permute-done | bytes 524320 | tf_op jit(solution)/shard_map/ppermute | solution.py:1123
  57.5 0.0 copy-start.8
  57.5 0.0 collective-permute-done.3.t1
  57.5 0.0 copy-start.9
  57.5 0.0 copy-done.7
  57.5 0.8 copy-done.8
  58.3 0.2 copy-done.9
  58.5 14.4 %embed_joined.1 = (bf16[1024,1024]{1,0:T(8,128)(2,1)}, bf16[1024,1024]{1,0:T(8,128)(2,1)}, bf16[1024,1024]{1,0:T(8,128)(2,1)}, f32[1024,1024]{1,0:T(8,128)}, bf1...) custom-call(bf16[1024,1024]{1,0:T(8,128)(2,1)} %emb.1, s32[2,1,512]{2,1,0:T(1,128)} %reshape.187.ci.refs_11_, ...), custom_call_target="tpu_custom_call" | custom-call | flops 6442450944 | bytes 27262976 | tf_op jit(solution)/shard_map/embed_joined/pallas_call | solution.py:142
  72.9 20.0 %attention.1 = (bf16[1024,1024]{1,0:T(8,128)(2,1)}, f32[2,4,4,512]{3,2,1,0:T(4,128)}) custom-call(bf16[1024,1024]{1,0:T(8,128)(2,1)} %get-tuple-element.45.q.refs_0_, bf16[1024,1024]{1,0:T(8,128)(2,1)} %get-tuple-element.46.k.refs_1_, bf16[1024,1024]{1,0:T(8,128)(2,1)} %get-tuple-element.47.v.refs_2_), custom_call_target="tpu_custom_call" | custom-call | flops 14000000000 | bytes 8388608 | tf_op jit(solution)/shard_map/attention/pallas_call | solution.py:347
  92.9 49.3 %ffn_forward.1 = (bf16[1024,1024]{1,0:T(8,128)(2,1)}, f32[1024,1024]{1,0:T(8,128)}, bf16[1024,1024]{1,0:T(8,128)(2,1)}, f32[1024,1]{1,0:T(8,128)}, bf16[1024,409...) custom-call(bf16[1024,1024]{1,0:T(8,128)(2,1)} %get-tuple-element.48, ...), custom_call_target="tpu_custom_call" | custom-call | flops 19327352832 | bytes 62914560 | tf_op jit(solution)/shard_map/ffn_forward/pallas_call | solution.py:443
  142.2 1.3 reshape.191
  143.5 87.5 %ffn_backward_grads.1 = (f32[1024,1024]{1,0:T(8,128)}, bf16[1024,1024]{1,0:T(8,128)(2,1)}, f32[1,4096]{1,0:T(1,128)}, f32[3,1024]{1,0:T(4,128)}, bf16[2,4,4,64,1...) custom-call(bf16[1024,1024]{1,0:T(8,128)(2,1)} %get-tuple-element.51.gffn_in, ...), custom_call_target="tpu_custom_call" | custom-call | flops 38654705664 | bytes 62914560 | tf_op jit(solution)/shard_map/ffn_backward_grads/pallas_call | solution.py:650
  231.0 0.7 reshape.190
  231.8 0.0 copy-start.3
  231.8 0.0 copy-start.4
  231.8 68.5 %attention_joined_embed_back.1 = (f32[1024,1024]{1,0:T(8,128)}, bf16[256,1024]{1,0:T(8,128)(2,1)}, f32[2,1024]{1,0:T(2,128)}, f32[2,1024]{1,0:T(2,128)}, bf16[2,...) custom-call(bf16[1024,1024]{1,0:T(8,128)(2,1)} %get-tuple-element.45.q.refs_0_, ...), custom_call_target="tpu_custom_call" | custom-call | flops 70000001024 | bytes 41943040 | tf_op jit(solution)/shard_map/attention_joined_embed_back/pallas_call | solution.py:828
  300.3 0.7 bitcast_dynamic-update-slice_fusion.1
  301.0 0.0 copy-done.3
  301.0 0.7 bitcast_dynamic-update-slice_fusion
  301.7 0.0 copy-done.4
  301.7 0.0 copy-start.6
  301.7 0.6 copy-done.6
  302.3 0.0 copy-start
  302.3 0.0 copy-start.1
  302.4 74.6 %closing.1 = (bf16[2,2,2,2,2,128,256]{6,5,4,3,2,1,0:T(8,128)(2,1)}, f32[2,64,768]{2,1,0:T(8,128)}, f32[112,128]{1,0:T(8,128)}) custom-call(bf16[256,1024]{1,0:T(8,128)(2,1)} %get-tuple-element.66.cells, s32[4,2,256]{2,1,0:T(2,128)} %pad_add_fusion.1.idx, f32[112,128]{1,0:T(8,128)} %bitcast.89, bf16[2,4,4,64,768]{4,3,2,1,0:T(8,128)(2,1)} %get-tuple-element.72.ga, ...), custom_call_target="tpu_custom_call" | custom-call | flops 2147483648 | bytes 25165824 | tf_op jit(solution)/shard_map/closing/pallas_call | solution.py:1068
  376.9 1.3 slice_bitcast_fusion.6
  378.3 0.7 fusion.2
  379.0 0.0 copy-done
  379.0 0.7 slice.149
  379.6 0.8 slice.150
  380.5 0.0 copy-done.1
  380.5 0.1 maximum_bitcast_fusion
  380.6 1.0 copy.24
  381.6 6.7 %table_write.1 = f32[1001,1,1024]{2,1,0:T(1,128)} custom-call(bf16[2,2,2,2,2,128,256]{6,5,4,3,2,1,0:T(8,128)(2,1)} %get-tuple-element.74.a.b, bf16[2,2,2,2,2,128,256]{6,5,4,3,2,1,0:T(8,128)(2,1)} %get-tuple-element.74.a.b), custom_call_target="tpu_custom_call" | custom-call | bytes 6291456 | tf_op jit(solution)/shard_map/table_write/pallas_call | solution.py:1105
  388.3 0.6 pad_maximum_fusion.2
  388.9 0.6 pad_maximum_fusion.1
  389.5 0.6 pad_maximum_fusion
  390.1 0.0 copy-start.2
  390.2 4.8 %copy.35 = f32[1024,1024]{1,0:T(8,128)} copy(f32[1024,1024]{1,0:T(8,128)} %get-tuple-element.135) | data formatting | bytes 8388608
  395.0 0.0 copy-done.2
  395.0 0.7 copy.36
  (8 shorter events, 0.1 us)
Async XLA Ops:
  1.6 9.2 %collective-permute-start.2 = (s32[2,256]{1,0:T(2,128)S(1)}, s32[2,256]{1,0:T(2,128)S(1)}, u32[]{:S(2)}, u32[]{:S(2)}) collective-permute-start(s32[2,256]{1,0:T(2,128)S(1)} %get-tuple-element.116), channel_id=1, source_target_pairs={{0,3},{1,0},{2,1},{3,2},{4,7},{5,4},{6,5},{7,6},{8,11},{9,8},{10,9... | collective-permute-start | bytes 6152 | tf_op jit(solution)/shard_map/ppermute | solution.py:1123
  6.7 4.5 %collective-permute-start.1 = (s32[2,256]{1,0:T(2,128)S(1)}, s32[2,256]{1,0:T(2,128)S(1)}, u32[]{:S(2)}, u32[]{:S(2)}) collective-permute-start(s32[2,256]{1,0:T(2,128)S(1)} %get-tuple-element.117), channel_id=1, source_target_pairs={{0,2},{1,3},{2,0},{3,1},{4,6},{5,7},{6,4},{7,5},{8,10},{9,11},{10,... | collective-permute-start | bytes 6152 | tf_op jit(solution)/shard_map/ppermute | solution.py:1123
  6.8 5.4 %collective-permute-start = (s32[2,256]{1,0:T(2,128)S(1)}, s32[2,256]{1,0:T(2,128)S(1)}, u32[]{:S(2)}, u32[]{:S(2)}) collective-permute-start(s32[2,256]{1,0:T(2,128)S(1)} %get-tuple-element.118), channel_id=1, source_target_pairs={{0,1},{1,2},{2,3},{3,0},{4,5},{5,6},{6,7},{7,4},{8,9},{9,10},{10,1... | collective-permute-start | bytes 6152 | tf_op jit(solution)/shard_map/ppermute | solution.py:1123
  18.3 6.6 %copy-start.5 = (s32[2,512]{1,0:T(2,128)S(1)}, s32[2,512]{1,0:T(2,128)}, u32[]{:S(2)}) copy-start(s32[2,512]{1,0:T(2,128)} %param.14) | copy-start | bytes 12292
  20.9 16.7 %collective-permute-start.5 = (bf16[256,1024]{1,0:T(8,128)(2,1)S(1)}, bf16[256,1024]{1,0:T(8,128)(2,1)S(1)}, u32[]{:S(2)}, u32[]{:S(2)}) collective-permute-start(bf16[256,1024]{1,0:T(8,128)(2,1)S(1)} %get-tuple-element.96), channel_id=1, source_target_pairs={{0,1},{1,2},{2,3},{3,0},{4,5},{5,6},{6,7},{7,4},{8,9},{9,10},{10,1... | collective-permute-start | bytes 1572872 | tf_op jit(solution)/shard_map/ppermute | solution.py:1123
  22.1 35.4 %collective-permute-start.4 = (bf16[256,1024]{1,0:T(8,128)(2,1)S(1)}, bf16[256,1024]{1,0:T(8,128)(2,1)S(1)}, u32[]{:S(2)}, u32[]{:S(2)}) collective-permute-start(bf16[256,1024]{1,0:T(8,128)(2,1)S(1)} %get-tuple-element.97), channel_id=1, source_target_pairs={{0,2},{1,3},{2,0},{3,1},{4,6},{5,7},{6,4},{7,5},{8,10},{9,11},{10,... | collective-permute-start | bytes 1572872 | tf_op jit(solution)/shard_map/ppermute | solution.py:1123
  23.0 34.5 %collective-permute-start.3 = (bf16[256,1024]{1,0:T(8,128)(2,1)S(1)}, bf16[256,1024]{1,0:T(8,128)(2,1)S(1)}, u32[]{:S(2)}, u32[]{:S(2)}) collective-permute-start(bf16[256,1024]{1,0:T(8,128)(2,1)S(1)} %get-tuple-element.98), channel_id=1, source_target_pairs={{0,3},{1,0},{2,1},{3,2},{4,7},{5,4},{6,5},{7,6},{8,11},{9,8},{10,9... | collective-permute-start | bytes 1572872 | tf_op jit(solution)/shard_map/ppermute | solution.py:1123
  37.6 20.0 %copy-start.7 = (bf16[256,1024]{1,0:T(8,128)(2,1)}, bf16[256,1024]{1,0:T(8,128)(2,1)S(1)}, u32[]{:S(2)}) copy-start(bf16[256,1024]{1,0:T(8,128)(2,1)S(1)} %collective-permute-done.5.t3) | copy-start | bytes 1572868
  57.5 0.8 copy-start.8
  57.5 1.0 copy-start.9
  231.8 69.3 %copy-start.3 = (f32[3072]{0:T(1024)S(1)}, f32[3072]{0:T(1024)}, u32[]{:S(2)}) copy-start(f32[3072]{0:T(1024)} %reshape.191) | copy-start | bytes 36868
  231.8 70.0 %copy-start.4 = (f32[1,4096]{1,0:T(1,128)S(1)}, f32[1,4096]{1,0:T(1,128)}, u32[]{:S(2)}) copy-start(f32[1,4096]{1,0:T(1,128)} %get-tuple-element.71) | copy-start | bytes 49156
  301.7 0.6 copy-start.6
  302.3 76.6 %copy-start = (f32[2,64,1280]{2,1,0:T(8,128)S(1)}, f32[2,64,1280]{2,1,0:T(8,128)}, u32[]{:S(2)}) copy-start(f32[2,64,1280]{2,1,0:T(8,128)} %get-tuple-element.76) | copy-start | bytes 1966084
  302.3 78.1 %copy-start.1 = (f32[2,256,256]{2,1,0:T(8,128)S(1)}, f32[2,256,256]{2,1,0:T(8,128)}, u32[]{:S(2)}) copy-start(f32[2,256,256]{2,1,0:T(8,128)} %get-tuple-element.77) | copy-start | bytes 1572868
  390.1 4.8 %copy-start.2 = (f32[2,64,768]{2,1,0:T(8,128)S(1)}, f32[2,64,768]{2,1,0:T(8,128)}, u32[]{:S(2)}) copy-start(f32[2,64,768]{2,1,0:T(8,128)} %get-tuple-element.75) | copy-start | bytes 1179652

commit v6 on v5

--- a/solution.py
+++ b/solution.py
@@ -408,13 +408,19 @@
     low = after.astype(BF)
     low_out[...] = low
     total = after + bias[3:4]
-    for j in range(ff // FWD):
-        cols = slice(j * FWD, (j + 1) * FWD)
-        act, slope = gelu_parts(dot(low, we[:, cols], NN) + hb[:, cols])
-        act = act.astype(BF)
-        act_out[:, cols] = act
-        slope_out[:, cols] = slope.astype(BF)
-        total = total + dot(act, wr[cols, :], NN)
+    count = ff // FWD
+    hidden = []
+    for j in range(count + 1):
+        if j < count:
+            cols = slice(j * FWD, (j + 1) * FWD)
+            hidden.append(dot(low, we[:, cols], NN) + hb[:, cols])
+        if j > 0:
+            cols = slice((j - 1) * FWD, j * FWD)
+            act, slope = gelu_parts(hidden[j - 1])
+            act = act.astype(BF)
+            act_out[:, cols] = act
+            slope_out[:, cols] = slope.astype(BF)
+            total = total + dot(act, wr[cols, :], NN)
     xh, rstd = norm_stats(total)
     out[...] = (xh * gains[2:3] + shifts[2:3]).astype(BF)
     y = cot[...].astype(F32)
@@ -536,13 +542,13 @@
     4: [(0, 0)],
     8: [(1, 0), (1, 1)],
     10: [(2, 0), (1, 2)],
-    11: [(2, 1), (1, 3)],
-    12: [(3, 0)],
-    13: [(2, 2)],
-    14: [(3, 1)],
-    15: [(2, 3)],
-    16: [(3, 2)],
-    17: [(3, 3)],
+    12: [(2, 1), (1, 3)],
+    13: [(3, 0)],
+    14: [(2, 2)],
+    15: [(3, 1)],
+    16: [(2, 3)],
+    17: [(3, 2)],
+    18: [(3, 3)],
 }
 N_TOK, N_TAB = 8, 4
 
@@ -951,7 +957,7 @@
 
 
 def closing_kernel(
-    cells, idx, small, ga, gb, done, joined, small_out,
+    cells, idx, sums0, sums1, sums2, sums_qv, hidden_sum, ga, gb, done, joined, small_out,
     ring, total, ring_sent, ring_got, held, arrived, small_sent, small_got, *scratch,
 ):
     summing = Summing((ga, gb), joined, scratch[:8])
@@ -1007,7 +1013,12 @@
 
     pass_on(0, 0).start()
     pass_on(0, 1).start()
-    held[0] = small[...]
+    at, width = 0, cells.shape[1]
+    for part in (sums0, sums1, sums2, sums_qv):
+        held[0, at : at + part.shape[0]] = part[...]
+        at += part.shape[0]
+    for n in range(hidden_sum.shape[1] // width):
+        held[0, at + n : at + n + 1] = hidden_sum[:, n * width : (n + 1) * width]
     small_copy(0).start()
     summing.start()
     total[...] = dot(pick(0), cells[...], NN)
@@ -1058,8 +1069,9 @@
         small_copy(n).wait_send()
 
 
-def closing(cells, idx, small, grads):
+def closing(cells, idx, sums, grads):
     count, width = cells.shape
+    small = (sum(part.size for part in sums) // width, width)
     rows, cols = grads[0].shape[3:]
     wide = width // 4
     part = lambda *n: pltpu.VMEM((2, 2, *n, BLOCK, wide), BF)
@@ -1068,51 +1080,92 @@
     return pl.pallas_call(
         closing_kernel,
         grid=(1,),
-        in_specs=[full(cells.shape), full(idx.shape), full(small.shape)]
+        in_specs=[full(cells.shape), full(idx.shape)]
+        + [full(part.shape) for part in sums]
         + [pl.BlockSpec(memory_space=pl.ANY)] * 2,
-        out_specs=[full(done), full((2, rows, cols)), full(small.shape)],
+        out_specs=[full(done), full((2, rows, cols)), full(small)],
         out_shape=[
             jax.ShapeDtypeStruct(done, BF),
             jax.ShapeDtypeStruct((2, rows, cols), F32),
-            jax.ShapeDtypeStruct(small.shape, F32),
+            jax.ShapeDtypeStruct(small, F32),
         ],
         scratch_shapes=[
             pltpu.VMEM((3, count, width), BF), pltpu.VMEM((8 * BLOCK, width), F32),
             dma((3, 2)), dma((3, 2)),
-            pltpu.VMEM((5, *small.shape), F32), pltpu.VMEM((5, *small.shape), F32), dma((5,)), dma((5,)),
+            pltpu.VMEM((5, *small), F32), pltpu.VMEM((5, *small), F32), dma((5,)), dma((5,)),
         ]
         + sum_scratch(rows, cols)
         + [part(2, 2, 2), part(2, 2), part(2), part(), dma((6, 2, 2)), dma((6, 2, 2))],
         compiler_params=params(has_side_effects=True, collective_id=3),
         cost_estimate=cost(8 * count * width * 1024, 24 << 20),
         name="closing",
-    )(cells, idx, small, *grads)
-
-
-def table_out_kernel(a, b, out):
+    )(cells, idx, *sums, *grads)
+
+
+def write_kernel(
+    a, b, embed, reduce_sum, expand_sum, joined_sum, small,
+    table, embed_out, reduce_out, expand_out, output_out, joined_out,
+    gains, shifts, biases, hidden_bias,
+):
     wide = a.shape[6]
+    lanes = table.shape[1]
     for n, piece in enumerate((a, b)):
         for u in range(2):
-            at = (2 * u + n) * wide
-            out[:, 0, at : at + wide] = piece[0, u, 0, 0, 0].astype(F32)
-
-
-def table_out(done, table_rows):
+            value = piece[0, u, 0, 0, 0].astype(F32)
+            for k in range(wide // lanes):
+                row = ((2 * u + n) * wide) // lanes + k
+                table[pl.ds(row, BLOCK, stride=4 * wide // lanes), :] = value[
+                    :, k * lanes : (k + 1) * lanes
+                ]
+    embed_out[...] = embed[...]
+
+    @pl.when(pl.program_id(0) == 0)
+    def _():
+        cols = reduce_sum.shape[2]
+        rows = expand_sum.shape[1]
+        wide = expand_out.shape[1]
+        for n in range(2):
+            reduce_out[n * cols : (n + 1) * cols, :] = reduce_sum[n].T
+            expand_out[n * rows : (n + 1) * rows, :] = expand_sum[n, :, :wide]
+            output_out[n * rows : (n + 1) * rows, :] = expand_sum[n, :, wide:]
+            joined_out[n * rows : (n + 1) * rows, :] = joined_sum[n]
+        for out, order in ((gains, (0, 2, 5)), (shifts, (1, 3, 6)), (biases, (8, 9, 4, 7))):
+            for n, row in enumerate(order):
+                out[n : n + 1, :] = small[row : row + 1, :]
+        for n in range(hidden_bias.shape[0]):
+            hidden_bias[n : n + 1, :] = small[10 + n : 11 + n, :]
+
+
+def write(done, embed, reduce_sum, expand_sum, joined_sum, small, table_rows, ff):
     wide = done.shape[6]
+    width = 4 * wide
+    tokens = embed.shape[0]
     block = (1, 2, 1, 1, 1, BLOCK, wide)
     first = lambda i: (0, 0, i % 2, (i // 2) % 2, i // 4, 0, 0)
     second = lambda i: (1, 0, i % 2, i // 4, (i // 2) % 2, 0, 0)
-    out = pl.pallas_call(
-        table_out_kernel,
+    rows = 2 * expand_sum.shape[1]
+    cols = ff // N_TAB
+    f32 = lambda *n: jax.ShapeDtypeStruct(n, F32)
+    shapes = [
+        f32(2 * reduce_sum.shape[2], reduce_sum.shape[1]), f32(rows, cols),
+        f32(rows, expand_sum.shape[2] - cols), f32(rows, joined_sum.shape[2]),
+        f32(3, width), f32(3, width), f32(4, width), f32(ff // width, width),
+    ]
+    lanes = 128
+    part = pl.BlockSpec((tokens // 8, width), lambda i: (i, 0))
+    table, *rest = pl.pallas_call(
+        write_kernel,
         grid=(8,),
-        in_specs=[pl.BlockSpec(block, first), pl.BlockSpec(block, second)],
-        out_specs=pl.BlockSpec((BLOCK, 1, 4 * wide), lambda i: (i, 0, 0)),
-        out_shape=jax.ShapeDtypeStruct((table_rows, 1, 4 * wide), F32),
+        in_specs=[pl.BlockSpec(block, first), pl.BlockSpec(block, second), part]
+        + [full(v.shape) for v in (reduce_sum, expand_sum, joined_sum, small)],
+        out_specs=[pl.BlockSpec((BLOCK * width // lanes, lanes), lambda i: (i, 0)), part]
+        + [full(v.shape) for v in shapes],
+        out_shape=[f32(table_rows * width // lanes, lanes), f32(tokens, width)] + shapes,
         compiler_params=params(),
-        cost_estimate=cost(0, 6 << 20),
-        name="table_write",
-    )(done, done)
-    return out.transpose(1, 0, 2)
+        cost_estimate=cost(0, 16 << 20),
+        name="write",
+    )(done, done, embed, reduce_sum, expand_sum, joined_sum, small)
+    return table.reshape(1, table_rows, width), *rest
 
 
 def flip_tok(value, bit, size):
@@ -1197,35 +1250,28 @@
     else:
         gj = more[0]
 
-    small = jnp.concatenate(
-        [
-            sums0.reshape(-1), sums1.reshape(-1), sums2.reshape(-1),
-            sums_qv.reshape(-1), hidden_sum.reshape(-1),
-        ]
-    ).reshape(-1, 128)
+    sums = (sums0, sums1, sums2, sums_qv, hidden_sum)
     if cubic:
-        done, joined_sum, small = closing(cell_grad, group_index, small, parts)
-        tables_grad = table_out(done, table_rows)
+        done, joined_sum, small = closing(cell_grad, group_index, sums, parts)
+        (
+            tables_grad, embedded_grad, reduce_grad, expand_grad, output_grad, joined_grad,
+            gains_grad, shifts_grad, biases_grad, hidden_bias_grad,
+        ) = write(
+            done, embedded_grad, reduce_sum, expand_sum[0], joined_sum, small, table_rows, ff
+        )
+        hidden_bias_grad = hidden_bias_grad.reshape(-1)
     else:
         cell_grads = [cell_grad] + [shift_tab(cell_grad, s, n_tab) for s in range(1, n_tab)]
         part_a, part_b = table_part(jnp.zeros_like(tok), group_index, cell_grads, 8)
         both = jnp.concatenate([part_a, part_b], axis=2).astype(F32)
         tables_grad = lax.psum(both.reshape(1, -1, width)[:, :table_rows], "tok")
-        small = small_sum(small, n_tok, n_tab)
-    small = small.reshape(-1)
-    row = small.reshape(-1, width)
-    gains_grad = jnp.stack([row[0], row[2], row[5]])
-    shifts_grad = jnp.stack([row[1], row[3], row[6]])
-    biases_grad = jnp.stack([row[8], row[9], row[4], row[7]])
-    hidden_bias_grad = small[10 * width :]
-
-    if cubic:
-        reduce_grad = jnp.concatenate([reduce_sum[0], reduce_sum[1]], axis=1).T
-        expand_sum = expand_sum[0].reshape(-1, expand_sum[0].shape[2])
-        expand_grad = expand_sum[:, : ff // 4]
-        output_grad = expand_sum[:, ff // 4 :]
-        joined_grad = joined_sum.reshape(-1, joined_sum.shape[2])
-    else:
+        small = jnp.concatenate([part.reshape(-1) for part in sums]).reshape(-1, 128)
+        small = small_sum(small, n_tok, n_tab).reshape(-1)
+        row = small.reshape(-1, width)
+        gains_grad = jnp.stack([row[0], row[2], row[5]])
+        shifts_grad = jnp.stack([row[1], row[3], row[6]])
+        biases_grad = jnp.stack([row[8], row[9], row[4], row[7]])
+        hidden_bias_grad = small[10 * width :]
         both = lambda a, b: jnp.einsum("ta,tb->ab", a, b, preferred_element_type=F32).astype(BF)
 
         def scattered(part):

time: 402 us -> 382 us (0.950)
  local copies, waits for them, and re-layouts: 21.5 us -> 8.54 us
  Pallas kernels: 327 us -> 322 us
    unnamed x27 -> x9, local copies, waits for them, and re-layouts: 9.59 us -> 2.29 us
    pallas_call x1, Pallas kernels: 87.5 us -> 82 us  [ffn_grads(): pl.pallas_call(ffn_grads_kernel, grid=(2 * N_TOK + N_TAB,), in_specs=[any...]
where the time goes in v6:
time: 382 us; the launch traced here: 377 us
  Pallas kernels  322 us (84%)
  waiting for transfers between devices  33.3 us (9%)
  starting transfers between devices  10.2 us (3%)
  local copies, waits for them, and re-layouts  8.54 us (2%)
    pallas_call x1, Pallas kernels, ffn_grads(): pl.pallas_call(ffn_grads_kernel, grid=(2 * N_TOK + N_TAB,), in_specs=[any...  82 us
    pallas_call x1, Pallas kernels, closing(): pl.pallas_call(closing_kernel, grid=(1,), in_specs=[full(cells.shape), fu...  75.1 us
    pallas_call x1, Pallas kernels, back(): pl.pallas_call(functools.partial(back_kernel, pages=pages, summed=summed)...  68.6 us
    pallas_call x1, Pallas kernels, ffn_fwd(): pl.pallas_call(ffn_fwd_kernel, grid=(tokens // tile,), in_specs=[rows, ro...  46.6 us
    ppermute x6, waiting for transfers between devices, shift_tab(): lax.ppermute(value, 'tab', [(i, (i + shift) % size) for i in range(size)])  33.3 us
    pallas_call x1, Pallas kernels, attn_fwd(): pl.pallas_call(attn_fwd_kernel, grid=(pages, steps), in_specs=[blk] * 3,...  20 us
    pallas_call x1, Pallas kernels, embed(): pl.pallas_call(embed_kernel, grid=(pages,), in_specs=[rows, pl.BlockSpec(...  14.4 us
    ppermute x6, starting transfers between devices, shift_tab(): lax.ppermute(value, 'tab', [(i, (i + shift) % size) for i in range(size)])  10.2 us
  transfers between devices with their start and end apart: 6, of which 4 were waited for; matrix products, arithmetic and copies ran while one was open for 1% of the time, Pallas kernels for 0%

profile of v6, /device:TPU:0, one launch (start us, length us, event | category | flops | bytes accessed | tf_op | source)
XLA Modules:
  0.0 376.8 jit_solution(15677124657919625670)
XLA Ops:
  0.7 0.8 fusion
  1.6 5.1 %collective-permute-start.2 = (s32[2,256]{1,0:T(2,128)S(1)}, s32[2,256]{1,0:T(2,128)S(1)}, u32[]{:S(2)}, u32[]{:S(2)}) collective-permute-start(s32[2,256]{1,0:T(2,128)S(1)} %get-tuple-element.135), channel_id=1, source_target_pairs={{0,3},{1,0},{2,1},{3,2},{4,7},{5,4},{6,5},{7,6},{8,11},{9,8},{10,9... | collective-permute-start | bytes 6152 | tf_op jit(solution)/shard_map/ppermute | solution.py:1176
  6.7 0.0 collective-permute-start.1
  6.8 1.0 collective-permute-start
  7.8 3.1 pad.6.table
  10.9 0.0 collective-permute-done.2
  10.9 0.4 collective-permute-done.1
  11.2 0.9 collective-permute-done
  12.1 0.6 pad_add_fusion.1.idx
  12.7 5.6 %lookup.1 = bf16[4,256,1024]{2,1,0:T(8,128)(2,1)} custom-call(s32[4,2,256]{2,1,0:T(2,128)} %pad_add_fusion.1.idx, bf16[1024,1024]{1,0:T(8,128)(2,1)} %pad.6.table), custom_call_target="tpu_custom_call" | custom-call | flops 2147483648 | bytes 2097152 | tf_op jit(solution)/shard_map/lookup/pallas_call | solution.py:100
  18.3 0.0 copy-start
  18.3 2.5 slice_bitcast_fusion
  20.9 1.2 collective-permute-start.5
  22.1 0.9 collective-permute-start.4
  23.0 1.9 collective-permute-start.3
  24.9 0.0 copy-done
  24.9 0.6 reshape.157.ci.refs_11_
  25.5 12.0 %collective-permute-done.5.t3 = bf16[256,1024]{1,0:T(8,128)(2,1)S(1)} collective-permute-done((bf16[256,1024]{1,0:T(8,128)(2,1)S(1)}, bf16[256,1024]{1,0:T(8,128)(2,1)S(1)}, u32[]{:S(2)}, u32[]{:S(2)}) %collective-permute-start.5) | collective-permute-done | bytes 524320 | tf_op jit(solution)/shard_map/ppermute | solution.py:1176
  37.6 0.0 copy-start.1
  37.6 19.9 %collective-permute-done.4.t2 = bf16[256,1024]{1,0:T(8,128)(2,1)S(1)} collective-permute-done((bf16[256,1024]{1,0:T(8,128)(2,1)S(1)}, bf16[256,1024]{1,0:T(8,128)(2,1)S(1)}, u32[]{:S(2)}, u32[]{:S(2)}) %collective-permute-start.4) | collective-permute-done | bytes 524320 | tf_op jit(solution)/shard_map/ppermute | solution.py:1176
  57.5 0.0 copy-start.2
  57.5 0.0 collective-permute-done.3.t1
  57.5 0.0 copy-start.3
  57.5 0.0 copy-done.1
  57.5 0.8 copy-done.2
  58.3 0.2 copy-done.3
  58.5 14.4 %embed_joined.1 = (bf16[1024,1024]{1,0:T(8,128)(2,1)}, bf16[1024,1024]{1,0:T(8,128)(2,1)}, bf16[1024,1024]{1,0:T(8,128)(2,1)}, f32[1024,1024]{1,0:T(8,128)}, bf1...) custom-call(bf16[1024,1024]{1,0:T(8,128)(2,1)} %emb.1, s32[2,1,512]{2,1,0:T(1,128)} %reshape.157.ci.refs_11_, ...), custom_call_target="tpu_custom_call" | custom-call | flops 6442450944 | bytes 27262976 | tf_op jit(solution)/shard_map/embed_joined/pallas_call | solution.py:142
  72.9 20.0 %attention.1 = (bf16[1024,1024]{1,0:T(8,128)(2,1)}, f32[2,4,4,512]{3,2,1,0:T(4,128)}) custom-call(bf16[1024,1024]{1,0:T(8,128)(2,1)} %get-tuple-element.55.q.refs_0_, bf16[1024,1024]{1,0:T(8,128)(2,1)} %get-tuple-element.56.k.refs_1_, bf16[1024,1024]{1,0:T(8,128)(2,1)} %get-tuple-element.57.v.refs_2_), custom_call_target="tpu_custom_call" | custom-call | flops 14000000000 | bytes 8388608 | tf_op jit(solution)/shard_map/attention/pallas_call | solution.py:347
  92.9 46.6 %ffn_forward.1 = (bf16[1024,1024]{1,0:T(8,128)(2,1)}, f32[1024,1024]{1,0:T(8,128)}, bf16[1024,1024]{1,0:T(8,128)(2,1)}, f32[1024,1]{1,0:T(8,128)}, bf16[1024,409...) custom-call(bf16[1024,1024]{1,0:T(8,128)(2,1)} %get-tuple-element.58, ...), custom_call_target="tpu_custom_call" | custom-call | flops 19327352832 | bytes 62914560 | tf_op jit(solution)/shard_map/ffn_forward/pallas_call | solution.py:449
  139.5 82.0 %ffn_backward_grads.1 = (f32[1024,1024]{1,0:T(8,128)}, bf16[1024,1024]{1,0:T(8,128)(2,1)}, f32[1,4096]{1,0:T(1,128)}, f32[3,1024]{1,0:T(4,128)}, bf16[2,4,4,64,1...) custom-call(bf16[1024,1024]{1,0:T(8,128)(2,1)} %get-tuple-element.61.gffn_in, ...), custom_call_target="tpu_custom_call" | custom-call | flops 38654705664 | bytes 62914560 | tf_op jit(solution)/shard_map/ffn_backward_grads/pallas_call | solution.py:656
  221.5 68.6 %attention_joined_embed_back.1 = (f32[1024,1024]{1,0:T(8,128)}, bf16[256,1024]{1,0:T(8,128)(2,1)}, f32[2,1024]{1,0:T(2,128)}, f32[2,1024]{1,0:T(2,128)}, bf16[2,...) custom-call(bf16[1024,1024]{1,0:T(8,128)(2,1)} %get-tuple-element.55.q.refs_0_, ...), custom_call_target="tpu_custom_call" | custom-call | flops 70000001024 | bytes 41943040 | tf_op jit(solution)/shard_map/attention_joined_embed_back/pallas_call | solution.py:834
  290.1 75.1 %closing.1 = (bf16[2,2,2,2,2,128,256]{6,5,4,3,2,1,0:T(8,128)(2,1)}, f32[2,64,768]{2,1,0:T(8,128)}, f32[14,1024]{1,0:T(8,128)}) custom-call(bf16[256,1024]{1,0:T(8,128)(2,1)} %get-tuple-element.75.cells, s32[4,2,256]{2,1,0:T(2,128)} %pad_add_fusion.1.idx, f32[2,1024]{1,0:T(2,128)} %get-tuple-element.76.sums0, f32[3,1024]{1,0:T(4,128)} %get-tuple-element.77.sums1, ...), custom_call_target="tpu_custom_call" | custom-call | flops 2147483648 | bytes 25165824 | tf_op jit(solution)/shard_map/closing/pallas_call | solution.py:1080
  365.2 10.0 %write.1 = (f32[8008,128]{1,0:T(8,128)}, f32[1024,1024]{1,0:T(8,128)}, f32[512,256]{1,0:T(8,128)}, f32[128,1024]{1,0:T(8,128)}, f32[128,256]{1,0:T(8,128)}, /*in...) custom-call(bf16[2,2,2,2,2,128,256]{6,5,4,3,2,1,0:T(8,128)(2,1)} %get-tupl, ...), custom_call_target="tpu_custom_call" | custom-call | bytes 16777216 | tf_op jit(solution)/shard_map/write/pallas_call | solution.py:1156
  375.2 1.3 copy.28
  (4 shorter events, 0.0 us)
Async XLA Ops:
  1.6 9.2 %collective-permute-start.2 = (s32[2,256]{1,0:T(2,128)S(1)}, s32[2,256]{1,0:T(2,128)S(1)}, u32[]{:S(2)}, u32[]{:S(2)}) collective-permute-start(s32[2,256]{1,0:T(2,128)S(1)} %get-tuple-element.135), channel_id=1, source_target_pairs={{0,3},{1,0},{2,1},{3,2},{4,7},{5,4},{6,5},{7,6},{8,11},{9,8},{10,9... | collective-permute-start | bytes 6152 | tf_op jit(solution)/shard_map/ppermute | solution.py:1176
  6.7 4.5 %collective-permute-start.1 = (s32[2,256]{1,0:T(2,128)S(1)}, s32[2,256]{1,0:T(2,128)S(1)}, u32[]{:S(2)}, u32[]{:S(2)}) collective-permute-start(s32[2,256]{1,0:T(2,128)S(1)} %get-tuple-element.136), channel_id=1, source_target_pairs={{0,2},{1,3},{2,0},{3,1},{4,6},{5,7},{6,4},{7,5},{8,10},{9,11},{10,... | collective-permute-start | bytes 6152 | tf_op jit(solution)/shard_map/ppermute | solution.py:1176
  6.8 5.4 %collective-permute-start = (s32[2,256]{1,0:T(2,128)S(1)}, s32[2,256]{1,0:T(2,128)S(1)}, u32[]{:S(2)}, u32[]{:S(2)}) collective-permute-start(s32[2,256]{1,0:T(2,128)S(1)} %get-tuple-element.137), channel_id=1, source_target_pairs={{0,1},{1,2},{2,3},{3,0},{4,5},{5,6},{6,7},{7,4},{8,9},{9,10},{10,1... | collective-permute-start | bytes 6152 | tf_op jit(solution)/shard_map/ppermute | solution.py:1176
  18.3 6.6 %copy-start = (s32[2,512]{1,0:T(2,128)S(1)}, s32[2,512]{1,0:T(2,128)}, u32[]{:S(2)}) copy-start(s32[2,512]{1,0:T(2,128)} %param.14) | copy-start | bytes 12292
  20.9 16.7 %collective-permute-start.5 = (bf16[256,1024]{1,0:T(8,128)(2,1)S(1)}, bf16[256,1024]{1,0:T(8,128)(2,1)S(1)}, u32[]{:S(2)}, u32[]{:S(2)}) collective-permute-start(bf16[256,1024]{1,0:T(8,128)(2,1)S(1)} %get-tuple-element.127), channel_id=1, source_target_pairs={{0,1},{1,2},{2,3},{3,0},{4,5},{5,6},{6,7},{7,4},{8,9},{9,10},{10,1... | collective-permute-start | bytes 1572872 | tf_op jit(solution)/shard_map/ppermute | solution.py:1176
  22.1 35.4 %collective-permute-start.4 = (bf16[256,1024]{1,0:T(8,128)(2,1)S(1)}, bf16[256,1024]{1,0:T(8,128)(2,1)S(1)}, u32[]{:S(2)}, u32[]{:S(2)}) collective-permute-start(bf16[256,1024]{1,0:T(8,128)(2,1)S(1)} %get-tuple-element.128), channel_id=1, source_target_pairs={{0,2},{1,3},{2,0},{3,1},{4,6},{5,7},{6,4},{7,5},{8,10},{9,11},{10,... | collective-permute-start | bytes 1572872 | tf_op jit(solution)/shard_map/ppermute | solution.py:1176
  23.0 34.5 %collective-permute-start.3 = (bf16[256,1024]{1,0:T(8,128)(2,1)S(1)}, bf16[256,1024]{1,0:T(8,128)(2,1)S(1)}, u32[]{:S(2)}, u32[]{:S(2)}) collective-permute-start(bf16[256,1024]{1,0:T(8,128)(2,1)S(1)} %get-tuple-element.129), channel_id=1, source_target_pairs={{0,3},{1,0},{2,1},{3,2},{4,7},{5,4},{6,5},{7,6},{8,11},{9,8},{10,9... | collective-permute-start | bytes 1572872 | tf_op jit(solution)/shard_map/ppermute | solution.py:1176
  37.6 20.0 %copy-start.1 = (bf16[256,1024]{1,0:T(8,128)(2,1)}, bf16[256,1024]{1,0:T(8,128)(2,1)S(1)}, u32[]{:S(2)}) copy-start(bf16[256,1024]{1,0:T(8,128)(2,1)S(1)} %collective-permute-done.5.t3) | copy-start | bytes 1572868
  57.5 0.8 copy-start.2
  57.5 1.0 copy-start.3

commit v7 on v6

--- a/solution.py
+++ b/solution.py
@@ -113,11 +113,11 @@
 
 
 def embed_kernel(
-    emb, ci, t0, t1, t2, t3, w, gains, shifts, bias, q, k, v, normed, low, rstd_out
+    emb, ci, terms, w, gains, shifts, bias, q, k, v, normed, low, rstd_out
 ):
     width = emb.shape[1]
     tokens = emb.shape[0]
-    cells = jnp.concatenate([t0[...], t1[...], t2[...], t3[...]], axis=0)
+    cells = terms[...].reshape(4 * CELLS, width)
     number = lax.broadcasted_iota(jnp.int32, (CELLS, tokens), 0)
     pick = (number == ci[0]).astype(F32).astype(BF)
     pick = jnp.concatenate([pick] * 4, axis=0)
@@ -137,20 +137,19 @@
     tokens, width = emb.shape
     pages, length = ci.shape
     rows = pl.BlockSpec((length, width), lambda i: (i, 0))
-    cell_rows = pl.BlockSpec((CELLS, width), lambda i: (i, 0))
     shape = lambda dt, n=width: jax.ShapeDtypeStruct((tokens, n), dt)
     return pl.pallas_call(
         embed_kernel,
         grid=(pages,),
         in_specs=[rows, pl.BlockSpec((1, 1, length), lambda i: (i, 0, 0))]
-        + [cell_rows] * 4
+        + [pl.BlockSpec((4, CELLS, width), lambda i: (0, i, 0))]
         + [full(w.shape), full(gains.shape), full(shifts.shape), full(bias.shape)],
         out_specs=[rows] * 5 + [pl.BlockSpec((length, 1), lambda i: (i, 0))],
         out_shape=[shape(BF), shape(BF), shape(BF), shape(F32), shape(BF), shape(F32, 1)],
         compiler_params=params(),
         cost_estimate=cost(2 * tokens * width * 3 * width, 26 << 20),
         name="embed_joined",
-    )(emb, ci.reshape(pages, 1, length), *terms, w, gains, shifts, bias)
+    )(emb, ci.reshape(pages, 1, length), terms, w, gains, shifts, bias)
 
 
 STAGES = 4
@@ -307,6 +306,142 @@
         sum_scratch(rows, cols),
         {"has_side_effects": True, "collective_id": number},
     )
+
+
+BLOCK = 128
+
+
+def spread_kernel(
+    idx, table, found, group_idx,
+    held, numbers, ring_sent, ring_got, plane_sent, plane_got, idx_sent, idx_got,
+):
+    tok, z = lax.axis_index("tok"), lax.axis_index("tab")
+    core, x, y, peers = neighbours()
+    c, cx, cy = tok % 2, (tok // 2) % 2, tok // 4
+    first, second = (x, y), (y, x)
+    f, g = (cx, cy), (cy, cx)
+    meet([core, x, y, *peers])
+    half = table.shape[1] // 2
+    count = idx.shape[2]
+
+    def ring(k, ch):
+        if k == 0:
+            start = pl.multiple_of(tok * BLOCK, BLOCK)
+            src = table.at[pl.ds(start, BLOCK), pl.ds(ch * half, half)]
+        else:
+            src = held.at[k - 1, ch, c, g[ch], f[ch]]
+        return pltpu.make_async_remote_copy(
+            src_ref=src, dst_ref=held.at[k, ch, c, g[ch], f[ch]],
+            send_sem=ring_sent.at[k, ch], recv_sem=ring_got.at[k, ch],
+            device_id=peers[0], device_id_type=pl.DeviceIdType.MESH,
+        )
+
+    def plane(stage, k, ch):
+        src, to = (
+            (held.at[k, ch, c, g[ch], f[ch]], first[ch]),
+            (held.at[k, ch, c, g[ch]], second[ch]),
+            (held.at[k, ch, c], core),
+        )[stage]
+        return pltpu.make_async_remote_copy(
+            src_ref=src, dst_ref=src,
+            send_sem=plane_sent.at[stage, k, ch], recv_sem=plane_got.at[stage, k, ch],
+            device_id=to, device_id_type=pl.DeviceIdType.MESH,
+        )
+
+    def number(s):
+        return pltpu.make_async_remote_copy(
+            src_ref=idx.at[(z + s) % 4], dst_ref=numbers.at[s - 1],
+            send_sem=idx_sent.at[s - 1], recv_sem=idx_got.at[s - 1],
+            device_id=peers[s - 1], device_id_type=pl.DeviceIdType.MESH,
+        )
+
+    def picks(owner):
+        out = []
+        for b in range(8):
+            row = lax.broadcasted_iota(jnp.int32, (BLOCK, count), 0) + b * BLOCK
+            one = (row == idx[owner, 0:1, :]).astype(F32)
+            two = (row == idx[owner, 1:2, :]).astype(F32)
+            out.append((one + two).astype(BF))
+        return out
+
+    def arrive(k):
+        for ch in range(2):
+            ring(k, ch).wait_recv()
+            if k < 2:
+                ring(k + 1, ch).start()
+            plane(0, k, ch).start()
+
+    def go_on(stage, k):
+        for ch in range(2):
+            plane(stage - 1, k, ch).wait_recv()
+            plane(stage, k, ch).start()
+
+    def look_up(k):
+        rows = picks((z + 3 - k) % 4)
+        for ch in range(2):
+            plane(2, k, ch).wait_recv()
+            order = [
+                4 * a + 2 * b + n if ch == 0 else 4 * b + 2 * a + n
+                for n in range(2)
+                for a in range(2)
+                for b in range(2)
+            ]
+            pick = jnp.concatenate([rows[b] for b in order], axis=0)
+            data = held[k, ch].reshape(8 * BLOCK, half)
+            found[k + 1, :, ch * half : (ch + 1) * half] = dot(pick, data, TN).astype(BF)
+
+    for ch in range(2):
+        ring(0, ch).start()
+    for s in range(1, 4):
+        number(s).start()
+    found[0] = dot(jnp.concatenate(picks(z), axis=0), table[...], TN).astype(BF)
+    arrive(0)
+    go_on(1, 0)
+    arrive(1)
+    go_on(1, 1)
+    go_on(2, 0)
+    arrive(2)
+    go_on(1, 2)
+    group_idx[0] = idx[z]
+    for s in range(1, 4):
+        number(s).wait_recv()
+        group_idx[s] = numbers[s - 1]
+    look_up(0)
+    go_on(2, 1)
+    look_up(1)
+    go_on(2, 2)
+    look_up(2)
+    for s in range(1, 4):
+        number(s).wait_send()
+    for k in range(3):
+        for ch in range(2):
+            ring(k, ch).wait_send()
+            for stage in range(3):
+                plane(stage, k, ch).wait_send()
+
+
+def spread(idx, table):
+    n_tab, _, count = idx.shape
+    rows, width = table.shape
+    dma = pltpu.SemaphoreType.DMA
+    return pl.pallas_call(
+        spread_kernel,
+        grid=(1,),
+        in_specs=[full(idx.shape), full(table.shape)],
+        out_specs=[full((n_tab, count, width)), full(idx.shape)],
+        out_shape=[
+            jax.ShapeDtypeStruct((n_tab, count, width), BF),
+            jax.ShapeDtypeStruct(idx.shape, jnp.int32),
+        ],
+        scratch_shapes=[
+            pltpu.VMEM((3, 2, 2, 2, 2, BLOCK, width // 2), BF),
+            pltpu.VMEM((3, 2, count), jnp.int32),
+            dma((3, 2)), dma((3, 2)), dma((3, 3, 2)), dma((3, 3, 2)), dma((3,)), dma((3,)),
+        ],
+        compiler_params=params(has_side_effects=True, collective_id=4),
+        cost_estimate=cost(8 * count * width * rows, 8 << 20),
+        name="spread",
+    )(idx, table)
 
 
 HP = 4
@@ -540,15 +675,15 @@
 
 FFN_PLAN = {
     4: [(0, 0)],
-    8: [(1, 0), (1, 1)],
-    10: [(2, 0), (1, 2)],
-    12: [(2, 1), (1, 3)],
-    13: [(3, 0)],
-    14: [(2, 2)],
-    15: [(3, 1)],
-    16: [(2, 3)],
-    17: [(3, 2)],
-    18: [(3, 3)],
+    8: [(1, 0)],
+    9: [(1, 1)],
+    11: [(2, 0), (1, 2)],
+    13: [(2, 1), (1, 3)],
+    15: [(3, 0)],
+    16: [(2, 2)],
+    17: [(3, 1), (2, 3)],
+    18: [(3, 2)],
+    19: [(3, 3)],
 }
 N_TOK, N_TAB = 8, 4
 
@@ -898,9 +1033,6 @@
     )(tok, idx, *grads)
 
 
-BLOCK = 128
-
-
 class TableSum:
     def __init__(self, scratch, done):
         self.part, self.r0, self.r1, self.r2, self.sent, self.got = scratch
@@ -1213,14 +1345,19 @@
             jnp.stack([bottom - top, none]),
         ]
     )
-    pick_table = lambda i: lax.dynamic_index_in_dim(index_table, i, 0, keepdims=False)
-    group_index = jnp.stack(
-        [pick_table(z)]
-        + [shift_tab(pick_table((z + s) % n_tab), s, n_tab) for s in range(1, n_tab)]
-    )
     padded = jnp.pad(box_tables[0], ((0, 1024 - table_rows), (0, 0)))
-    found = lookup(group_index, padded)
-    terms = [found[0]] + [shift_tab(found[s], n_tab - s, n_tab) for s in range(1, n_tab)]
+    if cubic:
+        terms, group_index = spread(index_table, padded)
+    else:
+        pick_table = lambda i: lax.dynamic_index_in_dim(index_table, i, 0, keepdims=False)
+        group_index = jnp.stack(
+            [pick_table(z)]
+            + [shift_tab(pick_table((z + s) % n_tab), s, n_tab) for s in range(1, n_tab)]
+        )
+        found = lookup(group_index, padded)
+        terms = jnp.stack(
+            [found[0]] + [shift_tab(found[s], n_tab - s, n_tab) for s in range(1, n_tab)]
+        )
 
     q, k, v, normed, normed_low, rstd0 = embed(
         embedded, cell_index, terms, joined_weight, norm_gains, norm_shifts, bias_rows

time: 382 us -> 373 us (0.976)
  Pallas kernels: 322 us -> 359 us
  waiting for transfers between devices: 33.3 us -> 0 us
  starting transfers between devices: 10.2 us -> 0 us
    pallas_call x1, Pallas kernels: 5.6 us -> 48.6 us  [spread(): pl.pallas_call(spread_kernel, grid=(1,), in_specs=[full(idx.shape), full(...]
    ppermute x6 -> x0, waiting for transfers between devices: 33.3 us -> none  [shift_tab(): lax.ppermute(value, 'tab', [(i, (i + shift) % size) for i in range(size)])]
    ppermute x6 -> x0, starting transfers between devices: 10.2 us -> none  [shift_tab(): lax.ppermute(value, 'tab', [(i, (i + shift) % size) for i in range(size)])]
    pallas_call x1, Pallas kernels: 82 us -> 71.8 us  [ffn_grads(): pl.pallas_call(ffn_grads_kernel, grid=(2 * N_TOK + N_TAB,), in_specs=[any...]
    pallas_call x1, Pallas kernels: 68.6 us -> 73.2 us  [back(): pl.pallas_call(functools.partial(back_kernel, pages=pages, summed=summed)...]
  transfers between devices with their start and end apart: 6 -> 0, of which waited for: 4 -> 0; matrix products, arithmetic and copies ran while one was open for 1% -> 0% of each run, Pallas kernels for 0% -> 0%
where the time goes in v7:
time: 373 us; the launch traced here: 367 us
  Pallas kernels  359 us (96%)
  local copies, waits for them, and re-layouts  5.71 us (2%)
    pallas_call x1, Pallas kernels, closing(): pl.pallas_call(closing_kernel, grid=(1,), in_specs=[full(cells.shape), fu...  74.1 us
    pallas_call x1, Pallas kernels, back(): pl.pallas_call(functools.partial(back_kernel, pages=pages, summed=summed)...  73.2 us
    pallas_call x1, Pallas kernels, ffn_grads(): pl.pallas_call(ffn_grads_kernel, grid=(2 * N_TOK + N_TAB,), in_specs=[any...  71.8 us
    pallas_call x1, Pallas kernels, spread(): pl.pallas_call(spread_kernel, grid=(1,), in_specs=[full(idx.shape), full(...  48.6 us
    pallas_call x1, Pallas kernels, ffn_fwd(): pl.pallas_call(ffn_fwd_kernel, grid=(tokens // tile,), in_specs=[rows, ro...  46.6 us
    pallas_call x1, Pallas kernels, attn_fwd(): pl.pallas_call(attn_fwd_kernel, grid=(pages, steps), in_specs=[blk] * 3,...  20 us
    pallas_call x1, Pallas kernels, embed(): pl.pallas_call(embed_kernel, grid=(pages,), in_specs=[rows, pl.BlockSpec(...  14.3 us
    pallas_call x1, Pallas kernels, write(): pl.pallas_call(write_kernel, grid=(8,), in_specs=[pl.BlockSpec(block, fir...  10 us

profile of v7, /device:TPU:0, one launch (start us, length us, event | category | flops | bytes accessed | tf_op | source)
XLA Modules:
  0.0 366.8 jit_solution(10183564436211763947)
XLA Ops:
  0.6 1.3 reshape.157.ci.refs_11_
  1.9 0.8 fusion
  2.8 0.6 pad_add_fusion.idx
  3.4 3.1 pad.6.table
  6.5 48.6 %spread.1 = (bf16[4,256,1024]{2,1,0:T(8,128)(2,1)}, s32[4,2,256]{2,1,0:T(2,128)}) custom-call(s32[4,2,256]{2,1,0:T(2,128)} %pad_add_fusion.idx, bf16[1024,1024]{1,0:T(8,128)(2,1)} %pad.6.table), custom_call_target="tpu_custom_call" | custom-call | flops 2147483648 | bytes 8388608 | tf_op jit(solution)/shard_map/spread/pallas_call | solution.py:427
  55.1 14.3 %embed_joined.1 = (bf16[1024,1024]{1,0:T(8,128)(2,1)}, bf16[1024,1024]{1,0:T(8,128)(2,1)}, bf16[1024,1024]{1,0:T(8,128)(2,1)}, f32[1024,1024]{1,0:T(8,128)}, bf1...) custom-call(bf16[1024,1024]{1,0:T(8,128)(2,1)} %emb.1, s32[2,1,512]{2,1,0:T(1,128)} %reshape.157.ci.refs_11_, ...), custom_call_target="tpu_custom_call" | custom-call | flops 6442450944 | bytes 27262976 | tf_op jit(solution)/shard_map/embed_joined/pallas_call | solution.py:141
  69.5 20.0 %attention.1 = (bf16[1024,1024]{1,0:T(8,128)(2,1)}, f32[2,4,4,512]{3,2,1,0:T(4,128)}) custom-call(bf16[1024,1024]{1,0:T(8,128)(2,1)} %get-tuple-element.58.q.refs_0_, bf16[1024,1024]{1,0:T(8,128)(2,1)} %get-tuple-element.59.k.refs_1_, bf16[1024,1024]{1,0:T(8,128)(2,1)} %get-tuple-element.60.v.refs_2_), custom_call_target="tpu_custom_call" | custom-call | flops 14000000000 | bytes 8388608 | tf_op jit(solution)/shard_map/attention/pallas_call | solution.py:482
  89.5 46.6 %ffn_forward.1 = (bf16[1024,1024]{1,0:T(8,128)(2,1)}, f32[1024,1024]{1,0:T(8,128)}, bf16[1024,1024]{1,0:T(8,128)(2,1)}, f32[1024,1]{1,0:T(8,128)}, bf16[1024,409...) custom-call(bf16[1024,1024]{1,0:T(8,128)(2,1)} %get-tuple-element.61, ...), custom_call_target="tpu_custom_call" | custom-call | flops 19327352832 | bytes 62914560 | tf_op jit(solution)/shard_map/ffn_forward/pallas_call | solution.py:584
  136.1 71.8 %ffn_backward_grads.1 = (f32[1024,1024]{1,0:T(8,128)}, bf16[1024,1024]{1,0:T(8,128)(2,1)}, f32[1,4096]{1,0:T(1,128)}, f32[3,1024]{1,0:T(4,128)}, bf16[2,4,4,64,1...) custom-call(bf16[1024,1024]{1,0:T(8,128)(2,1)} %get-tuple-element.64.gffn_in, ...), custom_call_target="tpu_custom_call" | custom-call | flops 38654705664 | bytes 62914560 | tf_op jit(solution)/shard_map/ffn_backward_grads/pallas_call | solution.py:791
  207.9 73.2 %attention_joined_embed_back.1 = (f32[1024,1024]{1,0:T(8,128)}, bf16[256,1024]{1,0:T(8,128)(2,1)}, f32[2,1024]{1,0:T(2,128)}, f32[2,1024]{1,0:T(2,128)}, bf16[2,...) custom-call(bf16[1024,1024]{1,0:T(8,128)(2,1)} %get-tuple-element.58.q.refs_0_, ...), custom_call_target="tpu_custom_call" | custom-call | flops 70000001024 | bytes 41943040 | tf_op jit(solution)/shard_map/attention_joined_embed_back/pallas_call | solution.py:969
  281.1 74.1 %closing.1 = (bf16[2,2,2,2,2,128,256]{6,5,4,3,2,1,0:T(8,128)(2,1)}, f32[2,64,768]{2,1,0:T(8,128)}, f32[14,1024]{1,0:T(8,128)}) custom-call(bf16[256,1024]{1,0:T(8,128)(2,1)} %get-tuple-element.78.cells, s32[4,2,256]{2,1,0:T(2,128)} %get-tuple-element.79.idx, f32[2,1024]{1,0:T(2,128)} %get-tuple-element.80.sums0, f32[3,1024]{1,0:T(4,128)} %get-tuple-element.81.sums1, ...), custom_call_target="tpu_custom_call" | custom-call | flops 2147483648 | bytes 25165824 | tf_op jit(solution)/shard_map/closing/pallas_call | solution.py:1212
  355.2 10.0 %write.1 = (f32[8008,128]{1,0:T(8,128)}, f32[1024,1024]{1,0:T(8,128)}, f32[512,256]{1,0:T(8,128)}, f32[128,1024]{1,0:T(8,128)}, f32[128,256]{1,0:T(8,128)}, /*in...) custom-call(bf16[2,2,2,2,2,128,256]{6,5,4,3,2,1,0:T(8,128)(2,1)} %get-tupl, ...), custom_call_target="tpu_custom_call" | custom-call | bytes 16777216 | tf_op jit(solution)/shard_map/write/pallas_call | solution.py:1288
  365.2 1.3 copy.28
  (2 shorter events, 0.0 us)

commit v8 on v7

--- a/solution.py
+++ b/solution.py
@@ -406,11 +406,17 @@
     for s in range(1, 4):
         number(s).wait_recv()
         group_idx[s] = numbers[s - 1]
-    look_up(0)
-    go_on(2, 1)
-    look_up(1)
-    go_on(2, 2)
-    look_up(2)
+
+    def finish(k, _):
+        look_up(k)
+
+        @pl.when(k < 2)
+        def _():
+            go_on(2, k + 1)
+
+        return 0
+
+    lax.fori_loop(0, 3, finish, 0)
     for s in range(1, 4):
         number(s).wait_send()
     for k in range(3):
@@ -732,21 +738,25 @@
 
     @pl.when((step >= N_TOK) & (step < 2 * N_TOK))
     def _():
-        part = jnp.zeros((1, slope.shape[1]), F32)
-        for m in range(0, tokens, MC):
-            rows = slice(m, m + MC)
+        def block(m, part):
+            rows = pl.ds(pl.multiple_of(m * MC, MC), MC)
             g = (dot(gffn[rows, :], wr[...], NT) * slope[rows, :].astype(F32)).astype(BF)
             gh[step - N_TOK, rows, :] = g
-            part = part + colsum(g.astype(F32))
             gs1_out[rows, :] = gs1_out[rows, :] + dot(g, we[...], NT)
-        hsum[...] = part
+            return part + colsum(g.astype(F32))
+
+        hsum[...] = lax.fori_loop(0, tokens // MC, block, jnp.zeros((1, slope.shape[1]), F32))
 
     @pl.when(step == 2 * N_TOK - 1)
     def _():
         second_norm_back(gs1_out, after, rstd, gains, shifts, gffn, sums)
-        for m in range(0, tokens, MC):
-            rows = slice(m, m + MC)
+
+        def block(m, _):
+            rows = pl.ds(pl.multiple_of(m * MC, MC), MC)
             gmixed_out[rows, :] = dot(gffn[rows, :], wo[...], NT).astype(BF)
+            return 0
+
+        lax.fori_loop(0, tokens // MC, block, 0)
 
     @pl.when(step >= 2 * N_TOK)
     def _():
@@ -754,9 +764,13 @@
         quarter = width // N_TAB
         rows = width // N_TOK
         wide = gh.shape[2]
-        for m in range(2):
+
+        def block(m, _):
             g = dot(low[...], gh[2 * n + m], TN).astype(BF)
-            put_rows(g, ga, gb, slice(m * wide, (m + 1) * wide), rows)
+            put_rows(g, ga, gb, pl.ds(pl.multiple_of(m * wide, wide), wide), rows)
+            return 0
+
+        lax.fori_loop(0, 2, block, 0)
         piece = gffn[:, pl.ds(pl.multiple_of(n * quarter, quarter), quarter)]
         g = dot(mixed[...], piece, TN).astype(BF)
         put_rows(g, ga, gb, slice(2 * wide, 2 * wide + quarter), rows)
@@ -889,15 +903,18 @@
 
     if summed:
         quarter = width // 4
-        for n in range(n_joined):
-
-            @pl.when(step == n_attn + n)
-            def _(n=n):
-                for m in range(3):
-                    third, at = (3 * n + m) // 4, (3 * n + m) % 4
-                    piece = gj[third, :, at * quarter : (at + 1) * quarter]
-                    g = dot(low[...], piece, TN).astype(BF)
-                    put_rows(g, ga, gb, slice(m * quarter, (m + 1) * quarter), width // 8)
+
+        @pl.when((step >= n_attn) & (step < n_attn + n_joined))
+        def _():
+            def block(m, _):
+                unit = 3 * (step - n_attn) + m
+                cols = pl.ds(pl.multiple_of((unit % 4) * quarter, quarter), quarter)
+                g = dot(low[...], gj[unit // 4, :, cols], TN).astype(BF)
+                at = pl.ds(pl.multiple_of(m * quarter, quarter), quarter)
+                put_rows(g, ga, gb, at, width // 8)
+                return 0
+
+            lax.fori_loop(0, 3, block, 0)
 
     @pl.when(step >= n_attn + n_joined)
     def _():
@@ -1163,7 +1180,6 @@
     summing.step(1, 2)
     small_step(3)
     relay(1, 1)
-    total[...] = total[...] + dot(pick(1), ring[0], NN)
     summing.step(2, 1)
     summing.step(1, 3)
     relay(2, 0)
@@ -1173,7 +1189,12 @@
     summing.step(3, 0)
     summing.step(3, 1)
     summing.step(2, 3)
-    total[...] = total[...] + dot(pick(2), ring[1], NN)
+
+    def add(k, _):
+        total[...] = total[...] + dot(pick(k + 1), ring[k], NN)
+        return 0
+
+    lax.fori_loop(0, 2, add, 0)
     last = pick(3)
     last_arrival(0)
     table.step(1, 0)

time: 373 us -> 376 us (level)
  no operation moved by 1% of the time
where the time goes in v8:
time: 376 us; the launch traced here: 370 us
  Pallas kernels  362 us (96%)
  local copies, waits for them, and re-layouts  5.71 us (2%)
    pallas_call x1, Pallas kernels, ffn_grads(): pl.pallas_call(ffn_grads_kernel, grid=(2 * N_TOK + N_TAB,), in_specs=[any...  74.3 us
    pallas_call x1, Pallas kernels, closing(): pl.pallas_call(closing_kernel, grid=(1,), in_specs=[full(cells.shape), fu...  74.1 us
    pallas_call x1, Pallas kernels, back(): pl.pallas_call(functools.partial(back_kernel, pages=pages, summed=summed)...  73.9 us
    pallas_call x1, Pallas kernels, spread(): pl.pallas_call(spread_kernel, grid=(1,), in_specs=[full(idx.shape), full(...  48.6 us
    pallas_call x1, Pallas kernels, ffn_fwd(): pl.pallas_call(ffn_fwd_kernel, grid=(tokens // tile,), in_specs=[rows, ro...  46.6 us
    pallas_call x1, Pallas kernels, attn_fwd(): pl.pallas_call(attn_fwd_kernel, grid=(pages, steps), in_specs=[blk] * 3,...  20 us
    pallas_call x1, Pallas kernels, embed(): pl.pallas_call(embed_kernel, grid=(pages,), in_specs=[rows, pl.BlockSpec(...  14.3 us
    pallas_call x1, Pallas kernels, write(): pl.pallas_call(write_kernel, grid=(8,), in_specs=[pl.BlockSpec(block, fir...  10 us

profile of v8, /device:TPU:0, one launch (start us, length us, event | category | flops | bytes accessed | tf_op | source)
XLA Modules:
  0.0 370.1 jit_solution(12965718063095288867)
XLA Ops:
  0.6 1.3 reshape.157.ci.refs_11_
  1.9 0.8 fusion
  2.8 0.6 pad_add_fusion.idx
  3.4 3.1 pad.6.table
  6.5 48.6 %spread.1 = (bf16[4,256,1024]{2,1,0:T(8,128)(2,1)}, s32[4,2,256]{2,1,0:T(2,128)}) custom-call(s32[4,2,256]{2,1,0:T(2,128)} %pad_add_fusion.idx, bf16[1024,1024]{1,0:T(8,128)(2,1)} %pad.6.table), custom_call_target="tpu_custom_call" | custom-call | flops 2147483648 | bytes 8388608 | tf_op jit(solution)/shard_map/spread/pallas_call | solution.py:433
  55.1 14.3 %embed_joined.1 = (bf16[1024,1024]{1,0:T(8,128)(2,1)}, bf16[1024,1024]{1,0:T(8,128)(2,1)}, bf16[1024,1024]{1,0:T(8,128)(2,1)}, f32[1024,1024]{1,0:T(8,128)}, bf1...) custom-call(bf16[1024,1024]{1,0:T(8,128)(2,1)} %emb.1, s32[2,1,512]{2,1,0:T(1,128)} %reshape.157.ci.refs_11_, ...), custom_call_target="tpu_custom_call" | custom-call | flops 6442450944 | bytes 27262976 | tf_op jit(solution)/shard_map/embed_joined/pallas_call | solution.py:141
  69.5 20.0 %attention.1 = (bf16[1024,1024]{1,0:T(8,128)(2,1)}, f32[2,4,4,512]{3,2,1,0:T(4,128)}) custom-call(bf16[1024,1024]{1,0:T(8,128)(2,1)} %get-tuple-element.58.q.refs_0_, bf16[1024,1024]{1,0:T(8,128)(2,1)} %get-tuple-element.59.k.refs_1_, bf16[1024,1024]{1,0:T(8,128)(2,1)} %get-tuple-element.60.v.refs_2_), custom_call_target="tpu_custom_call" | custom-call | flops 14000000000 | bytes 8388608 | tf_op jit(solution)/shard_map/attention/pallas_call | solution.py:488
  89.5 46.6 %ffn_forward.1 = (bf16[1024,1024]{1,0:T(8,128)(2,1)}, f32[1024,1024]{1,0:T(8,128)}, bf16[1024,1024]{1,0:T(8,128)(2,1)}, f32[1024,1]{1,0:T(8,128)}, bf16[1024,409...) custom-call(bf16[1024,1024]{1,0:T(8,128)(2,1)} %get-tuple-element.61, ...), custom_call_target="tpu_custom_call" | custom-call | flops 19327352832 | bytes 62914560 | tf_op jit(solution)/shard_map/ffn_forward/pallas_call | solution.py:590
  136.1 74.3 %ffn_backward_grads.1 = (f32[1024,1024]{1,0:T(8,128)}, bf16[1024,1024]{1,0:T(8,128)(2,1)}, f32[1,4096]{1,0:T(1,128)}, f32[3,1024]{1,0:T(4,128)}, bf16[2,4,4,64,1...) custom-call(bf16[1024,1024]{1,0:T(8,128)(2,1)} %get-tuple-element.64.gffn_in, ...), custom_call_target="tpu_custom_call" | custom-call | flops 38654705664 | bytes 62914560 | tf_op jit(solution)/shard_map/ffn_backward_grads/pallas_call | solution.py:805
  210.4 73.9 %attention_joined_embed_back.1 = (f32[1024,1024]{1,0:T(8,128)}, bf16[256,1024]{1,0:T(8,128)(2,1)}, f32[2,1024]{1,0:T(2,128)}, f32[2,1024]{1,0:T(2,128)}, bf16[2,...) custom-call(bf16[1024,1024]{1,0:T(8,128)(2,1)} %get-tuple-element.58.q.refs_0_, ...), custom_call_target="tpu_custom_call" | custom-call | flops 70000001024 | bytes 41943040 | tf_op jit(solution)/shard_map/attention_joined_embed_back/pallas_call | solution.py:986
  284.4 74.1 %closing.1 = (bf16[2,2,2,2,2,128,256]{6,5,4,3,2,1,0:T(8,128)(2,1)}, f32[2,64,768]{2,1,0:T(8,128)}, f32[14,1024]{1,0:T(8,128)}) custom-call(bf16[256,1024]{1,0:T(8,128)(2,1)} %get-tuple-element.78.cells, s32[4,2,256]{2,1,0:T(2,128)} %get-tuple-element.79.idx, f32[2,1024]{1,0:T(2,128)} %get-tuple-element.80.sums0, f32[3,1024]{1,0:T(4,128)} %get-tuple-element.81.sums1, ...), custom_call_target="tpu_custom_call" | custom-call | flops 2147483648 | bytes 25165824 | tf_op jit(solution)/shard_map/closing/pallas_call | solution.py:1233
  358.5 10.0 %write.1 = (f32[8008,128]{1,0:T(8,128)}, f32[1024,1024]{1,0:T(8,128)}, f32[512,256]{1,0:T(8,128)}, f32[128,1024]{1,0:T(8,128)}, f32[128,256]{1,0:T(8,128)}, /*in...) custom-call(bf16[2,2,2,2,2,128,256]{6,5,4,3,2,1,0:T(8,128)(2,1)} %get-tupl, ...), custom_call_target="tpu_custom_call" | custom-call | bytes 16777216 | tf_op jit(solution)/shard_map/write/pallas_call | solution.py:1309
  368.5 1.3 copy.28
  (2 shorter events, 0.0 us)

commit v9 on v8

--- a/solution.py
+++ b/solution.py
@@ -509,15 +509,15 @@
     def pick(x, h):
         return jnp.where(low_half, x, zero) if h == 0 else jnp.where(low_half, zero, x)
 
-    for p in range(HP // 2):
-        cols = slice(p * pair, (p + 1) * pair)
+    def pair_of_heads(p, _):
+        cols = pl.ds(pl.multiple_of(p * pair, pair), pair)
         qp, kp, vp, op, gp = q[:, cols], k[:, cols], v[:, cols], mixed[:, cols], go[:, cols]
         kt = kp.T
         prod_t = (op.astype(F32) * gp.astype(F32)).T
         dq_t, dk, dv = [], None, None
         for h in range(2):
             st = dot(pick(kp, h), qp, NT)
-            probs = jnp.exp2((st - lse[0, 0, 2 * p + h : 2 * p + h + 1, :]) * LOG2E)
+            probs = jnp.exp2((st - lse[0, 0, pl.ds(2 * p + h, 1), :]) * LOG2E)
             dv_h = dot(probs.astype(BF), pick(gp, h), NN)
             dpt = dot(pick(vp, h), gp, NT)
             delta = colsum(prod_t[h * HEAD_DIM : (h + 1) * HEAD_DIM])
@@ -528,6 +528,9 @@
             dk = dk_h if dk is None else dk + dk_h
         dq = (jnp.concatenate(dq_t, axis=0).T.astype(BF).astype(F32) * SCALE).astype(BF)
         put(p * pair, pair, dq, dk.astype(BF), dv.astype(BF))
+        return 0
+
+    lax.fori_loop(0, HP // 2, pair_of_heads, 0)
 
 
 FC = 512
@@ -738,14 +741,14 @@
 
     @pl.when((step >= N_TOK) & (step < 2 * N_TOK))
     def _():
-        def block(m, part):
-            rows = pl.ds(pl.multiple_of(m * MC, MC), MC)
+        part = jnp.zeros((1, slope.shape[1]), F32)
+        for m in range(0, tokens, MC):
+            rows = slice(m, m + MC)
             g = (dot(gffn[rows, :], wr[...], NT) * slope[rows, :].astype(F32)).astype(BF)
             gh[step - N_TOK, rows, :] = g
+            part = part + colsum(g.astype(F32))
             gs1_out[rows, :] = gs1_out[rows, :] + dot(g, we[...], NT)
-            return part + colsum(g.astype(F32))
-
-        hsum[...] = lax.fori_loop(0, tokens // MC, block, jnp.zeros((1, slope.shape[1]), F32))
+        hsum[...] = part
 
     @pl.when(step == 2 * N_TOK - 1)
     def _():
@@ -1264,12 +1267,13 @@
     lanes = table.shape[1]
     for n, piece in enumerate((a, b)):
         for u in range(2):
-            value = piece[0, u, 0, 0, 0].astype(F32)
-            for k in range(wide // lanes):
-                row = ((2 * u + n) * wide) // lanes + k
-                table[pl.ds(row, BLOCK, stride=4 * wide // lanes), :] = value[
-                    :, k * lanes : (k + 1) * lanes
-                ]
+            for c in range(2):
+                value = piece[0, u, c, 0, 0].astype(F32)
+                for k in range(wide // lanes):
+                    row = c * BLOCK * (4 * wide // lanes) + ((2 * u + n) * wide) // lanes + k
+                    table[pl.ds(row, BLOCK, stride=4 * wide // lanes), :] = value[
+                        :, k * lanes : (k + 1) * lanes
+                    ]
     embed_out[...] = embed[...]
 
     @pl.when(pl.program_id(0) == 0)
@@ -1293,9 +1297,9 @@
     wide = done.shape[6]
     width = 4 * wide
     tokens = embed.shape[0]
-    block = (1, 2, 1, 1, 1, BLOCK, wide)
-    first = lambda i: (0, 0, i % 2, (i // 2) % 2, i // 4, 0, 0)
-    second = lambda i: (1, 0, i % 2, i // 4, (i // 2) % 2, 0, 0)
+    block = (1, 2, 2, 1, 1, BLOCK, wide)
+    first = lambda i: (0, 0, 0, i % 2, i // 2, 0, 0)
+    second = lambda i: (1, 0, 0, i // 2, i % 2, 0, 0)
     rows = 2 * expand_sum.shape[1]
     cols = ff // N_TAB
     f32 = lambda *n: jax.ShapeDtypeStruct(n, F32)
@@ -1305,13 +1309,13 @@
         f32(3, width), f32(3, width), f32(4, width), f32(ff // width, width),
     ]
     lanes = 128
-    part = pl.BlockSpec((tokens // 8, width), lambda i: (i, 0))
+    part = pl.BlockSpec((tokens // 4, width), lambda i: (i, 0))
     table, *rest = pl.pallas_call(
         write_kernel,
-        grid=(8,),
+        grid=(4,),
         in_specs=[pl.BlockSpec(block, first), pl.BlockSpec(block, second), part]
         + [full(v.shape) for v in (reduce_sum, expand_sum, joined_sum, small)],
-        out_specs=[pl.BlockSpec((BLOCK * width // lanes, lanes), lambda i: (i, 0)), part]
+        out_specs=[pl.BlockSpec((2 * BLOCK * width // lanes, lanes), lambda i: (i, 0)), part]
         + [full(v.shape) for v in shapes],
         out_shape=[f32(table_rows * width // lanes, lanes), f32(tokens, width)] + shapes,
         compiler_params=params(),

time: 376 us -> 367 us (0.976); the launches traced: 370 us -> 367 us
  no operation moved by 1% of the time
where the time goes in v9:
time: 367 us
  Pallas kernels  359 us (98%)
  local copies, waits for them, and re-layouts  5.71 us (2%)
    pallas_call x1, Pallas kernels, back(): pl.pallas_call(functools.partial(back_kernel, pages=pages, summed=summed)...  74.7 us
    pallas_call x1, Pallas kernels, closing(): pl.pallas_call(closing_kernel, grid=(1,), in_specs=[full(cells.shape), fu...  74.2 us
    pallas_call x1, Pallas kernels, ffn_grads(): pl.pallas_call(ffn_grads_kernel, grid=(2 * N_TOK + N_TAB,), in_specs=[any...  72.5 us
    pallas_call x1, Pallas kernels, spread(): pl.pallas_call(spread_kernel, grid=(1,), in_specs=[full(idx.shape), full(...  48.6 us
    pallas_call x1, Pallas kernels, ffn_fwd(): pl.pallas_call(ffn_fwd_kernel, grid=(tokens // tile,), in_specs=[rows, ro...  46.5 us
    pallas_call x1, Pallas kernels, attn_fwd(): pl.pallas_call(attn_fwd_kernel, grid=(pages, steps), in_specs=[blk] * 3,...  20 us
    pallas_call x1, Pallas kernels, embed(): pl.pallas_call(embed_kernel, grid=(pages,), in_specs=[rows, pl.BlockSpec(...  14.3 us
    pallas_call x1, Pallas kernels, write(): pl.pallas_call(write_kernel, grid=(4,), in_specs=[pl.BlockSpec(block, fir...  7.99 us

profile of v9, /device:TPU:0, one launch (start us, length us, event | category | flops | bytes accessed | tf_op | source)
XLA Modules:
  0.0 366.7 jit_solution(17237442717318706446)
XLA Ops:
  0.6 1.3 reshape.157.ci.refs_11_
  1.9 0.8 fusion
  2.8 0.6 pad_add_fusion.idx
  3.4 3.1 pad.6.table
  6.5 48.6 %spread.1 = (bf16[4,256,1024]{2,1,0:T(8,128)(2,1)}, s32[4,2,256]{2,1,0:T(2,128)}) custom-call(s32[4,2,256]{2,1,0:T(2,128)} %pad_add_fusion.idx, bf16[1024,1024]{1,0:T(8,128)(2,1)} %pad.6.table), custom_call_target="tpu_custom_call" | custom-call | flops 2147483648 | bytes 8388608 | tf_op jit(solution)/shard_map/spread/pallas_call | solution.py:433
  55.1 14.3 %embed_joined.1 = (bf16[1024,1024]{1,0:T(8,128)(2,1)}, bf16[1024,1024]{1,0:T(8,128)(2,1)}, bf16[1024,1024]{1,0:T(8,128)(2,1)}, f32[1024,1024]{1,0:T(8,128)}, bf1...) custom-call(bf16[1024,1024]{1,0:T(8,128)(2,1)} %emb.1, s32[2,1,512]{2,1,0:T(1,128)} %reshape.157.ci.refs_11_, ...), custom_call_target="tpu_custom_call" | custom-call | flops 6442450944 | bytes 27262976 | tf_op jit(solution)/shard_map/embed_joined/pallas_call | solution.py:141
  69.5 20.0 %attention.1 = (bf16[1024,1024]{1,0:T(8,128)(2,1)}, f32[2,4,4,512]{3,2,1,0:T(4,128)}) custom-call(bf16[1024,1024]{1,0:T(8,128)(2,1)} %get-tuple-element.58.q.refs_0_, bf16[1024,1024]{1,0:T(8,128)(2,1)} %get-tuple-element.59.k.refs_1_, bf16[1024,1024]{1,0:T(8,128)(2,1)} %get-tuple-element.60.v.refs_2_), custom_call_target="tpu_custom_call" | custom-call | flops 14000000000 | bytes 8388608 | tf_op jit(solution)/shard_map/attention/pallas_call | solution.py:488
  89.5 46.5 %ffn_forward.1 = (bf16[1024,1024]{1,0:T(8,128)(2,1)}, f32[1024,1024]{1,0:T(8,128)}, bf16[1024,1024]{1,0:T(8,128)(2,1)}, f32[1024,1]{1,0:T(8,128)}, bf16[1024,409...) custom-call(bf16[1024,1024]{1,0:T(8,128)(2,1)} %get-tuple-element.61, ...), custom_call_target="tpu_custom_call" | custom-call | flops 19327352832 | bytes 62914560 | tf_op jit(solution)/shard_map/ffn_forward/pallas_call | solution.py:593
  136.0 72.5 %ffn_backward_grads.1 = (f32[1024,1024]{1,0:T(8,128)}, bf16[1024,1024]{1,0:T(8,128)(2,1)}, f32[1,4096]{1,0:T(1,128)}, f32[3,1024]{1,0:T(4,128)}, bf16[2,4,4,64,1...) custom-call(bf16[1024,1024]{1,0:T(8,128)(2,1)} %get-tuple-element.64.gffn_in, ...), custom_call_target="tpu_custom_call" | custom-call | flops 38654705664 | bytes 62914560 | tf_op jit(solution)/shard_map/ffn_backward_grads/pallas_call | solution.py:808
  208.5 74.7 %attention_joined_embed_back.1 = (f32[1024,1024]{1,0:T(8,128)}, bf16[256,1024]{1,0:T(8,128)(2,1)}, f32[2,1024]{1,0:T(2,128)}, f32[2,1024]{1,0:T(2,128)}, bf16[2,...) custom-call(bf16[1024,1024]{1,0:T(8,128)(2,1)} %get-tuple-element.58.q.refs_0_, ...), custom_call_target="tpu_custom_call" | custom-call | flops 70000001024 | bytes 41943040 | tf_op jit(solution)/shard_map/attention_joined_embed_back/pallas_call | solution.py:989
  283.2 74.2 %closing.1 = (bf16[2,2,2,2,2,128,256]{6,5,4,3,2,1,0:T(8,128)(2,1)}, f32[2,64,768]{2,1,0:T(8,128)}, f32[14,1024]{1,0:T(8,128)}) custom-call(bf16[256,1024]{1,0:T(8,128)(2,1)} %get-tuple-element.78.cells, s32[4,2,256]{2,1,0:T(2,128)} %get-tuple-element.79.idx, f32[2,1024]{1,0:T(2,128)} %get-tuple-element.80.sums0, f32[3,1024]{1,0:T(4,128)} %get-tuple-element.81.sums1, ...), custom_call_target="tpu_custom_call" | custom-call | flops 2147483648 | bytes 25165824 | tf_op jit(solution)/shard_map/closing/pallas_call | solution.py:1236
  357.4 8.0 %write.1 = (f32[8008,128]{1,0:T(8,128)}, f32[1024,1024]{1,0:T(8,128)}, f32[512,256]{1,0:T(8,128)}, f32[128,1024]{1,0:T(8,128)}, f32[128,256]{1,0:T(8,128)}, /*in...) custom-call(bf16[2,2,2,2,2,128,256]{6,5,4,3,2,1,0:T(8,128)(2,1)} %get-tupl, ...), custom_call_target="tpu_custom_call" | custom-call | bytes 16777216 | tf_op jit(solution)/shard_map/write/pallas_call | solution.py:1313
  365.4 1.3 copy.28
  (2 shorter events, 0.0 us)

commit v10 on v9

--- a/solution.py
+++ b/solution.py
@@ -703,9 +703,9 @@
 
 
 def ffn_grads_kernel(
-    gffn_in, gs2_in, after, rstd, low, mixed, wo, gains, shifts, act, slope, wr, we,
+    gffn_in, gs2_in, after_in, rstd, low_in, mixed_in, wo_in, gains, shifts, act, slope, wr, we,
     gs1_out, gmixed_out, hsum, sums, ga, gb, reduce_out,
-    gffn, gh, local, *scratch,
+    gffn, gh, after, low, mixed, wo, local, *scratch,
 ):
     step, last = pl.program_id(0), pl.num_programs(0) - 1
     tokens, width = after.shape
@@ -713,18 +713,25 @@
     both = scratch[0]
     z = lax.axis_index("tab")
     first = pltpu.make_async_copy(gffn_in, gffn, local.at[0])
-    later = pltpu.make_async_copy(gs2_in, gs1_out, local.at[1])
+    later = [
+        pltpu.make_async_copy(src, dst, local.at[1 + n])
+        for n, (src, dst) in enumerate(
+            ((gs2_in, gs1_out), (after_in, after), (wo_in, wo), (low_in, low), (mixed_in, mixed))
+        )
+    ]
 
     @pl.when(step == 0)
     def _():
         first.start()
-        later.start()
+        for copy in later:
+            copy.start()
         meet(summing.devices())
         first.wait()
 
     @pl.when(step == N_TOK)
     def _():
-        later.wait()
+        for copy in later:
+            copy.wait()
 
     summing.run(step, FFN_PLAN)
 
@@ -808,8 +815,8 @@
     return pl.pallas_call(
         ffn_grads_kernel,
         grid=(2 * N_TOK + N_TAB,),
-        in_specs=[anywhere, anywhere, whole, full((tokens, 1)), whole, whole]
-        + [full(a.shape) for a in (wo, gains, shifts)]
+        in_specs=[anywhere, anywhere, anywhere, full((tokens, 1)), anywhere, anywhere, anywhere]
+        + [full(a.shape) for a in (gains, shifts)]
         + [
             pl.BlockSpec((tokens, wide), act_block),
             pl.BlockSpec((tokens, wide), lambda s: (0, back(s))),
@@ -828,7 +835,9 @@
             jax.ShapeDtypeStruct((2, rows, cols), F32),
         ],
         scratch_shapes=[
-            pltpu.VMEM((tokens, width), BF), pltpu.VMEM((N_TOK, tokens, wide), BF), dma((2,)),
+            pltpu.VMEM((tokens, width), BF), pltpu.VMEM((N_TOK, tokens, wide), BF),
+            pltpu.VMEM((tokens, width), F32), pltpu.VMEM((tokens, width), BF),
+            pltpu.VMEM((tokens, width), BF), pltpu.VMEM(wo.shape, BF), dma((6,)),
             part(2, 2, 4, 4), part(2, 4, 4), part(2, 4, 2), part(2, 4), part(2, 3),
             dma((STAGES, 2, 4)), dma((STAGES, 2, 4)),
         ],
@@ -856,16 +865,16 @@
 
 
 def back_kernel(*refs, pages, summed):
-    q, k, v, mixed, go, lse, low, gs1, w, normed, rstd, ci, gains, shifts = refs[:14]
+    q, k, v, mixed, go, lse, low_in, gs1, w_in, normed, rstd, ci, gains, shifts = refs[:14]
     refs = refs[14:]
     grads, refs = refs[: 2 * summed], refs[2 * summed :]
     out, cells, sums0, sums_qv = refs[:4]
     refs = refs[4:]
     if summed:
-        ga, gb, summed_out, gj = refs[:4]
-        summing = Summing(grads, summed_out, refs[4:])
+        ga, gb, summed_out, gj, low, w, local = refs[:7]
+        summing = Summing(grads, summed_out, refs[7:])
     else:
-        gj_out, gj = refs
+        gj_out, gj, low, w, local = refs
     step = pl.program_id(0)
     width = gs1.shape[1]
     length = q.shape[0]
@@ -873,6 +882,20 @@
     wide = HP * HEAD_DIM
     n_attn = groups * pages
     n_joined = 4 if summed else 0
+    loads = [
+        pltpu.make_async_copy(low_in, low, local.at[0]),
+        pltpu.make_async_copy(w_in, w, local.at[1]),
+    ]
+
+    @pl.when(step == 0)
+    def _():
+        for copy in loads:
+            copy.start()
+
+    @pl.when(step == n_attn)
+    def _():
+        for copy in loads:
+            copy.wait()
 
     if summed:
 
@@ -992,9 +1015,9 @@
         in_specs=[blk] * 5
         + [
             pl.BlockSpec((1, 1, HP, length), lambda s: (at(s) % pages, at(s) // pages, 0, 0)),
-            full(low.shape),
+            pl.BlockSpec(memory_space=pl.ANY),
             rows,
-            full(w.shape),
+            pl.BlockSpec(memory_space=pl.ANY),
             rows,
             pl.BlockSpec((length, 1), lambda s: (page(s), 0)),
             pl.BlockSpec((1, 1, length), lambda s: (page(s), 0, 0)),
@@ -1004,7 +1027,11 @@
         + more_in,
         out_specs=out_specs + more_out,
         out_shape=out_shape + more_shape,
-        scratch_shapes=[pltpu.VMEM(whole_gj, BF)] + more_scratch,
+        scratch_shapes=[
+            pltpu.VMEM(whole_gj, BF), pltpu.VMEM(low.shape, BF), pltpu.VMEM(w.shape, BF),
+            pltpu.SemaphoreType.DMA((2,)),
+        ]
+        + more_scratch,
         compiler_params=params(**more),
         cost_estimate=cost(70e9, 40 << 20, pages * HEADS * length * length),
         name="attention_joined_embed_back",

time: 367 us -> 363 us (0.989)
  Pallas kernels: 359 us -> 354 us
where the time goes in v10:
time: 363 us; the launch traced here: 362 us
  Pallas kernels  354 us (98%)
  local copies, waits for them, and re-layouts  5.71 us (2%)
    pallas_call x1, Pallas kernels, closing(): pl.pallas_call(closing_kernel, grid=(1,), in_specs=[full(cells.shape), fu...  74.1 us
    pallas_call x1, Pallas kernels, back(): pl.pallas_call(functools.partial(back_kernel, pages=pages, summed=summed)...  71.3 us
    pallas_call x1, Pallas kernels, ffn_grads(): pl.pallas_call(ffn_grads_kernel, grid=(2 * N_TOK + N_TAB,), in_specs=[any...  71.3 us
    pallas_call x1, Pallas kernels, spread(): pl.pallas_call(spread_kernel, grid=(1,), in_specs=[full(idx.shape), full(...  48.6 us
    pallas_call x1, Pallas kernels, ffn_fwd(): pl.pallas_call(ffn_fwd_kernel, grid=(tokens // tile,), in_specs=[rows, ro...  46.5 us
    pallas_call x1, Pallas kernels, attn_fwd(): pl.pallas_call(attn_fwd_kernel, grid=(pages, steps), in_specs=[blk] * 3,...  20 us
    pallas_call x1, Pallas kernels, embed(): pl.pallas_call(embed_kernel, grid=(pages,), in_specs=[rows, pl.BlockSpec(...  14.3 us
    pallas_call x1, Pallas kernels, write(): pl.pallas_call(write_kernel, grid=(4,), in_specs=[pl.BlockSpec(block, fir...  7.99 us

profile of v10, /device:TPU:0, one launch (start us, length us, event | category | flops | bytes accessed | tf_op | source)
XLA Modules:
  0.0 362.1 jit_solution(694088016380512419)
XLA Ops:
  0.6 1.3 reshape.157.ci.refs_11_
  1.9 0.8 fusion
  2.8 0.6 pad_add_fusion.idx
  3.4 3.1 pad.6.table
  6.5 48.6 %spread.1 = (bf16[4,256,1024]{2,1,0:T(8,128)(2,1)}, s32[4,2,256]{2,1,0:T(2,128)}) custom-call(s32[4,2,256]{2,1,0:T(2,128)} %pad_add_fusion.idx, bf16[1024,1024]{1,0:T(8,128)(2,1)} %pad.6.table), custom_call_target="tpu_custom_call" | custom-call | flops 2147483648 | bytes 8388608 | tf_op jit(solution)/shard_map/spread/pallas_call | solution.py:433
  55.1 14.3 %embed_joined.1 = (bf16[1024,1024]{1,0:T(8,128)(2,1)}, bf16[1024,1024]{1,0:T(8,128)(2,1)}, bf16[1024,1024]{1,0:T(8,128)(2,1)}, f32[1024,1024]{1,0:T(8,128)}, bf1...) custom-call(bf16[1024,1024]{1,0:T(8,128)(2,1)} %emb.1, s32[2,1,512]{2,1,0:T(1,128)} %reshape.157.ci.refs_11_, ...), custom_call_target="tpu_custom_call" | custom-call | flops 6442450944 | bytes 27262976 | tf_op jit(solution)/shard_map/embed_joined/pallas_call | solution.py:141
  69.5 20.0 %attention.1 = (bf16[1024,1024]{1,0:T(8,128)(2,1)}, f32[2,4,4,512]{3,2,1,0:T(4,128)}) custom-call(bf16[1024,1024]{1,0:T(8,128)(2,1)} %get-tuple-element.58.q.refs_0_, bf16[1024,1024]{1,0:T(8,128)(2,1)} %get-tuple-element.59.k.refs_1_, bf16[1024,1024]{1,0:T(8,128)(2,1)} %get-tuple-element.60.v.refs_2_), custom_call_target="tpu_custom_call" | custom-call | flops 14000000000 | bytes 8388608 | tf_op jit(solution)/shard_map/attention/pallas_call | solution.py:488
  89.5 46.5 %ffn_forward.1 = (bf16[1024,1024]{1,0:T(8,128)(2,1)}, f32[1024,1024]{1,0:T(8,128)}, bf16[1024,1024]{1,0:T(8,128)(2,1)}, f32[1024,1]{1,0:T(8,128)}, bf16[1024,409...) custom-call(bf16[1024,1024]{1,0:T(8,128)(2,1)} %get-tuple-element.61, ...), custom_call_target="tpu_custom_call" | custom-call | flops 19327352832 | bytes 62914560 | tf_op jit(solution)/shard_map/ffn_forward/pallas_call | solution.py:593
  136.0 71.3 %ffn_backward_grads.1 = (f32[1024,1024]{1,0:T(8,128)}, bf16[1024,1024]{1,0:T(8,128)(2,1)}, f32[1,4096]{1,0:T(1,128)}, f32[3,1024]{1,0:T(4,128)}, bf16[2,4,4,64,1...) custom-call(bf16[1024,1024]{1,0:T(8,128)(2,1)} %get-tuple-element.64.gffn_in, ...), custom_call_target="tpu_custom_call" | custom-call | flops 38654705664 | bytes 62914560 | tf_op jit(solution)/shard_map/ffn_backward_grads/pallas_call | solution.py:815
  207.3 71.3 %attention_joined_embed_back.1 = (f32[1024,1024]{1,0:T(8,128)}, bf16[256,1024]{1,0:T(8,128)(2,1)}, f32[2,1024]{1,0:T(2,128)}, f32[2,1024]{1,0:T(2,128)}, bf16[2,...) custom-call(bf16[1024,1024]{1,0:T(8,128)(2,1)} %get-tuple-element.58.q.refs_0_, ...), custom_call_target="tpu_custom_call" | custom-call | flops 70000001024 | bytes 41943040 | tf_op jit(solution)/shard_map/attention_joined_embed_back/pallas_call | solution.py:1012
  278.7 74.1 %closing.1 = (bf16[2,2,2,2,2,128,256]{6,5,4,3,2,1,0:T(8,128)(2,1)}, f32[2,64,768]{2,1,0:T(8,128)}, f32[14,1024]{1,0:T(8,128)}) custom-call(bf16[256,1024]{1,0:T(8,128)(2,1)} %get-tuple-element.78.cells, s32[4,2,256]{2,1,0:T(2,128)} %get-tuple-element.79.idx, f32[2,1024]{1,0:T(2,128)} %get-tuple-element.80.sums0, f32[3,1024]{1,0:T(4,128)} %get-tuple-element.81.sums1, ...), custom_call_target="tpu_custom_call" | custom-call | flops 2147483648 | bytes 25165824 | tf_op jit(solution)/shard_map/closing/pallas_call | solution.py:1263
  352.8 8.0 %write.1 = (f32[8008,128]{1,0:T(8,128)}, f32[1024,1024]{1,0:T(8,128)}, f32[512,256]{1,0:T(8,128)}, f32[128,1024]{1,0:T(8,128)}, f32[128,256]{1,0:T(8,128)}, /*in...) custom-call(bf16[2,2,2,2,2,128,256]{6,5,4,3,2,1,0:T(8,128)(2,1)} %get-tupl, ...), custom_call_target="tpu_custom_call" | custom-call | bytes 16777216 | tf_op jit(solution)/shard_map/write/pallas_call | solution.py:1340
  360.8 1.3 copy.28
  (2 shorter events, 0.0 us)

commit v11 on v10

--- a/solution.py
+++ b/solution.py
@@ -540,9 +540,20 @@
 
 
 def ffn_fwd_kernel(
-    mixed, normed, wo, we, wr, hb, bias, gains, shifts, cot,
+    mixed, normed, wo, we_in, wr_in, hb, bias, gains, shifts, cot,
     out, after_out, low_out, rstd_out, act_out, slope_out, gs2_out, gffn_out, sums,
+    we, wr, local,
 ):
+    loads = [
+        pltpu.make_async_copy(we_in, we, local.at[0]),
+        pltpu.make_async_copy(wr_in, wr, local.at[1]),
+    ]
+
+    @pl.when(pl.program_id(0) == 0)
+    def _():
+        for copy in loads:
+            copy.start()
+
     ff = we.shape[1]
     attn_sum = normed[...] + (dot(mixed[...], wo[...], NN) + bias[2:3])
     xh, rstd = norm_stats(attn_sum)
@@ -552,6 +563,12 @@
     low = after.astype(BF)
     low_out[...] = low
     total = after + bias[3:4]
+
+    @pl.when(pl.program_id(0) == 0)
+    def _():
+        for copy in loads:
+            copy.wait()
+
     count = ff // FWD
     hidden = []
     for j in range(count + 1):
@@ -594,13 +611,18 @@
         ffn_fwd_kernel,
         grid=(tokens // tile,),
         in_specs=[rows, rows]
-        + [full(a.shape) for a in (wo, we, wr, hb, bias, gains, shifts)]
+        + [full(wo.shape)]
+        + [pl.BlockSpec(memory_space=pl.ANY)] * 2
+        + [full(a.shape) for a in (hb, bias, gains, shifts)]
         + [rows],
         out_specs=[rows, rows, rows, pl.BlockSpec((tile, 1), lambda i: (i, 0)), long, long, rows, rows]
         + [pl.BlockSpec((3, width), lambda i: (0, 0))],
         out_shape=[
             shape(BF), shape(F32), shape(BF), shape(F32, 1), shape(BF, ff), shape(BF, ff),
             shape(F32), shape(BF), jax.ShapeDtypeStruct((3, width), F32),
+        ],
+        scratch_shapes=[
+            pltpu.VMEM(we.shape, BF), pltpu.VMEM(wr.shape, BF), pltpu.SemaphoreType.DMA((2,)),
         ],
         compiler_params=params(),
         cost_estimate=cost(2 * tokens * width * (width + 2 * ff), 60 << 20, tokens * ff * 2),

time: 363 us -> 363 us (level)
  no operation moved by 1% of the time
where the time goes in v11:
time: 363 us
  Pallas kernels  355 us (98%)
  local copies, waits for them, and re-layouts  5.71 us (2%)
    pallas_call x1, Pallas kernels, closing(): pl.pallas_call(closing_kernel, grid=(1,), in_specs=[full(cells.shape), fu...  74.1 us
    pallas_call x1, Pallas kernels, ffn_grads(): pl.pallas_call(ffn_grads_kernel, grid=(2 * N_TOK + N_TAB,), in_specs=[any...  71.3 us
    pallas_call x1, Pallas kernels, back(): pl.pallas_call(functools.partial(back_kernel, pages=pages, summed=summed)...  71.3 us
    pallas_call x1, Pallas kernels, spread(): pl.pallas_call(spread_kernel, grid=(1,), in_specs=[full(idx.shape), full(...  48.6 us
    pallas_call x1, Pallas kernels, ffn_fwd(): pl.pallas_call(ffn_fwd_kernel, grid=(tokens // tile,), in_specs=[rows, ro...  47.3 us
    pallas_call x1, Pallas kernels, attn_fwd(): pl.pallas_call(attn_fwd_kernel, grid=(pages, steps), in_specs=[blk] * 3,...  20 us
    pallas_call x1, Pallas kernels, embed(): pl.pallas_call(embed_kernel, grid=(pages,), in_specs=[rows, pl.BlockSpec(...  14.3 us
    pallas_call x1, Pallas kernels, write(): pl.pallas_call(write_kernel, grid=(4,), in_specs=[pl.BlockSpec(block, fir...  7.99 us

profile of v11, /device:TPU:0, one launch (start us, length us, event | category | flops | bytes accessed | tf_op | source)
XLA Modules:
  0.0 362.9 jit_solution(10891098144166317358)
XLA Ops:
  0.6 1.3 reshape.157.ci.refs_11_
  1.9 0.8 fusion
  2.8 0.6 pad_add_fusion.idx
  3.4 3.1 pad.6.table
  6.5 48.6 %spread.1 = (bf16[4,256,1024]{2,1,0:T(8,128)(2,1)}, s32[4,2,256]{2,1,0:T(2,128)}) custom-call(s32[4,2,256]{2,1,0:T(2,128)} %pad_add_fusion.idx, bf16[1024,1024]{1,0:T(8,128)(2,1)} %pad.6.table), custom_call_target="tpu_custom_call" | custom-call | flops 2147483648 | bytes 8388608 | tf_op jit(solution)/shard_map/spread/pallas_call | solution.py:433
  55.1 14.3 %embed_joined.1 = (bf16[1024,1024]{1,0:T(8,128)(2,1)}, bf16[1024,1024]{1,0:T(8,128)(2,1)}, bf16[1024,1024]{1,0:T(8,128)(2,1)}, f32[1024,1024]{1,0:T(8,128)}, bf1...) custom-call(bf16[1024,1024]{1,0:T(8,128)(2,1)} %emb.1, s32[2,1,512]{2,1,0:T(1,128)} %reshape.157.ci.refs_11_, ...), custom_call_target="tpu_custom_call" | custom-call | flops 6442450944 | bytes 27262976 | tf_op jit(solution)/shard_map/embed_joined/pallas_call | solution.py:141
  69.5 20.0 %attention.1 = (bf16[1024,1024]{1,0:T(8,128)(2,1)}, f32[2,4,4,512]{3,2,1,0:T(4,128)}) custom-call(bf16[1024,1024]{1,0:T(8,128)(2,1)} %get-tuple-element.58.q.refs_0_, bf16[1024,1024]{1,0:T(8,128)(2,1)} %get-tuple-element.59.k.refs_1_, bf16[1024,1024]{1,0:T(8,128)(2,1)} %get-tuple-element.60.v.refs_2_), custom_call_target="tpu_custom_call" | custom-call | flops 14000000000 | bytes 8388608 | tf_op jit(solution)/shard_map/attention/pallas_call | solution.py:488
  89.5 47.3 %ffn_forward.1 = (bf16[1024,1024]{1,0:T(8,128)(2,1)}, f32[1024,1024]{1,0:T(8,128)}, bf16[1024,1024]{1,0:T(8,128)(2,1)}, f32[1024,1]{1,0:T(8,128)}, bf16[1024,409...) custom-call(bf16[1024,1024]{1,0:T(8,128)(2,1)} %get-tuple-element.61, ...), custom_call_target="tpu_custom_call" | custom-call | flops 19327352832 | bytes 62914560 | tf_op jit(solution)/shard_map/ffn_forward/pallas_call | solution.py:610
  136.8 71.3 %ffn_backward_grads.1 = (f32[1024,1024]{1,0:T(8,128)}, bf16[1024,1024]{1,0:T(8,128)(2,1)}, f32[1,4096]{1,0:T(1,128)}, f32[3,1024]{1,0:T(4,128)}, bf16[2,4,4,64,1...) custom-call(bf16[1024,1024]{1,0:T(8,128)(2,1)} %get-tuple-element.64.gffn_in, ...), custom_call_target="tpu_custom_call" | custom-call | flops 38654705664 | bytes 62914560 | tf_op jit(solution)/shard_map/ffn_backward_grads/pallas_call | solution.py:837
  208.2 71.3 %attention_joined_embed_back.1 = (f32[1024,1024]{1,0:T(8,128)}, bf16[256,1024]{1,0:T(8,128)(2,1)}, f32[2,1024]{1,0:T(2,128)}, f32[2,1024]{1,0:T(2,128)}, bf16[2,...) custom-call(bf16[1024,1024]{1,0:T(8,128)(2,1)} %get-tuple-element.58.q.refs_0_, ...), custom_call_target="tpu_custom_call" | custom-call | flops 70000001024 | bytes 41943040 | tf_op jit(solution)/shard_map/attention_joined_embed_back/pallas_call | solution.py:1034
  279.5 74.1 %closing.1 = (bf16[2,2,2,2,2,128,256]{6,5,4,3,2,1,0:T(8,128)(2,1)}, f32[2,64,768]{2,1,0:T(8,128)}, f32[14,1024]{1,0:T(8,128)}) custom-call(bf16[256,1024]{1,0:T(8,128)(2,1)} %get-tuple-element.78.cells, s32[4,2,256]{2,1,0:T(2,128)} %get-tuple-element.79.idx, f32[2,1024]{1,0:T(2,128)} %get-tuple-element.80.sums0, f32[3,1024]{1,0:T(4,128)} %get-tuple-element.81.sums1, ...), custom_call_target="tpu_custom_call" | custom-call | flops 2147483648 | bytes 25165824 | tf_op jit(solution)/shard_map/closing/pallas_call | solution.py:1285
  353.6 8.0 %write.1 = (f32[8008,128]{1,0:T(8,128)}, f32[1024,1024]{1,0:T(8,128)}, f32[512,256]{1,0:T(8,128)}, f32[128,1024]{1,0:T(8,128)}, f32[128,256]{1,0:T(8,128)}, /*in...) custom-call(bf16[2,2,2,2,2,128,256]{6,5,4,3,2,1,0:T(8,128)(2,1)} %get-tupl, ...), custom_call_target="tpu_custom_call" | custom-call | bytes 16777216 | tf_op jit(solution)/shard_map/write/pallas_call | solution.py:1362
  361.6 1.3 copy.28
  (2 shorter events, 0.0 us)
